TPU v7x, 128 devices: a whole 4x4x4 slice. The times are simulated.
128 devices in a mesh: level: 2 (over z_lo), subj: 8 (over y, core), gz: 8 (over z_hi, x).
Axes of the slice: x: 4, y: 4, z: 4 (z_hi: 2, z_lo: 2; z = z_hi * 2 + z_lo), core: 2. Of those that a mesh axis runs over, the one named last changes fastest.
Arguments:
- images: bfloat16 [16, 192, 192, 192], P('subj', 'gz'), may hold values from -6 to 6
- momenta: float32 [16, 96, 3, 96, 96], P('subj', 'gz'), may hold values from -18 to 18
- assign: int32 [16], replicated, may hold values from 0 to 15, as said below
Outputs:
- template: float32 [192, 192, 192], P('gz')
Inputs may be any that keep to these rules, and one draw needn't show every extreme that they name: assign is a permutation of 0 to 15 with assign[i] % 2 == i % 2 for every i.
All inputs are finite; a program needn't handle non-finite values.
Results may differ from a plain program's by a relative error of at most 0.00069.
Values may be sent and summed in bfloat16 or wider, within the bound.
No kernel may reach another device: no remote copies, remote signals or barrier semaphores. Data moves between devices by JAX's collectives and lax.ppermute only.
A program may use at most 128 MiB of HBM per device.

v0:
```python
import jax
import jax.numpy as jnp
import numpy as np
from jax import lax
from jax.experimental import pallas as pl
from jax.experimental.pallas import tpu as pltpu
from jax.sharding import PartitionSpec as P


F32 = jnp.float32
BF16 = jnp.bfloat16
HZ = 12
CY = 24
CZ = HZ // 2 + 2
CW = CY // 2 + 2
VR = CZ * CW
VROWS = 5 * VR
PROWS = 80
SCALE = 128.0


def lerp_table(fine):
    table = np.zeros((fine, fine // 2 + 2), np.float32)
    for row in range(fine):
        near = row // 2 + 1
        table[row, near] += 0.75
        table[row, near + 2 * (row % 2) - 1] += 0.25
    return table


def zy_table():
    return np.kron(lerp_table(HZ), lerp_table(CY))


def x_table(fine, slot):
    inner = lerp_table(fine)[:, 1:-1].T
    coarse = fine // 2
    table = np.zeros((256, 256), np.float32)
    for base in (0, 128):
        table[base : base + coarse, :128] = inner[:, :128]
        table[base : base + coarse, 128 + 64 * slot : 192 + 64 * slot] = inner[:, 128:]
    return table


def pack_plane(plane, put):
    count = plane.shape[1] // CY
    low = [plane[0][:, :128], plane[1][:, :128]]
    both = jnp.concatenate([plane[0][:, 128:], plane[1][:, 128:]], axis=1)
    parts = low + [both]
    row = lax.broadcasted_iota(jnp.int32, (8, 128), 0)
    for peer in range(count):
        start = CY * peer
        halo = jnp.zeros((8, 128), F32)
        for index, part in enumerate(parts):
            if peer > 0:
                halo = jnp.where(row == 2 * index, part[start - 1 : start], halo)
            if peer < count - 1:
                halo = jnp.where(row == 2 * index + 1, part[start + CY : start + CY + 1], halo)
        blocks = [part[start : start + CY] for part in parts] + [halo]
        put(peer, jnp.concatenate(blocks, axis=0))


GROUPS = ((0, 3), (3, 3), (6, 3), (9, 3))


def pack_kernel(info, images, *rest):
    outs = rest[:8]
    held, stage, sems, gone = rest[8:]
    level, me = info[0], info[1]
    loads = []
    for index, (first, count) in enumerate(GROUPS):
        rows = pl.ds(HZ * level + first, count)
        loads.append(
            pltpu.make_async_copy(
                images.at[:, rows], held.at[:, pl.ds(first, count)], sems.at[index]
            )
        )
    for copy in loads:
        copy.start()
    sent = []
    for index, (first, count) in enumerate(GROUPS):
        loads[index].wait()

        def step(z, carry):
            def put(peer, value):
                stage[peer, z] = value.astype(BF16)

            pack_plane(held[:, z].astype(F32), put)
            return carry

        lax.fori_loop(first, first + count, step, 0)
        for k, out in enumerate(outs):
            rows = pl.ds(first, count)
            copy = pltpu.make_async_copy(
                stage.at[me ^ k, rows], out.at[rows], gone.at[8 * index + k]
            )
            copy.start()
            sent.append(copy)
    for copy in sent:
        copy.wait()


def pack_images(info, images):
    hbm = pl.BlockSpec(memory_space=pl.ANY)
    return pl.pallas_call(
        pack_kernel,
        grid=(),
        in_specs=[pl.BlockSpec(memory_space=pltpu.SMEM), hbm],
        out_specs=[hbm] * 8,
        out_shape=[jax.ShapeDtypeStruct((HZ, PROWS, 128), BF16)] * 8,
        scratch_shapes=[
            pltpu.VMEM((2, HZ, 192, 192), BF16),
            pltpu.VMEM((8, HZ, PROWS, 128), BF16),
            pltpu.SemaphoreType.DMA((len(GROUPS),)),
            pltpu.SemaphoreType.DMA((8 * len(GROUPS),)),
        ],
        name="pack_images",
    )(info, images)


def blur_kernel(info, momenta, halo, other, *rest):
    outs = rest[:8]
    held, stage, tall, wide, third, piece, sems, gone = rest[8:]
    level, me = info[0], info[1]
    half = info[2] * 2 + level
    own = pltpu.make_async_copy(
        momenta.at[:, pl.ds(3 * level, 9)], held.at[:, pl.ds(3 - 3 * level, 9)], sems.at[0]
    )
    sides = [
        pltpu.make_async_copy(rows, held.at[j, pl.ds(9 * level, 3)], sems.at[1 + j])
        for j, rows in enumerate((halo, other))
    ]
    for copy in [own] + sides:
        copy.start()
    for held_rows in (tall, wide):
        held_rows[:, :8] = jnp.zeros((CZ, 8, 128), F32)
        held_rows[:, 104:] = jnp.zeros((CZ, 8, 128), F32)
    for copy in [own] + sides:
        copy.wait()
    first = (half > 0).astype(F32)
    last = (half < 15).astype(F32)
    spare = jnp.zeros((96, 32), F32)
    plane_lane = lax.broadcasted_iota(jnp.int32, (96, 128), 1)
    for subject, component in ((1, 0), (0, 0), (0, 1), (0, 2), (1, 1), (1, 2)):

        def row(r, carry, subject=subject, component=component):
            def m(t):
                return held[subject, r + t, component]

            z = (m(0) + m(4)) * 0.0625 + (m(1) + m(3)) * 0.25 + m(2) * 0.375
            z = z * jnp.where(r == 0, first, jnp.where(r == CZ - 1, last, 1.0))
            z = jnp.concatenate([z, spare], axis=1)

            def lane(k):
                return pltpu.roll(z, k % 128, 1)

            x = (lane(2) + lane(-2)) * 0.0625 + (lane(1) + lane(-1)) * 0.25 + z * 0.375
            tall[r, 8:104] = x
            y = (tall[r, 6:102] + tall[r, 10:106]) * 0.0625
            y += (tall[r, 7:103] + tall[r, 9:105]) * 0.25
            y += x * 0.375
            if (subject, component) == (1, 0):
                third[r] = y
            elif subject == 0:
                extra = pltpu.roll(third[r], 96 - 32 * component, 1)
                wide[r, 8:104] = jnp.where(plane_lane < 96, y, extra)
            else:
                wide[r, 8:104] = y
            return carry

        lax.fori_loop(0, CZ, row, 0, unroll=2)
        if (subject, component) == (1, 0):
            continue
        block = 2 * subject + component
        for peer in range(8):
            start = 8 + (CY // 2) * peer - 1
            for r in range(CZ):
                piece[CW * r : CW * (r + 1)] = wide[r, start : start + CW]
            stage[peer, VR * block : VR * (block + 1)] = piece[...].astype(BF16)
    sent = [
        pltpu.make_async_copy(stage.at[me ^ k], out, gone.at[k]) for k, out in enumerate(outs)
    ]
    for copy in sent:
        copy.start()
    for copy in sent:
        copy.wait()


def blur(info, momenta, halo, other):
    rows = VROWS
    return pl.pallas_call(
        blur_kernel,
        grid=(),
        in_specs=[
            pl.BlockSpec(memory_space=pltpu.SMEM),
            pl.BlockSpec(memory_space=pl.ANY),
            pl.BlockSpec(memory_space=pl.ANY),
            pl.BlockSpec(memory_space=pl.ANY),
        ],
        out_specs=[pl.BlockSpec(memory_space=pl.ANY)] * 8,
        out_shape=[jax.ShapeDtypeStruct((rows, 128), BF16)] * 8,
        scratch_shapes=[
            pltpu.VMEM((2, 12, 3, 96, 96), F32),
            pltpu.VMEM((8, rows, 128), BF16),
            pltpu.VMEM((CZ, 112, 128), F32),
            pltpu.VMEM((CZ, 112, 128), F32),
            pltpu.VMEM((CZ, 96, 128), F32),
            pltpu.VMEM((VR, 128), F32),
            pltpu.SemaphoreType.DMA((3,)),
            pltpu.SemaphoreType.DMA((8,)),
        ],
        name="blur_momenta",
    )(info, momenta, halo, other)


def edge_kernel(*refs):
    planes, below, above = refs[:8], refs[8], refs[9]
    low, high, sems, gone = refs[10:]
    copies = []
    for k, plane in enumerate(planes):
        copies.append(pltpu.make_async_copy(plane.at[0], low.at[k], sems.at[k]))
        copies.append(pltpu.make_async_copy(plane.at[HZ - 1], high.at[k], sems.at[8 + k]))
    for copy in copies:
        copy.start()
    for copy in copies:
        copy.wait()
    leaving = [
        pltpu.make_async_copy(low, below, gone.at[0]),
        pltpu.make_async_copy(high, above, gone.at[1]),
    ]
    for copy in leaving:
        copy.start()
    for copy in leaving:
        copy.wait()


def edges(planes):
    hbm = pl.BlockSpec(memory_space=pl.ANY)
    shape = (8, PROWS, 128)
    return pl.pallas_call(
        edge_kernel,
        grid=(),
        in_specs=[hbm] * 8,
        out_specs=[hbm] * 2,
        out_shape=[jax.ShapeDtypeStruct(shape, BF16)] * 2,
        scratch_shapes=[
            pltpu.VMEM(shape, BF16),
            pltpu.VMEM(shape, BF16),
            pltpu.SemaphoreType.DMA((16,)),
            pltpu.SemaphoreType.DMA((2,)),
        ],
        name="cut_edges",
    )(*planes)


def warp_kernel(info, assign, zy, x0, x1, *rest):
    planes, fields, below, above = rest[:8], rest[8:16], rest[16], rest[17]
    chunk, edge = rest[18:20]
    image, field, even, odd, acc, sems = rest[20:]
    level, me = info[0], info[1]
    copies = [
        pltpu.make_async_copy(below, image.at[:, 0], sems.at[16]),
        pltpu.make_async_copy(above, image.at[:, HZ + 1], sems.at[17]),
    ]
    for k in range(8):
        copies.append(
            pltpu.make_async_copy(planes[k], image.at[k, 1 : HZ + 1], sems.at[k])
        )
        copies.append(pltpu.make_async_copy(fields[k], field.at[k], sems.at[8 + k]))
    for copy in copies:
        copy.start()
    acc[...] = jnp.zeros_like(acc)
    for copy in copies:
        copy.wait()
    lane = lax.broadcasted_iota(jnp.int32, (CY, 128), 1)
    sub = lax.broadcasted_iota(jnp.int32, (CY, 128), 0)
    coarse_lane = lax.broadcasted_iota(jnp.int32, (VR, 128), 1)

    def neighbours(part):
        left0, left1, left2 = (pltpu.roll(p, 1, 1) for p in part)
        right0, right1, right2 = (pltpu.roll(p, 127, 1) for p in part)
        left2 = jnp.where(lane == 0, left0, jnp.where(lane == 64, pltpu.roll(part[1], 65, 1), left2))
        left0 = jnp.where(lane == 0, 0.0, left0)
        left1 = jnp.where(lane == 0, 0.0, left1)
        right0 = jnp.where(lane == 127, right2, right0)
        right1 = jnp.where(lane == 127, pltpu.roll(part[2], 63, 1), right1)
        right2 = jnp.where(lane % 64 == 63, 0.0, right2)
        return (left0, left1, left2), (right0, right1, right2)

    def interpolate(k, velocity):
        base = 2 * (me ^ k)
        slots = [(assign[base + j] // 2) ^ me for j in range(2)]
        stacked = [[], []]
        for c in range(3):
            parts = [field[slots[0], VR * c : VR * (c + 1)]]
            if c > 0:
                parts.append(field[slots[1], VR * (c + 2) : VR * (c + 3)])
            else:
                spread = [
                    pltpu.roll(
                        field[slots[1], VR * t : VR * (t + 1)].astype(F32), 32 * t + 32, 1
                    )
                    for t in range(3)
                ]
                third = jnp.where(
                    coarse_lane < 32, spread[0], jnp.where(coarse_lane < 64, spread[1], spread[2])
                )
                parts.append(third.astype(BF16))
            rough = jnp.dot(
                zy[...], jnp.concatenate(parts, axis=1), preferred_element_type=F32
            )
            high = rough.astype(BF16)
            low = (rough - high.astype(F32)).astype(BF16)
            for j in range(2):
                own = slice(128 * j, 128 * j + 128)
                stacked[j].append(jnp.concatenate([high[:, own], low[:, own]], axis=1))
        fine = [
            jnp.dot(jnp.concatenate(stacked[j], axis=0), table[...], preferred_element_type=F32)
            for j, table in enumerate((x0, x1))
        ]
        velocity[0] = fine[0][:, :128]
        velocity[1] = fine[1][:, :128]
        velocity[2] = fine[0][:, 128:] + fine[1][:, 128:]

    def apply(k, velocity):
        for z in range(HZ):
            before = image[k, z].astype(F32)
            centre = image[k, z + 1].astype(F32)
            after = image[k, z + 2].astype(F32)
            part = [centre[CY * b : CY * (b + 1)] for b in range(3)]
            halo = centre[3 * CY :]
            left, right = neighbours(part)
            warped = []
            for b in range(3):
                own = slice(CY * b, CY * (b + 1))
                up = jnp.where(sub == 0, halo[2 * b : 2 * b + 1], pltpu.roll(part[b], 1, 0))
                down = jnp.where(
                    sub == CY - 1, halo[2 * b + 1 : 2 * b + 2], pltpu.roll(part[b], CY - 1, 0)
                )

                def v(c):
                    start = HZ * CY * c + CY * z
                    return velocity[b, start : start + CY]

                push = v(0) * (right[b] - left[b]) + v(1) * (down - up)
                push += v(2) * (after[own] - before[own])
                warped.append(part[b] - 0.5 * push)
            rows = slice(CY * z, CY * (z + 1))
            acc[0, rows] += warped[0] + warped[1]
            acc[1, rows] += warped[2]

    interpolate(0, even)

    def turn(step, carry):
        interpolate(2 * step + 1, odd)
        apply(2 * step, even)
        interpolate(jnp.minimum(2 * step + 2, 7), even)
        apply(2 * step + 1, odd)
        return carry

    lax.fori_loop(0, 4, turn, 0)
    weight = SCALE / 16.0
    chunk[: HZ * CY] = pltpu.roll(acc[0] * weight, 64 * level, 1)
    wide = lax.broadcasted_iota(jnp.int32, (CY, 128), 1)

    def joined(z, other):
        one, two = (acc[1, pl.ds(pl.multiple_of(r * CY, 8), CY)] for r in (z, other))
        one = one + pltpu.roll(one, 64, 1)
        two = two + pltpu.roll(two, 64, 1)
        return jnp.where(wide < 64, one, two) * weight

    for z in range(HZ // 2):
        chunk[(HZ + z) * CY : (HZ + z + 1) * CY] = joined(z, z + HZ // 2)
    outer = (HZ - 2) * level
    rim = acc[0, pl.ds(pl.multiple_of(outer * CY, 8), 2 * CY)] * weight
    edge[: 2 * CY] = pltpu.roll(rim, 64 - 64 * level, 1)
    edge[2 * CY :] = joined(outer, outer + 1)


def warp(info, assign, planes, fields, below, above):
    tables = [
        jnp.asarray(t, BF16) for t in (zy_table(), x_table(192, 0), x_table(192, 1))
    ]
    vmem = pl.BlockSpec(memory_space=pltpu.VMEM)
    smem = pl.BlockSpec(memory_space=pltpu.SMEM)
    hbm = pl.BlockSpec(memory_space=pl.ANY)
    return pl.pallas_call(
        warp_kernel,
        grid=(),
        in_specs=[smem, smem, vmem, vmem, vmem] + [hbm] * 18,
        out_specs=[vmem] * 2,
        out_shape=[
            jax.ShapeDtypeStruct((HZ * CY * 3 // 2, 128), F32),
            jax.ShapeDtypeStruct((3 * CY, 128), F32),
        ],
        scratch_shapes=[
            pltpu.VMEM((8, HZ + 2, PROWS, 128), BF16),
            pltpu.VMEM((8, VROWS, 128), BF16),
            pltpu.VMEM((3, 3 * HZ * CY, 128), F32),
            pltpu.VMEM((3, 3 * HZ * CY, 128), F32),
            pltpu.VMEM((2, HZ * CY, 128), F32),
            pltpu.SemaphoreType.DMA((18,)),
        ],
        name="warp_sum",
    )(info, assign, *tables, *planes, *fields, below, above)


def relax_kernel(info, chunks, out, flat, pair, flat2, pair2, ready, sems):
    level, me, zone = info[0], info[1], info[2]
    size = flat.shape[1] - 16
    for held in (flat, pair, flat2, pair2):
        held[:, :8] = jnp.zeros((held.shape[0], 8, 128), F32)
        held[:, size + 8 :] = jnp.zeros((held.shape[0], 8, 128), F32)
    for held in (flat, flat2):
        for z in (0, held.shape[0] - 1):
            held[z, 8 : 8 + size] = jnp.zeros((size, 128), F32)
    narrow = lax.broadcasted_iota(jnp.int32, (CY, 128), 1)
    tail = HZ * 3 // 2
    for peer in range(8):
        rows = slice(8 + CY * peer, 8 + CY * (peer + 1))
        slots = [(half ^ level) * 8 + (peer ^ me) for half in range(2)]

        def block(half, index):
            return chunks[slots[half], CY * index : CY * (index + 1)]

        for half in range(2):
            for z in range(HZ):
                flat[3 + 14 * half + z, rows] = block(half, z)
            for z in range(2):
                flat[1 + 28 * half + z, rows] = block(half, tail + z)
        packed = [HZ + z % (HZ // 2) for z in range(HZ)]
        sides = [z // (HZ // 2) for z in range(HZ)]
        lows = [(tail + 2, 0), (tail + 2, 1)] + list(zip(packed, sides))
        highs = list(zip(packed, sides)) + [(tail + 2, 0), (tail + 2, 1)]
        for index in range(14):
            low, high = block(0, lows[index][0]), block(1, highs[index][0])
            if lows[index][1] == 1:
                low = pltpu.roll(low, 64, 1)
            if highs[index][1] == 0:
                high = pltpu.roll(high, 64, 1)
            pair[1 + index, rows] = jnp.where(narrow < 64, low, high)

    def mirror(planes, both):
        body = slice(8, 8 + size)
        both[0, body] = pltpu.roll(both[14, body], 64, 1)
        both[15, body] = pltpu.roll(both[1, body], 64, 1)
        planes[16, body] = pltpu.roll(planes[14, body], 64, 1)
        planes[15, body] = pltpu.roll(planes[17, body], 64, 1)

    mirror(flat, pair)
    count = 2 * CY
    lane = lax.broadcasted_iota(jnp.int32, (count, 128), 1)

    def swept(planes, index, start, scale):
        refs = [(planes[0], index), (planes[0], index + 16), (planes[1], index)]
        part = [held[z, start : start + count] for held, z in refs]
        left = [pltpu.roll(p, 1, 1) for p in part]
        right = [pltpu.roll(p, 127, 1) for p in part]
        left[2] = jnp.where(lane == 0, left[0], jnp.where(lane == 64, left[1], left[2]))
        left[0] = jnp.where(lane == 0, 0.0, left[0])
        left[1] = jnp.where(lane == 64, 0.0, left[1])
        right[0] = jnp.where(lane == 127, right[2], right[0])
        right[1] = jnp.where(lane == 63, right[2], right[1])
        right[2] = jnp.where(lane % 64 == 63, 0.0, right[2])
        done = []
        for b, (held, z) in enumerate(refs):
            around = held[z - 1, start : start + count] + held[z + 1, start : start + count]
            around += held[z, start - 1 : start - 1 + count] + held[z, start + 1 : start + 1 + count]
            around += left[b] + right[b]
            done.append((0.1 * scale) * part[b] + (0.15 * scale) * around)
        return done

    def first(index, carry):
        for start in range(8, 8 + size, count):
            done = swept((flat, pair), index, start, 1.0)
            flat2[index, start : start + count] = done[0]
            flat2[index + 16, start : start + count] = done[1]
            pair2[index, start : start + count] = done[2]
        return carry

    lax.fori_loop(1, 15, first, 0)
    whole = lax.broadcasted_iota(jnp.int32, (size, 128), 1)

    @pl.when(zone == 0)
    def _():
        flat2[2, 8 : 8 + size] = jnp.zeros((size, 128), F32)
        pair2[2, 8 : 8 + size] = jnp.where(whole < 64, 0.0, pair2[2, 8 : 8 + size])

    @pl.when(zone == 7)
    def _():
        flat2[29, 8 : 8 + size] = jnp.zeros((size, 128), F32)
        pair2[13, 8 : 8 + size] = jnp.where(whole < 64, pair2[13, 8 : 8 + size], 0.0)

    mirror(flat2, pair2)

    def emit(z):
        return pltpu.make_async_copy(ready.at[z + 2], out.at[z], sems.at[z])

    def second(index, carry):
        for start in range(8, 8 + size, count):
            done = swept((flat2, pair2), index, start, 1.0 / SCALE)
            rows = slice(start - 8, start - 8 + count)
            ready[index - 1, rows, :128] = done[0]
            ready[index - 1, rows, 128:] = done[2][:, :64]
            ready[index + 13, rows, :128] = pltpu.roll(done[1], 64, 1)
            ready[index + 13, rows, 128:] = pltpu.roll(done[2], 64, 1)[:, :64]

        @pl.when(index >= 3)
        def _():
            emit(index - 3).start()

        @pl.when(index <= 12)
        def _():
            emit(index + 11).start()

        return carry

    lax.fori_loop(1, 15, second, 0)

    def finish(z, carry):
        emit(z).wait()
        return carry

    lax.fori_loop(0, 24, finish, 0)


def relax(info, chunks):
    vmem = pl.BlockSpec(memory_space=pltpu.VMEM)
    return pl.pallas_call(
        relax_kernel,
        grid=(),
        in_specs=[pl.BlockSpec(memory_space=pltpu.SMEM), vmem],
        out_specs=pl.BlockSpec(memory_space=pl.ANY),
        out_shape=jax.ShapeDtypeStruct((24, 192, 192), F32),
        scratch_shapes=[
            pltpu.VMEM((32, 208, 128), F32),
            pltpu.VMEM((16, 208, 128), F32),
            pltpu.VMEM((32, 208, 128), F32),
            pltpu.VMEM((16, 208, 128), F32),
            pltpu.VMEM((28, 192, 192), F32),
            pltpu.SemaphoreType.DMA((24,)),
        ],
        name="relax",
    )(info, chunks)


def update(images, momenta, assign):
    level = lax.axis_index("level")
    me = lax.axis_index("subj")
    zone = lax.axis_index("gz")
    info = jnp.stack([level, me, zone]).astype(jnp.int32)
    zones = lax.axis_size("gz")
    outward = [(g, g + 1) for g in range(zones - 1)]
    outward += [(zones + g + 1, zones + g) for g in range(zones - 1)]
    nearest = ("level", "gz")
    cross = [(zones + g, g + 1) for g in range(zones - 1)]
    cross += [(g + 1, zones + g) for g in range(zones - 1)]
    climb = [(g, zones + g) for g in range(zones)]
    climb += [(zones + g, g + 1) for g in range(zones - 1)]
    rim = lax.dynamic_slice_in_dim(momenta[0], 9 * (1 - level), 3, axis=0)
    other = lax.dynamic_slice_in_dim(momenta[1], 9 * level, 3, axis=0)
    rim = lax.ppermute(rim, nearest, outward)
    other = lax.ppermute(other, nearest, cross)

    def spread(parts):
        return [parts[0]] + [
            lax.ppermute(parts[k], "subj", [(i, i ^ k) for i in range(8)]) for k in range(1, 8)
        ]

    packed = pack_images(info, images)
    planes = spread(packed)
    blurred = blur(info, momenta, rim, other)
    fields = spread(blurred)
    low, high = edges(planes)
    below = lax.ppermute(high, nearest, climb)
    above = lax.ppermute(low, nearest, [(b, a) for a, b in climb])
    chunk, edge = warp(info, assign, planes, fields, below, above)
    edge = lax.ppermute(edge.astype(jnp.float16), nearest, cross)
    chunk = jnp.concatenate([chunk.astype(jnp.float16), edge], axis=0)
    gathered = []
    for far in range(2):
        for step in range(4):
            part = chunk
            if far or step:
                perm = [
                    (8 * a + i, 8 * (a ^ far) + (i ^ (2 * step))) for a in range(2) for i in range(8)
                ]
                part = lax.ppermute(chunk, ("level", "subj"), perm)
            gathered.append(part)
            gathered.append(lax.ppermute(part, "subj", [(i, i ^ 1) for i in range(8)]))
    chunks = jnp.stack(gathered).astype(F32)
    return relax(info, chunks)


def solution(mesh):
    return jax.shard_map(
        update,
        mesh=mesh,
        in_specs=(P("subj", "gz", None, None), P("subj", "gz", None, None, None), P()),
        out_specs=P("gz", None, None),
        check_vma=False,
    )
```

profile of v0, /device:TPU:96, one launch (start us, length us, event | category | flops | bytes accessed | tf_op | source)
XLA Modules:
  0.0 139.7 jit_solution(10348912108048260501)
XLA Ops:
  0.0 0.6 pad_add_fusion.info
  0.6 4.3 %pack_images.1 = (bf16[12,80,128]{2,1,0:T(8,128)(2,1)}, bf16[12,80,128]{2,1,0:T(8,128)(2,1)}, bf16[12,80,128]{2,1,0:T(8,128)(2,1)}, bf16[12,80,128]{2,1,0:T(8,12...) custom-call(s32[3]{0:T(128)} %pad_add_fusion.info, ...), custom_call_target="tpu_custom_call" | custom-call | tf_op jit(solution)/shard_map/pack_images/pallas_call | solution.py:105
  5.0 0.1 collective-permute-start
  5.1 1.7 %collective-permute-start.1 = (bf16[12,80,128]{2,1,0:T(8,128)(2,1)}, bf16[12,80,128]{2,1,0:T(8,128)(2,1)}, u32[]{:S(2)}, u32[]{:S(2)}) collective-permute-start(bf16[12,80,128]{2,1,0:T(8,128)(2,1)} %get-tuple-element.27), channel_id=1, source_target_pairs={{0,16},{8,24},{16,0},{24,8},{32,48},{40,56},{48,32},{56,40},{1,17}... | collective-permute-start | bytes 737288 | tf_op jit(solution)/shard_map/ppermute | solution.py:567
  6.7 0.2 collective-permute-start.2
  6.9 3.2 %collective-permute-start.3 = (bf16[12,80,128]{2,1,0:T(8,128)(2,1)}, bf16[12,80,128]{2,1,0:T(8,128)(2,1)}, u32[]{:S(2)}, u32[]{:S(2)}) collective-permute-start(bf16[12,80,128]{2,1,0:T(8,128)(2,1)} %get-tuple-element.29), channel_id=1, source_target_pairs={{0,32},{8,40},{16,48},{24,56},{32,0},{40,8},{48,16},{56,24},{1,33}... | collective-permute-start | bytes 737288 | tf_op jit(solution)/shard_map/ppermute | solution.py:567
  10.1 2.1 %fusion = (f32[1,12,3,96,96]{4,3,2,1,0:T(8,128)}, f32[1,12,3,96,96]{4,3,2,1,0:T(8,128)}) fusion(f32[2,12,3,96,96]{4,3,2,1,0:T(8,128)S(1)} %copy-done), kind=kLoop, calls=%fused_computation.20 | loop fusion | bytes 5308416 | tf_op jit(solution)/shard_map/slice | solution.py:561
  12.2 1.0 dynamic-slice_bitcast_fusion.1
  13.3 4.7 %collective-permute-start.7 = (f32[3,3,96,96]{3,2,1,0:T(8,128)S(1)}, f32[3,3,96,96]{3,2,1,0:T(8,128)S(1)}, u32[]{:S(2)}, u32[]{:S(2)}) collective-permute-start(f32[3,3,96,96]{3,2,1,0:T(8,128)S(1)} %dynamic-slice_bitcast_fusion.1), channel_id=1, source_target_pairs={{0,1},{1,2},{2,3},{3,4},{4,5},{5,6},{6,7},{65,64},{66,65},{67,66},... | collective-permute-start | bytes 995336 | tf_op jit(solution)/shard_map/ppermute | solution.py:562
  17.9 1.0 dynamic-slice_bitcast_fusion
  19.0 0.0 collective-permute-done.refs_1_.rest_1_
  19.0 2.0 %collective-permute-start.8 = (f32[3,3,96,96]{3,2,1,0:T(8,128)S(1)}, f32[3,3,96,96]{3,2,1,0:T(8,128)S(1)}, u32[]{:S(2)}, u32[]{:S(2)}) collective-permute-start(f32[3,3,96,96]{3,2,1,0:T(8,128)S(1)} %dynamic-slice_bitcast_fusion), channel_id=1, source_target_pairs={{64,1},{65,2},{66,3},{67,4},{68,5},{69,6},{70,7},{1,64},{2,65},{3,... | collective-permute-start | bytes 995336 | tf_op jit(solution)/shard_map/ppermute | solution.py:563
  21.0 0.0 collective-permute-done.1.refs_2_.rest_2_
  21.0 0.1 collective-permute-start.4
  21.1 2.7 %collective-permute-start.5 = (bf16[12,80,128]{2,1,0:T(8,128)(2,1)}, bf16[12,80,128]{2,1,0:T(8,128)(2,1)S(1)}, u32[]{:S(2)}, u32[]{:S(2)}) collective-permute-start(bf16[12,80,128]{2,1,0:T(8,128)(2,1)} %get-tuple-element.31), channel_id=1, source_target_pairs={{0,48},{8,56},{16,32},{24,40},{32,16},{40,24},{48,0},{56,8},{1,49}... | collective-permute-start | bytes 737288 | tf_op jit(solution)/shard_map/ppermute | solution.py:567
  23.8 3.6 %collective-permute-done.3.refs_4_.rest_4_ = bf16[12,80,128]{2,1,0:T(8,128)(2,1)} collective-permute-done((bf16[12,80,128]{2,1,0:T(8,128)(2,1)}, bf16[12,80,128]{2,1,0:T(8,128)(2,1)}, u32[]{:S(2)}, u32[]{:S(2)}) %collective-permute-start.3) | collective-permute-done | bytes 245792 | tf_op jit(solution)/shard_map/ppermute | solution.py:567
  27.4 4.1 %collective-permute-done.4.refs_5_.rest_5_ = bf16[12,80,128]{2,1,0:T(8,128)(2,1)S(1)} collective-permute-done((bf16[12,80,128]{2,1,0:T(8,128)(2,1)}, bf16[12,80,128]{2,1,0:T(8,128)(2,1)S(1)}, u32[]{:S(2)}, u32[]{:S(2)}) %collective-permute-start.4) | collective-permute-done | bytes 245792 | tf_op jit(solution)/shard_map/ppermute | solution.py:567
  31.4 5.8 %collective-permute-done.5.refs_6_.rest_6_ = bf16[12,80,128]{2,1,0:T(8,128)(2,1)S(1)} collective-permute-done((bf16[12,80,128]{2,1,0:T(8,128)(2,1)}, bf16[12,80,128]{2,1,0:T(8,128)(2,1)S(1)}, u32[]{:S(2)}, u32[]{:S(2)}) %collective-permute-start.5) | collective-permute-done | bytes 245792 | tf_op jit(solution)/shard_map/ppermute | solution.py:567
  37.2 5.2 %collective-permute-done.6.refs_7_.rest_7_ = bf16[12,80,128]{2,1,0:T(8,128)(2,1)S(1)} collective-permute-done((bf16[12,80,128]{2,1,0:T(8,128)(2,1)}, bf16[12,80,128]{2,1,0:T(8,128)(2,1)S(1)}, u32[]{:S(2)}, u32[]{:S(2)}) %collective-permute-start.6) | collective-permute-done | bytes 245792 | tf_op jit(solution)/shard_map/ppermute | solution.py:567
  42.4 0.7 copy-done.3
  43.1 1.8 %cut_edges.1 = (bf16[8,80,128]{2,1,0:T(8,128)(2,1)}, bf16[8,80,128]{2,1,0:T(8,128)(2,1)}) custom-call(bf16[12,80,128]{2,1,0:T(8,128)(2,1)} %get-tuple-element.25.refs_0_.rest_0_, bf16[12,80,128]{2,1,0:T(8,128)(2,1)} %collective-permute-done.refs_1_.rest_1_, bf16[12,80,128]{2,1,0:T(8,128)(2,1)} %collective-permute-done.1.refs_2_.rest_2_, ...), custom_call_target="tpu_custom_call" | custom-call | tf_op jit(solution)/shard_map/cut_edges/pallas_call | solution.py:240
  44.9 3.6 %collective-permute-start.16 = (bf16[8,80,128]{2,1,0:T(8,128)(2,1)}, bf16[8,80,128]{2,1,0:T(8,128)(2,1)S(1)}, u32[]{:S(2)}, u32[]{:S(2)}) collective-permute-start(bf16[8,80,128]{2,1,0:T(8,128)(2,1)} %get-tuple-element.41), channel_id=1, source_target_pairs={{0,64},{1,65},{2,66},{3,67},{4,68},{5,69},{6,70},{7,71},{64,1},{65... | collective-permute-start | bytes 491528 | tf_op jit(solution)/shard_map/ppermute | solution.py:575
  48.5 2.2 %collective-permute-start.17 = (bf16[8,80,128]{2,1,0:T(8,128)(2,1)}, bf16[8,80,128]{2,1,0:T(8,128)(2,1)S(1)}, u32[]{:S(2)}, u32[]{:S(2)}) collective-permute-start(bf16[8,80,128]{2,1,0:T(8,128)(2,1)} %get-tuple-element.42), channel_id=1, source_target_pairs={{64,0},{65,1},{66,2},{67,3},{68,4},{69,5},{70,6},{71,7},{1,64},{2,... | collective-permute-start | bytes 491528 | tf_op jit(solution)/shard_map/ppermute | solution.py:576
  50.8 0.0 copy-start.4
  50.8 0.7 copy-done.4
  51.5 0.8 copy-done.5
  52.3 9.1 %blur_momenta.1 = (bf16[560,128]{1,0:T(8,128)(2,1)}, bf16[560,128]{1,0:T(8,128)(2,1)}, bf16[560,128]{1,0:T(8,128)(2,1)}, bf16[560,128]{1,0:T(8,128)(2,1)}, bf16[...) custom-call(s32[3]{0:T(128)} %pad_add_fusion.info, ...), custom_call_target="tpu_custom_call" | custom-call | tf_op jit(solution)/shard_map/blur_momenta/pallas_call | solution.py:191
  61.4 0.1 collective-permute-start.9
  61.5 0.3 collective-permute-start.10
  61.7 1.6 %collective-permute-start.11 = (bf16[560,128]{1,0:T(8,128)(2,1)}, bf16[560,128]{1,0:T(8,128)(2,1)S(1)}, u32[]{:S(2)}, u32[]{:S(2)}) collective-permute-start(bf16[560,128]{1,0:T(8,128)(2,1)} %get-tuple-element.36), channel_id=1, source_target_pairs={{0,24},{8,16},{16,8},{24,0},{32,56},{40,48},{48,40},{56,32},{1,25}... | collective-permute-start | bytes 430088 | tf_op jit(solution)/shard_map/ppermute | solution.py:567
  63.3 0.7 collective-permute-start.12
  64.0 2.6 %collective-permute-start.13 = (bf16[560,128]{1,0:T(8,128)(2,1)}, bf16[560,128]{1,0:T(8,128)(2,1)S(1)}, u32[]{:S(2)}, u32[]{:S(2)}) collective-permute-start(bf16[560,128]{1,0:T(8,128)(2,1)} %get-tuple-element.38), channel_id=1, source_target_pairs={{0,40},{8,32},{16,56},{24,48},{32,8},{40,0},{48,24},{56,16},{1,41}... | collective-permute-start | bytes 430088 | tf_op jit(solution)/shard_map/ppermute | solution.py:567
  66.6 0.8 collective-permute-start.14
  67.4 1.0 collective-permute-done.10.rest_10_
  68.4 1.2 collective-permute-start.15
  69.6 0.8 collective-permute-done.11.rest_11_
  70.4 4.5 %collective-permute-done.12.rest_12_ = bf16[560,128]{1,0:T(8,128)(2,1)S(1)} collective-permute-done((bf16[560,128]{1,0:T(8,128)(2,1)}, bf16[560,128]{1,0:T(8,128)(2,1)S(1)}, u32[]{:S(2)}, u32[]{:S(2)}) %collective-permute-start.12) | collective-permute-done | bytes 143392 | tf_op jit(solution)/shard_map/ppermute | solution.py:567
  74.9 2.0 %collective-permute-done.13.rest_13_ = bf16[560,128]{1,0:T(8,128)(2,1)S(1)} collective-permute-done((bf16[560,128]{1,0:T(8,128)(2,1)}, bf16[560,128]{1,0:T(8,128)(2,1)S(1)}, u32[]{:S(2)}, u32[]{:S(2)}) %collective-permute-start.13) | collective-permute-done | bytes 143392 | tf_op jit(solution)/shard_map/ppermute | solution.py:567
  76.9 3.4 %collective-permute-done.14.rest_14_ = bf16[560,128]{1,0:T(8,128)(2,1)S(1)} collective-permute-done((bf16[560,128]{1,0:T(8,128)(2,1)}, bf16[560,128]{1,0:T(8,128)(2,1)S(1)}, u32[]{:S(2)}, u32[]{:S(2)}) %collective-permute-start.14) | collective-permute-done | bytes 143392 | tf_op jit(solution)/shard_map/ppermute | solution.py:567
  80.3 2.5 %collective-permute-done.15.rest_15_ = bf16[560,128]{1,0:T(8,128)(2,1)S(1)} collective-permute-done((bf16[560,128]{1,0:T(8,128)(2,1)}, bf16[560,128]{1,0:T(8,128)(2,1)S(1)}, u32[]{:S(2)}, u32[]{:S(2)}) %collective-permute-start.15) | collective-permute-done | bytes 143392 | tf_op jit(solution)/shard_map/ppermute | solution.py:567
  82.9 0.6 copy-done.14
  83.5 9.5 %warp_sum.1 = (f32[432,128]{1,0:T(8,128)}, f32[72,128]{1,0:T(8,128)}) custom-call(s32[3]{0:T(128)} %pad_add_fusion.info, s32[16]{0:T(128)} %assign.1, bf16[288,112]{1,0:T(8,128)(2,1)} %constant.29.clone.zy, bf16[256,256]{1,0:T(8,128)(2,1)} %constant.30.clone.x0, bf16[256,256]{1,0:T(8,128)(2,1)} %constant.31.clone.x1, ...), custom_call_target="tpu_custom_call" | custom-call | tf_op jit(solution)/shard_map/warp_sum/pallas_call | solution.py:387
  93.0 0.8 convert_element_type.10
  93.8 4.7 %collective-permute-start.18 = (f16[72,128]{1,0:T(8,128)(2,1)S(1)}, f16[72,128]{1,0:T(8,128)(2,1)S(1)}, u32[]{:S(2)}, u32[]{:S(2)}) collective-permute-start(f16[72,128]{1,0:T(8,128)(2,1)S(1)} %convert_element_type.10), channel_id=1, source_target_pairs={{64,1},{65,2},{66,3},{67,4},{68,5},{69,6},{70,7},{1,64},{2,65},{3,... | collective-permute-start | bytes 55304 | tf_op jit(solution)/shard_map/ppermute | solution.py:578
  98.5 1.0 convert_element_type.9
  99.4 0.9 collective-permute-done.18
  100.4 0.1 collective-permute-start.20
  100.5 0.1 collective-permute-start.19
  100.6 4.7 %collective-permute-start.30 = (f16[504,128]{1,0:T(8,128)(2,1)S(1)}, f16[504,128]{1,0:T(8,128)(2,1)S(1)}, u32[]{:S(2)}, u32[]{:S(2)}) collective-permute-start(f16[504,128]{1,0:T(8,128)(2,1)S(1)} %pad_maximum_fusion), channel_id=1, source_target_pairs={{0,96},{8,104},{16,112},{24,120},{32,64},{40,72},{48,80},{56,88},{... | collective-permute-start | bytes 387080 | tf_op jit(solution)/shard_map/ppermute | solution.py:588
  105.3 0.2 collective-permute-start.28
  105.5 0.9 collective-permute-start.26
  106.4 2.9 %collective-permute-start.24 = (f16[504,128]{1,0:T(8,128)(2,1)S(1)}, f16[504,128]{1,0:T(8,128)(2,1)S(1)}, u32[]{:S(2)}, u32[]{:S(2)}) collective-permute-start(f16[504,128]{1,0:T(8,128)(2,1)S(1)} %pad_maximum_fusion), channel_id=1, source_target_pairs={{0,48},{8,56},{16,32},{24,40},{32,16},{40,24},{48,0},{56,8},{64,11... | collective-permute-start | bytes 387080 | tf_op jit(solution)/shard_map/ppermute | solution.py:588
  109.4 1.2 collective-permute-done.21
  110.7 2.0 %collective-permute-start.22 = (f16[504,128]{1,0:T(8,128)(2,1)S(1)}, f16[504,128]{1,0:T(8,128)(2,1)S(1)}, u32[]{:S(2)}, u32[]{:S(2)}) collective-permute-start(f16[504,128]{1,0:T(8,128)(2,1)S(1)} %pad_maximum_fusion), channel_id=1, source_target_pairs={{0,32},{8,40},{16,48},{24,56},{32,0},{40,8},{48,16},{56,24},{64,96... | collective-permute-start | bytes 387080 | tf_op jit(solution)/shard_map/ppermute | solution.py:588
  112.7 2.1 %collective-permute-start.32 = (f16[504,128]{1,0:T(8,128)(2,1)S(1)}, f16[504,128]{1,0:T(8,128)(2,1)S(1)}, u32[]{:S(2)}, u32[]{:S(2)}) collective-permute-start(f16[504,128]{1,0:T(8,128)(2,1)S(1)} %pad_maximum_fusion), channel_id=1, source_target_pairs={{0,112},{8,120},{16,96},{24,104},{32,80},{40,88},{48,64},{56,72},{... | collective-permute-start | bytes 387080 | tf_op jit(solution)/shard_map/ppermute | solution.py:588
  114.8 3.0 %collective-permute-done.22 = f16[504,128]{1,0:T(8,128)(2,1)S(1)} collective-permute-done((f16[504,128]{1,0:T(8,128)(2,1)S(1)}, f16[504,128]{1,0:T(8,128)(2,1)S(1)}, u32[]{:S(2)}, u32[]{:S(2)}) %collective-permute-start.22) | collective-permute-done | bytes 129056 | tf_op jit(solution)/shard_map/ppermute | solution.py:588
  117.8 0.8 collective-permute-start.31
  118.6 0.1 collective-permute-start.29
  118.7 0.4 collective-permute-start.27
  119.1 2.4 %collective-permute-done.32 = f16[504,128]{1,0:T(8,128)(2,1)S(1)} collective-permute-done((f16[504,128]{1,0:T(8,128)(2,1)S(1)}, f16[504,128]{1,0:T(8,128)(2,1)S(1)}, u32[]{:S(2)}, u32[]{:S(2)}) %collective-permute-start.32) | collective-permute-done | bytes 129056 | tf_op jit(solution)/shard_map/ppermute | solution.py:588
  121.5 0.5 collective-permute-start.33
  122.1 0.7 collective-permute-done.25
  123.3 2.2 %convert_element_type.11.chunks = f32[16,504,128]{2,1,0:T(8,128)} convert(f16[16,504,128]{2,1,0:T(8,128)(2,1)S(1)} %bitcast_dynamic-update-slice_fusion) | non-fusion elementwise | flops 1032192 | bytes 6193152 | tf_op jit(solution)/shard_map/convert_element_type | solution.py:591
  125.5 14.0 %relax.1 = f32[24,192,192]{2,1,0:T(8,128)} custom-call(s32[3]{0:T(128)} %pad_add_fusion.info, f32[16,504,128]{2,1,0:T(8,128)} %convert_element_type.11.chunks), custom_call_target="tpu_custom_call" | custom-call | tf_op jit(solution)/shard_map/relax/pallas_call | solution.py:529
  (63 shorter events, 0.9 us)
Async XLA Ops:
  0.6 9.5 %copy-start = (f32[2,12,3,96,96]{4,3,2,1,0:T(8,128)S(1)}, f32[2,12,3,96,96]{4,3,2,1,0:T(8,128)}, u32[]{:S(2)}) copy-start(f32[2,12,3,96,96]{4,3,2,1,0:T(8,128)} %momenta.1) | copy-start | bytes 7962628
  5.0 14.0 %collective-permute-start = (bf16[12,80,128]{2,1,0:T(8,128)(2,1)}, bf16[12,80,128]{2,1,0:T(8,128)(2,1)}, u32[]{:S(2)}, u32[]{:S(2)}) collective-permute-start(bf16[12,80,128]{2,1,0:T(8,128)(2,1)} %get-tuple-element.26), channel_id=1, source_target_pairs={{0,8},{8,0},{16,24},{24,16},{32,40},{40,32},{48,56},{56,48},{1,9},... | collective-permute-start | bytes 737288 | tf_op jit(solution)/shard_map/ppermute | solution.py:567
  5.1 15.9 %collective-permute-start.1 = (bf16[12,80,128]{2,1,0:T(8,128)(2,1)}, bf16[12,80,128]{2,1,0:T(8,128)(2,1)}, u32[]{:S(2)}, u32[]{:S(2)}) collective-permute-start(bf16[12,80,128]{2,1,0:T(8,128)(2,1)} %get-tuple-element.27), channel_id=1, source_target_pairs={{0,16},{8,24},{16,0},{24,8},{32,48},{40,56},{48,32},{56,40},{1,17}... | collective-permute-start | bytes 737288 | tf_op jit(solution)/shard_map/ppermute | solution.py:567
  6.7 14.3 %collective-permute-start.2 = (bf16[12,80,128]{2,1,0:T(8,128)(2,1)}, bf16[12,80,128]{2,1,0:T(8,128)(2,1)}, u32[]{:S(2)}, u32[]{:S(2)}) collective-permute-start(bf16[12,80,128]{2,1,0:T(8,128)(2,1)} %get-tuple-element.28), channel_id=1, source_target_pairs={{0,24},{8,16},{16,8},{24,0},{32,56},{40,48},{48,40},{56,32},{1,25}... | collective-permute-start | bytes 737288 | tf_op jit(solution)/shard_map/ppermute | solution.py:567
  6.9 20.5 %collective-permute-start.3 = (bf16[12,80,128]{2,1,0:T(8,128)(2,1)}, bf16[12,80,128]{2,1,0:T(8,128)(2,1)}, u32[]{:S(2)}, u32[]{:S(2)}) collective-permute-start(bf16[12,80,128]{2,1,0:T(8,128)(2,1)} %get-tuple-element.29), channel_id=1, source_target_pairs={{0,32},{8,40},{16,48},{24,56},{32,0},{40,8},{48,16},{56,24},{1,33}... | collective-permute-start | bytes 737288 | tf_op jit(solution)/shard_map/ppermute | solution.py:567
  13.3 37.5 %collective-permute-start.7 = (f32[3,3,96,96]{3,2,1,0:T(8,128)S(1)}, f32[3,3,96,96]{3,2,1,0:T(8,128)S(1)}, u32[]{:S(2)}, u32[]{:S(2)}) collective-permute-start(f32[3,3,96,96]{3,2,1,0:T(8,128)S(1)} %dynamic-slice_bitcast_fusion.1), channel_id=1, source_target_pairs={{0,1},{1,2},{2,3},{3,4},{4,5},{5,6},{6,7},{65,64},{66,65},{67,66},... | collective-permute-start | bytes 995336 | tf_op jit(solution)/shard_map/ppermute | solution.py:562
  19.0 31.8 %collective-permute-start.8 = (f32[3,3,96,96]{3,2,1,0:T(8,128)S(1)}, f32[3,3,96,96]{3,2,1,0:T(8,128)S(1)}, u32[]{:S(2)}, u32[]{:S(2)}) collective-permute-start(f32[3,3,96,96]{3,2,1,0:T(8,128)S(1)} %dynamic-slice_bitcast_fusion), channel_id=1, source_target_pairs={{64,1},{65,2},{66,3},{67,4},{68,5},{69,6},{70,7},{1,64},{2,65},{3,... | collective-permute-start | bytes 995336 | tf_op jit(solution)/shard_map/ppermute | solution.py:563
  21.0 10.5 %collective-permute-start.4 = (bf16[12,80,128]{2,1,0:T(8,128)(2,1)}, bf16[12,80,128]{2,1,0:T(8,128)(2,1)S(1)}, u32[]{:S(2)}, u32[]{:S(2)}) collective-permute-start(bf16[12,80,128]{2,1,0:T(8,128)(2,1)} %get-tuple-element.30), channel_id=1, source_target_pairs={{0,40},{8,32},{16,56},{24,48},{32,8},{40,0},{48,24},{56,16},{1,41}... | collective-permute-start | bytes 737288 | tf_op jit(solution)/shard_map/ppermute | solution.py:567
  21.1 16.1 %collective-permute-start.5 = (bf16[12,80,128]{2,1,0:T(8,128)(2,1)}, bf16[12,80,128]{2,1,0:T(8,128)(2,1)S(1)}, u32[]{:S(2)}, u32[]{:S(2)}) collective-permute-start(bf16[12,80,128]{2,1,0:T(8,128)(2,1)} %get-tuple-element.31), channel_id=1, source_target_pairs={{0,48},{8,56},{16,32},{24,40},{32,16},{40,24},{48,0},{56,8},{1,49}... | collective-permute-start | bytes 737288 | tf_op jit(solution)/shard_map/ppermute | solution.py:567
  27.4 15.0 %collective-permute-start.6 = (bf16[12,80,128]{2,1,0:T(8,128)(2,1)}, bf16[12,80,128]{2,1,0:T(8,128)(2,1)S(1)}, u32[]{:S(2)}, u32[]{:S(2)}) collective-permute-start(bf16[12,80,128]{2,1,0:T(8,128)(2,1)} %get-tuple-element.32), channel_id=1, source_target_pairs={{0,56},{8,48},{16,40},{24,32},{32,24},{40,16},{48,8},{56,0},{1,57}... | collective-permute-start | bytes 737288 | tf_op jit(solution)/shard_map/ppermute | solution.py:567
  31.4 10.9 %copy-start.1 = (bf16[12,80,128]{2,1,0:T(8,128)(2,1)}, bf16[12,80,128]{2,1,0:T(8,128)(2,1)S(1)}, u32[]{:S(2)}) copy-start(bf16[12,80,128]{2,1,0:T(8,128)(2,1)S(1)} %collective-permute-done.4.refs_5_.rest_5_) | copy-start | bytes 737284
  37.2 5.2 %copy-start.2 = (bf16[12,80,128]{2,1,0:T(8,128)(2,1)}, bf16[12,80,128]{2,1,0:T(8,128)(2,1)S(1)}, u32[]{:S(2)}) copy-start(bf16[12,80,128]{2,1,0:T(8,128)(2,1)S(1)} %collective-permute-done.5.refs_6_.rest_6_) | copy-start | bytes 737284
  42.4 0.7 copy-start.3
  44.9 18.4 %collective-permute-start.16 = (bf16[8,80,128]{2,1,0:T(8,128)(2,1)}, bf16[8,80,128]{2,1,0:T(8,128)(2,1)S(1)}, u32[]{:S(2)}, u32[]{:S(2)}) collective-permute-start(bf16[8,80,128]{2,1,0:T(8,128)(2,1)} %get-tuple-element.41), channel_id=1, source_target_pairs={{0,64},{1,65},{2,66},{3,67},{4,68},{5,69},{6,70},{7,71},{64,1},{65... | collective-permute-start | bytes 491528 | tf_op jit(solution)/shard_map/ppermute | solution.py:575
  48.5 15.5 %collective-permute-start.17 = (bf16[8,80,128]{2,1,0:T(8,128)(2,1)}, bf16[8,80,128]{2,1,0:T(8,128)(2,1)S(1)}, u32[]{:S(2)}, u32[]{:S(2)}) collective-permute-start(bf16[8,80,128]{2,1,0:T(8,128)(2,1)} %get-tuple-element.42), channel_id=1, source_target_pairs={{64,0},{65,1},{66,2},{67,3},{68,4},{69,5},{70,6},{71,7},{1,64},{2,... | collective-permute-start | bytes 491528 | tf_op jit(solution)/shard_map/ppermute | solution.py:576
  50.8 0.8 copy-start.4
  51.5 0.8 copy-start.5
  61.4 5.2 %collective-permute-start.9 = (bf16[560,128]{1,0:T(8,128)(2,1)}, bf16[560,128]{1,0:T(8,128)(2,1)S(1)}, u32[]{:S(2)}, u32[]{:S(2)}) collective-permute-start(bf16[560,128]{1,0:T(8,128)(2,1)} %get-tuple-element.34), channel_id=1, source_target_pairs={{0,8},{8,0},{16,24},{24,16},{32,40},{40,32},{48,56},{56,48},{1,9},... | collective-permute-start | bytes 430088 | tf_op jit(solution)/shard_map/ppermute | solution.py:567
  61.5 6.9 %collective-permute-start.10 = (bf16[560,128]{1,0:T(8,128)(2,1)}, bf16[560,128]{1,0:T(8,128)(2,1)S(1)}, u32[]{:S(2)}, u32[]{:S(2)}) collective-permute-start(bf16[560,128]{1,0:T(8,128)(2,1)} %get-tuple-element.35), channel_id=1, source_target_pairs={{0,16},{8,24},{16,0},{24,8},{32,48},{40,56},{48,32},{56,40},{1,17}... | collective-permute-start | bytes 430088 | tf_op jit(solution)/shard_map/ppermute | solution.py:567
  61.7 8.6 %collective-permute-start.11 = (bf16[560,128]{1,0:T(8,128)(2,1)}, bf16[560,128]{1,0:T(8,128)(2,1)S(1)}, u32[]{:S(2)}, u32[]{:S(2)}) collective-permute-start(bf16[560,128]{1,0:T(8,128)(2,1)} %get-tuple-element.36), channel_id=1, source_target_pairs={{0,24},{8,16},{16,8},{24,0},{32,56},{40,48},{48,40},{56,32},{1,25}... | collective-permute-start | bytes 430088 | tf_op jit(solution)/shard_map/ppermute | solution.py:567
  63.3 19.5 %copy-start.6 = (bf16[8,80,128]{2,1,0:T(8,128)(2,1)}, bf16[8,80,128]{2,1,0:T(8,128)(2,1)S(1)}, u32[]{:S(2)}) copy-start(bf16[8,80,128]{2,1,0:T(8,128)(2,1)S(1)} %collective-permute-done.16.rest_16_) | copy-start | bytes 491524
  63.3 11.5 %collective-permute-start.12 = (bf16[560,128]{1,0:T(8,128)(2,1)}, bf16[560,128]{1,0:T(8,128)(2,1)S(1)}, u32[]{:S(2)}, u32[]{:S(2)}) collective-permute-start(bf16[560,128]{1,0:T(8,128)(2,1)} %get-tuple-element.37), channel_id=1, source_target_pairs={{0,32},{8,40},{16,48},{24,56},{32,0},{40,8},{48,16},{56,24},{1,33}... | collective-permute-start | bytes 430088 | tf_op jit(solution)/shard_map/ppermute | solution.py:567
  64.0 18.8 %copy-start.7 = (bf16[8,80,128]{2,1,0:T(8,128)(2,1)}, bf16[8,80,128]{2,1,0:T(8,128)(2,1)S(1)}, u32[]{:S(2)}) copy-start(bf16[8,80,128]{2,1,0:T(8,128)(2,1)S(1)} %collective-permute-done.17.rest_17_) | copy-start | bytes 491524
  64.0 12.8 %collective-permute-start.13 = (bf16[560,128]{1,0:T(8,128)(2,1)}, bf16[560,128]{1,0:T(8,128)(2,1)S(1)}, u32[]{:S(2)}, u32[]{:S(2)}) collective-permute-start(bf16[560,128]{1,0:T(8,128)(2,1)} %get-tuple-element.38), channel_id=1, source_target_pairs={{0,40},{8,32},{16,56},{24,48},{32,8},{40,0},{48,24},{56,16},{1,41}... | collective-permute-start | bytes 430088 | tf_op jit(solution)/shard_map/ppermute | solution.py:567
  66.6 16.3 %copy-start.8 = (bf16[560,128]{1,0:T(8,128)(2,1)}, bf16[560,128]{1,0:T(8,128)(2,1)S(1)}, u32[]{:S(2)}) copy-start(bf16[560,128]{1,0:T(8,128)(2,1)S(1)} %collective-permute-done.9.rest_9_) | copy-start | bytes 430084
  66.6 13.7 %collective-permute-start.14 = (bf16[560,128]{1,0:T(8,128)(2,1)}, bf16[560,128]{1,0:T(8,128)(2,1)S(1)}, u32[]{:S(2)}, u32[]{:S(2)}) collective-permute-start(bf16[560,128]{1,0:T(8,128)(2,1)} %get-tuple-element.39), channel_id=1, source_target_pairs={{0,48},{8,56},{16,32},{24,40},{32,16},{40,24},{48,0},{56,8},{1,49}... | collective-permute-start | bytes 430088 | tf_op jit(solution)/shard_map/ppermute | solution.py:567
  68.4 14.4 %copy-start.9 = (bf16[560,128]{1,0:T(8,128)(2,1)}, bf16[560,128]{1,0:T(8,128)(2,1)S(1)}, u32[]{:S(2)}) copy-start(bf16[560,128]{1,0:T(8,128)(2,1)S(1)} %collective-permute-done.10.rest_10_) | copy-start | bytes 430084
  68.4 14.4 %collective-permute-start.15 = (bf16[560,128]{1,0:T(8,128)(2,1)}, bf16[560,128]{1,0:T(8,128)(2,1)S(1)}, u32[]{:S(2)}, u32[]{:S(2)}) collective-permute-start(bf16[560,128]{1,0:T(8,128)(2,1)} %get-tuple-element.40), channel_id=1, source_target_pairs={{0,56},{8,48},{16,40},{24,32},{32,24},{40,16},{48,8},{56,0},{1,57}... | collective-permute-start | bytes 430088 | tf_op jit(solution)/shard_map/ppermute | solution.py:567
  70.4 12.5 %copy-start.10 = (bf16[560,128]{1,0:T(8,128)(2,1)}, bf16[560,128]{1,0:T(8,128)(2,1)S(1)}, u32[]{:S(2)}) copy-start(bf16[560,128]{1,0:T(8,128)(2,1)S(1)} %collective-permute-done.11.rest_11_) | copy-start | bytes 430084
  74.9 8.0 %copy-start.11 = (bf16[560,128]{1,0:T(8,128)(2,1)}, bf16[560,128]{1,0:T(8,128)(2,1)S(1)}, u32[]{:S(2)}) copy-start(bf16[560,128]{1,0:T(8,128)(2,1)S(1)} %collective-permute-done.12.rest_12_) | copy-start | bytes 430084
  76.9 6.0 %copy-start.12 = (bf16[560,128]{1,0:T(8,128)(2,1)}, bf16[560,128]{1,0:T(8,128)(2,1)S(1)}, u32[]{:S(2)}) copy-start(bf16[560,128]{1,0:T(8,128)(2,1)S(1)} %collective-permute-done.13.rest_13_) | copy-start | bytes 430084
  80.3 2.6 %copy-start.13 = (bf16[560,128]{1,0:T(8,128)(2,1)}, bf16[560,128]{1,0:T(8,128)(2,1)S(1)}, u32[]{:S(2)}) copy-start(bf16[560,128]{1,0:T(8,128)(2,1)S(1)} %collective-permute-done.14.rest_14_) | copy-start | bytes 430084
  82.8 0.7 copy-start.14
  93.8 6.5 %collective-permute-start.18 = (f16[72,128]{1,0:T(8,128)(2,1)S(1)}, f16[72,128]{1,0:T(8,128)(2,1)S(1)}, u32[]{:S(2)}, u32[]{:S(2)}) collective-permute-start(f16[72,128]{1,0:T(8,128)(2,1)S(1)} %convert_element_type.10), channel_id=1, source_target_pairs={{64,1},{65,2},{66,3},{67,4},{68,5},{69,6},{70,7},{1,64},{2,65},{3,... | collective-permute-start | bytes 55304 | tf_op jit(solution)/shard_map/ppermute | solution.py:578
  100.4 6.0 %collective-permute-start.20 = (f16[504,128]{1,0:T(8,128)(2,1)S(1)}, f16[504,128]{1,0:T(8,128)(2,1)S(1)}, u32[]{:S(2)}, u32[]{:S(2)}) collective-permute-start(f16[504,128]{1,0:T(8,128)(2,1)S(1)} %pad_maximum_fusion), channel_id=1, source_target_pairs={{0,16},{8,24},{16,0},{24,8},{32,48},{40,56},{48,32},{56,40},{64,80... | collective-permute-start | bytes 387080 | tf_op jit(solution)/shard_map/ppermute | solution.py:588
  100.5 8.9 %collective-permute-start.19 = (f16[504,128]{1,0:T(8,128)(2,1)S(1)}, f16[504,128]{1,0:T(8,128)(2,1)S(1)}, u32[]{:S(2)}, u32[]{:S(2)}) collective-permute-start(f16[504,128]{1,0:T(8,128)(2,1)S(1)} %pad_maximum_fusion), channel_id=1, source_target_pairs={{0,8},{8,0},{16,24},{24,16},{32,40},{40,32},{48,56},{56,48},{1,9},... | collective-permute-start | bytes 387080 | tf_op jit(solution)/shard_map/ppermute | solution.py:590
  100.6 12.1 %collective-permute-start.30 = (f16[504,128]{1,0:T(8,128)(2,1)S(1)}, f16[504,128]{1,0:T(8,128)(2,1)S(1)}, u32[]{:S(2)}, u32[]{:S(2)}) collective-permute-start(f16[504,128]{1,0:T(8,128)(2,1)S(1)} %pad_maximum_fusion), channel_id=1, source_target_pairs={{0,96},{8,104},{16,112},{24,120},{32,64},{40,72},{48,80},{56,88},{... | collective-permute-start | bytes 387080 | tf_op jit(solution)/shard_map/ppermute | solution.py:588
  105.3 12.5 %collective-permute-start.28 = (f16[504,128]{1,0:T(8,128)(2,1)S(1)}, f16[504,128]{1,0:T(8,128)(2,1)S(1)}, u32[]{:S(2)}, u32[]{:S(2)}) collective-permute-start(f16[504,128]{1,0:T(8,128)(2,1)S(1)} %pad_maximum_fusion), channel_id=1, source_target_pairs={{0,80},{8,88},{16,64},{24,72},{32,112},{40,120},{48,96},{56,104},{... | collective-permute-start | bytes 387080 | tf_op jit(solution)/shard_map/ppermute | solution.py:588
  105.5 13.1 %collective-permute-start.26 = (f16[504,128]{1,0:T(8,128)(2,1)S(1)}, f16[504,128]{1,0:T(8,128)(2,1)S(1)}, u32[]{:S(2)}, u32[]{:S(2)}) collective-permute-start(f16[504,128]{1,0:T(8,128)(2,1)S(1)} %pad_maximum_fusion), channel_id=1, source_target_pairs={{0,64},{8,72},{16,80},{24,88},{32,96},{40,104},{48,112},{56,120},{... | collective-permute-start | bytes 387080 | tf_op jit(solution)/shard_map/ppermute | solution.py:588
  106.4 12.3 %collective-permute-start.24 = (f16[504,128]{1,0:T(8,128)(2,1)S(1)}, f16[504,128]{1,0:T(8,128)(2,1)S(1)}, u32[]{:S(2)}, u32[]{:S(2)}) collective-permute-start(f16[504,128]{1,0:T(8,128)(2,1)S(1)} %pad_maximum_fusion), channel_id=1, source_target_pairs={{0,48},{8,56},{16,32},{24,40},{32,16},{40,24},{48,0},{56,8},{64,11... | collective-permute-start | bytes 387080 | tf_op jit(solution)/shard_map/ppermute | solution.py:588
  109.3 1.3 collective-permute-start.21
  110.7 7.1 %collective-permute-start.22 = (f16[504,128]{1,0:T(8,128)(2,1)S(1)}, f16[504,128]{1,0:T(8,128)(2,1)S(1)}, u32[]{:S(2)}, u32[]{:S(2)}) collective-permute-start(f16[504,128]{1,0:T(8,128)(2,1)S(1)} %pad_maximum_fusion), channel_id=1, source_target_pairs={{0,32},{8,40},{16,48},{24,56},{32,0},{40,8},{48,16},{56,24},{64,96... | collective-permute-start | bytes 387080 | tf_op jit(solution)/shard_map/ppermute | solution.py:588
  112.7 8.7 %collective-permute-start.32 = (f16[504,128]{1,0:T(8,128)(2,1)S(1)}, f16[504,128]{1,0:T(8,128)(2,1)S(1)}, u32[]{:S(2)}, u32[]{:S(2)}) collective-permute-start(f16[504,128]{1,0:T(8,128)(2,1)S(1)} %pad_maximum_fusion), channel_id=1, source_target_pairs={{0,112},{8,120},{16,96},{24,104},{32,80},{40,88},{48,64},{56,72},{... | collective-permute-start | bytes 387080 | tf_op jit(solution)/shard_map/ppermute | solution.py:588
  117.8 3.7 %collective-permute-start.23 = (f16[504,128]{1,0:T(8,128)(2,1)S(1)}, f16[504,128]{1,0:T(8,128)(2,1)S(1)}, u32[]{:S(2)}, u32[]{:S(2)}) collective-permute-start(f16[504,128]{1,0:T(8,128)(2,1)S(1)} %collective-permute-done.22), channel_id=1, source_target_pairs={{0,8},{8,0},{16,24},{24,16},{32,40},{40,32},{48,56},{56,48},{1,9},... | collective-permute-start | bytes 387080 | tf_op jit(solution)/shard_map/ppermute | solution.py:590
  117.8 5.3 %collective-permute-start.31 = (f16[504,128]{1,0:T(8,128)(2,1)S(1)}, f16[504,128]{1,0:T(8,128)(2,1)S(1)}, u32[]{:S(2)}, u32[]{:S(2)}) collective-permute-start(f16[504,128]{1,0:T(8,128)(2,1)S(1)} %collective-permute-done.30), channel_id=1, source_target_pairs={{0,8},{8,0},{16,24},{24,16},{32,40},{40,32},{48,56},{56,48},{1,9},... | collective-permute-start | bytes 387080 | tf_op jit(solution)/shard_map/ppermute | solution.py:590
  118.6 4.4 %collective-permute-start.29 = (f16[504,128]{1,0:T(8,128)(2,1)S(1)}, f16[504,128]{1,0:T(8,128)(2,1)S(1)}, u32[]{:S(2)}, u32[]{:S(2)}) collective-permute-start(f16[504,128]{1,0:T(8,128)(2,1)S(1)} %collective-permute-done.28), channel_id=1, source_target_pairs={{0,8},{8,0},{16,24},{24,16},{32,40},{40,32},{48,56},{56,48},{1,9},... | collective-permute-start | bytes 387080 | tf_op jit(solution)/shard_map/ppermute | solution.py:590
  118.7 4.2 %collective-permute-start.27 = (f16[504,128]{1,0:T(8,128)(2,1)S(1)}, f16[504,128]{1,0:T(8,128)(2,1)S(1)}, u32[]{:S(2)}, u32[]{:S(2)}) collective-permute-start(f16[504,128]{1,0:T(8,128)(2,1)S(1)} %collective-permute-done.26), channel_id=1, source_target_pairs={{0,8},{8,0},{16,24},{24,16},{32,40},{40,32},{48,56},{56,48},{1,9},... | collective-permute-start | bytes 387080 | tf_op jit(solution)/shard_map/ppermute | solution.py:590
  121.5 1.3 collective-permute-start.25
  121.5 1.7 %collective-permute-start.33 = (f16[504,128]{1,0:T(8,128)(2,1)S(1)}, f16[504,128]{1,0:T(8,128)(2,1)S(1)}, u32[]{:S(2)}, u32[]{:S(2)}) collective-permute-start(f16[504,128]{1,0:T(8,128)(2,1)S(1)} %collective-permute-done.32), channel_id=1, source_target_pairs={{0,8},{8,0},{16,24},{24,16},{32,40},{40,32},{48,56},{56,48},{1,9},... | collective-permute-start | bytes 387080 | tf_op jit(solution)/shard_map/ppermute | solution.py:590
where the time goes:
time: 141 us; the launch traced here: 140 us
  starting transfers between devices  46.9 us (33%)
  waiting for transfers between devices  41.2 us (29%)
  Pallas kernels  38.8 us (28%)
  local copies, waits for them, and re-layouts  7.72 us (5%)
  other arithmetic  4.65 us (3%)
    ppermute x14, waiting for transfers between devices, spread(): lax.ppermute(parts[k], 'subj', [(i, i ^ k) for i in range(8)])  32.9 us
    ppermute x14, starting transfers between devices, spread(): lax.ppermute(parts[k], 'subj', [(i, i ^ k) for i in range(8)])  15 us
    pallas_call x1, Pallas kernels, relax(): pl.pallas_call(relax_kernel, grid=(), in_specs=[pl.BlockSpec(memory_space...  14 us
    ppermute x7, starting transfers between devices, update(): part = lax.ppermute(chunk, ('level', 'subj'), perm)  12.8 us
    pallas_call x1, Pallas kernels, warp(): pl.pallas_call(warp_kernel, grid=(), in_specs=[smem, smem, vmem, vmem, vm...  9.54 us
    pallas_call x1, Pallas kernels, blur(): pl.pallas_call(blur_kernel, grid=(), in_specs=[pl.BlockSpec(memory_space=...  9.06 us
    ppermute x7, waiting for transfers between devices, update(): part = lax.ppermute(chunk, ('level', 'subj'), perm)  5.36 us
    ppermute x1, starting transfers between devices, update(): rim = lax.ppermute(rim, nearest, outward)  4.66 us
  transfers between devices with their start and end apart: 34, of which 15 were waited for; matrix products, arithmetic and copies ran while one was open for 4% of the time, Pallas kernels for 8%

commit v1 on v0

--- a/solution.py
+++ b/solution.py
@@ -127,7 +127,7 @@
         momenta.at[:, pl.ds(3 * level, 9)], held.at[:, pl.ds(3 - 3 * level, 9)], sems.at[0]
     )
     sides = [
-        pltpu.make_async_copy(rows, held.at[j, pl.ds(9 * level, 3)], sems.at[1 + j])
+        pltpu.make_async_copy(rows.at[0], held.at[j, pl.ds(9 * level, 3)], sems.at[1 + j])
         for j, rows in enumerate((halo, other))
     ]
     for copy in [own] + sides:
@@ -405,7 +405,7 @@
     )(info, assign, *tables, *planes, *fields, below, above)
 
 
-def relax_kernel(info, chunks, out, flat, pair, flat2, pair2, ready, sems):
+def relax_kernel(info, chunks, out, flat, pair, flat2, pair2, even, odd, ready, sems):
     level, me, zone = info[0], info[1], info[2]
     size = flat.shape[1] - 16
     for held in (flat, pair, flat2, pair2):
@@ -451,34 +451,56 @@
     count = 2 * CY
     lane = lax.broadcasted_iota(jnp.int32, (count, 128), 1)
 
-    def swept(planes, index, start, scale):
+    def shift(planes, index, sums):
+        for start in range(8, 8 + size, count):
+            refs = [(planes[0], index), (planes[0], index + 16), (planes[1], index)]
+            part = [held[z, start : start + count] for held, z in refs]
+            left = [pltpu.roll(p, 1, 1) for p in part]
+            right = [pltpu.roll(p, 127, 1) for p in part]
+            left[2] = jnp.where(lane == 0, left[0], jnp.where(lane == 64, left[1], left[2]))
+            left[0] = jnp.where(lane == 0, 0.0, left[0])
+            left[1] = jnp.where(lane == 64, 0.0, left[1])
+            right[0] = jnp.where(lane == 127, right[2], right[0])
+            right[1] = jnp.where(lane == 63, right[2], right[1])
+            right[2] = jnp.where(lane % 64 == 63, 0.0, right[2])
+            for b in range(3):
+                sums[b, start - 8 : start - 8 + count] = left[b] + right[b]
+
+    def swept(planes, index, sums, start, scale):
         refs = [(planes[0], index), (planes[0], index + 16), (planes[1], index)]
-        part = [held[z, start : start + count] for held, z in refs]
-        left = [pltpu.roll(p, 1, 1) for p in part]
-        right = [pltpu.roll(p, 127, 1) for p in part]
-        left[2] = jnp.where(lane == 0, left[0], jnp.where(lane == 64, left[1], left[2]))
-        left[0] = jnp.where(lane == 0, 0.0, left[0])
-        left[1] = jnp.where(lane == 64, 0.0, left[1])
-        right[0] = jnp.where(lane == 127, right[2], right[0])
-        right[1] = jnp.where(lane == 63, right[2], right[1])
-        right[2] = jnp.where(lane % 64 == 63, 0.0, right[2])
         done = []
         for b, (held, z) in enumerate(refs):
             around = held[z - 1, start : start + count] + held[z + 1, start : start + count]
             around += held[z, start - 1 : start - 1 + count] + held[z, start + 1 : start + 1 + count]
-            around += left[b] + right[b]
-            done.append((0.1 * scale) * part[b] + (0.15 * scale) * around)
+            around += sums[b, start - 8 : start - 8 + count]
+            done.append(
+                (0.1 * scale) * held[z, start : start + count] + (0.15 * scale) * around
+            )
         return done
 
-    def first(index, carry):
-        for start in range(8, 8 + size, count):
-            done = swept((flat, pair), index, start, 1.0)
-            flat2[index, start : start + count] = done[0]
-            flat2[index + 16, start : start + count] = done[1]
-            pair2[index, start : start + count] = done[2]
-        return carry
-
-    lax.fori_loop(1, 15, first, 0)
+    def sweep(planes, store, scale, after):
+        shift(planes, 1, even)
+
+        def turn(step, carry):
+            index = 2 * step + 1
+            shift(planes, index + 1, odd)
+            for start in range(8, 8 + size, count):
+                store(index, start, swept(planes, index, even, start, scale))
+            shift(planes, jnp.minimum(index + 2, 14), even)
+            for start in range(8, 8 + size, count):
+                store(index + 1, start, swept(planes, index + 1, odd, start, scale))
+            after(index)
+            after(index + 1)
+            return carry
+
+        lax.fori_loop(0, 7, turn, 0)
+
+    def first(index, start, done):
+        flat2[index, start : start + count] = done[0]
+        flat2[index + 16, start : start + count] = done[1]
+        pair2[index, start : start + count] = done[2]
+
+    sweep((flat, pair), first, 1.0, lambda index: None)
     whole = lax.broadcasted_iota(jnp.int32, (size, 128), 1)
 
     @pl.when(zone == 0)
@@ -496,15 +518,14 @@
     def emit(z):
         return pltpu.make_async_copy(ready.at[z + 2], out.at[z], sems.at[z])
 
-    def second(index, carry):
-        for start in range(8, 8 + size, count):
-            done = swept((flat2, pair2), index, start, 1.0 / SCALE)
-            rows = slice(start - 8, start - 8 + count)
-            ready[index - 1, rows, :128] = done[0]
-            ready[index - 1, rows, 128:] = done[2][:, :64]
-            ready[index + 13, rows, :128] = pltpu.roll(done[1], 64, 1)
-            ready[index + 13, rows, 128:] = pltpu.roll(done[2], 64, 1)[:, :64]
-
+    def second(index, start, done):
+        rows = slice(start - 8, start - 8 + count)
+        ready[index - 1, rows, :128] = done[0]
+        ready[index - 1, rows, 128:] = done[2][:, :64]
+        ready[index + 13, rows, :128] = pltpu.roll(done[1], 64, 1)
+        ready[index + 13, rows, 128:] = pltpu.roll(done[2], 64, 1)[:, :64]
+
+    def depart(index):
         @pl.when(index >= 3)
         def _():
             emit(index - 3).start()
@@ -513,9 +534,7 @@
         def _():
             emit(index + 11).start()
 
-        return carry
-
-    lax.fori_loop(1, 15, second, 0)
+    sweep((flat2, pair2), second, 1.0 / SCALE, depart)
 
     def finish(z, carry):
         emit(z).wait()
@@ -537,6 +556,8 @@
             pltpu.VMEM((16, 208, 128), F32),
             pltpu.VMEM((32, 208, 128), F32),
             pltpu.VMEM((16, 208, 128), F32),
+            pltpu.VMEM((3, 192, 128), F32),
+            pltpu.VMEM((3, 192, 128), F32),
             pltpu.VMEM((28, 192, 192), F32),
             pltpu.SemaphoreType.DMA((24,)),
         ],
@@ -557,15 +578,17 @@
     cross += [(g + 1, zones + g) for g in range(zones - 1)]
     climb = [(g, zones + g) for g in range(zones)]
     climb += [(zones + g, g + 1) for g in range(zones - 1)]
-    rim = lax.dynamic_slice_in_dim(momenta[0], 9 * (1 - level), 3, axis=0)
-    other = lax.dynamic_slice_in_dim(momenta[1], 9 * level, 3, axis=0)
+    part = (1, 3) + momenta.shape[2:]
+    rim = lax.dynamic_slice(momenta, (0, 9 * (1 - level), 0, 0, 0), part)
+    other = lax.dynamic_slice(momenta, (1, 9 * level, 0, 0, 0), part)
     rim = lax.ppermute(rim, nearest, outward)
     other = lax.ppermute(other, nearest, cross)
 
     def spread(parts):
-        return [parts[0]] + [
-            lax.ppermute(parts[k], "subj", [(i, i ^ k) for i in range(8)]) for k in range(1, 8)
-        ]
+        arrived = {0: parts[0]}
+        for k in (3, 7, 5, 2, 6, 4, 1):
+            arrived[k] = lax.ppermute(parts[k], "subj", [(i, i ^ k) for i in range(8)])
+        return [arrived[k] for k in range(8)]
 
     packed = pack_images(info, images)
     planes = spread(packed)
@@ -577,17 +600,15 @@
     chunk, edge = warp(info, assign, planes, fields, below, above)
     edge = lax.ppermute(edge.astype(jnp.float16), nearest, cross)
     chunk = jnp.concatenate([chunk.astype(jnp.float16), edge], axis=0)
+    mine = {(0, 0): chunk}
+    for far, step in ((0, 1), (0, 3), (1, 0), (0, 2), (1, 1), (1, 3), (1, 2)):
+        perm = [(8 * a + i, 8 * (a ^ far) + (i ^ (2 * step))) for a in range(2) for i in range(8)]
+        mine[far, step] = lax.ppermute(chunk, ("level", "subj"), perm)
     gathered = []
     for far in range(2):
         for step in range(4):
-            part = chunk
-            if far or step:
-                perm = [
-                    (8 * a + i, 8 * (a ^ far) + (i ^ (2 * step))) for a in range(2) for i in range(8)
-                ]
-                part = lax.ppermute(chunk, ("level", "subj"), perm)
-            gathered.append(part)
-            gathered.append(lax.ppermute(part, "subj", [(i, i ^ 1) for i in range(8)]))
+            part = mine[far, step]
+            gathered += [part, lax.ppermute(part, "subj", [(i, i ^ 1) for i in range(8)])]
     chunks = jnp.stack(gathered).astype(F32)
     return relax(info, chunks)
 

time: 141 us -> 137 us (0.972)
  Pallas kernels: 38.8 us -> 35.1 us
  local copies, waits for them, and re-layouts: 7.72 us -> 4.74 us
  waiting for transfers between devices: 41.2 us -> 43.6 us
    pallas_call x1, Pallas kernels: 14 us -> 10.9 us  [relax(): pl.pallas_call(relax_kernel, grid=(), in_specs=[pl.BlockSpec(memory_space...]
    slice x1 -> x0, local copies, waits for them, and re-layouts: 2.09 us -> none  [update(): other = lax.dynamic_slice_in_dim(momenta[1], 9 * level, 3, axis=0)]
    ppermute x29, waiting for transfers between devices: 40.2 us -> 42.2 us  [the longest x14 34.6 us: spread(): arrived[k] = lax.ppermute(parts[k], 'subj', [(i, i ^ k) for i in range(8)])]
    unnamed x44 -> x50, local copies, waits for them, and re-layouts: 3.5 us -> 3.49 us
  transfers between devices with their start and end apart: 34 -> 34, of which waited for: 15 -> 15; matrix products, arithmetic and copies ran while one was open for 4% -> 2% of each run, Pallas kernels for 8% -> 8%
where the time goes in v1:
time: 137 us; the launch traced here: 136 us
  starting transfers between devices  47.4 us (35%)
  waiting for transfers between devices  43.6 us (32%)
  Pallas kernels  35.1 us (26%)
  local copies, waits for them, and re-layouts  4.74 us (3%)
  other arithmetic  4.57 us (3%)
    ppermute x14, waiting for transfers between devices, spread(): arrived[k] = lax.ppermute(parts[k], 'subj', [(i, i ^ k) for i in range(8)])  34.6 us
    ppermute x14, starting transfers between devices, spread(): arrived[k] = lax.ppermute(parts[k], 'subj', [(i, i ^ k) for i in range(8)])  14.3 us
    ppermute x7, starting transfers between devices, update(): mine[far, step] = lax.ppermute(chunk, ('level', 'subj'), perm)  13.1 us
    pallas_call x1, Pallas kernels, relax(): pl.pallas_call(relax_kernel, grid=(), in_specs=[pl.BlockSpec(memory_space...  10.9 us
    pallas_call x1, Pallas kernels, warp(): pl.pallas_call(warp_kernel, grid=(), in_specs=[smem, smem, vmem, vmem, vm...  9.54 us
    pallas_call x1, Pallas kernels, blur(): pl.pallas_call(blur_kernel, grid=(), in_specs=[pl.BlockSpec(memory_space=...  9.05 us
    ppermute x7, waiting for transfers between devices, update(): mine[far, step] = lax.ppermute(chunk, ('level', 'subj'), perm)  5.54 us
    ppermute x1, starting transfers between devices, update(): rim = lax.ppermute(rim, nearest, outward)  5.16 us
  transfers between devices with their start and end apart: 34, of which 15 were waited for; matrix products, arithmetic and copies ran while one was open for 2% of the time, Pallas kernels for 8%

profile of v1, /device:TPU:96, one launch (start us, length us, event | category | flops | bytes accessed | tf_op | source)
XLA Modules:
  0.0 136.0 jit_solution(181411264070990847)
XLA Ops:
  0.0 0.6 pad_add_fusion.info
  0.6 3.9 %pack_images.1 = (bf16[12,80,128]{2,1,0:T(8,128)(2,1)}, bf16[12,80,128]{2,1,0:T(8,128)(2,1)}, bf16[12,80,128]{2,1,0:T(8,128)(2,1)}, bf16[12,80,128]{2,1,0:T(8,12...) custom-call(s32[3]{0:T(128)} %pad_add_fusion.info, ...), custom_call_target="tpu_custom_call" | custom-call | tf_op jit(solution)/shard_map/pack_images/pallas_call | solution.py:105
  4.4 0.1 collective-permute-start
  4.5 1.7 %collective-permute-start.1 = (bf16[12,80,128]{2,1,0:T(8,128)(2,1)}, bf16[12,80,128]{2,1,0:T(8,128)(2,1)S(1)}, u32[]{:S(2)}, u32[]{:S(2)}) collective-permute-start(bf16[12,80,128]{2,1,0:T(8,128)(2,1)} %get-tuple-element.27), channel_id=1, source_target_pairs={{0,16},{8,24},{16,0},{24,8},{32,48},{40,56},{48,32},{56,40},{1,17}... | collective-permute-start | bytes 737288 | tf_op jit(solution)/shard_map/ppermute | solution.py:590
  6.2 0.2 collective-permute-start.2
  6.4 3.2 %collective-permute-start.3 = (bf16[12,80,128]{2,1,0:T(8,128)(2,1)}, bf16[12,80,128]{2,1,0:T(8,128)(2,1)S(1)}, u32[]{:S(2)}, u32[]{:S(2)}) collective-permute-start(bf16[12,80,128]{2,1,0:T(8,128)(2,1)} %get-tuple-element.29), channel_id=1, source_target_pairs={{0,32},{8,40},{16,48},{24,56},{32,0},{40,8},{48,16},{56,24},{1,33}... | collective-permute-start | bytes 737288 | tf_op jit(solution)/shard_map/ppermute | solution.py:590
  9.6 1.2 constant_dynamic-slice_fusion
  10.8 3.2 %collective-permute-start.8 = (f32[1,3,3,96,96]{4,3,2,1,0:T(8,128)S(1)}, f32[1,3,3,96,96]{4,3,2,1,0:T(8,128)S(1)}, u32[]{:S(2)}, u32[]{:S(2)}) collective-permute-start(f32[1,3,3,96,96]{4,3,2,1,0:T(8,128)S(1)} %get-tuple-element.45), channel_id=1, source_target_pairs={{64,1},{65,2},{66,3},{67,4},{68,5},{69,6},{70,7},{1,64},{2,65},{3,... | collective-permute-start | bytes 995336 | tf_op jit(solution)/shard_map/ppermute | solution.py:585
  14.0 0.0 collective-permute-done.refs_1_.rest_1_
  14.0 5.2 %collective-permute-start.7 = (f32[1,3,3,96,96]{4,3,2,1,0:T(8,128)S(1)}, f32[1,3,3,96,96]{4,3,2,1,0:T(8,128)S(1)}, u32[]{:S(2)}, u32[]{:S(2)}) collective-permute-start(f32[1,3,3,96,96]{4,3,2,1,0:T(8,128)S(1)} %get-tuple-element.46), channel_id=1, source_target_pairs={{0,1},{1,2},{2,3},{3,4},{4,5},{5,6},{6,7},{65,64},{66,65},{67,66},... | collective-permute-start | bytes 995336 | tf_op jit(solution)/shard_map/ppermute | solution.py:584
  19.2 0.0 collective-permute-done.1.refs_2_.rest_2_
  19.2 0.1 collective-permute-start.4
  19.3 0.0 collective-permute-done.2.refs_3_.rest_3_
  19.3 2.5 %collective-permute-start.5 = (bf16[12,80,128]{2,1,0:T(8,128)(2,1)}, bf16[12,80,128]{2,1,0:T(8,128)(2,1)S(1)}, u32[]{:S(2)}, u32[]{:S(2)}) collective-permute-start(bf16[12,80,128]{2,1,0:T(8,128)(2,1)} %get-tuple-element.31), channel_id=1, source_target_pairs={{0,48},{8,56},{16,32},{24,40},{32,16},{40,24},{48,0},{56,8},{1,49}... | collective-permute-start | bytes 737288 | tf_op jit(solution)/shard_map/ppermute | solution.py:590
  21.8 4.9 %collective-permute-done.3.refs_4_.rest_4_ = bf16[12,80,128]{2,1,0:T(8,128)(2,1)S(1)} collective-permute-done((bf16[12,80,128]{2,1,0:T(8,128)(2,1)}, bf16[12,80,128]{2,1,0:T(8,128)(2,1)S(1)}, u32[]{:S(2)}, u32[]{:S(2)}) %collective-permute-start.3) | collective-permute-done | bytes 245792 | tf_op jit(solution)/shard_map/ppermute | solution.py:590
  26.7 0.0 collective-permute-start.6
  26.7 4.2 %collective-permute-done.4.refs_5_.rest_5_ = bf16[12,80,128]{2,1,0:T(8,128)(2,1)S(1)} collective-permute-done((bf16[12,80,128]{2,1,0:T(8,128)(2,1)}, bf16[12,80,128]{2,1,0:T(8,128)(2,1)S(1)}, u32[]{:S(2)}, u32[]{:S(2)}) %collective-permute-start.4) | collective-permute-done | bytes 245792 | tf_op jit(solution)/shard_map/ppermute | solution.py:590
  30.9 5.8 %collective-permute-done.5.refs_6_.rest_6_ = bf16[12,80,128]{2,1,0:T(8,128)(2,1)S(1)} collective-permute-done((bf16[12,80,128]{2,1,0:T(8,128)(2,1)}, bf16[12,80,128]{2,1,0:T(8,128)(2,1)S(1)}, u32[]{:S(2)}, u32[]{:S(2)}) %collective-permute-start.5) | collective-permute-done | bytes 245792 | tf_op jit(solution)/shard_map/ppermute | solution.py:590
  36.7 5.2 %collective-permute-done.6.refs_7_.rest_7_ = bf16[12,80,128]{2,1,0:T(8,128)(2,1)S(1)} collective-permute-done((bf16[12,80,128]{2,1,0:T(8,128)(2,1)}, bf16[12,80,128]{2,1,0:T(8,128)(2,1)S(1)}, u32[]{:S(2)}, u32[]{:S(2)}) %collective-permute-start.6) | collective-permute-done | bytes 245792 | tf_op jit(solution)/shard_map/ppermute | solution.py:590
  41.9 0.7 copy-done.6
  42.5 1.8 %cut_edges.1 = (bf16[8,80,128]{2,1,0:T(8,128)(2,1)}, bf16[8,80,128]{2,1,0:T(8,128)(2,1)}) custom-call(bf16[12,80,128]{2,1,0:T(8,128)(2,1)} %get-tuple-element.25.refs_0_.rest_0_, bf16[12,80,128]{2,1,0:T(8,128)(2,1)} %copy-done, bf16[12,80,128]{2,1,0:T(8,128)(2,1)} %copy-done.1, bf16[12,80,128]{2,1,0:T(8,128)(2,1)} %copy-done.2, ...), custom_call_target="tpu_custom_call" | custom-call | tf_op jit(solution)/shard_map/cut_edges/pallas_call | solution.py:240
  44.3 3.3 %collective-permute-start.16 = (bf16[8,80,128]{2,1,0:T(8,128)(2,1)}, bf16[8,80,128]{2,1,0:T(8,128)(2,1)S(1)}, u32[]{:S(2)}, u32[]{:S(2)}) collective-permute-start(bf16[8,80,128]{2,1,0:T(8,128)(2,1)} %get-tuple-element.41), channel_id=1, source_target_pairs={{0,64},{1,65},{2,66},{3,67},{4,68},{5,69},{6,70},{7,71},{64,1},{65... | collective-permute-start | bytes 491528 | tf_op jit(solution)/shard_map/ppermute | solution.py:598
  47.6 2.5 %collective-permute-start.17 = (bf16[8,80,128]{2,1,0:T(8,128)(2,1)}, bf16[8,80,128]{2,1,0:T(8,128)(2,1)S(1)}, u32[]{:S(2)}, u32[]{:S(2)}) collective-permute-start(bf16[8,80,128]{2,1,0:T(8,128)(2,1)} %get-tuple-element.42), channel_id=1, source_target_pairs={{64,0},{65,1},{66,2},{67,3},{68,4},{69,5},{70,6},{71,7},{1,64},{2,... | collective-permute-start | bytes 491528 | tf_op jit(solution)/shard_map/ppermute | solution.py:599
  50.2 0.0 collective-permute-done.8.other
  50.2 0.8 copy-done.7
  51.0 0.8 copy-done.8
  51.7 9.1 %blur_momenta.1 = (bf16[560,128]{1,0:T(8,128)(2,1)}, bf16[560,128]{1,0:T(8,128)(2,1)}, bf16[560,128]{1,0:T(8,128)(2,1)}, bf16[560,128]{1,0:T(8,128)(2,1)}, bf16[...) custom-call(s32[3]{0:T(128)} %pad_add_fusion.info, ...), custom_call_target="tpu_custom_call" | custom-call | tf_op jit(solution)/shard_map/blur_momenta/pallas_call | solution.py:191
  60.8 0.1 collective-permute-start.9
  60.9 0.3 collective-permute-start.10
  61.2 1.6 %collective-permute-start.11 = (bf16[560,128]{1,0:T(8,128)(2,1)}, bf16[560,128]{1,0:T(8,128)(2,1)S(1)}, u32[]{:S(2)}, u32[]{:S(2)}) collective-permute-start(bf16[560,128]{1,0:T(8,128)(2,1)} %get-tuple-element.36), channel_id=1, source_target_pairs={{0,24},{8,16},{16,8},{24,0},{32,56},{40,48},{48,40},{56,32},{1,25}... | collective-permute-start | bytes 430088 | tf_op jit(solution)/shard_map/ppermute | solution.py:590
  62.8 0.7 collective-permute-start.12
  63.4 2.5 %collective-permute-start.13 = (bf16[560,128]{1,0:T(8,128)(2,1)}, bf16[560,128]{1,0:T(8,128)(2,1)S(1)}, u32[]{:S(2)}, u32[]{:S(2)}) collective-permute-start(bf16[560,128]{1,0:T(8,128)(2,1)} %get-tuple-element.38), channel_id=1, source_target_pairs={{0,40},{8,32},{16,56},{24,48},{32,8},{40,0},{48,24},{56,16},{1,41}... | collective-permute-start | bytes 430088 | tf_op jit(solution)/shard_map/ppermute | solution.py:590
  66.0 0.3 collective-permute-start.14
  66.3 1.6 %collective-permute-done.10.rest_10_ = bf16[560,128]{1,0:T(8,128)(2,1)S(1)} collective-permute-done((bf16[560,128]{1,0:T(8,128)(2,1)}, bf16[560,128]{1,0:T(8,128)(2,1)S(1)}, u32[]{:S(2)}, u32[]{:S(2)}) %collective-permute-start.10) | collective-permute-done | bytes 143392 | tf_op jit(solution)/shard_map/ppermute | solution.py:590
  67.8 1.2 collective-permute-start.15
  69.0 0.8 collective-permute-done.11.rest_11_
  69.8 4.0 %collective-permute-done.12.rest_12_ = bf16[560,128]{1,0:T(8,128)(2,1)S(1)} collective-permute-done((bf16[560,128]{1,0:T(8,128)(2,1)}, bf16[560,128]{1,0:T(8,128)(2,1)S(1)}, u32[]{:S(2)}, u32[]{:S(2)}) %collective-permute-start.12) | collective-permute-done | bytes 143392 | tf_op jit(solution)/shard_map/ppermute | solution.py:590
  73.8 2.0 %collective-permute-done.13.rest_13_ = bf16[560,128]{1,0:T(8,128)(2,1)S(1)} collective-permute-done((bf16[560,128]{1,0:T(8,128)(2,1)}, bf16[560,128]{1,0:T(8,128)(2,1)S(1)}, u32[]{:S(2)}, u32[]{:S(2)}) %collective-permute-start.13) | collective-permute-done | bytes 143392 | tf_op jit(solution)/shard_map/ppermute | solution.py:590
  75.8 3.6 %collective-permute-done.14.rest_14_ = bf16[560,128]{1,0:T(8,128)(2,1)S(1)} collective-permute-done((bf16[560,128]{1,0:T(8,128)(2,1)}, bf16[560,128]{1,0:T(8,128)(2,1)S(1)}, u32[]{:S(2)}, u32[]{:S(2)}) %collective-permute-start.14) | collective-permute-done | bytes 143392 | tf_op jit(solution)/shard_map/ppermute | solution.py:590
  79.4 2.7 %collective-permute-done.15.rest_15_ = bf16[560,128]{1,0:T(8,128)(2,1)S(1)} collective-permute-done((bf16[560,128]{1,0:T(8,128)(2,1)}, bf16[560,128]{1,0:T(8,128)(2,1)S(1)}, u32[]{:S(2)}, u32[]{:S(2)}) %collective-permute-start.15) | collective-permute-done | bytes 143392 | tf_op jit(solution)/shard_map/ppermute | solution.py:590
  82.1 0.6 copy-done.17
  82.7 9.5 %warp_sum.1 = (f32[432,128]{1,0:T(8,128)}, f32[72,128]{1,0:T(8,128)}) custom-call(s32[3]{0:T(128)} %pad_add_fusion.info, s32[16]{0:T(128)} %assign.1, bf16[288,112]{1,0:T(8,128)(2,1)} %constant.27.clone.zy, bf16[256,256]{1,0:T(8,128)(2,1)} %constant.28.clone.x0, bf16[256,256]{1,0:T(8,128)(2,1)} %constant.29.clone.x1, ...), custom_call_target="tpu_custom_call" | custom-call | tf_op jit(solution)/shard_map/warp_sum/pallas_call | solution.py:387
  92.3 0.8 convert_element_type.10
  93.0 4.2 %collective-permute-start.18 = (f16[72,128]{1,0:T(8,128)(2,1)S(1)}, f16[72,128]{1,0:T(8,128)(2,1)S(1)}, u32[]{:S(2)}, u32[]{:S(2)}) collective-permute-start(f16[72,128]{1,0:T(8,128)(2,1)S(1)} %convert_element_type.10), channel_id=1, source_target_pairs={{64,1},{65,2},{66,3},{67,4},{68,5},{69,6},{70,7},{1,64},{2,65},{3,... | collective-permute-start | bytes 55304 | tf_op jit(solution)/shard_map/ppermute | solution.py:601
  97.2 1.0 convert_element_type.9
  98.2 1.4 %collective-permute-done.18 = f16[72,128]{1,0:T(8,128)(2,1)S(1)} collective-permute-done((f16[72,128]{1,0:T(8,128)(2,1)S(1)}, f16[72,128]{1,0:T(8,128)(2,1)S(1)}, u32[]{:S(2)}, u32[]{:S(2)}) %collective-permute-start.18) | collective-permute-done | bytes 18464 | tf_op jit(solution)/shard_map/ppermute | solution.py:601
  99.6 0.1 collective-permute-start.20
  99.7 0.1 collective-permute-start.19
  99.8 5.0 %collective-permute-start.30 = (f16[504,128]{1,0:T(8,128)(2,1)S(1)}, f16[504,128]{1,0:T(8,128)(2,1)S(1)}, u32[]{:S(2)}, u32[]{:S(2)}) collective-permute-start(f16[504,128]{1,0:T(8,128)(2,1)S(1)} %pad_maximum_fusion), channel_id=1, source_target_pairs={{0,96},{8,104},{16,112},{24,120},{32,64},{40,72},{48,80},{56,88},{... | collective-permute-start | bytes 387080 | tf_op jit(solution)/shard_map/ppermute | solution.py:606
  104.8 0.1 collective-permute-start.28
  105.0 0.9 collective-permute-start.26
  105.9 2.9 %collective-permute-start.24 = (f16[504,128]{1,0:T(8,128)(2,1)S(1)}, f16[504,128]{1,0:T(8,128)(2,1)S(1)}, u32[]{:S(2)}, u32[]{:S(2)}) collective-permute-start(f16[504,128]{1,0:T(8,128)(2,1)S(1)} %pad_maximum_fusion), channel_id=1, source_target_pairs={{0,48},{8,56},{16,32},{24,40},{32,16},{40,24},{48,0},{56,8},{64,11... | collective-permute-start | bytes 387080 | tf_op jit(solution)/shard_map/ppermute | solution.py:606
  108.9 1.2 collective-permute-done.21
  110.2 2.0 %collective-permute-start.22 = (f16[504,128]{1,0:T(8,128)(2,1)S(1)}, f16[504,128]{1,0:T(8,128)(2,1)S(1)}, u32[]{:S(2)}, u32[]{:S(2)}) collective-permute-start(f16[504,128]{1,0:T(8,128)(2,1)S(1)} %pad_maximum_fusion), channel_id=1, source_target_pairs={{0,32},{8,40},{16,48},{24,56},{32,0},{40,8},{48,16},{56,24},{64,96... | collective-permute-start | bytes 387080 | tf_op jit(solution)/shard_map/ppermute | solution.py:606
  112.2 2.1 %collective-permute-start.32 = (f16[504,128]{1,0:T(8,128)(2,1)S(1)}, f16[504,128]{1,0:T(8,128)(2,1)S(1)}, u32[]{:S(2)}, u32[]{:S(2)}) collective-permute-start(f16[504,128]{1,0:T(8,128)(2,1)S(1)} %pad_maximum_fusion), channel_id=1, source_target_pairs={{0,112},{8,120},{16,96},{24,104},{32,80},{40,88},{48,64},{56,72},{... | collective-permute-start | bytes 387080 | tf_op jit(solution)/shard_map/ppermute | solution.py:606
  114.2 3.0 %collective-permute-done.22 = f16[504,128]{1,0:T(8,128)(2,1)S(1)} collective-permute-done((f16[504,128]{1,0:T(8,128)(2,1)S(1)}, f16[504,128]{1,0:T(8,128)(2,1)S(1)}, u32[]{:S(2)}, u32[]{:S(2)}) %collective-permute-start.22) | collective-permute-done | bytes 129056 | tf_op jit(solution)/shard_map/ppermute | solution.py:606
  117.3 0.6 collective-permute-start.31
  117.9 0.3 collective-permute-start.29
  118.2 0.2 collective-permute-start.27
  118.4 2.5 %collective-permute-done.32 = f16[504,128]{1,0:T(8,128)(2,1)S(1)} collective-permute-done((f16[504,128]{1,0:T(8,128)(2,1)S(1)}, f16[504,128]{1,0:T(8,128)(2,1)S(1)}, u32[]{:S(2)}, u32[]{:S(2)}) %collective-permute-start.32) | collective-permute-done | bytes 129056 | tf_op jit(solution)/shard_map/ppermute | solution.py:606
  120.9 0.5 collective-permute-start.33
  121.5 0.7 collective-permute-done.25
  122.8 2.2 %convert_element_type.11.chunks = f32[16,504,128]{2,1,0:T(8,128)} convert(f16[16,504,128]{2,1,0:T(8,128)(2,1)S(1)} %bitcast_dynamic-update-slice_fusion) | non-fusion elementwise | flops 1032192 | bytes 6193152 | tf_op jit(solution)/shard_map/convert_element_type | solution.py:612
  125.0 10.9 %relax.1 = f32[24,192,192]{2,1,0:T(8,128)} custom-call(s32[3]{0:T(128)} %pad_add_fusion.info, f32[16,504,128]{2,1,0:T(8,128)} %convert_element_type.11.chunks), custom_call_target="tpu_custom_call" | custom-call | tf_op jit(solution)/shard_map/relax/pallas_call | solution.py:548
  (67 shorter events, 0.9 us)
Async XLA Ops:
  4.4 9.6 %collective-permute-start = (bf16[12,80,128]{2,1,0:T(8,128)(2,1)}, bf16[12,80,128]{2,1,0:T(8,128)(2,1)S(1)}, u32[]{:S(2)}, u32[]{:S(2)}) collective-permute-start(bf16[12,80,128]{2,1,0:T(8,128)(2,1)} %get-tuple-element.26), channel_id=1, source_target_pairs={{0,8},{8,0},{16,24},{24,16},{32,40},{40,32},{48,56},{56,48},{1,9},... | collective-permute-start | bytes 737288 | tf_op jit(solution)/shard_map/ppermute | solution.py:590
  4.5 14.7 %collective-permute-start.1 = (bf16[12,80,128]{2,1,0:T(8,128)(2,1)}, bf16[12,80,128]{2,1,0:T(8,128)(2,1)S(1)}, u32[]{:S(2)}, u32[]{:S(2)}) collective-permute-start(bf16[12,80,128]{2,1,0:T(8,128)(2,1)} %get-tuple-element.27), channel_id=1, source_target_pairs={{0,16},{8,24},{16,0},{24,8},{32,48},{40,56},{48,32},{56,40},{1,17}... | collective-permute-start | bytes 737288 | tf_op jit(solution)/shard_map/ppermute | solution.py:590
  6.2 13.1 %collective-permute-start.2 = (bf16[12,80,128]{2,1,0:T(8,128)(2,1)}, bf16[12,80,128]{2,1,0:T(8,128)(2,1)S(1)}, u32[]{:S(2)}, u32[]{:S(2)}) collective-permute-start(bf16[12,80,128]{2,1,0:T(8,128)(2,1)} %get-tuple-element.28), channel_id=1, source_target_pairs={{0,24},{8,16},{16,8},{24,0},{32,56},{40,48},{48,40},{56,32},{1,25}... | collective-permute-start | bytes 737288 | tf_op jit(solution)/shard_map/ppermute | solution.py:590
  6.4 20.4 %collective-permute-start.3 = (bf16[12,80,128]{2,1,0:T(8,128)(2,1)}, bf16[12,80,128]{2,1,0:T(8,128)(2,1)S(1)}, u32[]{:S(2)}, u32[]{:S(2)}) collective-permute-start(bf16[12,80,128]{2,1,0:T(8,128)(2,1)} %get-tuple-element.29), channel_id=1, source_target_pairs={{0,32},{8,40},{16,48},{24,56},{32,0},{40,8},{48,16},{56,24},{1,33}... | collective-permute-start | bytes 737288 | tf_op jit(solution)/shard_map/ppermute | solution.py:590
  10.8 39.4 %collective-permute-start.8 = (f32[1,3,3,96,96]{4,3,2,1,0:T(8,128)S(1)}, f32[1,3,3,96,96]{4,3,2,1,0:T(8,128)S(1)}, u32[]{:S(2)}, u32[]{:S(2)}) collective-permute-start(f32[1,3,3,96,96]{4,3,2,1,0:T(8,128)S(1)} %get-tuple-element.45), channel_id=1, source_target_pairs={{64,1},{65,2},{66,3},{67,4},{68,5},{69,6},{70,7},{1,64},{2,65},{3,... | collective-permute-start | bytes 995336 | tf_op jit(solution)/shard_map/ppermute | solution.py:585
  14.0 27.8 %copy-start = (bf16[12,80,128]{2,1,0:T(8,128)(2,1)}, bf16[12,80,128]{2,1,0:T(8,128)(2,1)S(1)}, u32[]{:S(2)}) copy-start(bf16[12,80,128]{2,1,0:T(8,128)(2,1)S(1)} %collective-permute-done.refs_1_.rest_1_) | copy-start | bytes 737284
  14.0 36.2 %collective-permute-start.7 = (f32[1,3,3,96,96]{4,3,2,1,0:T(8,128)S(1)}, f32[1,3,3,96,96]{4,3,2,1,0:T(8,128)S(1)}, u32[]{:S(2)}, u32[]{:S(2)}) collective-permute-start(f32[1,3,3,96,96]{4,3,2,1,0:T(8,128)S(1)} %get-tuple-element.46), channel_id=1, source_target_pairs={{0,1},{1,2},{2,3},{3,4},{4,5},{5,6},{6,7},{65,64},{66,65},{67,66},... | collective-permute-start | bytes 995336 | tf_op jit(solution)/shard_map/ppermute | solution.py:584
  19.2 22.6 %copy-start.1 = (bf16[12,80,128]{2,1,0:T(8,128)(2,1)}, bf16[12,80,128]{2,1,0:T(8,128)(2,1)S(1)}, u32[]{:S(2)}) copy-start(bf16[12,80,128]{2,1,0:T(8,128)(2,1)S(1)} %collective-permute-done.1.refs_2_.rest_2_) | copy-start | bytes 737284
  19.2 11.7 %collective-permute-start.4 = (bf16[12,80,128]{2,1,0:T(8,128)(2,1)}, bf16[12,80,128]{2,1,0:T(8,128)(2,1)S(1)}, u32[]{:S(2)}, u32[]{:S(2)}) collective-permute-start(bf16[12,80,128]{2,1,0:T(8,128)(2,1)} %get-tuple-element.30), channel_id=1, source_target_pairs={{0,40},{8,32},{16,56},{24,48},{32,8},{40,0},{48,24},{56,16},{1,41}... | collective-permute-start | bytes 737288 | tf_op jit(solution)/shard_map/ppermute | solution.py:590
  19.3 22.5 %copy-start.2 = (bf16[12,80,128]{2,1,0:T(8,128)(2,1)}, bf16[12,80,128]{2,1,0:T(8,128)(2,1)S(1)}, u32[]{:S(2)}) copy-start(bf16[12,80,128]{2,1,0:T(8,128)(2,1)S(1)} %collective-permute-done.2.refs_3_.rest_3_) | copy-start | bytes 737284
  19.3 17.3 %collective-permute-start.5 = (bf16[12,80,128]{2,1,0:T(8,128)(2,1)}, bf16[12,80,128]{2,1,0:T(8,128)(2,1)S(1)}, u32[]{:S(2)}, u32[]{:S(2)}) collective-permute-start(bf16[12,80,128]{2,1,0:T(8,128)(2,1)} %get-tuple-element.31), channel_id=1, source_target_pairs={{0,48},{8,56},{16,32},{24,40},{32,16},{40,24},{48,0},{56,8},{1,49}... | collective-permute-start | bytes 737288 | tf_op jit(solution)/shard_map/ppermute | solution.py:590
  26.7 15.1 %copy-start.3 = (bf16[12,80,128]{2,1,0:T(8,128)(2,1)}, bf16[12,80,128]{2,1,0:T(8,128)(2,1)S(1)}, u32[]{:S(2)}) copy-start(bf16[12,80,128]{2,1,0:T(8,128)(2,1)S(1)} %collective-permute-done.3.refs_4_.rest_4_) | copy-start | bytes 737284
  26.7 15.1 %collective-permute-start.6 = (bf16[12,80,128]{2,1,0:T(8,128)(2,1)}, bf16[12,80,128]{2,1,0:T(8,128)(2,1)S(1)}, u32[]{:S(2)}, u32[]{:S(2)}) collective-permute-start(bf16[12,80,128]{2,1,0:T(8,128)(2,1)} %get-tuple-element.32), channel_id=1, source_target_pairs={{0,56},{8,48},{16,40},{24,32},{32,24},{40,16},{48,8},{56,0},{1,57}... | collective-permute-start | bytes 737288 | tf_op jit(solution)/shard_map/ppermute | solution.py:590
  30.9 11.0 %copy-start.4 = (bf16[12,80,128]{2,1,0:T(8,128)(2,1)}, bf16[12,80,128]{2,1,0:T(8,128)(2,1)S(1)}, u32[]{:S(2)}) copy-start(bf16[12,80,128]{2,1,0:T(8,128)(2,1)S(1)} %collective-permute-done.4.refs_5_.rest_5_) | copy-start | bytes 737284
  36.7 5.2 %copy-start.5 = (bf16[12,80,128]{2,1,0:T(8,128)(2,1)}, bf16[12,80,128]{2,1,0:T(8,128)(2,1)S(1)}, u32[]{:S(2)}) copy-start(bf16[12,80,128]{2,1,0:T(8,128)(2,1)S(1)} %collective-permute-done.5.refs_6_.rest_6_) | copy-start | bytes 737284
  41.8 0.7 copy-start.6
  44.3 18.4 %collective-permute-start.16 = (bf16[8,80,128]{2,1,0:T(8,128)(2,1)}, bf16[8,80,128]{2,1,0:T(8,128)(2,1)S(1)}, u32[]{:S(2)}, u32[]{:S(2)}) collective-permute-start(bf16[8,80,128]{2,1,0:T(8,128)(2,1)} %get-tuple-element.41), channel_id=1, source_target_pairs={{0,64},{1,65},{2,66},{3,67},{4,68},{5,69},{6,70},{7,71},{64,1},{65... | collective-permute-start | bytes 491528 | tf_op jit(solution)/shard_map/ppermute | solution.py:598
  47.6 15.8 %collective-permute-start.17 = (bf16[8,80,128]{2,1,0:T(8,128)(2,1)}, bf16[8,80,128]{2,1,0:T(8,128)(2,1)S(1)}, u32[]{:S(2)}, u32[]{:S(2)}) collective-permute-start(bf16[8,80,128]{2,1,0:T(8,128)(2,1)} %get-tuple-element.42), channel_id=1, source_target_pairs={{64,0},{65,1},{66,2},{67,3},{68,4},{69,5},{70,6},{71,7},{1,64},{2,... | collective-permute-start | bytes 491528 | tf_op jit(solution)/shard_map/ppermute | solution.py:599
  50.2 0.8 copy-start.7
  51.0 0.8 copy-start.8
  60.8 5.2 %collective-permute-start.9 = (bf16[560,128]{1,0:T(8,128)(2,1)}, bf16[560,128]{1,0:T(8,128)(2,1)S(1)}, u32[]{:S(2)}, u32[]{:S(2)}) collective-permute-start(bf16[560,128]{1,0:T(8,128)(2,1)} %get-tuple-element.34), channel_id=1, source_target_pairs={{0,8},{8,0},{16,24},{24,16},{32,40},{40,32},{48,56},{56,48},{1,9},... | collective-permute-start | bytes 430088 | tf_op jit(solution)/shard_map/ppermute | solution.py:590
  60.9 6.9 %collective-permute-start.10 = (bf16[560,128]{1,0:T(8,128)(2,1)}, bf16[560,128]{1,0:T(8,128)(2,1)S(1)}, u32[]{:S(2)}, u32[]{:S(2)}) collective-permute-start(bf16[560,128]{1,0:T(8,128)(2,1)} %get-tuple-element.35), channel_id=1, source_target_pairs={{0,16},{8,24},{16,0},{24,8},{32,48},{40,56},{48,32},{56,40},{1,17}... | collective-permute-start | bytes 430088 | tf_op jit(solution)/shard_map/ppermute | solution.py:590
  61.2 8.6 %collective-permute-start.11 = (bf16[560,128]{1,0:T(8,128)(2,1)}, bf16[560,128]{1,0:T(8,128)(2,1)S(1)}, u32[]{:S(2)}, u32[]{:S(2)}) collective-permute-start(bf16[560,128]{1,0:T(8,128)(2,1)} %get-tuple-element.36), channel_id=1, source_target_pairs={{0,24},{8,16},{16,8},{24,0},{32,56},{40,48},{48,40},{56,32},{1,25}... | collective-permute-start | bytes 430088 | tf_op jit(solution)/shard_map/ppermute | solution.py:590
  62.8 19.3 %copy-start.9 = (bf16[8,80,128]{2,1,0:T(8,128)(2,1)}, bf16[8,80,128]{2,1,0:T(8,128)(2,1)S(1)}, u32[]{:S(2)}) copy-start(bf16[8,80,128]{2,1,0:T(8,128)(2,1)S(1)} %collective-permute-done.16.rest_16_) | copy-start | bytes 491524
  62.8 11.0 %collective-permute-start.12 = (bf16[560,128]{1,0:T(8,128)(2,1)}, bf16[560,128]{1,0:T(8,128)(2,1)S(1)}, u32[]{:S(2)}, u32[]{:S(2)}) collective-permute-start(bf16[560,128]{1,0:T(8,128)(2,1)} %get-tuple-element.37), channel_id=1, source_target_pairs={{0,32},{8,40},{16,48},{24,56},{32,0},{40,8},{48,16},{56,24},{1,33}... | collective-permute-start | bytes 430088 | tf_op jit(solution)/shard_map/ppermute | solution.py:590
  63.4 18.6 %copy-start.10 = (bf16[8,80,128]{2,1,0:T(8,128)(2,1)}, bf16[8,80,128]{2,1,0:T(8,128)(2,1)S(1)}, u32[]{:S(2)}) copy-start(bf16[8,80,128]{2,1,0:T(8,128)(2,1)S(1)} %collective-permute-done.17.rest_17_) | copy-start | bytes 491524
  63.4 12.3 %collective-permute-start.13 = (bf16[560,128]{1,0:T(8,128)(2,1)}, bf16[560,128]{1,0:T(8,128)(2,1)S(1)}, u32[]{:S(2)}, u32[]{:S(2)}) collective-permute-start(bf16[560,128]{1,0:T(8,128)(2,1)} %get-tuple-element.38), channel_id=1, source_target_pairs={{0,40},{8,32},{16,56},{24,48},{32,8},{40,0},{48,24},{56,16},{1,41}... | collective-permute-start | bytes 430088 | tf_op jit(solution)/shard_map/ppermute | solution.py:590
  66.0 16.1 %copy-start.11 = (bf16[560,128]{1,0:T(8,128)(2,1)}, bf16[560,128]{1,0:T(8,128)(2,1)S(1)}, u32[]{:S(2)}) copy-start(bf16[560,128]{1,0:T(8,128)(2,1)S(1)} %collective-permute-done.9.rest_9_) | copy-start | bytes 430084
  66.0 13.4 %collective-permute-start.14 = (bf16[560,128]{1,0:T(8,128)(2,1)}, bf16[560,128]{1,0:T(8,128)(2,1)S(1)}, u32[]{:S(2)}, u32[]{:S(2)}) collective-permute-start(bf16[560,128]{1,0:T(8,128)(2,1)} %get-tuple-element.39), channel_id=1, source_target_pairs={{0,48},{8,56},{16,32},{24,40},{32,16},{40,24},{48,0},{56,8},{1,49}... | collective-permute-start | bytes 430088 | tf_op jit(solution)/shard_map/ppermute | solution.py:590
  67.8 14.3 %copy-start.12 = (bf16[560,128]{1,0:T(8,128)(2,1)}, bf16[560,128]{1,0:T(8,128)(2,1)S(1)}, u32[]{:S(2)}) copy-start(bf16[560,128]{1,0:T(8,128)(2,1)S(1)} %collective-permute-done.10.rest_10_) | copy-start | bytes 430084
  67.8 14.2 %collective-permute-start.15 = (bf16[560,128]{1,0:T(8,128)(2,1)}, bf16[560,128]{1,0:T(8,128)(2,1)S(1)}, u32[]{:S(2)}, u32[]{:S(2)}) collective-permute-start(bf16[560,128]{1,0:T(8,128)(2,1)} %get-tuple-element.40), channel_id=1, source_target_pairs={{0,56},{8,48},{16,40},{24,32},{32,24},{40,16},{48,8},{56,0},{1,57}... | collective-permute-start | bytes 430088 | tf_op jit(solution)/shard_map/ppermute | solution.py:590
  69.8 12.3 %copy-start.13 = (bf16[560,128]{1,0:T(8,128)(2,1)}, bf16[560,128]{1,0:T(8,128)(2,1)S(1)}, u32[]{:S(2)}) copy-start(bf16[560,128]{1,0:T(8,128)(2,1)S(1)} %collective-permute-done.11.rest_11_) | copy-start | bytes 430084
  73.8 8.3 %copy-start.14 = (bf16[560,128]{1,0:T(8,128)(2,1)}, bf16[560,128]{1,0:T(8,128)(2,1)S(1)}, u32[]{:S(2)}) copy-start(bf16[560,128]{1,0:T(8,128)(2,1)S(1)} %collective-permute-done.12.rest_12_) | copy-start | bytes 430084
  75.8 6.4 %copy-start.15 = (bf16[560,128]{1,0:T(8,128)(2,1)}, bf16[560,128]{1,0:T(8,128)(2,1)S(1)}, u32[]{:S(2)}) copy-start(bf16[560,128]{1,0:T(8,128)(2,1)S(1)} %collective-permute-done.13.rest_13_) | copy-start | bytes 430084
  79.4 2.7 %copy-start.16 = (bf16[560,128]{1,0:T(8,128)(2,1)}, bf16[560,128]{1,0:T(8,128)(2,1)S(1)}, u32[]{:S(2)}) copy-start(bf16[560,128]{1,0:T(8,128)(2,1)S(1)} %collective-permute-done.14.rest_14_) | copy-start | bytes 430084
  82.1 0.7 copy-start.17
  93.0 6.5 %collective-permute-start.18 = (f16[72,128]{1,0:T(8,128)(2,1)S(1)}, f16[72,128]{1,0:T(8,128)(2,1)S(1)}, u32[]{:S(2)}, u32[]{:S(2)}) collective-permute-start(f16[72,128]{1,0:T(8,128)(2,1)S(1)} %convert_element_type.10), channel_id=1, source_target_pairs={{64,1},{65,2},{66,3},{67,4},{68,5},{69,6},{70,7},{1,64},{2,65},{3,... | collective-permute-start | bytes 55304 | tf_op jit(solution)/shard_map/ppermute | solution.py:601
  99.6 6.3 %collective-permute-start.20 = (f16[504,128]{1,0:T(8,128)(2,1)S(1)}, f16[504,128]{1,0:T(8,128)(2,1)S(1)}, u32[]{:S(2)}, u32[]{:S(2)}) collective-permute-start(f16[504,128]{1,0:T(8,128)(2,1)S(1)} %pad_maximum_fusion), channel_id=1, source_target_pairs={{0,16},{8,24},{16,0},{24,8},{32,48},{40,56},{48,32},{56,40},{64,80... | collective-permute-start | bytes 387080 | tf_op jit(solution)/shard_map/ppermute | solution.py:606
  99.7 9.1 %collective-permute-start.19 = (f16[504,128]{1,0:T(8,128)(2,1)S(1)}, f16[504,128]{1,0:T(8,128)(2,1)S(1)}, u32[]{:S(2)}, u32[]{:S(2)}) collective-permute-start(f16[504,128]{1,0:T(8,128)(2,1)S(1)} %pad_maximum_fusion), channel_id=1, source_target_pairs={{0,8},{8,0},{16,24},{24,16},{32,40},{40,32},{48,56},{56,48},{1,9},... | collective-permute-start | bytes 387080 | tf_op jit(solution)/shard_map/ppermute | solution.py:611
  99.8 12.4 %collective-permute-start.30 = (f16[504,128]{1,0:T(8,128)(2,1)S(1)}, f16[504,128]{1,0:T(8,128)(2,1)S(1)}, u32[]{:S(2)}, u32[]{:S(2)}) collective-permute-start(f16[504,128]{1,0:T(8,128)(2,1)S(1)} %pad_maximum_fusion), channel_id=1, source_target_pairs={{0,96},{8,104},{16,112},{24,120},{32,64},{40,72},{48,80},{56,88},{... | collective-permute-start | bytes 387080 | tf_op jit(solution)/shard_map/ppermute | solution.py:606
  104.8 12.5 %collective-permute-start.28 = (f16[504,128]{1,0:T(8,128)(2,1)S(1)}, f16[504,128]{1,0:T(8,128)(2,1)S(1)}, u32[]{:S(2)}, u32[]{:S(2)}) collective-permute-start(f16[504,128]{1,0:T(8,128)(2,1)S(1)} %pad_maximum_fusion), channel_id=1, source_target_pairs={{0,80},{8,88},{16,64},{24,72},{32,112},{40,120},{48,96},{56,104},{... | collective-permute-start | bytes 387080 | tf_op jit(solution)/shard_map/ppermute | solution.py:606
  105.0 12.9 %collective-permute-start.26 = (f16[504,128]{1,0:T(8,128)(2,1)S(1)}, f16[504,128]{1,0:T(8,128)(2,1)S(1)}, u32[]{:S(2)}, u32[]{:S(2)}) collective-permute-start(f16[504,128]{1,0:T(8,128)(2,1)S(1)} %pad_maximum_fusion), channel_id=1, source_target_pairs={{0,64},{8,72},{16,80},{24,88},{32,96},{40,104},{48,112},{56,120},{... | collective-permute-start | bytes 387080 | tf_op jit(solution)/shard_map/ppermute | solution.py:606
  105.9 12.2 %collective-permute-start.24 = (f16[504,128]{1,0:T(8,128)(2,1)S(1)}, f16[504,128]{1,0:T(8,128)(2,1)S(1)}, u32[]{:S(2)}, u32[]{:S(2)}) collective-permute-start(f16[504,128]{1,0:T(8,128)(2,1)S(1)} %pad_maximum_fusion), channel_id=1, source_target_pairs={{0,48},{8,56},{16,32},{24,40},{32,16},{40,24},{48,0},{56,8},{64,11... | collective-permute-start | bytes 387080 | tf_op jit(solution)/shard_map/ppermute | solution.py:606
  108.8 1.3 collective-permute-start.21
  110.2 7.1 %collective-permute-start.22 = (f16[504,128]{1,0:T(8,128)(2,1)S(1)}, f16[504,128]{1,0:T(8,128)(2,1)S(1)}, u32[]{:S(2)}, u32[]{:S(2)}) collective-permute-start(f16[504,128]{1,0:T(8,128)(2,1)S(1)} %pad_maximum_fusion), channel_id=1, source_target_pairs={{0,32},{8,40},{16,48},{24,56},{32,0},{40,8},{48,16},{56,24},{64,96... | collective-permute-start | bytes 387080 | tf_op jit(solution)/shard_map/ppermute | solution.py:606
  112.2 8.7 %collective-permute-start.32 = (f16[504,128]{1,0:T(8,128)(2,1)S(1)}, f16[504,128]{1,0:T(8,128)(2,1)S(1)}, u32[]{:S(2)}, u32[]{:S(2)}) collective-permute-start(f16[504,128]{1,0:T(8,128)(2,1)S(1)} %pad_maximum_fusion), channel_id=1, source_target_pairs={{0,112},{8,120},{16,96},{24,104},{32,80},{40,88},{48,64},{56,72},{... | collective-permute-start | bytes 387080 | tf_op jit(solution)/shard_map/ppermute | solution.py:606
  117.2 3.7 %collective-permute-start.23 = (f16[504,128]{1,0:T(8,128)(2,1)S(1)}, f16[504,128]{1,0:T(8,128)(2,1)S(1)}, u32[]{:S(2)}, u32[]{:S(2)}) collective-permute-start(f16[504,128]{1,0:T(8,128)(2,1)S(1)} %collective-permute-done.22), channel_id=1, source_target_pairs={{0,8},{8,0},{16,24},{24,16},{32,40},{40,32},{48,56},{56,48},{1,9},... | collective-permute-start | bytes 387080 | tf_op jit(solution)/shard_map/ppermute | solution.py:611
  117.3 5.3 %collective-permute-start.31 = (f16[504,128]{1,0:T(8,128)(2,1)S(1)}, f16[504,128]{1,0:T(8,128)(2,1)S(1)}, u32[]{:S(2)}, u32[]{:S(2)}) collective-permute-start(f16[504,128]{1,0:T(8,128)(2,1)S(1)} %collective-permute-done.30), channel_id=1, source_target_pairs={{0,8},{8,0},{16,24},{24,16},{32,40},{40,32},{48,56},{56,48},{1,9},... | collective-permute-start | bytes 387080 | tf_op jit(solution)/shard_map/ppermute | solution.py:611
  117.9 4.6 %collective-permute-start.29 = (f16[504,128]{1,0:T(8,128)(2,1)S(1)}, f16[504,128]{1,0:T(8,128)(2,1)S(1)}, u32[]{:S(2)}, u32[]{:S(2)}) collective-permute-start(f16[504,128]{1,0:T(8,128)(2,1)S(1)} %collective-permute-done.28), channel_id=1, source_target_pairs={{0,8},{8,0},{16,24},{24,16},{32,40},{40,32},{48,56},{56,48},{1,9},... | collective-permute-start | bytes 387080 | tf_op jit(solution)/shard_map/ppermute | solution.py:611
  118.2 4.2 %collective-permute-start.27 = (f16[504,128]{1,0:T(8,128)(2,1)S(1)}, f16[504,128]{1,0:T(8,128)(2,1)S(1)}, u32[]{:S(2)}, u32[]{:S(2)}) collective-permute-start(f16[504,128]{1,0:T(8,128)(2,1)S(1)} %collective-permute-done.26), channel_id=1, source_target_pairs={{0,8},{8,0},{16,24},{24,16},{32,40},{40,32},{48,56},{56,48},{1,9},... | collective-permute-start | bytes 387080 | tf_op jit(solution)/shard_map/ppermute | solution.py:611
  120.9 1.3 collective-permute-start.25
  120.9 1.7 %collective-permute-start.33 = (f16[504,128]{1,0:T(8,128)(2,1)S(1)}, f16[504,128]{1,0:T(8,128)(2,1)S(1)}, u32[]{:S(2)}, u32[]{:S(2)}) collective-permute-start(f16[504,128]{1,0:T(8,128)(2,1)S(1)} %collective-permute-done.32), channel_id=1, source_target_pairs={{0,8},{8,0},{16,24},{24,16},{32,40},{40,32},{48,56},{56,48},{1,9},... | collective-permute-start | bytes 387080 | tf_op jit(solution)/shard_map/ppermute | solution.py:611

commit v2 on v1

--- a/solution.py
+++ b/solution.py
@@ -16,6 +16,8 @@
 VR = CZ * CW
 VROWS = 5 * VR
 PROWS = 80
+SPREAD = (1, 3, 7, 5, 2, 6, 4)
+GATHER = ((0, 1), (0, 3), (0, 2), (1, 0), (1, 1), (1, 3), (1, 2))
 SCALE = 128.0
 
 
@@ -255,9 +257,9 @@
 
 def warp_kernel(info, assign, zy, x0, x1, *rest):
     planes, fields, below, above = rest[:8], rest[8:16], rest[16], rest[17]
-    chunk, edge = rest[18:20]
-    image, field, even, odd, acc, sems = rest[20:]
-    level, me = info[0], info[1]
+    chunk, upward, downward = rest[18:21]
+    image, field, even, odd, acc, sems = rest[21:]
+    me = info[1]
     copies = [
         pltpu.make_async_copy(below, image.at[:, 0], sems.at[16]),
         pltpu.make_async_copy(above, image.at[:, HZ + 1], sems.at[17]),
@@ -360,21 +362,23 @@
 
     lax.fori_loop(0, 4, turn, 0)
     weight = SCALE / 16.0
-    chunk[: HZ * CY] = pltpu.roll(acc[0] * weight, 64 * level, 1)
-    wide = lax.broadcasted_iota(jnp.int32, (CY, 128), 1)
-
-    def joined(z, other):
-        one, two = (acc[1, pl.ds(pl.multiple_of(r * CY, 8), CY)] for r in (z, other))
+    middle = HZ * CY // 2
+    chunk[:middle] = acc[0, :middle] * weight
+    chunk[middle : 2 * middle] = pltpu.roll(acc[0, middle:] * weight, 64, 1)
+
+    def joined(one, two):
+        one, two = (acc[1, r * CY : (r + 1) * CY] for r in (one, two))
         one = one + pltpu.roll(one, 64, 1)
         two = two + pltpu.roll(two, 64, 1)
-        return jnp.where(wide < 64, one, two) * weight
+        return jnp.where(lane < 64, one, two) * weight
 
     for z in range(HZ // 2):
         chunk[(HZ + z) * CY : (HZ + z + 1) * CY] = joined(z, z + HZ // 2)
-    outer = (HZ - 2) * level
-    rim = acc[0, pl.ds(pl.multiple_of(outer * CY, 8), 2 * CY)] * weight
-    edge[: 2 * CY] = pltpu.roll(rim, 64 - 64 * level, 1)
-    edge[2 * CY :] = joined(outer, outer + 1)
+    rows = slice((HZ - 2) * CY, HZ * CY)
+    upward[: 2 * CY] = acc[0, rows] * weight
+    upward[2 * CY :] = joined(HZ - 2, HZ - 1)
+    downward[: 2 * CY] = pltpu.roll(acc[0, : 2 * CY] * weight, 64, 1)
+    downward[2 * CY :] = joined(1, 0)
 
 
 def warp(info, assign, planes, fields, below, above):
@@ -388,9 +392,10 @@
         warp_kernel,
         grid=(),
         in_specs=[smem, smem, vmem, vmem, vmem] + [hbm] * 18,
-        out_specs=[vmem] * 2,
+        out_specs=[vmem] * 3,
         out_shape=[
             jax.ShapeDtypeStruct((HZ * CY * 3 // 2, 128), F32),
+            jax.ShapeDtypeStruct((3 * CY, 128), F32),
             jax.ShapeDtypeStruct((3 * CY, 128), F32),
         ],
         scratch_shapes=[
@@ -405,9 +410,16 @@
     )(info, assign, *tables, *planes, *fields, below, above)
 
 
-def relax_kernel(info, chunks, out, flat, pair, flat2, pair2, even, odd, ready, sems):
-    level, me, zone = info[0], info[1], info[2]
+COUNT = HZ // 2 + 2
+
+
+def relax_kernel(info, chunks, *rest):
+    out, flat, pair, flat2, pair2, even, odd, ready, sems = rest[-9:]
+    far = len(rest) - 9
+    me, zone = info[1], info[2]
+    half = info[0] ^ far
     size = flat.shape[1] - 16
+    high = COUNT + 2
     for held in (flat, pair, flat2, pair2):
         held[:, :8] = jnp.zeros((held.shape[0], 8, 128), F32)
         held[:, size + 8 :] = jnp.zeros((held.shape[0], 8, 128), F32)
@@ -418,34 +430,29 @@
     tail = HZ * 3 // 2
     for peer in range(8):
         rows = slice(8 + CY * peer, 8 + CY * (peer + 1))
-        slots = [(half ^ level) * 8 + (peer ^ me) for half in range(2)]
-
-        def block(half, index):
-            return chunks[slots[half], CY * index : CY * (index + 1)]
-
-        for half in range(2):
-            for z in range(HZ):
-                flat[3 + 14 * half + z, rows] = block(half, z)
-            for z in range(2):
-                flat[1 + 28 * half + z, rows] = block(half, tail + z)
-        packed = [HZ + z % (HZ // 2) for z in range(HZ)]
-        sides = [z // (HZ // 2) for z in range(HZ)]
-        lows = [(tail + 2, 0), (tail + 2, 1)] + list(zip(packed, sides))
-        highs = list(zip(packed, sides)) + [(tail + 2, 0), (tail + 2, 1)]
-        for index in range(14):
-            low, high = block(0, lows[index][0]), block(1, highs[index][0])
-            if lows[index][1] == 1:
-                low = pltpu.roll(low, 64, 1)
-            if highs[index][1] == 0:
-                high = pltpu.roll(high, 64, 1)
-            pair[1 + index, rows] = jnp.where(narrow < 64, low, high)
+        slot = peer ^ me
+
+        def block(index):
+            return chunks[slot, CY * index : CY * (index + 1)]
+
+        for z in range(HZ // 2):
+            flat[3 + z, rows] = block(z)
+            flat[high + 1 + z, rows] = block(z + HZ // 2)
+        for z in range(2):
+            flat[1 + z, rows] = block(tail + z)
+            flat[high + COUNT - 1 + z, rows] = block(tail + 3 + z)
+        under, over = block(tail + 2), block(tail + 5)
+        lows = [under, pltpu.roll(under, 64, 1)] + [block(HZ + z) for z in range(HZ // 2)]
+        highs = [block(HZ + z) for z in range(HZ // 2)] + [over, pltpu.roll(over, 64, 1)]
+        for index in range(COUNT):
+            pair[1 + index, rows] = jnp.where(narrow < 64, lows[index], highs[index])
 
     def mirror(planes, both):
         body = slice(8, 8 + size)
-        both[0, body] = pltpu.roll(both[14, body], 64, 1)
-        both[15, body] = pltpu.roll(both[1, body], 64, 1)
-        planes[16, body] = pltpu.roll(planes[14, body], 64, 1)
-        planes[15, body] = pltpu.roll(planes[17, body], 64, 1)
+        both[0, body] = pltpu.roll(both[COUNT, body], 64, 1)
+        both[COUNT + 1, body] = pltpu.roll(both[1, body], 64, 1)
+        planes[high, body] = pltpu.roll(planes[COUNT, body], 64, 1)
+        planes[COUNT + 1, body] = pltpu.roll(planes[high + 1, body], 64, 1)
 
     mirror(flat, pair)
     count = 2 * CY
@@ -453,7 +460,7 @@
 
     def shift(planes, index, sums):
         for start in range(8, 8 + size, count):
-            refs = [(planes[0], index), (planes[0], index + 16), (planes[1], index)]
+            refs = [(planes[0], index), (planes[0], index + high), (planes[1], index)]
             part = [held[z, start : start + count] for held, z in refs]
             left = [pltpu.roll(p, 1, 1) for p in part]
             right = [pltpu.roll(p, 127, 1) for p in part]
@@ -467,7 +474,7 @@
                 sums[b, start - 8 : start - 8 + count] = left[b] + right[b]
 
     def swept(planes, index, sums, start, scale):
-        refs = [(planes[0], index), (planes[0], index + 16), (planes[1], index)]
+        refs = [(planes[0], index), (planes[0], index + high), (planes[1], index)]
         done = []
         for b, (held, z) in enumerate(refs):
             around = held[z - 1, start : start + count] + held[z + 1, start : start + count]
@@ -486,53 +493,53 @@
             shift(planes, index + 1, odd)
             for start in range(8, 8 + size, count):
                 store(index, start, swept(planes, index, even, start, scale))
-            shift(planes, jnp.minimum(index + 2, 14), even)
+            shift(planes, jnp.minimum(index + 2, COUNT), even)
             for start in range(8, 8 + size, count):
                 store(index + 1, start, swept(planes, index + 1, odd, start, scale))
             after(index)
             after(index + 1)
             return carry
 
-        lax.fori_loop(0, 7, turn, 0)
+        lax.fori_loop(0, COUNT // 2, turn, 0)
 
     def first(index, start, done):
         flat2[index, start : start + count] = done[0]
-        flat2[index + 16, start : start + count] = done[1]
+        flat2[index + high, start : start + count] = done[1]
         pair2[index, start : start + count] = done[2]
 
     sweep((flat, pair), first, 1.0, lambda index: None)
     whole = lax.broadcasted_iota(jnp.int32, (size, 128), 1)
 
-    @pl.when(zone == 0)
+    @pl.when(jnp.logical_and(zone == 0, half == 0))
     def _():
         flat2[2, 8 : 8 + size] = jnp.zeros((size, 128), F32)
         pair2[2, 8 : 8 + size] = jnp.where(whole < 64, 0.0, pair2[2, 8 : 8 + size])
 
-    @pl.when(zone == 7)
+    @pl.when(jnp.logical_and(zone == 7, half == 1))
     def _():
-        flat2[29, 8 : 8 + size] = jnp.zeros((size, 128), F32)
-        pair2[13, 8 : 8 + size] = jnp.where(whole < 64, pair2[13, 8 : 8 + size], 0.0)
+        flat2[high + COUNT - 1, 8 : 8 + size] = jnp.zeros((size, 128), F32)
+        pair2[COUNT - 1, 8 : 8 + size] = jnp.where(whole < 64, pair2[COUNT - 1, 8 : 8 + size], 0.0)
 
     mirror(flat2, pair2)
 
     def emit(z):
-        return pltpu.make_async_copy(ready.at[z + 2], out.at[z], sems.at[z])
+        return pltpu.make_async_copy(ready.at[z + 2], out.at[HZ * half + z], sems.at[z])
 
     def second(index, start, done):
         rows = slice(start - 8, start - 8 + count)
         ready[index - 1, rows, :128] = done[0]
         ready[index - 1, rows, 128:] = done[2][:, :64]
-        ready[index + 13, rows, :128] = pltpu.roll(done[1], 64, 1)
-        ready[index + 13, rows, 128:] = pltpu.roll(done[2], 64, 1)[:, :64]
+        ready[index + COUNT - 1, rows, :128] = pltpu.roll(done[1], 64, 1)
+        ready[index + COUNT - 1, rows, 128:] = pltpu.roll(done[2], 64, 1)[:, :64]
 
     def depart(index):
         @pl.when(index >= 3)
         def _():
             emit(index - 3).start()
 
-        @pl.when(index <= 12)
+        @pl.when(index <= COUNT - 2)
         def _():
-            emit(index + 11).start()
+            emit(index + COUNT - 3).start()
 
     sweep((flat2, pair2), second, 1.0 / SCALE, depart)
 
@@ -540,29 +547,33 @@
         emit(z).wait()
         return carry
 
-    lax.fori_loop(0, 24, finish, 0)
-
-
-def relax(info, chunks):
+    lax.fori_loop(0, HZ, finish, 0)
+
+
+def relax(info, chunks, *before):
+    hbm = pl.BlockSpec(memory_space=pl.ANY)
     vmem = pl.BlockSpec(memory_space=pltpu.VMEM)
+    held = [
+        pltpu.VMEM((2 * COUNT + 4, 208, 128), F32),
+        pltpu.VMEM((COUNT + 2, 208, 128), F32),
+    ]
     return pl.pallas_call(
         relax_kernel,
         grid=(),
-        in_specs=[pl.BlockSpec(memory_space=pltpu.SMEM), vmem],
-        out_specs=pl.BlockSpec(memory_space=pl.ANY),
+        in_specs=[pl.BlockSpec(memory_space=pltpu.SMEM), vmem] + [hbm] * len(before),
+        out_specs=hbm,
         out_shape=jax.ShapeDtypeStruct((24, 192, 192), F32),
-        scratch_shapes=[
-            pltpu.VMEM((32, 208, 128), F32),
-            pltpu.VMEM((16, 208, 128), F32),
-            pltpu.VMEM((32, 208, 128), F32),
-            pltpu.VMEM((16, 208, 128), F32),
+        input_output_aliases={2: 0} if before else {},
+        scratch_shapes=held
+        + held
+        + [
             pltpu.VMEM((3, 192, 128), F32),
             pltpu.VMEM((3, 192, 128), F32),
-            pltpu.VMEM((28, 192, 192), F32),
-            pltpu.SemaphoreType.DMA((24,)),
+            pltpu.VMEM((2 * COUNT, 192, 192), F32),
+            pltpu.SemaphoreType.DMA((HZ,)),
         ],
         name="relax",
-    )(info, chunks)
+    )(info, chunks, *before)
 
 
 def update(images, momenta, assign):
@@ -586,7 +597,7 @@
 
     def spread(parts):
         arrived = {0: parts[0]}
-        for k in (3, 7, 5, 2, 6, 4, 1):
+        for k in SPREAD:
             arrived[k] = lax.ppermute(parts[k], "subj", [(i, i ^ k) for i in range(8)])
         return [arrived[k] for k in range(8)]
 
@@ -597,20 +608,24 @@
     low, high = edges(planes)
     below = lax.ppermute(high, nearest, climb)
     above = lax.ppermute(low, nearest, [(b, a) for a, b in climb])
-    chunk, edge = warp(info, assign, planes, fields, below, above)
-    edge = lax.ppermute(edge.astype(jnp.float16), nearest, cross)
-    chunk = jnp.concatenate([chunk.astype(jnp.float16), edge], axis=0)
+    chunk, upward, downward = warp(info, assign, planes, fields, below, above)
+    half = jnp.float16
+    back = [(b, a) for a, b in climb]
+    under = lax.ppermute(upward.astype(half), nearest, climb)
+    over = lax.ppermute(downward.astype(half), nearest, back)
+    chunk = jnp.concatenate([chunk.astype(half), under, over], axis=0)
     mine = {(0, 0): chunk}
-    for far, step in ((0, 1), (0, 3), (1, 0), (0, 2), (1, 1), (1, 3), (1, 2)):
+    for far, step in GATHER:
         perm = [(8 * a + i, 8 * (a ^ far) + (i ^ (2 * step))) for a in range(2) for i in range(8)]
         mine[far, step] = lax.ppermute(chunk, ("level", "subj"), perm)
-    gathered = []
+    result = ()
     for far in range(2):
+        parts = []
         for step in range(4):
             part = mine[far, step]
-            gathered += [part, lax.ppermute(part, "subj", [(i, i ^ 1) for i in range(8)])]
-    chunks = jnp.stack(gathered).astype(F32)
-    return relax(info, chunks)
+            parts += [part, lax.ppermute(part, "subj", [(i, i ^ 1) for i in range(8)])]
+        result = (relax(info, jnp.stack(parts).astype(F32), *result),)
+    return result[0]
 
 
 def solution(mesh):

time: 137 us -> 152 us (1.11)
  waiting for transfers between devices: 43.6 us -> 54.7 us
  Pallas kernels: 35.1 us -> 38.3 us
  other arithmetic: 4.57 us -> 6.38 us
    ppermute x7, waiting for transfers between devices: 5.54 us -> 16.4 us  [update(): mine[far, step] = lax.ppermute(chunk, ('level', 'subj'), perm)]
    ppermute x7, starting transfers between devices: 13.1 us -> 9.09 us  [update(): mine[far, step] = lax.ppermute(chunk, ('level', 'subj'), perm)]
    pallas_call x1 -> x2, Pallas kernels: 10.9 us -> 14.1 us  [relax(): pl.pallas_call(relax_kernel, grid=(), in_specs=[pl.BlockSpec(memory_space...]
    ppermute x9 -> x10, starting transfers between devices: 5.88 us -> 8.43 us  [the longest x1 4.47 us: update(): over = lax.ppermute(downward.astype(half), nearest, back)]
    convert_element_type x3 -> x5, other arithmetic: 3.94 us -> 5.69 us  [the longest x2 3.19 us: update(): result = (relax(info, jnp.stack(parts).astype(F32), *result),)]
    ppermute x9 -> x10, waiting for transfers between devices: 3.4 us -> 3.66 us  [the longest x1 2.42 us: update(): under = lax.ppermute(upward.astype(half), nearest, climb)]
    unnamed x50 -> x51, local copies, waits for them, and re-layouts: 3.49 us -> 3.47 us
  transfers between devices with their start and end apart: 34 -> 35, of which waited for: 15 -> 15; matrix products, arithmetic and copies ran while one was open for 2% -> 3% of each run, Pallas kernels for 8% -> 7%
where the time goes in v2:
time: 152 us; the launch traced here: 151 us
  waiting for transfers between devices  54.7 us (36%)
  starting transfers between devices  46 us (30%)
  Pallas kernels  38.3 us (25%)
  other arithmetic  6.38 us (4%)
  local copies, waits for them, and re-layouts  4.82 us (3%)
    ppermute x14, waiting for transfers between devices, spread(): arrived[k] = lax.ppermute(parts[k], 'subj', [(i, i ^ k) for i in range(8)])  34.6 us
    ppermute x7, waiting for transfers between devices, update(): mine[far, step] = lax.ppermute(chunk, ('level', 'subj'), perm)  16.4 us
    ppermute x14, starting transfers between devices, spread(): arrived[k] = lax.ppermute(parts[k], 'subj', [(i, i ^ k) for i in range(8)])  14.3 us
    pallas_call x2, Pallas kernels, relax(): pl.pallas_call(relax_kernel, grid=(), in_specs=[pl.BlockSpec(memory_space...  14.1 us
    pallas_call x1, Pallas kernels, warp(): pl.pallas_call(warp_kernel, grid=(), in_specs=[smem, smem, vmem, vmem, vm...  9.5 us
    ppermute x7, starting transfers between devices, update(): mine[far, step] = lax.ppermute(chunk, ('level', 'subj'), perm)  9.09 us
    pallas_call x1, Pallas kernels, blur(): pl.pallas_call(blur_kernel, grid=(), in_specs=[pl.BlockSpec(memory_space=...  9.08 us
    ppermute x1, starting transfers between devices, update(): rim = lax.ppermute(rim, nearest, outward)  5.16 us
  transfers between devices with their start and end apart: 35, of which 15 were waited for; matrix products, arithmetic and copies ran while one was open for 3% of the time, Pallas kernels for 7%

profile of v2, /device:TPU:96, one launch (start us, length us, event | category | flops | bytes accessed | tf_op | source)
XLA Modules:
  0.0 150.8 jit_solution(15044125104286693749)
XLA Ops:
  0.0 0.6 pad_add_fusion.info
  0.6 3.9 %pack_images.1 = (bf16[12,80,128]{2,1,0:T(8,128)(2,1)}, bf16[12,80,128]{2,1,0:T(8,128)(2,1)}, bf16[12,80,128]{2,1,0:T(8,128)(2,1)}, bf16[12,80,128]{2,1,0:T(8,12...) custom-call(s32[3]{0:T(128)} %pad_add_fusion.info, ...), custom_call_target="tpu_custom_call" | custom-call | tf_op jit(solution)/shard_map/pack_images/pallas_call | solution.py:107
  4.5 0.1 collective-permute-start
  4.6 1.7 %collective-permute-start.1 = (bf16[12,80,128]{2,1,0:T(8,128)(2,1)}, bf16[12,80,128]{2,1,0:T(8,128)(2,1)S(1)}, u32[]{:S(2)}, u32[]{:S(2)}) collective-permute-start(bf16[12,80,128]{2,1,0:T(8,128)(2,1)} %get-tuple-element.28), channel_id=1, source_target_pairs={{0,16},{8,24},{16,0},{24,8},{32,48},{40,56},{48,32},{56,40},{1,17}... | collective-permute-start | bytes 737288 | tf_op jit(solution)/shard_map/ppermute | solution.py:601
  6.2 0.2 collective-permute-start.2
  6.4 3.2 %collective-permute-start.3 = (bf16[12,80,128]{2,1,0:T(8,128)(2,1)}, bf16[12,80,128]{2,1,0:T(8,128)(2,1)S(1)}, u32[]{:S(2)}, u32[]{:S(2)}) collective-permute-start(bf16[12,80,128]{2,1,0:T(8,128)(2,1)} %get-tuple-element.30), channel_id=1, source_target_pairs={{0,32},{8,40},{16,48},{24,56},{32,0},{40,8},{48,16},{56,24},{1,33}... | collective-permute-start | bytes 737288 | tf_op jit(solution)/shard_map/ppermute | solution.py:601
  9.6 1.2 constant_dynamic-slice_fusion
  10.9 3.2 %collective-permute-start.8 = (f32[1,3,3,96,96]{4,3,2,1,0:T(8,128)S(1)}, f32[1,3,3,96,96]{4,3,2,1,0:T(8,128)S(1)}, u32[]{:S(2)}, u32[]{:S(2)}) collective-permute-start(f32[1,3,3,96,96]{4,3,2,1,0:T(8,128)S(1)} %get-tuple-element.47), channel_id=1, source_target_pairs={{64,1},{65,2},{66,3},{67,4},{68,5},{69,6},{70,7},{1,64},{2,65},{3,... | collective-permute-start | bytes 995336 | tf_op jit(solution)/shard_map/ppermute | solution.py:596
  14.1 5.2 %collective-permute-start.7 = (f32[1,3,3,96,96]{4,3,2,1,0:T(8,128)S(1)}, f32[1,3,3,96,96]{4,3,2,1,0:T(8,128)S(1)}, u32[]{:S(2)}, u32[]{:S(2)}) collective-permute-start(f32[1,3,3,96,96]{4,3,2,1,0:T(8,128)S(1)} %get-tuple-element.48), channel_id=1, source_target_pairs={{0,1},{1,2},{2,3},{3,4},{4,5},{5,6},{6,7},{65,64},{66,65},{67,66},... | collective-permute-start | bytes 995336 | tf_op jit(solution)/shard_map/ppermute | solution.py:595
  19.3 0.1 collective-permute-start.4
  19.4 2.5 %collective-permute-start.5 = (bf16[12,80,128]{2,1,0:T(8,128)(2,1)}, bf16[12,80,128]{2,1,0:T(8,128)(2,1)S(1)}, u32[]{:S(2)}, u32[]{:S(2)}) collective-permute-start(bf16[12,80,128]{2,1,0:T(8,128)(2,1)} %get-tuple-element.32), channel_id=1, source_target_pairs={{0,48},{8,56},{16,32},{24,40},{32,16},{40,24},{48,0},{56,8},{1,49}... | collective-permute-start | bytes 737288 | tf_op jit(solution)/shard_map/ppermute | solution.py:601
  21.9 4.9 %collective-permute-done.3.refs_4_.rest_4_ = bf16[12,80,128]{2,1,0:T(8,128)(2,1)S(1)} collective-permute-done((bf16[12,80,128]{2,1,0:T(8,128)(2,1)}, bf16[12,80,128]{2,1,0:T(8,128)(2,1)S(1)}, u32[]{:S(2)}, u32[]{:S(2)}) %collective-permute-start.3) | collective-permute-done | bytes 245792 | tf_op jit(solution)/shard_map/ppermute | solution.py:601
  26.8 4.2 %collective-permute-done.4.refs_5_.rest_5_ = bf16[12,80,128]{2,1,0:T(8,128)(2,1)S(1)} collective-permute-done((bf16[12,80,128]{2,1,0:T(8,128)(2,1)}, bf16[12,80,128]{2,1,0:T(8,128)(2,1)S(1)}, u32[]{:S(2)}, u32[]{:S(2)}) %collective-permute-start.4) | collective-permute-done | bytes 245792 | tf_op jit(solution)/shard_map/ppermute | solution.py:601
  30.9 5.8 %collective-permute-done.5.refs_6_.rest_6_ = bf16[12,80,128]{2,1,0:T(8,128)(2,1)S(1)} collective-permute-done((bf16[12,80,128]{2,1,0:T(8,128)(2,1)}, bf16[12,80,128]{2,1,0:T(8,128)(2,1)S(1)}, u32[]{:S(2)}, u32[]{:S(2)}) %collective-permute-start.5) | collective-permute-done | bytes 245792 | tf_op jit(solution)/shard_map/ppermute | solution.py:601
  36.7 5.2 %collective-permute-done.6.refs_7_.rest_7_ = bf16[12,80,128]{2,1,0:T(8,128)(2,1)S(1)} collective-permute-done((bf16[12,80,128]{2,1,0:T(8,128)(2,1)S(1)}, bf16[12,80,128]{2,1,0:T(8,128)(2,1)S(1)}, u32[]{:S(2)}, u32[]{:S(2)}) %collective-permute-start.6) | collective-permute-done | bytes 245792 | tf_op jit(solution)/shard_map/ppermute | solution.py:601
  41.9 0.7 copy-done.6
  42.6 1.8 %cut_edges.1 = (bf16[8,80,128]{2,1,0:T(8,128)(2,1)}, bf16[8,80,128]{2,1,0:T(8,128)(2,1)}) custom-call(bf16[12,80,128]{2,1,0:T(8,128)(2,1)} %get-tuple-element.26.refs_0_.rest_0_, bf16[12,80,128]{2,1,0:T(8,128)(2,1)} %copy-done, bf16[12,80,128]{2,1,0:T(8,128)(2,1)} %copy-done.1, bf16[12,80,128]{2,1,0:T(8,128)(2,1)} %copy-done.2, ...), custom_call_target="tpu_custom_call" | custom-call | tf_op jit(solution)/shard_map/cut_edges/pallas_call | solution.py:242
  44.4 3.3 %collective-permute-start.16 = (bf16[8,80,128]{2,1,0:T(8,128)(2,1)}, bf16[8,80,128]{2,1,0:T(8,128)(2,1)S(1)}, u32[]{:S(2)}, u32[]{:S(2)}) collective-permute-start(bf16[8,80,128]{2,1,0:T(8,128)(2,1)} %get-tuple-element.42), channel_id=1, source_target_pairs={{0,64},{1,65},{2,66},{3,67},{4,68},{5,69},{6,70},{7,71},{64,1},{65... | collective-permute-start | bytes 491528 | tf_op jit(solution)/shard_map/ppermute | solution.py:609
  47.7 2.5 %collective-permute-start.17 = (bf16[8,80,128]{2,1,0:T(8,128)(2,1)}, bf16[8,80,128]{2,1,0:T(8,128)(2,1)S(1)}, u32[]{:S(2)}, u32[]{:S(2)}) collective-permute-start(bf16[8,80,128]{2,1,0:T(8,128)(2,1)} %get-tuple-element.43), channel_id=1, source_target_pairs={{64,0},{65,1},{66,2},{67,3},{68,4},{69,5},{70,6},{71,7},{1,64},{2,... | collective-permute-start | bytes 491528 | tf_op jit(solution)/shard_map/ppermute | solution.py:610
  50.3 0.7 copy-done.7
  51.0 0.8 copy-done.8
  51.8 9.1 %blur_momenta.1 = (bf16[560,128]{1,0:T(8,128)(2,1)}, bf16[560,128]{1,0:T(8,128)(2,1)}, bf16[560,128]{1,0:T(8,128)(2,1)}, bf16[560,128]{1,0:T(8,128)(2,1)}, bf16[...) custom-call(s32[3]{0:T(128)} %pad_add_fusion.info, ...), custom_call_target="tpu_custom_call" | custom-call | tf_op jit(solution)/shard_map/blur_momenta/pallas_call | solution.py:193
  60.9 0.1 collective-permute-start.9
  60.9 0.3 collective-permute-start.10
  61.2 1.6 %collective-permute-start.11 = (bf16[560,128]{1,0:T(8,128)(2,1)}, bf16[560,128]{1,0:T(8,128)(2,1)S(1)}, u32[]{:S(2)}, u32[]{:S(2)}) collective-permute-start(bf16[560,128]{1,0:T(8,128)(2,1)} %get-tuple-element.37), channel_id=1, source_target_pairs={{0,24},{8,16},{16,8},{24,0},{32,56},{40,48},{48,40},{56,32},{1,25}... | collective-permute-start | bytes 430088 | tf_op jit(solution)/shard_map/ppermute | solution.py:601
  62.8 0.7 collective-permute-start.12
  63.5 2.5 %collective-permute-start.13 = (bf16[560,128]{1,0:T(8,128)(2,1)}, bf16[560,128]{1,0:T(8,128)(2,1)S(1)}, u32[]{:S(2)}, u32[]{:S(2)}) collective-permute-start(bf16[560,128]{1,0:T(8,128)(2,1)} %get-tuple-element.39), channel_id=1, source_target_pairs={{0,40},{8,32},{16,56},{24,48},{32,8},{40,0},{48,24},{56,16},{1,41}... | collective-permute-start | bytes 430088 | tf_op jit(solution)/shard_map/ppermute | solution.py:601
  66.0 0.3 collective-permute-start.14
  66.3 1.6 %collective-permute-done.10.rest_10_ = bf16[560,128]{1,0:T(8,128)(2,1)S(1)} collective-permute-done((bf16[560,128]{1,0:T(8,128)(2,1)}, bf16[560,128]{1,0:T(8,128)(2,1)S(1)}, u32[]{:S(2)}, u32[]{:S(2)}) %collective-permute-start.10) | collective-permute-done | bytes 143392 | tf_op jit(solution)/shard_map/ppermute | solution.py:601
  67.9 1.2 collective-permute-start.15
  69.0 0.8 collective-permute-done.11.rest_11_
  69.8 4.0 %collective-permute-done.12.rest_12_ = bf16[560,128]{1,0:T(8,128)(2,1)S(1)} collective-permute-done((bf16[560,128]{1,0:T(8,128)(2,1)}, bf16[560,128]{1,0:T(8,128)(2,1)S(1)}, u32[]{:S(2)}, u32[]{:S(2)}) %collective-permute-start.12) | collective-permute-done | bytes 143392 | tf_op jit(solution)/shard_map/ppermute | solution.py:601
  73.8 2.0 %collective-permute-done.13.rest_13_ = bf16[560,128]{1,0:T(8,128)(2,1)S(1)} collective-permute-done((bf16[560,128]{1,0:T(8,128)(2,1)}, bf16[560,128]{1,0:T(8,128)(2,1)S(1)}, u32[]{:S(2)}, u32[]{:S(2)}) %collective-permute-start.13) | collective-permute-done | bytes 143392 | tf_op jit(solution)/shard_map/ppermute | solution.py:601
  75.8 3.6 %collective-permute-done.14.rest_14_ = bf16[560,128]{1,0:T(8,128)(2,1)S(1)} collective-permute-done((bf16[560,128]{1,0:T(8,128)(2,1)}, bf16[560,128]{1,0:T(8,128)(2,1)S(1)}, u32[]{:S(2)}, u32[]{:S(2)}) %collective-permute-start.14) | collective-permute-done | bytes 143392 | tf_op jit(solution)/shard_map/ppermute | solution.py:601
  79.4 2.7 %collective-permute-done.15.rest_15_ = bf16[560,128]{1,0:T(8,128)(2,1)S(1)} collective-permute-done((bf16[560,128]{1,0:T(8,128)(2,1)}, bf16[560,128]{1,0:T(8,128)(2,1)S(1)}, u32[]{:S(2)}, u32[]{:S(2)}) %collective-permute-start.15) | collective-permute-done | bytes 143392 | tf_op jit(solution)/shard_map/ppermute | solution.py:601
  82.2 0.6 copy-done.17
  82.8 9.5 %warp_sum.1 = (f32[432,128]{1,0:T(8,128)}, f32[72,128]{1,0:T(8,128)}, f32[72,128]{1,0:T(8,128)}) custom-call(s32[3]{0:T(128)} %pad_add_fusion.info, s32[16]{0:T(128)} %assign.1, bf16[288,112]{1,0:T(8,128)(2,1)} %constant.27.clone.zy, bf16[256,256]{1,0:T(8,128)(2,1)} %constant.28.clone.x0, bf16[256,256]{1,0:T(8,128)(2,1)} %constant.29.clone.x1, ...), custom_call_target="tpu_custom_call" | custom-call | tf_op jit(solution)/shard_map/warp_sum/pallas_call | solution.py:391
  92.3 0.8 convert_element_type.16
  93.1 0.8 convert_element_type.17
  93.8 4.5 %collective-permute-start.19 = (f16[72,128]{1,0:T(8,128)(2,1)S(1)}, f16[72,128]{1,0:T(8,128)(2,1)S(1)}, u32[]{:S(2)}, u32[]{:S(2)}) collective-permute-start(f16[72,128]{1,0:T(8,128)(2,1)S(1)} %convert_element_type.17), channel_id=1, source_target_pairs={{64,0},{65,1},{66,2},{67,3},{68,4},{69,5},{70,6},{71,7},{1,64},{2,... | collective-permute-start | bytes 55304 | tf_op jit(solution)/shard_map/ppermute | solution.py:615
  98.3 2.3 %collective-permute-start.18 = (f16[72,128]{1,0:T(8,128)(2,1)S(1)}, f16[72,128]{1,0:T(8,128)(2,1)S(1)}, u32[]{:S(2)}, u32[]{:S(2)}) collective-permute-start(f16[72,128]{1,0:T(8,128)(2,1)S(1)} %convert_element_type.16), channel_id=1, source_target_pairs={{0,64},{1,65},{2,66},{3,67},{4,68},{5,69},{6,70},{7,71},{64,1},{65... | collective-permute-start | bytes 55304 | tf_op jit(solution)/shard_map/ppermute | solution.py:614
  100.6 1.0 convert_element_type.15
  101.5 2.4 %collective-permute-done.18 = f16[72,128]{1,0:T(8,128)(2,1)S(1)} collective-permute-done((f16[72,128]{1,0:T(8,128)(2,1)S(1)}, f16[72,128]{1,0:T(8,128)(2,1)S(1)}, u32[]{:S(2)}, u32[]{:S(2)}) %collective-permute-start.18) | collective-permute-done | bytes 18464 | tf_op jit(solution)/shard_map/ppermute | solution.py:614
  104.0 0.1 collective-permute-start.28
  104.1 0.1 collective-permute-start.31
  104.2 1.3 collective-permute-start.29
  105.5 2.8 %collective-permute-start.33 = (f16[576,128]{1,0:T(8,128)(2,1)S(1)}, f16[576,128]{1,0:T(8,128)(2,1)S(1)}, u32[]{:S(2)}, u32[]{:S(2)}) collective-permute-start(f16[576,128]{1,0:T(8,128)(2,1)S(1)} %pad_maximum_fusion), channel_id=1, source_target_pairs={{0,48},{8,56},{16,32},{24,40},{32,16},{40,24},{48,0},{56,8},{64,11... | collective-permute-start | bytes 442376 | tf_op jit(solution)/shard_map/ppermute | solution.py:620
  108.3 2.2 %collective-permute-start.26 = (f16[576,128]{1,0:T(8,128)(2,1)S(1)}, f16[576,128]{1,0:T(8,128)(2,1)S(1)}, u32[]{:S(2)}, u32[]{:S(2)}) collective-permute-start(f16[576,128]{1,0:T(8,128)(2,1)S(1)} %pad_maximum_fusion), channel_id=1, source_target_pairs={{0,112},{8,120},{16,96},{24,104},{32,80},{40,88},{48,64},{56,72},{... | collective-permute-start | bytes 442376 | tf_op jit(solution)/shard_map/ppermute | solution.py:620
  110.5 0.3 collective-permute-start.24
  110.9 1.9 %collective-permute-done.29 = f16[576,128]{1,0:T(8,128)(2,1)S(1)} collective-permute-done((f16[576,128]{1,0:T(8,128)(2,1)S(1)}, f16[576,128]{1,0:T(8,128)(2,1)S(1)}, u32[]{:S(2)}, u32[]{:S(2)}) %collective-permute-start.29) | collective-permute-done | bytes 147488 | tf_op jit(solution)/shard_map/ppermute | solution.py:620
  112.8 2.3 %collective-permute-start.20 = (f16[576,128]{1,0:T(8,128)(2,1)S(1)}, f16[576,128]{1,0:T(8,128)(2,1)S(1)}, u32[]{:S(2)}, u32[]{:S(2)}) collective-permute-start(f16[576,128]{1,0:T(8,128)(2,1)S(1)} %pad_maximum_fusion), channel_id=1, source_target_pairs={{0,64},{8,72},{16,80},{24,88},{32,96},{40,104},{48,112},{56,120},{... | collective-permute-start | bytes 442376 | tf_op jit(solution)/shard_map/ppermute | solution.py:620
  115.1 9.8 %collective-permute-done.20 = f16[576,128]{1,0:T(8,128)(2,1)S(1)} collective-permute-done((f16[576,128]{1,0:T(8,128)(2,1)S(1)}, f16[576,128]{1,0:T(8,128)(2,1)S(1)}, u32[]{:S(2)}, u32[]{:S(2)}) %collective-permute-start.20) | collective-permute-done | bytes 147488 | tf_op jit(solution)/shard_map/ppermute | solution.py:620
  125.0 0.1 collective-permute-start.22
  125.1 1.2 collective-permute-done.30
  126.4 0.1 collective-permute-start.32
  126.6 0.4 collective-permute-start.21
  127.1 0.3 collective-permute-start.34
  127.3 0.2 collective-permute-start.27
  127.6 4.7 %collective-permute-done.22 = f16[576,128]{1,0:T(8,128)(2,1)S(1)} collective-permute-done((f16[576,128]{1,0:T(8,128)(2,1)S(1)}, f16[576,128]{1,0:T(8,128)(2,1)S(1)}, u32[]{:S(2)}, u32[]{:S(2)}) %collective-permute-start.22) | collective-permute-done | bytes 147488 | tf_op jit(solution)/shard_map/ppermute | solution.py:620
  132.3 0.5 collective-permute-start.23
  133.0 1.6 %convert_element_type.19.chunks = f32[8,576,128]{2,1,0:T(8,128)} convert(f16[8,576,128]{2,1,0:T(8,128)(2,1)S(1)} %bitcast_dynamic-update-slice_fusion) | non-fusion elementwise | flops 589824 | bytes 3538944 | tf_op jit(solution)/shard_map/convert_element_type | solution.py:627
  135.0 1.6 %convert_element_type.18.chunks = f32[8,576,128]{2,1,0:T(8,128)} convert(f16[8,576,128]{2,1,0:T(8,128)(2,1)S(1)} %bitcast_dynamic-update-slice_fusion.8) | non-fusion elementwise | flops 589824 | bytes 3538944 | tf_op jit(solution)/shard_map/convert_element_type | solution.py:627
  136.5 7.0 %relax.2.rest_0_ = f32[24,192,192]{2,1,0:T(8,128)} custom-call(s32[3]{0:T(128)} %pad_add_fusion.info, f32[8,576,128]{2,1,0:T(8,128)} %convert_element_type.19.chunks), custom_call_target="tpu_custom_call" | custom-call | tf_op jit(solution)/shard_map/relax/pallas_call | solution.py:560
  143.6 7.0 %relax.3 = f32[24,192,192]{2,1,0:T(8,128)} custom-call(s32[3]{0:T(128)} %pad_add_fusion.info, f32[8,576,128]{2,1,0:T(8,128)} %convert_element_type.18.chunks, f32[24,192,192]{2,1,0:T(8,128)} %relax.2.rest_0_), custom_call_target="tpu_custom_call", output_to_operand_aliasing={{}: (2, {})} | custom-call | tf_op jit(solution)/shard_map/relax/pallas_call | solution.py:560
  (74 shorter events, 1.0 us)
Async XLA Ops:
  4.5 9.6 %collective-permute-start = (bf16[12,80,128]{2,1,0:T(8,128)(2,1)}, bf16[12,80,128]{2,1,0:T(8,128)(2,1)S(1)}, u32[]{:S(2)}, u32[]{:S(2)}) collective-permute-start(bf16[12,80,128]{2,1,0:T(8,128)(2,1)} %get-tuple-element.27), channel_id=1, source_target_pairs={{0,8},{8,0},{16,24},{24,16},{32,40},{40,32},{48,56},{56,48},{1,9},... | collective-permute-start | bytes 737288 | tf_op jit(solution)/shard_map/ppermute | solution.py:601
  4.6 14.7 %collective-permute-start.1 = (bf16[12,80,128]{2,1,0:T(8,128)(2,1)}, bf16[12,80,128]{2,1,0:T(8,128)(2,1)S(1)}, u32[]{:S(2)}, u32[]{:S(2)}) collective-permute-start(bf16[12,80,128]{2,1,0:T(8,128)(2,1)} %get-tuple-element.28), channel_id=1, source_target_pairs={{0,16},{8,24},{16,0},{24,8},{32,48},{40,56},{48,32},{56,40},{1,17}... | collective-permute-start | bytes 737288 | tf_op jit(solution)/shard_map/ppermute | solution.py:601
  6.2 13.2 %collective-permute-start.2 = (bf16[12,80,128]{2,1,0:T(8,128)(2,1)}, bf16[12,80,128]{2,1,0:T(8,128)(2,1)S(1)}, u32[]{:S(2)}, u32[]{:S(2)}) collective-permute-start(bf16[12,80,128]{2,1,0:T(8,128)(2,1)} %get-tuple-element.29), channel_id=1, source_target_pairs={{0,24},{8,16},{16,8},{24,0},{32,56},{40,48},{48,40},{56,32},{1,25}... | collective-permute-start | bytes 737288 | tf_op jit(solution)/shard_map/ppermute | solution.py:601
  6.4 20.4 %collective-permute-start.3 = (bf16[12,80,128]{2,1,0:T(8,128)(2,1)}, bf16[12,80,128]{2,1,0:T(8,128)(2,1)S(1)}, u32[]{:S(2)}, u32[]{:S(2)}) collective-permute-start(bf16[12,80,128]{2,1,0:T(8,128)(2,1)} %get-tuple-element.30), channel_id=1, source_target_pairs={{0,32},{8,40},{16,48},{24,56},{32,0},{40,8},{48,16},{56,24},{1,33}... | collective-permute-start | bytes 737288 | tf_op jit(solution)/shard_map/ppermute | solution.py:601
  9.6 17.2 %copy-start.18 = (bf16[12,80,128]{2,1,0:T(8,128)(2,1)S(1)}, bf16[12,80,128]{2,1,0:T(8,128)(2,1)}, u32[]{:S(2)}) copy-start(bf16[12,80,128]{2,1,0:T(8,128)(2,1)} %get-tuple-element.33) | copy-start | bytes 737284
  10.9 39.4 %collective-permute-start.8 = (f32[1,3,3,96,96]{4,3,2,1,0:T(8,128)S(1)}, f32[1,3,3,96,96]{4,3,2,1,0:T(8,128)S(1)}, u32[]{:S(2)}, u32[]{:S(2)}) collective-permute-start(f32[1,3,3,96,96]{4,3,2,1,0:T(8,128)S(1)} %get-tuple-element.47), channel_id=1, source_target_pairs={{64,1},{65,2},{66,3},{67,4},{68,5},{69,6},{70,7},{1,64},{2,65},{3,... | collective-permute-start | bytes 995336 | tf_op jit(solution)/shard_map/ppermute | solution.py:596
  14.1 27.7 %copy-start = (bf16[12,80,128]{2,1,0:T(8,128)(2,1)}, bf16[12,80,128]{2,1,0:T(8,128)(2,1)S(1)}, u32[]{:S(2)}) copy-start(bf16[12,80,128]{2,1,0:T(8,128)(2,1)S(1)} %collective-permute-done.refs_1_.rest_1_) | copy-start | bytes 737284
  14.1 36.1 %collective-permute-start.7 = (f32[1,3,3,96,96]{4,3,2,1,0:T(8,128)S(1)}, f32[1,3,3,96,96]{4,3,2,1,0:T(8,128)S(1)}, u32[]{:S(2)}, u32[]{:S(2)}) collective-permute-start(f32[1,3,3,96,96]{4,3,2,1,0:T(8,128)S(1)} %get-tuple-element.48), channel_id=1, source_target_pairs={{0,1},{1,2},{2,3},{3,4},{4,5},{5,6},{6,7},{65,64},{66,65},{67,66},... | collective-permute-start | bytes 995336 | tf_op jit(solution)/shard_map/ppermute | solution.py:595
  19.3 22.6 %copy-start.1 = (bf16[12,80,128]{2,1,0:T(8,128)(2,1)}, bf16[12,80,128]{2,1,0:T(8,128)(2,1)S(1)}, u32[]{:S(2)}) copy-start(bf16[12,80,128]{2,1,0:T(8,128)(2,1)S(1)} %collective-permute-done.1.refs_2_.rest_2_) | copy-start | bytes 737284
  19.3 11.6 %collective-permute-start.4 = (bf16[12,80,128]{2,1,0:T(8,128)(2,1)}, bf16[12,80,128]{2,1,0:T(8,128)(2,1)S(1)}, u32[]{:S(2)}, u32[]{:S(2)}) collective-permute-start(bf16[12,80,128]{2,1,0:T(8,128)(2,1)} %get-tuple-element.31), channel_id=1, source_target_pairs={{0,40},{8,32},{16,56},{24,48},{32,8},{40,0},{48,24},{56,16},{1,41}... | collective-permute-start | bytes 737288 | tf_op jit(solution)/shard_map/ppermute | solution.py:601
  19.4 22.5 %copy-start.2 = (bf16[12,80,128]{2,1,0:T(8,128)(2,1)}, bf16[12,80,128]{2,1,0:T(8,128)(2,1)S(1)}, u32[]{:S(2)}) copy-start(bf16[12,80,128]{2,1,0:T(8,128)(2,1)S(1)} %collective-permute-done.2.refs_3_.rest_3_) | copy-start | bytes 737284
  19.4 17.3 %collective-permute-start.5 = (bf16[12,80,128]{2,1,0:T(8,128)(2,1)}, bf16[12,80,128]{2,1,0:T(8,128)(2,1)S(1)}, u32[]{:S(2)}, u32[]{:S(2)}) collective-permute-start(bf16[12,80,128]{2,1,0:T(8,128)(2,1)} %get-tuple-element.32), channel_id=1, source_target_pairs={{0,48},{8,56},{16,32},{24,40},{32,16},{40,24},{48,0},{56,8},{1,49}... | collective-permute-start | bytes 737288 | tf_op jit(solution)/shard_map/ppermute | solution.py:601
  26.8 15.1 %copy-start.3 = (bf16[12,80,128]{2,1,0:T(8,128)(2,1)}, bf16[12,80,128]{2,1,0:T(8,128)(2,1)S(1)}, u32[]{:S(2)}) copy-start(bf16[12,80,128]{2,1,0:T(8,128)(2,1)S(1)} %collective-permute-done.3.refs_4_.rest_4_) | copy-start | bytes 737284
  26.8 15.1 %collective-permute-start.6 = (bf16[12,80,128]{2,1,0:T(8,128)(2,1)S(1)}, bf16[12,80,128]{2,1,0:T(8,128)(2,1)S(1)}, u32[]{:S(2)}, u32[]{:S(2)}) collective-permute-start(bf16[12,80,128]{2,1,0:T(8,128)(2,1)S(1)} %copy-done.18), channel_id=1, source_target_pairs={{0,56},{8,48},{16,40},{24,32},{32,24},{40,16},{48,8},{56,0},{1,57}... | collective-permute-start | bytes 737288 | tf_op jit(solution)/shard_map/ppermute | solution.py:601
  30.9 11.0 %copy-start.4 = (bf16[12,80,128]{2,1,0:T(8,128)(2,1)}, bf16[12,80,128]{2,1,0:T(8,128)(2,1)S(1)}, u32[]{:S(2)}) copy-start(bf16[12,80,128]{2,1,0:T(8,128)(2,1)S(1)} %collective-permute-done.4.refs_5_.rest_5_) | copy-start | bytes 737284
  36.7 5.2 %copy-start.5 = (bf16[12,80,128]{2,1,0:T(8,128)(2,1)}, bf16[12,80,128]{2,1,0:T(8,128)(2,1)S(1)}, u32[]{:S(2)}) copy-start(bf16[12,80,128]{2,1,0:T(8,128)(2,1)S(1)} %collective-permute-done.5.refs_6_.rest_6_) | copy-start | bytes 737284
  41.9 0.7 copy-start.6
  44.4 18.4 %collective-permute-start.16 = (bf16[8,80,128]{2,1,0:T(8,128)(2,1)}, bf16[8,80,128]{2,1,0:T(8,128)(2,1)S(1)}, u32[]{:S(2)}, u32[]{:S(2)}) collective-permute-start(bf16[8,80,128]{2,1,0:T(8,128)(2,1)} %get-tuple-element.42), channel_id=1, source_target_pairs={{0,64},{1,65},{2,66},{3,67},{4,68},{5,69},{6,70},{7,71},{64,1},{65... | collective-permute-start | bytes 491528 | tf_op jit(solution)/shard_map/ppermute | solution.py:609
  47.7 15.8 %collective-permute-start.17 = (bf16[8,80,128]{2,1,0:T(8,128)(2,1)}, bf16[8,80,128]{2,1,0:T(8,128)(2,1)S(1)}, u32[]{:S(2)}, u32[]{:S(2)}) collective-permute-start(bf16[8,80,128]{2,1,0:T(8,128)(2,1)} %get-tuple-element.43), channel_id=1, source_target_pairs={{64,0},{65,1},{66,2},{67,3},{68,4},{69,5},{70,6},{71,7},{1,64},{2,... | collective-permute-start | bytes 491528 | tf_op jit(solution)/shard_map/ppermute | solution.py:610
  50.2 0.8 copy-start.7
  51.0 0.8 copy-start.8
  60.9 5.2 %collective-permute-start.9 = (bf16[560,128]{1,0:T(8,128)(2,1)}, bf16[560,128]{1,0:T(8,128)(2,1)S(1)}, u32[]{:S(2)}, u32[]{:S(2)}) collective-permute-start(bf16[560,128]{1,0:T(8,128)(2,1)} %get-tuple-element.35), channel_id=1, source_target_pairs={{0,8},{8,0},{16,24},{24,16},{32,40},{40,32},{48,56},{56,48},{1,9},... | collective-permute-start | bytes 430088 | tf_op jit(solution)/shard_map/ppermute | solution.py:601
  60.9 6.9 %collective-permute-start.10 = (bf16[560,128]{1,0:T(8,128)(2,1)}, bf16[560,128]{1,0:T(8,128)(2,1)S(1)}, u32[]{:S(2)}, u32[]{:S(2)}) collective-permute-start(bf16[560,128]{1,0:T(8,128)(2,1)} %get-tuple-element.36), channel_id=1, source_target_pairs={{0,16},{8,24},{16,0},{24,8},{32,48},{40,56},{48,32},{56,40},{1,17}... | collective-permute-start | bytes 430088 | tf_op jit(solution)/shard_map/ppermute | solution.py:601
  61.2 8.6 %collective-permute-start.11 = (bf16[560,128]{1,0:T(8,128)(2,1)}, bf16[560,128]{1,0:T(8,128)(2,1)S(1)}, u32[]{:S(2)}, u32[]{:S(2)}) collective-permute-start(bf16[560,128]{1,0:T(8,128)(2,1)} %get-tuple-element.37), channel_id=1, source_target_pairs={{0,24},{8,16},{16,8},{24,0},{32,56},{40,48},{48,40},{56,32},{1,25}... | collective-permute-start | bytes 430088 | tf_op jit(solution)/shard_map/ppermute | solution.py:601
  62.8 19.3 %copy-start.9 = (bf16[8,80,128]{2,1,0:T(8,128)(2,1)}, bf16[8,80,128]{2,1,0:T(8,128)(2,1)S(1)}, u32[]{:S(2)}) copy-start(bf16[8,80,128]{2,1,0:T(8,128)(2,1)S(1)} %collective-permute-done.16.rest_16_) | copy-start | bytes 491524
  62.8 11.0 %collective-permute-start.12 = (bf16[560,128]{1,0:T(8,128)(2,1)}, bf16[560,128]{1,0:T(8,128)(2,1)S(1)}, u32[]{:S(2)}, u32[]{:S(2)}) collective-permute-start(bf16[560,128]{1,0:T(8,128)(2,1)} %get-tuple-element.38), channel_id=1, source_target_pairs={{0,32},{8,40},{16,48},{24,56},{32,0},{40,8},{48,16},{56,24},{1,33}... | collective-permute-start | bytes 430088 | tf_op jit(solution)/shard_map/ppermute | solution.py:601
  63.5 18.6 %copy-start.10 = (bf16[8,80,128]{2,1,0:T(8,128)(2,1)}, bf16[8,80,128]{2,1,0:T(8,128)(2,1)S(1)}, u32[]{:S(2)}) copy-start(bf16[8,80,128]{2,1,0:T(8,128)(2,1)S(1)} %collective-permute-done.17.rest_17_) | copy-start | bytes 491524
  63.5 12.3 %collective-permute-start.13 = (bf16[560,128]{1,0:T(8,128)(2,1)}, bf16[560,128]{1,0:T(8,128)(2,1)S(1)}, u32[]{:S(2)}, u32[]{:S(2)}) collective-permute-start(bf16[560,128]{1,0:T(8,128)(2,1)} %get-tuple-element.39), channel_id=1, source_target_pairs={{0,40},{8,32},{16,56},{24,48},{32,8},{40,0},{48,24},{56,16},{1,41}... | collective-permute-start | bytes 430088 | tf_op jit(solution)/shard_map/ppermute | solution.py:601
  66.0 16.1 %copy-start.11 = (bf16[560,128]{1,0:T(8,128)(2,1)}, bf16[560,128]{1,0:T(8,128)(2,1)S(1)}, u32[]{:S(2)}) copy-start(bf16[560,128]{1,0:T(8,128)(2,1)S(1)} %collective-permute-done.9.rest_9_) | copy-start | bytes 430084
  66.0 13.4 %collective-permute-start.14 = (bf16[560,128]{1,0:T(8,128)(2,1)}, bf16[560,128]{1,0:T(8,128)(2,1)S(1)}, u32[]{:S(2)}, u32[]{:S(2)}) collective-permute-start(bf16[560,128]{1,0:T(8,128)(2,1)} %get-tuple-element.40), channel_id=1, source_target_pairs={{0,48},{8,56},{16,32},{24,40},{32,16},{40,24},{48,0},{56,8},{1,49}... | collective-permute-start | bytes 430088 | tf_op jit(solution)/shard_map/ppermute | solution.py:601
  67.9 14.3 %copy-start.12 = (bf16[560,128]{1,0:T(8,128)(2,1)}, bf16[560,128]{1,0:T(8,128)(2,1)S(1)}, u32[]{:S(2)}) copy-start(bf16[560,128]{1,0:T(8,128)(2,1)S(1)} %collective-permute-done.10.rest_10_) | copy-start | bytes 430084
  67.9 14.2 %collective-permute-start.15 = (bf16[560,128]{1,0:T(8,128)(2,1)}, bf16[560,128]{1,0:T(8,128)(2,1)S(1)}, u32[]{:S(2)}, u32[]{:S(2)}) collective-permute-start(bf16[560,128]{1,0:T(8,128)(2,1)} %get-tuple-element.41), channel_id=1, source_target_pairs={{0,56},{8,48},{16,40},{24,32},{32,24},{40,16},{48,8},{56,0},{1,57}... | collective-permute-start | bytes 430088 | tf_op jit(solution)/shard_map/ppermute | solution.py:601
  69.8 12.3 %copy-start.13 = (bf16[560,128]{1,0:T(8,128)(2,1)}, bf16[560,128]{1,0:T(8,128)(2,1)S(1)}, u32[]{:S(2)}) copy-start(bf16[560,128]{1,0:T(8,128)(2,1)S(1)} %collective-permute-done.11.rest_11_) | copy-start | bytes 430084
  73.8 8.3 %copy-start.14 = (bf16[560,128]{1,0:T(8,128)(2,1)}, bf16[560,128]{1,0:T(8,128)(2,1)S(1)}, u32[]{:S(2)}) copy-start(bf16[560,128]{1,0:T(8,128)(2,1)S(1)} %collective-permute-done.12.rest_12_) | copy-start | bytes 430084
  75.8 6.4 %copy-start.15 = (bf16[560,128]{1,0:T(8,128)(2,1)}, bf16[560,128]{1,0:T(8,128)(2,1)S(1)}, u32[]{:S(2)}) copy-start(bf16[560,128]{1,0:T(8,128)(2,1)S(1)} %collective-permute-done.13.rest_13_) | copy-start | bytes 430084
  79.4 2.7 %copy-start.16 = (bf16[560,128]{1,0:T(8,128)(2,1)}, bf16[560,128]{1,0:T(8,128)(2,1)S(1)}, u32[]{:S(2)}) copy-start(bf16[560,128]{1,0:T(8,128)(2,1)S(1)} %collective-permute-done.14.rest_14_) | copy-start | bytes 430084
  82.1 0.7 copy-start.17
  93.8 7.7 %collective-permute-start.19 = (f16[72,128]{1,0:T(8,128)(2,1)S(1)}, f16[72,128]{1,0:T(8,128)(2,1)S(1)}, u32[]{:S(2)}, u32[]{:S(2)}) collective-permute-start(f16[72,128]{1,0:T(8,128)(2,1)S(1)} %convert_element_type.17), channel_id=1, source_target_pairs={{64,0},{65,1},{66,2},{67,3},{68,4},{69,5},{70,6},{71,7},{1,64},{2,... | collective-permute-start | bytes 55304 | tf_op jit(solution)/shard_map/ppermute | solution.py:615
  98.3 5.7 %collective-permute-start.18 = (f16[72,128]{1,0:T(8,128)(2,1)S(1)}, f16[72,128]{1,0:T(8,128)(2,1)S(1)}, u32[]{:S(2)}, u32[]{:S(2)}) collective-permute-start(f16[72,128]{1,0:T(8,128)(2,1)S(1)} %convert_element_type.16), channel_id=1, source_target_pairs={{0,64},{1,65},{2,66},{3,67},{4,68},{5,69},{6,70},{7,71},{64,1},{65... | collective-permute-start | bytes 55304 | tf_op jit(solution)/shard_map/ppermute | solution.py:614
  104.0 6.5 %collective-permute-start.28 = (f16[576,128]{1,0:T(8,128)(2,1)S(1)}, f16[576,128]{1,0:T(8,128)(2,1)S(1)}, u32[]{:S(2)}, u32[]{:S(2)}) collective-permute-start(f16[576,128]{1,0:T(8,128)(2,1)S(1)} %pad_maximum_fusion), channel_id=1, source_target_pairs={{0,8},{8,0},{16,24},{24,16},{32,40},{40,32},{48,56},{56,48},{1,9},... | collective-permute-start | bytes 442376 | tf_op jit(solution)/shard_map/ppermute | solution.py:626
  104.1 20.9 %collective-permute-start.31 = (f16[576,128]{1,0:T(8,128)(2,1)S(1)}, f16[576,128]{1,0:T(8,128)(2,1)S(1)}, u32[]{:S(2)}, u32[]{:S(2)}) collective-permute-start(f16[576,128]{1,0:T(8,128)(2,1)S(1)} %pad_maximum_fusion), channel_id=1, source_target_pairs={{0,32},{8,40},{16,48},{24,56},{32,0},{40,8},{48,16},{56,24},{64,96... | collective-permute-start | bytes 442376 | tf_op jit(solution)/shard_map/ppermute | solution.py:620
  104.2 8.6 %collective-permute-start.29 = (f16[576,128]{1,0:T(8,128)(2,1)S(1)}, f16[576,128]{1,0:T(8,128)(2,1)S(1)}, u32[]{:S(2)}, u32[]{:S(2)}) collective-permute-start(f16[576,128]{1,0:T(8,128)(2,1)S(1)} %pad_maximum_fusion), channel_id=1, source_target_pairs={{0,16},{8,24},{16,0},{24,8},{32,48},{40,56},{48,32},{56,40},{64,80... | collective-permute-start | bytes 442376 | tf_op jit(solution)/shard_map/ppermute | solution.py:620
  105.5 21.1 %collective-permute-start.33 = (f16[576,128]{1,0:T(8,128)(2,1)S(1)}, f16[576,128]{1,0:T(8,128)(2,1)S(1)}, u32[]{:S(2)}, u32[]{:S(2)}) collective-permute-start(f16[576,128]{1,0:T(8,128)(2,1)S(1)} %pad_maximum_fusion), channel_id=1, source_target_pairs={{0,48},{8,56},{16,32},{24,40},{32,16},{40,24},{48,0},{56,8},{64,11... | collective-permute-start | bytes 442376 | tf_op jit(solution)/shard_map/ppermute | solution.py:620
  108.3 18.8 %collective-permute-start.26 = (f16[576,128]{1,0:T(8,128)(2,1)S(1)}, f16[576,128]{1,0:T(8,128)(2,1)S(1)}, u32[]{:S(2)}, u32[]{:S(2)}) collective-permute-start(f16[576,128]{1,0:T(8,128)(2,1)S(1)} %pad_maximum_fusion), channel_id=1, source_target_pairs={{0,112},{8,120},{16,96},{24,104},{32,80},{40,88},{48,64},{56,72},{... | collective-permute-start | bytes 442376 | tf_op jit(solution)/shard_map/ppermute | solution.py:620
  110.5 16.8 %collective-permute-start.24 = (f16[576,128]{1,0:T(8,128)(2,1)S(1)}, f16[576,128]{1,0:T(8,128)(2,1)S(1)}, u32[]{:S(2)}, u32[]{:S(2)}) collective-permute-start(f16[576,128]{1,0:T(8,128)(2,1)S(1)} %pad_maximum_fusion), channel_id=1, source_target_pairs={{0,96},{8,104},{16,112},{24,120},{32,64},{40,72},{48,80},{56,88},{... | collective-permute-start | bytes 442376 | tf_op jit(solution)/shard_map/ppermute | solution.py:620
  112.8 12.2 %collective-permute-start.20 = (f16[576,128]{1,0:T(8,128)(2,1)S(1)}, f16[576,128]{1,0:T(8,128)(2,1)S(1)}, u32[]{:S(2)}, u32[]{:S(2)}) collective-permute-start(f16[576,128]{1,0:T(8,128)(2,1)S(1)} %pad_maximum_fusion), channel_id=1, source_target_pairs={{0,64},{8,72},{16,80},{24,88},{32,96},{40,104},{48,112},{56,120},{... | collective-permute-start | bytes 442376 | tf_op jit(solution)/shard_map/ppermute | solution.py:620
  125.0 1.4 collective-permute-start.30
  125.0 7.2 %collective-permute-start.22 = (f16[576,128]{1,0:T(8,128)(2,1)S(1)}, f16[576,128]{1,0:T(8,128)(2,1)S(1)}, u32[]{:S(2)}, u32[]{:S(2)}) collective-permute-start(f16[576,128]{1,0:T(8,128)(2,1)S(1)} %pad_maximum_fusion), channel_id=1, source_target_pairs={{0,80},{8,88},{16,64},{24,72},{32,112},{40,120},{48,96},{56,104},{... | collective-permute-start | bytes 442376 | tf_op jit(solution)/shard_map/ppermute | solution.py:620
  126.4 5.9 %collective-permute-start.32 = (f16[576,128]{1,0:T(8,128)(2,1)S(1)}, f16[576,128]{1,0:T(8,128)(2,1)S(1)}, u32[]{:S(2)}, u32[]{:S(2)}) collective-permute-start(f16[576,128]{1,0:T(8,128)(2,1)S(1)} %collective-permute-done.31), channel_id=1, source_target_pairs={{0,8},{8,0},{16,24},{24,16},{32,40},{40,32},{48,56},{56,48},{1,9},... | collective-permute-start | bytes 442376 | tf_op jit(solution)/shard_map/ppermute | solution.py:626
  126.6 8.0 %collective-permute-start.21 = (f16[576,128]{1,0:T(8,128)(2,1)S(1)}, f16[576,128]{1,0:T(8,128)(2,1)S(1)}, u32[]{:S(2)}, u32[]{:S(2)}) collective-permute-start(f16[576,128]{1,0:T(8,128)(2,1)S(1)} %collective-permute-done.20), channel_id=1, source_target_pairs={{0,8},{8,0},{16,24},{24,16},{32,40},{40,32},{48,56},{56,48},{1,9},... | collective-permute-start | bytes 442376 | tf_op jit(solution)/shard_map/ppermute | solution.py:626
  127.1 5.8 %collective-permute-start.34 = (f16[576,128]{1,0:T(8,128)(2,1)S(1)}, f16[576,128]{1,0:T(8,128)(2,1)S(1)}, u32[]{:S(2)}, u32[]{:S(2)}) collective-permute-start(f16[576,128]{1,0:T(8,128)(2,1)S(1)} %collective-permute-done.33), channel_id=1, source_target_pairs={{0,8},{8,0},{16,24},{24,16},{32,40},{40,32},{48,56},{56,48},{1,9},... | collective-permute-start | bytes 442376 | tf_op jit(solution)/shard_map/ppermute | solution.py:626
  127.3 7.6 %collective-permute-start.27 = (f16[576,128]{1,0:T(8,128)(2,1)S(1)}, f16[576,128]{1,0:T(8,128)(2,1)S(1)}, u32[]{:S(2)}, u32[]{:S(2)}) collective-permute-start(f16[576,128]{1,0:T(8,128)(2,1)S(1)} %collective-permute-done.26), channel_id=1, source_target_pairs={{0,8},{8,0},{16,24},{24,16},{32,40},{40,32},{48,56},{56,48},{1,9},... | collective-permute-start | bytes 442376 | tf_op jit(solution)/shard_map/ppermute | solution.py:626
  132.3 2.5 %collective-permute-start.25 = (f16[576,128]{1,0:T(8,128)(2,1)S(1)}, f16[576,128]{1,0:T(8,128)(2,1)S(1)}, u32[]{:S(2)}, u32[]{:S(2)}) collective-permute-start(f16[576,128]{1,0:T(8,128)(2,1)S(1)} %collective-permute-done.24), channel_id=1, source_target_pairs={{0,8},{8,0},{16,24},{24,16},{32,40},{40,32},{48,56},{56,48},{1,9},... | collective-permute-start | bytes 442376 | tf_op jit(solution)/shard_map/ppermute | solution.py:626
  132.3 2.4 %collective-permute-start.23 = (f16[576,128]{1,0:T(8,128)(2,1)S(1)}, f16[576,128]{1,0:T(8,128)(2,1)S(1)}, u32[]{:S(2)}, u32[]{:S(2)}) collective-permute-start(f16[576,128]{1,0:T(8,128)(2,1)S(1)} %collective-permute-done.22), channel_id=1, source_target_pairs={{0,8},{8,0},{16,24},{24,16},{32,40},{40,32},{48,56},{56,48},{1,9},... | collective-permute-start | bytes 442376 | tf_op jit(solution)/shard_map/ppermute | solution.py:626

commit v3 on v1

--- a/solution.py
+++ b/solution.py
@@ -16,6 +16,7 @@
 VR = CZ * CW
 VROWS = 5 * VR
 PROWS = 80
+SPREAD = (1, 3, 7, 5, 2, 6, 4)
 SCALE = 128.0
 
 
@@ -418,10 +419,9 @@
     tail = HZ * 3 // 2
     for peer in range(8):
         rows = slice(8 + CY * peer, 8 + CY * (peer + 1))
-        slots = [(half ^ level) * 8 + (peer ^ me) for half in range(2)]
 
         def block(half, index):
-            return chunks[slots[half], CY * index : CY * (index + 1)]
+            return chunks[peer ^ me, half ^ level, CY * index : CY * (index + 1)]
 
         for half in range(2):
             for z in range(HZ):
@@ -473,9 +473,8 @@
             around = held[z - 1, start : start + count] + held[z + 1, start : start + count]
             around += held[z, start - 1 : start - 1 + count] + held[z, start + 1 : start + 1 + count]
             around += sums[b, start - 8 : start - 8 + count]
-            done.append(
-                (0.1 * scale) * held[z, start : start + count] + (0.15 * scale) * around
-            )
+            value = around + (2.0 / 3.0) * held[z, start : start + count]
+            done.append(value if scale is None else scale * value)
         return done
 
     def sweep(planes, store, scale, after):
@@ -500,7 +499,7 @@
         flat2[index + 16, start : start + count] = done[1]
         pair2[index, start : start + count] = done[2]
 
-    sweep((flat, pair), first, 1.0, lambda index: None)
+    sweep((flat, pair), first, None, lambda index: None)
     whole = lax.broadcasted_iota(jnp.int32, (size, 128), 1)
 
     @pl.when(zone == 0)
@@ -534,7 +533,7 @@
         def _():
             emit(index + 11).start()
 
-    sweep((flat2, pair2), second, 1.0 / SCALE, depart)
+    sweep((flat2, pair2), second, 0.15 * 0.15 / SCALE, depart)
 
     def finish(z, carry):
         emit(z).wait()
@@ -586,7 +585,7 @@
 
     def spread(parts):
         arrived = {0: parts[0]}
-        for k in (3, 7, 5, 2, 6, 4, 1):
+        for k in SPREAD:
             arrived[k] = lax.ppermute(parts[k], "subj", [(i, i ^ k) for i in range(8)])
         return [arrived[k] for k in range(8)]
 
@@ -598,19 +597,24 @@
     below = lax.ppermute(high, nearest, climb)
     above = lax.ppermute(low, nearest, [(b, a) for a, b in climb])
     chunk, edge = warp(info, assign, planes, fields, below, above)
-    edge = lax.ppermute(edge.astype(jnp.float16), nearest, cross)
-    chunk = jnp.concatenate([chunk.astype(jnp.float16), edge], axis=0)
-    mine = {(0, 0): chunk}
-    for far, step in ((0, 1), (0, 3), (1, 0), (0, 2), (1, 1), (1, 3), (1, 2)):
-        perm = [(8 * a + i, 8 * (a ^ far) + (i ^ (2 * step))) for a in range(2) for i in range(8)]
-        mine[far, step] = lax.ppermute(chunk, ("level", "subj"), perm)
+    edge = edge.astype(jnp.float16)
+    chunk = chunk.astype(jnp.float16)
+    inward = [(g + 1, g) for g in range(zones - 1)]
+    inward += [(zones + g, zones + g + 1) for g in range(zones - 1)]
+    swapped = lax.ppermute(chunk, "level", [(0, 1), (1, 0)])
+    own_edge = lax.ppermute(edge, nearest, cross)
+    far_edge = lax.ppermute(edge, nearest, inward)
+    both = jnp.concatenate([chunk, own_edge, swapped, far_edge], axis=0)
+    arrived = {0: both}
+    for step in (1, 3, 2):
+        perm = [(i, i ^ (2 * step)) for i in range(8)]
+        arrived[step] = lax.ppermute(both, "subj", perm)
     gathered = []
-    for far in range(2):
-        for step in range(4):
-            part = mine[far, step]
-            gathered += [part, lax.ppermute(part, "subj", [(i, i ^ 1) for i in range(8)])]
+    for step in range(4):
+        part = arrived[step]
+        gathered += [part, lax.ppermute(part, "subj", [(i, i ^ 1) for i in range(8)])]
     chunks = jnp.stack(gathered).astype(F32)
-    return relax(info, chunks)
+    return relax(info, chunks.reshape(8, 2, -1, 128))
 
 
 def solution(mesh):

time: 137 us -> 141 us (1.029)
  the two profiles are of different devices: /device:TPU:96 before, /device:TPU:39 now
where the time goes in v3:
time: 141 us
  starting transfers between devices  52.9 us (38%)
  waiting for transfers between devices  43.1 us (31%)
  Pallas kernels  35.1 us (25%)
  other arithmetic  4.68 us (3%)
  local copies, waits for them, and re-layouts  4.62 us (3%)
    ppermute x14, waiting for transfers between devices, spread(): arrived[k] = lax.ppermute(parts[k], 'subj', [(i, i ^ k) for i in range(8)])  34.1 us
    ppermute x14, starting transfers between devices, spread(): arrived[k] = lax.ppermute(parts[k], 'subj', [(i, i ^ k) for i in range(8)])  18.7 us
    pallas_call x1, Pallas kernels, relax(): pl.pallas_call(relax_kernel, grid=(), in_specs=[pl.BlockSpec(memory_space...  10.9 us
    ppermute x4, starting transfers between devices, update(): lax.ppermute(part, 'subj', [(i, i ^ 1) for i in range(8)])  10.6 us
    pallas_call x1, Pallas kernels, warp(): pl.pallas_call(warp_kernel, grid=(), in_specs=[smem, smem, vmem, vmem, vm...  9.56 us
    pallas_call x1, Pallas kernels, blur(): pl.pallas_call(blur_kernel, grid=(), in_specs=[pl.BlockSpec(memory_space=...  9.05 us
    ppermute x1, starting transfers between devices, update(): far_edge = lax.ppermute(edge, nearest, inward)  6.06 us
    ppermute x1, waiting for transfers between devices, update(): own_edge = lax.ppermute(edge, nearest, cross)  4.68 us
  transfers between devices with their start and end apart: 28, of which 15 were waited for; matrix products, arithmetic and copies ran while one was open for 2% of the time, Pallas kernels for 8%

profile of v3, /device:TPU:39, one launch (start us, length us, event | category | flops | bytes accessed | tf_op | source)
XLA Modules:
  0.0 140.9 jit_solution(7430433299515056167)
XLA Ops:
  0.0 0.7 pad_add_fusion.info
  0.7 3.9 %pack_images.1 = (bf16[12,80,128]{2,1,0:T(8,128)(2,1)}, bf16[12,80,128]{2,1,0:T(8,128)(2,1)}, bf16[12,80,128]{2,1,0:T(8,128)(2,1)}, bf16[12,80,128]{2,1,0:T(8,12...) custom-call(s32[3]{0:T(128)} %pad_add_fusion.info, ...), custom_call_target="tpu_custom_call" | custom-call | tf_op jit(solution)/shard_map/pack_images/pallas_call | solution.py:106
  4.5 0.8 collective-permute-start
  5.3 1.3 collective-permute-start.1
  6.6 0.4 collective-permute-start.2
  7.0 2.9 %collective-permute-start.3 = (bf16[12,80,128]{2,1,0:T(8,128)(2,1)}, bf16[12,80,128]{2,1,0:T(8,128)(2,1)S(1)}, u32[]{:S(2)}, u32[]{:S(2)}) collective-permute-start(bf16[12,80,128]{2,1,0:T(8,128)(2,1)} %get-tuple-element.29), channel_id=1, source_target_pairs={{0,32},{8,40},{16,48},{24,56},{32,0},{40,8},{48,16},{56,24},{1,33}... | collective-permute-start | bytes 737288 | tf_op jit(solution)/shard_map/ppermute | solution.py:589
  9.9 1.2 constant_dynamic-slice_fusion
  11.1 3.5 %collective-permute-start.8 = (f32[1,3,3,96,96]{4,3,2,1,0:T(8,128)S(1)}, f32[1,3,3,96,96]{4,3,2,1,0:T(8,128)S(1)}, u32[]{:S(2)}, u32[]{:S(2)}) collective-permute-start(f32[1,3,3,96,96]{4,3,2,1,0:T(8,128)S(1)} %get-tuple-element.45), channel_id=1, source_target_pairs={{64,1},{65,2},{66,3},{67,4},{68,5},{69,6},{70,7},{1,64},{2,65},{3,... | collective-permute-start | bytes 995336 | tf_op jit(solution)/shard_map/ppermute | solution.py:584
  14.6 1.9 %collective-permute-start.7 = (f32[1,3,3,96,96]{4,3,2,1,0:T(8,128)S(1)}, f32[1,3,3,96,96]{4,3,2,1,0:T(8,128)S(1)}, u32[]{:S(2)}, u32[]{:S(2)}) collective-permute-start(f32[1,3,3,96,96]{4,3,2,1,0:T(8,128)S(1)} %get-tuple-element.46), channel_id=1, source_target_pairs={{0,1},{1,2},{2,3},{3,4},{4,5},{5,6},{6,7},{65,64},{66,65},{67,66},... | collective-permute-start | bytes 995336 | tf_op jit(solution)/shard_map/ppermute | solution.py:583
  16.6 0.7 collective-permute-start.4
  17.3 2.0 %collective-permute-done.2.refs_3_.rest_3_ = bf16[12,80,128]{2,1,0:T(8,128)(2,1)S(1)} collective-permute-done((bf16[12,80,128]{2,1,0:T(8,128)(2,1)}, bf16[12,80,128]{2,1,0:T(8,128)(2,1)S(1)}, u32[]{:S(2)}, u32[]{:S(2)}) %collective-permute-start.2) | collective-permute-done | bytes 245792 | tf_op jit(solution)/shard_map/ppermute | solution.py:589
  19.3 2.7 %collective-permute-start.5 = (bf16[12,80,128]{2,1,0:T(8,128)(2,1)}, bf16[12,80,128]{2,1,0:T(8,128)(2,1)S(1)}, u32[]{:S(2)}, u32[]{:S(2)}) collective-permute-start(bf16[12,80,128]{2,1,0:T(8,128)(2,1)} %get-tuple-element.31), channel_id=1, source_target_pairs={{0,48},{8,56},{16,32},{24,40},{32,16},{40,24},{48,0},{56,8},{1,49}... | collective-permute-start | bytes 737288 | tf_op jit(solution)/shard_map/ppermute | solution.py:589
  22.0 3.9 %collective-permute-done.3.refs_4_.rest_4_ = bf16[12,80,128]{2,1,0:T(8,128)(2,1)S(1)} collective-permute-done((bf16[12,80,128]{2,1,0:T(8,128)(2,1)}, bf16[12,80,128]{2,1,0:T(8,128)(2,1)S(1)}, u32[]{:S(2)}, u32[]{:S(2)}) %collective-permute-start.3) | collective-permute-done | bytes 245792 | tf_op jit(solution)/shard_map/ppermute | solution.py:589
  25.9 1.4 collective-permute-start.6
  27.3 4.4 %collective-permute-done.4.refs_5_.rest_5_ = bf16[12,80,128]{2,1,0:T(8,128)(2,1)S(1)} collective-permute-done((bf16[12,80,128]{2,1,0:T(8,128)(2,1)}, bf16[12,80,128]{2,1,0:T(8,128)(2,1)S(1)}, u32[]{:S(2)}, u32[]{:S(2)}) %collective-permute-start.4) | collective-permute-done | bytes 245792 | tf_op jit(solution)/shard_map/ppermute | solution.py:589
  31.8 5.2 %collective-permute-done.5.refs_6_.rest_6_ = bf16[12,80,128]{2,1,0:T(8,128)(2,1)S(1)} collective-permute-done((bf16[12,80,128]{2,1,0:T(8,128)(2,1)}, bf16[12,80,128]{2,1,0:T(8,128)(2,1)S(1)}, u32[]{:S(2)}, u32[]{:S(2)}) %collective-permute-start.5) | collective-permute-done | bytes 245792 | tf_op jit(solution)/shard_map/ppermute | solution.py:589
  37.0 5.3 %collective-permute-done.6.refs_7_.rest_7_ = bf16[12,80,128]{2,1,0:T(8,128)(2,1)S(1)} collective-permute-done((bf16[12,80,128]{2,1,0:T(8,128)(2,1)}, bf16[12,80,128]{2,1,0:T(8,128)(2,1)S(1)}, u32[]{:S(2)}, u32[]{:S(2)}) %collective-permute-start.6) | collective-permute-done | bytes 245792 | tf_op jit(solution)/shard_map/ppermute | solution.py:589
  42.3 0.7 copy-done.6
  42.9 1.8 %cut_edges.1 = (bf16[8,80,128]{2,1,0:T(8,128)(2,1)}, bf16[8,80,128]{2,1,0:T(8,128)(2,1)}) custom-call(bf16[12,80,128]{2,1,0:T(8,128)(2,1)} %get-tuple-element.25.refs_0_.rest_0_, bf16[12,80,128]{2,1,0:T(8,128)(2,1)} %copy-done, bf16[12,80,128]{2,1,0:T(8,128)(2,1)} %copy-done.1, bf16[12,80,128]{2,1,0:T(8,128)(2,1)} %copy-done.2, ...), custom_call_target="tpu_custom_call" | custom-call | tf_op jit(solution)/shard_map/cut_edges/pallas_call | solution.py:241
  44.7 3.5 %collective-permute-start.16 = (bf16[8,80,128]{2,1,0:T(8,128)(2,1)}, bf16[8,80,128]{2,1,0:T(8,128)(2,1)S(1)}, u32[]{:S(2)}, u32[]{:S(2)}) collective-permute-start(bf16[8,80,128]{2,1,0:T(8,128)(2,1)} %get-tuple-element.41), channel_id=1, source_target_pairs={{0,64},{1,65},{2,66},{3,67},{4,68},{5,69},{6,70},{7,71},{64,1},{65... | collective-permute-start | bytes 491528 | tf_op jit(solution)/shard_map/ppermute | solution.py:597
  48.2 1.9 %collective-permute-start.17 = (bf16[8,80,128]{2,1,0:T(8,128)(2,1)}, bf16[8,80,128]{2,1,0:T(8,128)(2,1)S(1)}, u32[]{:S(2)}, u32[]{:S(2)}) collective-permute-start(bf16[8,80,128]{2,1,0:T(8,128)(2,1)} %get-tuple-element.42), channel_id=1, source_target_pairs={{64,0},{65,1},{66,2},{67,3},{68,4},{69,5},{70,6},{71,7},{1,64},{2,... | collective-permute-start | bytes 491528 | tf_op jit(solution)/shard_map/ppermute | solution.py:598
  50.2 0.7 copy-done.7
  50.9 0.8 copy-done.8
  51.7 9.0 %blur_momenta.1 = (bf16[560,128]{1,0:T(8,128)(2,1)}, bf16[560,128]{1,0:T(8,128)(2,1)}, bf16[560,128]{1,0:T(8,128)(2,1)}, bf16[560,128]{1,0:T(8,128)(2,1)}, bf16[...) custom-call(s32[3]{0:T(128)} %pad_add_fusion.info, ...), custom_call_target="tpu_custom_call" | custom-call | tf_op jit(solution)/shard_map/blur_momenta/pallas_call | solution.py:192
  60.7 0.9 collective-permute-start.9
  61.7 1.7 %collective-permute-start.11 = (bf16[560,128]{1,0:T(8,128)(2,1)}, bf16[560,128]{1,0:T(8,128)(2,1)S(1)}, u32[]{:S(2)}, u32[]{:S(2)}) collective-permute-start(bf16[560,128]{1,0:T(8,128)(2,1)} %get-tuple-element.36), channel_id=1, source_target_pairs={{0,24},{8,16},{16,8},{24,0},{32,56},{40,48},{48,40},{56,32},{1,25}... | collective-permute-start | bytes 430088 | tf_op jit(solution)/shard_map/ppermute | solution.py:589
  63.4 0.3 collective-permute-start.12
  63.8 2.9 %collective-permute-start.13 = (bf16[560,128]{1,0:T(8,128)(2,1)}, bf16[560,128]{1,0:T(8,128)(2,1)S(1)}, u32[]{:S(2)}, u32[]{:S(2)}) collective-permute-start(bf16[560,128]{1,0:T(8,128)(2,1)} %get-tuple-element.38), channel_id=1, source_target_pairs={{0,40},{8,32},{16,56},{24,48},{32,8},{40,0},{48,24},{56,16},{1,41}... | collective-permute-start | bytes 430088 | tf_op jit(solution)/shard_map/ppermute | solution.py:589
  66.7 0.4 collective-permute-done.10.rest_10_
  67.1 2.5 %collective-permute-start.15 = (bf16[560,128]{1,0:T(8,128)(2,1)}, bf16[560,128]{1,0:T(8,128)(2,1)S(1)}, u32[]{:S(2)}, u32[]{:S(2)}) collective-permute-start(bf16[560,128]{1,0:T(8,128)(2,1)} %get-tuple-element.40), channel_id=1, source_target_pairs={{0,56},{8,48},{16,40},{24,32},{32,24},{40,16},{48,8},{56,0},{1,57}... | collective-permute-start | bytes 430088 | tf_op jit(solution)/shard_map/ppermute | solution.py:589
  69.6 1.7 %collective-permute-done.11.rest_11_ = bf16[560,128]{1,0:T(8,128)(2,1)S(1)} collective-permute-done((bf16[560,128]{1,0:T(8,128)(2,1)}, bf16[560,128]{1,0:T(8,128)(2,1)S(1)}, u32[]{:S(2)}, u32[]{:S(2)}) %collective-permute-start.11) | collective-permute-done | bytes 143392 | tf_op jit(solution)/shard_map/ppermute | solution.py:589
  71.3 1.7 %collective-permute-done.12.rest_12_ = bf16[560,128]{1,0:T(8,128)(2,1)S(1)} collective-permute-done((bf16[560,128]{1,0:T(8,128)(2,1)}, bf16[560,128]{1,0:T(8,128)(2,1)S(1)}, u32[]{:S(2)}, u32[]{:S(2)}) %collective-permute-start.12) | collective-permute-done | bytes 143392 | tf_op jit(solution)/shard_map/ppermute | solution.py:589
  73.0 3.4 %collective-permute-done.13.rest_13_ = bf16[560,128]{1,0:T(8,128)(2,1)S(1)} collective-permute-done((bf16[560,128]{1,0:T(8,128)(2,1)}, bf16[560,128]{1,0:T(8,128)(2,1)S(1)}, u32[]{:S(2)}, u32[]{:S(2)}) %collective-permute-start.13) | collective-permute-done | bytes 143392 | tf_op jit(solution)/shard_map/ppermute | solution.py:589
  76.3 3.0 %collective-permute-done.14.rest_14_ = bf16[560,128]{1,0:T(8,128)(2,1)S(1)} collective-permute-done((bf16[560,128]{1,0:T(8,128)(2,1)}, bf16[560,128]{1,0:T(8,128)(2,1)S(1)}, u32[]{:S(2)}, u32[]{:S(2)}) %collective-permute-start.14) | collective-permute-done | bytes 143392 | tf_op jit(solution)/shard_map/ppermute | solution.py:589
  79.4 3.1 %collective-permute-done.15.rest_15_ = bf16[560,128]{1,0:T(8,128)(2,1)S(1)} collective-permute-done((bf16[560,128]{1,0:T(8,128)(2,1)}, bf16[560,128]{1,0:T(8,128)(2,1)S(1)}, u32[]{:S(2)}, u32[]{:S(2)}) %collective-permute-start.15) | collective-permute-done | bytes 143392 | tf_op jit(solution)/shard_map/ppermute | solution.py:589
  82.5 0.6 copy-done.17
  83.1 9.6 %warp_sum.1 = (f32[432,128]{1,0:T(8,128)}, f32[72,128]{1,0:T(8,128)}) custom-call(s32[3]{0:T(128)} %pad_add_fusion.info, s32[16]{0:T(128)} %assign.1, bf16[288,112]{1,0:T(8,128)(2,1)} %constant.27.clone.zy, bf16[256,256]{1,0:T(8,128)(2,1)} %constant.28.clone.x0, bf16[256,256]{1,0:T(8,128)(2,1)} %constant.29.clone.x1, ...), custom_call_target="tpu_custom_call" | custom-call | tf_op jit(solution)/shard_map/warp_sum/pallas_call | solution.py:388
  92.7 1.0 convert_element_type.10
  93.6 0.8 collective-permute-start.19
  94.4 0.8 convert_element_type.11
  95.2 6.1 %collective-permute-start.20 = (f16[72,128]{1,0:T(8,128)(2,1)S(1)}, f16[72,128]{1,0:T(8,128)(2,1)S(1)}, u32[]{:S(2)}, u32[]{:S(2)}) collective-permute-start(f16[72,128]{1,0:T(8,128)(2,1)S(1)} %convert_element_type.11), channel_id=1, source_target_pairs={{1,0},{2,1},{3,2},{4,3},{5,4},{6,5},{7,6},{64,65},{65,66},{66,67},... | collective-permute-start | bytes 55304 | tf_op jit(solution)/shard_map/ppermute | solution.py:606
  101.2 1.9 %collective-permute-start.18 = (f16[72,128]{1,0:T(8,128)(2,1)S(1)}, f16[72,128]{1,0:T(8,128)(2,1)S(1)}, u32[]{:S(2)}, u32[]{:S(2)}) collective-permute-start(f16[72,128]{1,0:T(8,128)(2,1)S(1)} %convert_element_type.11), channel_id=1, source_target_pairs={{64,1},{65,2},{66,3},{67,4},{68,5},{69,6},{70,7},{1,64},{2,65},{3,... | collective-permute-start | bytes 55304 | tf_op jit(solution)/shard_map/ppermute | solution.py:605
  103.2 4.7 %collective-permute-done.18 = f16[72,128]{1,0:T(8,128)(2,1)S(1)} collective-permute-done((f16[72,128]{1,0:T(8,128)(2,1)S(1)}, f16[72,128]{1,0:T(8,128)(2,1)S(1)}, u32[]{:S(2)}, u32[]{:S(2)}) %collective-permute-start.18) | collective-permute-done | bytes 18464 | tf_op jit(solution)/shard_map/ppermute | solution.py:605
  107.8 0.1 pad_maximum_fusion
  107.9 0.1 collective-permute-start.22
  108.0 1.5 %collective-permute-start.24 = (f16[1008,128]{1,0:T(8,128)(2,1)S(1)}, f16[1008,128]{1,0:T(8,128)(2,1)S(1)}, u32[]{:S(2)}, u32[]{:S(2)}) collective-permute-start(f16[1008,128]{1,0:T(8,128)(2,1)S(1)} %pad_maximum_fusion), channel_id=1, source_target_pairs={{0,32},{8,40},{16,48},{24,56},{32,0},{40,8},{48,16},{56,24},{1,33}... | collective-permute-start | bytes 774152 | tf_op jit(solution)/shard_map/ppermute | solution.py:611
  109.6 2.5 %collective-permute-start.21 = (f16[1008,128]{1,0:T(8,128)(2,1)S(1)}, f16[1008,128]{1,0:T(8,128)(2,1)S(1)}, u32[]{:S(2)}, u32[]{:S(2)}) collective-permute-start(f16[1008,128]{1,0:T(8,128)(2,1)S(1)} %pad_maximum_fusion), channel_id=1, source_target_pairs={{0,8},{8,0},{16,24},{24,16},{32,40},{40,32},{48,56},{56,48},{1,9},... | collective-permute-start | bytes 774152 | tf_op jit(solution)/shard_map/ppermute | solution.py:615
  112.0 2.5 %collective-permute-start.26 = (f16[1008,128]{1,0:T(8,128)(2,1)S(1)}, f16[1008,128]{1,0:T(8,128)(2,1)S(1)}, u32[]{:S(2)}, u32[]{:S(2)}) collective-permute-start(f16[1008,128]{1,0:T(8,128)(2,1)S(1)} %pad_maximum_fusion), channel_id=1, source_target_pairs={{0,48},{8,56},{16,32},{24,40},{32,16},{40,24},{48,0},{56,8},{1,49}... | collective-permute-start | bytes 774152 | tf_op jit(solution)/shard_map/ppermute | solution.py:611
  114.5 4.7 %collective-permute-start.23 = (f16[1008,128]{1,0:T(8,128)(2,1)S(1)}, f16[1008,128]{1,0:T(8,128)(2,1)S(1)}, u32[]{:S(2)}, u32[]{:S(2)}) collective-permute-start(f16[1008,128]{1,0:T(8,128)(2,1)S(1)} %collective-permute-done.22), channel_id=1, source_target_pairs={{0,8},{8,0},{16,24},{24,16},{32,40},{40,32},{48,56},{56,48},{1,9},... | collective-permute-start | bytes 774152 | tf_op jit(solution)/shard_map/ppermute | solution.py:615
  119.2 0.1 constant_dynamic-update-slice_fusion.7
  119.3 0.2 collective-permute-done.24
  119.5 2.9 %collective-permute-start.25 = (f16[1008,128]{1,0:T(8,128)(2,1)S(1)}, f16[1008,128]{1,0:T(8,128)(2,1)S(1)}, u32[]{:S(2)}, u32[]{:S(2)}) collective-permute-start(f16[1008,128]{1,0:T(8,128)(2,1)S(1)} %collective-permute-done.24), channel_id=1, source_target_pairs={{0,8},{8,0},{16,24},{24,16},{32,40},{40,32},{48,56},{56,48},{1,9},... | collective-permute-start | bytes 774152 | tf_op jit(solution)/shard_map/ppermute | solution.py:615
  122.4 0.1 constant_dynamic-update-slice_fusion.6
  122.4 0.1 constant_dynamic-update-slice_fusion.5
  122.5 3.3 %collective-permute-done.26 = f16[1008,128]{1,0:T(8,128)(2,1)S(1)} collective-permute-done((f16[1008,128]{1,0:T(8,128)(2,1)S(1)}, f16[1008,128]{1,0:T(8,128)(2,1)S(1)}, u32[]{:S(2)}, u32[]{:S(2)}) %collective-permute-start.26) | collective-permute-done | bytes 258080 | tf_op jit(solution)/shard_map/ppermute | solution.py:611
  125.8 0.6 collective-permute-start.27
  126.4 0.1 constant_dynamic-update-slice_fusion.4
  126.5 0.1 constant_dynamic-update-slice_fusion.3
  126.6 0.1 constant_dynamic-update-slice_fusion.2
  126.7 0.1 constant_dynamic-update-slice_fusion.1
  126.7 0.8 collective-permute-done.27
  127.6 0.1 constant_dynamic-update-slice_fusion
  127.6 2.2 %convert_element_type.12.chunks = f32[8,2,504,128]{3,2,1,0:T(8,128)} convert(f16[8,2,504,128]{3,2,1,0:T(8,128)(2,1)S(1)} %constant_dynamic-update-slice_fusion) | non-fusion elementwise | flops 1032192 | bytes 6193152 | tf_op jit(solution)/shard_map/convert_element_type | solution.py:616
  129.8 10.9 %relax.1 = f32[24,192,192]{2,1,0:T(8,128)} custom-call(s32[3]{0:T(128)} %pad_add_fusion.info, f32[8,2,504,128]{3,2,1,0:T(8,128)} %convert_element_type.12.chunks), custom_call_target="tpu_custom_call" | custom-call | tf_op jit(solution)/shard_map/relax/pallas_call | solution.py:547
  (47 shorter events, 0.1 us)
Async XLA Ops:
  4.5 10.1 %collective-permute-start = (bf16[12,80,128]{2,1,0:T(8,128)(2,1)}, bf16[12,80,128]{2,1,0:T(8,128)(2,1)S(1)}, u32[]{:S(2)}, u32[]{:S(2)}) collective-permute-start(bf16[12,80,128]{2,1,0:T(8,128)(2,1)} %get-tuple-element.26), channel_id=1, source_target_pairs={{0,8},{8,0},{16,24},{24,16},{32,40},{40,32},{48,56},{56,48},{1,9},... | collective-permute-start | bytes 737288 | tf_op jit(solution)/shard_map/ppermute | solution.py:589
  5.3 11.3 %collective-permute-start.1 = (bf16[12,80,128]{2,1,0:T(8,128)(2,1)}, bf16[12,80,128]{2,1,0:T(8,128)(2,1)S(1)}, u32[]{:S(2)}, u32[]{:S(2)}) collective-permute-start(bf16[12,80,128]{2,1,0:T(8,128)(2,1)} %get-tuple-element.27), channel_id=1, source_target_pairs={{0,16},{8,24},{16,0},{24,8},{32,48},{40,56},{48,32},{56,40},{1,17}... | collective-permute-start | bytes 737288 | tf_op jit(solution)/shard_map/ppermute | solution.py:589
  6.6 12.7 %collective-permute-start.2 = (bf16[12,80,128]{2,1,0:T(8,128)(2,1)}, bf16[12,80,128]{2,1,0:T(8,128)(2,1)S(1)}, u32[]{:S(2)}, u32[]{:S(2)}) collective-permute-start(bf16[12,80,128]{2,1,0:T(8,128)(2,1)} %get-tuple-element.28), channel_id=1, source_target_pairs={{0,24},{8,16},{16,8},{24,0},{32,56},{40,48},{48,40},{56,32},{1,25}... | collective-permute-start | bytes 737288 | tf_op jit(solution)/shard_map/ppermute | solution.py:589
  7.0 18.9 %collective-permute-start.3 = (bf16[12,80,128]{2,1,0:T(8,128)(2,1)}, bf16[12,80,128]{2,1,0:T(8,128)(2,1)S(1)}, u32[]{:S(2)}, u32[]{:S(2)}) collective-permute-start(bf16[12,80,128]{2,1,0:T(8,128)(2,1)} %get-tuple-element.29), channel_id=1, source_target_pairs={{0,32},{8,40},{16,48},{24,56},{32,0},{40,8},{48,16},{56,24},{1,33}... | collective-permute-start | bytes 737288 | tf_op jit(solution)/shard_map/ppermute | solution.py:589
  11.1 39.0 %collective-permute-start.8 = (f32[1,3,3,96,96]{4,3,2,1,0:T(8,128)S(1)}, f32[1,3,3,96,96]{4,3,2,1,0:T(8,128)S(1)}, u32[]{:S(2)}, u32[]{:S(2)}) collective-permute-start(f32[1,3,3,96,96]{4,3,2,1,0:T(8,128)S(1)} %get-tuple-element.45), channel_id=1, source_target_pairs={{64,1},{65,2},{66,3},{67,4},{68,5},{69,6},{70,7},{1,64},{2,65},{3,... | collective-permute-start | bytes 995336 | tf_op jit(solution)/shard_map/ppermute | solution.py:584
  14.6 27.6 %copy-start = (bf16[12,80,128]{2,1,0:T(8,128)(2,1)}, bf16[12,80,128]{2,1,0:T(8,128)(2,1)S(1)}, u32[]{:S(2)}) copy-start(bf16[12,80,128]{2,1,0:T(8,128)(2,1)S(1)} %collective-permute-done.refs_1_.rest_1_) | copy-start | bytes 737284
  14.6 35.6 %collective-permute-start.7 = (f32[1,3,3,96,96]{4,3,2,1,0:T(8,128)S(1)}, f32[1,3,3,96,96]{4,3,2,1,0:T(8,128)S(1)}, u32[]{:S(2)}, u32[]{:S(2)}) collective-permute-start(f32[1,3,3,96,96]{4,3,2,1,0:T(8,128)S(1)} %get-tuple-element.46), channel_id=1, source_target_pairs={{0,1},{1,2},{2,3},{3,4},{4,5},{5,6},{6,7},{65,64},{66,65},{67,66},... | collective-permute-start | bytes 995336 | tf_op jit(solution)/shard_map/ppermute | solution.py:583
  16.5 25.7 %copy-start.1 = (bf16[12,80,128]{2,1,0:T(8,128)(2,1)}, bf16[12,80,128]{2,1,0:T(8,128)(2,1)S(1)}, u32[]{:S(2)}) copy-start(bf16[12,80,128]{2,1,0:T(8,128)(2,1)S(1)} %collective-permute-done.1.refs_2_.rest_2_) | copy-start | bytes 737284
  16.6 15.2 %collective-permute-start.4 = (bf16[12,80,128]{2,1,0:T(8,128)(2,1)}, bf16[12,80,128]{2,1,0:T(8,128)(2,1)S(1)}, u32[]{:S(2)}, u32[]{:S(2)}) collective-permute-start(bf16[12,80,128]{2,1,0:T(8,128)(2,1)} %get-tuple-element.30), channel_id=1, source_target_pairs={{0,40},{8,32},{16,56},{24,48},{32,8},{40,0},{48,24},{56,16},{1,41}... | collective-permute-start | bytes 737288 | tf_op jit(solution)/shard_map/ppermute | solution.py:589
  19.3 23.0 %copy-start.2 = (bf16[12,80,128]{2,1,0:T(8,128)(2,1)}, bf16[12,80,128]{2,1,0:T(8,128)(2,1)S(1)}, u32[]{:S(2)}) copy-start(bf16[12,80,128]{2,1,0:T(8,128)(2,1)S(1)} %collective-permute-done.2.refs_3_.rest_3_) | copy-start | bytes 737284
  19.3 17.7 %collective-permute-start.5 = (bf16[12,80,128]{2,1,0:T(8,128)(2,1)}, bf16[12,80,128]{2,1,0:T(8,128)(2,1)S(1)}, u32[]{:S(2)}, u32[]{:S(2)}) collective-permute-start(bf16[12,80,128]{2,1,0:T(8,128)(2,1)} %get-tuple-element.31), channel_id=1, source_target_pairs={{0,48},{8,56},{16,32},{24,40},{32,16},{40,24},{48,0},{56,8},{1,49}... | collective-permute-start | bytes 737288 | tf_op jit(solution)/shard_map/ppermute | solution.py:589
  25.9 16.3 %copy-start.3 = (bf16[12,80,128]{2,1,0:T(8,128)(2,1)}, bf16[12,80,128]{2,1,0:T(8,128)(2,1)S(1)}, u32[]{:S(2)}) copy-start(bf16[12,80,128]{2,1,0:T(8,128)(2,1)S(1)} %collective-permute-done.3.refs_4_.rest_4_) | copy-start | bytes 737284
  25.9 16.3 %collective-permute-start.6 = (bf16[12,80,128]{2,1,0:T(8,128)(2,1)}, bf16[12,80,128]{2,1,0:T(8,128)(2,1)S(1)}, u32[]{:S(2)}, u32[]{:S(2)}) collective-permute-start(bf16[12,80,128]{2,1,0:T(8,128)(2,1)} %get-tuple-element.32), channel_id=1, source_target_pairs={{0,56},{8,48},{16,40},{24,32},{32,24},{40,16},{48,8},{56,0},{1,57}... | collective-permute-start | bytes 737288 | tf_op jit(solution)/shard_map/ppermute | solution.py:589
  31.8 10.5 %copy-start.4 = (bf16[12,80,128]{2,1,0:T(8,128)(2,1)}, bf16[12,80,128]{2,1,0:T(8,128)(2,1)S(1)}, u32[]{:S(2)}) copy-start(bf16[12,80,128]{2,1,0:T(8,128)(2,1)S(1)} %collective-permute-done.4.refs_5_.rest_5_) | copy-start | bytes 737284
  37.0 5.3 %copy-start.5 = (bf16[12,80,128]{2,1,0:T(8,128)(2,1)}, bf16[12,80,128]{2,1,0:T(8,128)(2,1)S(1)}, u32[]{:S(2)}) copy-start(bf16[12,80,128]{2,1,0:T(8,128)(2,1)S(1)} %collective-permute-done.5.refs_6_.rest_6_) | copy-start | bytes 737284
  42.2 0.7 copy-start.6
  44.7 18.7 %collective-permute-start.16 = (bf16[8,80,128]{2,1,0:T(8,128)(2,1)}, bf16[8,80,128]{2,1,0:T(8,128)(2,1)S(1)}, u32[]{:S(2)}, u32[]{:S(2)}) collective-permute-start(bf16[8,80,128]{2,1,0:T(8,128)(2,1)} %get-tuple-element.41), channel_id=1, source_target_pairs={{0,64},{1,65},{2,66},{3,67},{4,68},{5,69},{6,70},{7,71},{64,1},{65... | collective-permute-start | bytes 491528 | tf_op jit(solution)/shard_map/ppermute | solution.py:597
  48.2 15.5 %collective-permute-start.17 = (bf16[8,80,128]{2,1,0:T(8,128)(2,1)}, bf16[8,80,128]{2,1,0:T(8,128)(2,1)S(1)}, u32[]{:S(2)}, u32[]{:S(2)}) collective-permute-start(bf16[8,80,128]{2,1,0:T(8,128)(2,1)} %get-tuple-element.42), channel_id=1, source_target_pairs={{64,0},{65,1},{66,2},{67,3},{68,4},{69,5},{70,6},{71,7},{1,64},{2,... | collective-permute-start | bytes 491528 | tf_op jit(solution)/shard_map/ppermute | solution.py:598
  50.2 0.8 copy-start.7
  50.9 0.8 copy-start.8
  60.7 6.0 %collective-permute-start.9 = (bf16[560,128]{1,0:T(8,128)(2,1)}, bf16[560,128]{1,0:T(8,128)(2,1)S(1)}, u32[]{:S(2)}, u32[]{:S(2)}) collective-permute-start(bf16[560,128]{1,0:T(8,128)(2,1)} %get-tuple-element.34), channel_id=1, source_target_pairs={{0,8},{8,0},{16,24},{24,16},{32,40},{40,32},{48,56},{56,48},{1,9},... | collective-permute-start | bytes 430088 | tf_op jit(solution)/shard_map/ppermute | solution.py:589
  61.7 5.4 %collective-permute-start.10 = (bf16[560,128]{1,0:T(8,128)(2,1)}, bf16[560,128]{1,0:T(8,128)(2,1)S(1)}, u32[]{:S(2)}, u32[]{:S(2)}) collective-permute-start(bf16[560,128]{1,0:T(8,128)(2,1)} %get-tuple-element.35), channel_id=1, source_target_pairs={{0,16},{8,24},{16,0},{24,8},{32,48},{40,56},{48,32},{56,40},{1,17}... | collective-permute-start | bytes 430088 | tf_op jit(solution)/shard_map/ppermute | solution.py:589
  61.7 9.6 %collective-permute-start.11 = (bf16[560,128]{1,0:T(8,128)(2,1)}, bf16[560,128]{1,0:T(8,128)(2,1)S(1)}, u32[]{:S(2)}, u32[]{:S(2)}) collective-permute-start(bf16[560,128]{1,0:T(8,128)(2,1)} %get-tuple-element.36), channel_id=1, source_target_pairs={{0,24},{8,16},{16,8},{24,0},{32,56},{40,48},{48,40},{56,32},{1,25}... | collective-permute-start | bytes 430088 | tf_op jit(solution)/shard_map/ppermute | solution.py:589
  63.4 19.1 %copy-start.9 = (bf16[8,80,128]{2,1,0:T(8,128)(2,1)}, bf16[8,80,128]{2,1,0:T(8,128)(2,1)S(1)}, u32[]{:S(2)}) copy-start(bf16[8,80,128]{2,1,0:T(8,128)(2,1)S(1)} %collective-permute-done.16.rest_16_) | copy-start | bytes 491524
  63.4 9.6 %collective-permute-start.12 = (bf16[560,128]{1,0:T(8,128)(2,1)}, bf16[560,128]{1,0:T(8,128)(2,1)S(1)}, u32[]{:S(2)}, u32[]{:S(2)}) collective-permute-start(bf16[560,128]{1,0:T(8,128)(2,1)} %get-tuple-element.37), channel_id=1, source_target_pairs={{0,32},{8,40},{16,48},{24,56},{32,0},{40,8},{48,16},{56,24},{1,33}... | collective-permute-start | bytes 430088 | tf_op jit(solution)/shard_map/ppermute | solution.py:589
  63.8 18.7 %copy-start.10 = (bf16[8,80,128]{2,1,0:T(8,128)(2,1)}, bf16[8,80,128]{2,1,0:T(8,128)(2,1)S(1)}, u32[]{:S(2)}) copy-start(bf16[8,80,128]{2,1,0:T(8,128)(2,1)S(1)} %collective-permute-done.17.rest_17_) | copy-start | bytes 491524
  63.8 12.6 %collective-permute-start.13 = (bf16[560,128]{1,0:T(8,128)(2,1)}, bf16[560,128]{1,0:T(8,128)(2,1)S(1)}, u32[]{:S(2)}, u32[]{:S(2)}) collective-permute-start(bf16[560,128]{1,0:T(8,128)(2,1)} %get-tuple-element.38), channel_id=1, source_target_pairs={{0,40},{8,32},{16,56},{24,48},{32,8},{40,0},{48,24},{56,16},{1,41}... | collective-permute-start | bytes 430088 | tf_op jit(solution)/shard_map/ppermute | solution.py:589
  66.7 15.8 %copy-start.11 = (bf16[560,128]{1,0:T(8,128)(2,1)}, bf16[560,128]{1,0:T(8,128)(2,1)S(1)}, u32[]{:S(2)}) copy-start(bf16[560,128]{1,0:T(8,128)(2,1)S(1)} %collective-permute-done.9.rest_9_) | copy-start | bytes 430084
  66.7 12.7 %collective-permute-start.14 = (bf16[560,128]{1,0:T(8,128)(2,1)}, bf16[560,128]{1,0:T(8,128)(2,1)S(1)}, u32[]{:S(2)}, u32[]{:S(2)}) collective-permute-start(bf16[560,128]{1,0:T(8,128)(2,1)} %get-tuple-element.39), channel_id=1, source_target_pairs={{0,48},{8,56},{16,32},{24,40},{32,16},{40,24},{48,0},{56,8},{1,49}... | collective-permute-start | bytes 430088 | tf_op jit(solution)/shard_map/ppermute | solution.py:589
  67.1 15.4 %copy-start.12 = (bf16[560,128]{1,0:T(8,128)(2,1)}, bf16[560,128]{1,0:T(8,128)(2,1)S(1)}, u32[]{:S(2)}) copy-start(bf16[560,128]{1,0:T(8,128)(2,1)S(1)} %collective-permute-done.10.rest_10_) | copy-start | bytes 430084
  67.1 15.3 %collective-permute-start.15 = (bf16[560,128]{1,0:T(8,128)(2,1)}, bf16[560,128]{1,0:T(8,128)(2,1)S(1)}, u32[]{:S(2)}, u32[]{:S(2)}) collective-permute-start(bf16[560,128]{1,0:T(8,128)(2,1)} %get-tuple-element.40), channel_id=1, source_target_pairs={{0,56},{8,48},{16,40},{24,32},{32,24},{40,16},{48,8},{56,0},{1,57}... | collective-permute-start | bytes 430088 | tf_op jit(solution)/shard_map/ppermute | solution.py:589
  71.3 11.2 %copy-start.13 = (bf16[560,128]{1,0:T(8,128)(2,1)}, bf16[560,128]{1,0:T(8,128)(2,1)S(1)}, u32[]{:S(2)}) copy-start(bf16[560,128]{1,0:T(8,128)(2,1)S(1)} %collective-permute-done.11.rest_11_) | copy-start | bytes 430084
  73.0 9.5 %copy-start.14 = (bf16[560,128]{1,0:T(8,128)(2,1)}, bf16[560,128]{1,0:T(8,128)(2,1)S(1)}, u32[]{:S(2)}) copy-start(bf16[560,128]{1,0:T(8,128)(2,1)S(1)} %collective-permute-done.12.rest_12_) | copy-start | bytes 430084
  76.3 6.2 %copy-start.15 = (bf16[560,128]{1,0:T(8,128)(2,1)}, bf16[560,128]{1,0:T(8,128)(2,1)S(1)}, u32[]{:S(2)}) copy-start(bf16[560,128]{1,0:T(8,128)(2,1)S(1)} %collective-permute-done.13.rest_13_) | copy-start | bytes 430084
  79.4 3.1 %copy-start.16 = (bf16[560,128]{1,0:T(8,128)(2,1)}, bf16[560,128]{1,0:T(8,128)(2,1)S(1)}, u32[]{:S(2)}) copy-start(bf16[560,128]{1,0:T(8,128)(2,1)S(1)} %collective-permute-done.14.rest_14_) | copy-start | bytes 430084
  82.5 0.6 copy-start.17
  93.6 14.2 %collective-permute-start.19 = (f16[432,128]{1,0:T(8,128)(2,1)S(1)}, f16[432,128]{1,0:T(8,128)(2,1)S(1)}, u32[]{:S(2)}, u32[]{:S(2)}) collective-permute-start(f16[432,128]{1,0:T(8,128)(2,1)S(1)} %convert_element_type.10), channel_id=1, source_target_pairs={{0,64},{64,0},{1,65},{65,1},{2,66},{66,2},{3,67},{67,3},{4,68},{68... | collective-permute-start | bytes 331784 | tf_op jit(solution)/shard_map/ppermute | solution.py:604
  95.2 8.0 %collective-permute-start.20 = (f16[72,128]{1,0:T(8,128)(2,1)S(1)}, f16[72,128]{1,0:T(8,128)(2,1)S(1)}, u32[]{:S(2)}, u32[]{:S(2)}) collective-permute-start(f16[72,128]{1,0:T(8,128)(2,1)S(1)} %convert_element_type.11), channel_id=1, source_target_pairs={{1,0},{2,1},{3,2},{4,3},{5,4},{6,5},{7,6},{64,65},{65,66},{66,67},... | collective-permute-start | bytes 55304 | tf_op jit(solution)/shard_map/ppermute | solution.py:606
  101.2 6.6 %collective-permute-start.18 = (f16[72,128]{1,0:T(8,128)(2,1)S(1)}, f16[72,128]{1,0:T(8,128)(2,1)S(1)}, u32[]{:S(2)}, u32[]{:S(2)}) collective-permute-start(f16[72,128]{1,0:T(8,128)(2,1)S(1)} %convert_element_type.11), channel_id=1, source_target_pairs={{64,1},{65,2},{66,3},{67,4},{68,5},{69,6},{70,7},{1,64},{2,65},{3,... | collective-permute-start | bytes 55304 | tf_op jit(solution)/shard_map/ppermute | solution.py:605
  107.9 6.6 %collective-permute-start.22 = (f16[1008,128]{1,0:T(8,128)(2,1)S(1)}, f16[1008,128]{1,0:T(8,128)(2,1)S(1)}, u32[]{:S(2)}, u32[]{:S(2)}) collective-permute-start(f16[1008,128]{1,0:T(8,128)(2,1)S(1)} %pad_maximum_fusion), channel_id=1, source_target_pairs={{0,16},{8,24},{16,0},{24,8},{32,48},{40,56},{48,32},{56,40},{1,17}... | collective-permute-start | bytes 774152 | tf_op jit(solution)/shard_map/ppermute | solution.py:611
  108.0 11.4 %collective-permute-start.24 = (f16[1008,128]{1,0:T(8,128)(2,1)S(1)}, f16[1008,128]{1,0:T(8,128)(2,1)S(1)}, u32[]{:S(2)}, u32[]{:S(2)}) collective-permute-start(f16[1008,128]{1,0:T(8,128)(2,1)S(1)} %pad_maximum_fusion), channel_id=1, source_target_pairs={{0,32},{8,40},{16,48},{24,56},{32,0},{40,8},{48,16},{56,24},{1,33}... | collective-permute-start | bytes 774152 | tf_op jit(solution)/shard_map/ppermute | solution.py:611
  109.6 12.8 %collective-permute-start.21 = (f16[1008,128]{1,0:T(8,128)(2,1)S(1)}, f16[1008,128]{1,0:T(8,128)(2,1)S(1)}, u32[]{:S(2)}, u32[]{:S(2)}) collective-permute-start(f16[1008,128]{1,0:T(8,128)(2,1)S(1)} %pad_maximum_fusion), channel_id=1, source_target_pairs={{0,8},{8,0},{16,24},{24,16},{32,40},{40,32},{48,56},{56,48},{1,9},... | collective-permute-start | bytes 774152 | tf_op jit(solution)/shard_map/ppermute | solution.py:615
  112.0 13.8 %collective-permute-start.26 = (f16[1008,128]{1,0:T(8,128)(2,1)S(1)}, f16[1008,128]{1,0:T(8,128)(2,1)S(1)}, u32[]{:S(2)}, u32[]{:S(2)}) collective-permute-start(f16[1008,128]{1,0:T(8,128)(2,1)S(1)} %pad_maximum_fusion), channel_id=1, source_target_pairs={{0,48},{8,56},{16,32},{24,40},{32,16},{40,24},{48,0},{56,8},{1,49}... | collective-permute-start | bytes 774152 | tf_op jit(solution)/shard_map/ppermute | solution.py:611
  114.5 11.9 %collective-permute-start.23 = (f16[1008,128]{1,0:T(8,128)(2,1)S(1)}, f16[1008,128]{1,0:T(8,128)(2,1)S(1)}, u32[]{:S(2)}, u32[]{:S(2)}) collective-permute-start(f16[1008,128]{1,0:T(8,128)(2,1)S(1)} %collective-permute-done.22), channel_id=1, source_target_pairs={{0,8},{8,0},{16,24},{24,16},{32,40},{40,32},{48,56},{56,48},{1,9},... | collective-permute-start | bytes 774152 | tf_op jit(solution)/shard_map/ppermute | solution.py:615
  119.5 7.1 %collective-permute-start.25 = (f16[1008,128]{1,0:T(8,128)(2,1)S(1)}, f16[1008,128]{1,0:T(8,128)(2,1)S(1)}, u32[]{:S(2)}, u32[]{:S(2)}) collective-permute-start(f16[1008,128]{1,0:T(8,128)(2,1)S(1)} %collective-permute-done.24), channel_id=1, source_target_pairs={{0,8},{8,0},{16,24},{24,16},{32,40},{40,32},{48,56},{56,48},{1,9},... | collective-permute-start | bytes 774152 | tf_op jit(solution)/shard_map/ppermute | solution.py:615
  125.8 1.8 %collective-permute-start.27 = (f16[1008,128]{1,0:T(8,128)(2,1)S(1)}, f16[1008,128]{1,0:T(8,128)(2,1)S(1)}, u32[]{:S(2)}, u32[]{:S(2)}) collective-permute-start(f16[1008,128]{1,0:T(8,128)(2,1)S(1)} %collective-permute-done.26), channel_id=1, source_target_pairs={{0,8},{8,0},{16,24},{24,16},{32,40},{40,32},{48,56},{56,48},{1,9},... | collective-permute-start | bytes 774152 | tf_op jit(solution)/shard_map/ppermute | solution.py:615

commit v4 on v1

--- a/solution.py
+++ b/solution.py
@@ -16,6 +16,7 @@
 VR = CZ * CW
 VROWS = 5 * VR
 PROWS = 80
+SPREAD = (2, 1, 3)
 SCALE = 128.0
 
 
@@ -64,8 +65,8 @@
 
 
 def pack_kernel(info, images, *rest):
-    outs = rest[:8]
-    held, stage, sems, gone = rest[8:]
+    outs = rest[:4]
+    held, stage, sems, gone = rest[4:]
     level, me = info[0], info[1]
     loads = []
     for index, (first, count) in enumerate(GROUPS):
@@ -89,10 +90,10 @@
             return carry
 
         lax.fori_loop(first, first + count, step, 0)
-        for k, out in enumerate(outs):
+        for k in range(8):
             rows = pl.ds(first, count)
             copy = pltpu.make_async_copy(
-                stage.at[me ^ k, rows], out.at[rows], gone.at[8 * index + k]
+                stage.at[me ^ k, rows], outs[k // 2].at[k % 2, rows], gone.at[8 * index + k]
             )
             copy.start()
             sent.append(copy)
@@ -106,8 +107,8 @@
         pack_kernel,
         grid=(),
         in_specs=[pl.BlockSpec(memory_space=pltpu.SMEM), hbm],
-        out_specs=[hbm] * 8,
-        out_shape=[jax.ShapeDtypeStruct((HZ, PROWS, 128), BF16)] * 8,
+        out_specs=[hbm] * 4,
+        out_shape=[jax.ShapeDtypeStruct((2, HZ, PROWS, 128), BF16)] * 4,
         scratch_shapes=[
             pltpu.VMEM((2, HZ, 192, 192), BF16),
             pltpu.VMEM((8, HZ, PROWS, 128), BF16),
@@ -119,8 +120,8 @@
 
 
 def blur_kernel(info, momenta, halo, other, *rest):
-    outs = rest[:8]
-    held, stage, tall, wide, third, piece, sems, gone = rest[8:]
+    outs = rest[:4]
+    held, stage, tall, wide, third, piece, sems, gone = rest[4:]
     level, me = info[0], info[1]
     half = info[2] * 2 + level
     own = pltpu.make_async_copy(
@@ -178,7 +179,8 @@
                 piece[CW * r : CW * (r + 1)] = wide[r, start : start + CW]
             stage[peer, VR * block : VR * (block + 1)] = piece[...].astype(BF16)
     sent = [
-        pltpu.make_async_copy(stage.at[me ^ k], out, gone.at[k]) for k, out in enumerate(outs)
+        pltpu.make_async_copy(stage.at[me ^ k], outs[k // 2].at[k % 2], gone.at[k])
+        for k in range(8)
     ]
     for copy in sent:
         copy.start()
@@ -197,8 +199,8 @@
             pl.BlockSpec(memory_space=pl.ANY),
             pl.BlockSpec(memory_space=pl.ANY),
         ],
-        out_specs=[pl.BlockSpec(memory_space=pl.ANY)] * 8,
-        out_shape=[jax.ShapeDtypeStruct((rows, 128), BF16)] * 8,
+        out_specs=[pl.BlockSpec(memory_space=pl.ANY)] * 4,
+        out_shape=[jax.ShapeDtypeStruct((2, rows, 128), BF16)] * 4,
         scratch_shapes=[
             pltpu.VMEM((2, 12, 3, 96, 96), F32),
             pltpu.VMEM((8, rows, 128), BF16),
@@ -218,8 +220,8 @@
     low, high, sems, gone = refs[10:]
     copies = []
     for k, plane in enumerate(planes):
-        copies.append(pltpu.make_async_copy(plane.at[0], low.at[k], sems.at[k]))
-        copies.append(pltpu.make_async_copy(plane.at[HZ - 1], high.at[k], sems.at[8 + k]))
+        copies.append(pltpu.make_async_copy(plane.at[k % 2, 0], low.at[k], sems.at[k]))
+        copies.append(pltpu.make_async_copy(plane.at[k % 2, HZ - 1], high.at[k], sems.at[8 + k]))
     for copy in copies:
         copy.start()
     for copy in copies:
@@ -264,9 +266,9 @@
     ]
     for k in range(8):
         copies.append(
-            pltpu.make_async_copy(planes[k], image.at[k, 1 : HZ + 1], sems.at[k])
+            pltpu.make_async_copy(planes[k].at[k % 2], image.at[k, 1 : HZ + 1], sems.at[k])
         )
-        copies.append(pltpu.make_async_copy(fields[k], field.at[k], sems.at[8 + k]))
+        copies.append(pltpu.make_async_copy(fields[k].at[k % 2], field.at[k], sems.at[8 + k]))
     for copy in copies:
         copy.start()
     acc[...] = jnp.zeros_like(acc)
@@ -418,10 +420,9 @@
     tail = HZ * 3 // 2
     for peer in range(8):
         rows = slice(8 + CY * peer, 8 + CY * (peer + 1))
-        slots = [(half ^ level) * 8 + (peer ^ me) for half in range(2)]
 
         def block(half, index):
-            return chunks[slots[half], CY * index : CY * (index + 1)]
+            return chunks[half ^ level, peer ^ me, CY * index : CY * (index + 1)]
 
         for half in range(2):
             for z in range(HZ):
@@ -473,9 +474,8 @@
             around = held[z - 1, start : start + count] + held[z + 1, start : start + count]
             around += held[z, start - 1 : start - 1 + count] + held[z, start + 1 : start + 1 + count]
             around += sums[b, start - 8 : start - 8 + count]
-            done.append(
-                (0.1 * scale) * held[z, start : start + count] + (0.15 * scale) * around
-            )
+            value = around + (2.0 / 3.0) * held[z, start : start + count]
+            done.append(value if scale is None else scale * value)
         return done
 
     def sweep(planes, store, scale, after):
@@ -500,7 +500,7 @@
         flat2[index + 16, start : start + count] = done[1]
         pair2[index, start : start + count] = done[2]
 
-    sweep((flat, pair), first, 1.0, lambda index: None)
+    sweep((flat, pair), first, None, lambda index: None)
     whole = lax.broadcasted_iota(jnp.int32, (size, 128), 1)
 
     @pl.when(zone == 0)
@@ -534,7 +534,7 @@
         def _():
             emit(index + 11).start()
 
-    sweep((flat2, pair2), second, 1.0 / SCALE, depart)
+    sweep((flat2, pair2), second, 0.15 * 0.15 / SCALE, depart)
 
     def finish(z, carry):
         emit(z).wait()
@@ -586,9 +586,14 @@
 
     def spread(parts):
         arrived = {0: parts[0]}
-        for k in (3, 7, 5, 2, 6, 4, 1):
-            arrived[k] = lax.ppermute(parts[k], "subj", [(i, i ^ k) for i in range(8)])
-        return [arrived[k] for k in range(8)]
+        for step in SPREAD:
+            perm = [(i, i ^ (2 * step)) for i in range(8)]
+            arrived[step] = lax.ppermute(parts[step], "subj", perm)
+        result = []
+        for step in range(4):
+            other = lax.ppermute(arrived[step], "subj", [(i, i ^ 1) for i in range(8)])
+            result += [arrived[step], other]
+        return result
 
     packed = pack_images(info, images)
     planes = spread(packed)
@@ -600,17 +605,18 @@
     chunk, edge = warp(info, assign, planes, fields, below, above)
     edge = lax.ppermute(edge.astype(jnp.float16), nearest, cross)
     chunk = jnp.concatenate([chunk.astype(jnp.float16), edge], axis=0)
-    mine = {(0, 0): chunk}
-    for far, step in ((0, 1), (0, 3), (1, 0), (0, 2), (1, 1), (1, 3), (1, 2)):
-        perm = [(8 * a + i, 8 * (a ^ far) + (i ^ (2 * step))) for a in range(2) for i in range(8)]
-        mine[far, step] = lax.ppermute(chunk, ("level", "subj"), perm)
     gathered = []
     for far in range(2):
         for step in range(4):
-            part = mine[far, step]
+            part = chunk
+            if far or step:
+                perm = [
+                    (8 * a + i, 8 * (a ^ far) + (i ^ (2 * step))) for a in range(2) for i in range(8)
+                ]
+                part = lax.ppermute(chunk, ("level", "subj"), perm)
             gathered += [part, lax.ppermute(part, "subj", [(i, i ^ 1) for i in range(8)])]
     chunks = jnp.stack(gathered).astype(F32)
-    return relax(info, chunks)
+    return relax(info, chunks.reshape(2, 8, -1, 128))
 
 
 def solution(mesh):

time: 137 us -> 134 us (0.978)
  the two profiles are of different devices: /device:TPU:96 before, /device:TPU:7 now
where the time goes in v4:
time: 134 us; the launch traced here: 133 us
  starting transfers between devices  59 us (44%)
  Pallas kernels  35.2 us (26%)
  waiting for transfers between devices  29.6 us (22%)
  other arithmetic  4.66 us (3%)
  local copies, waits for them, and re-layouts  4.54 us (3%)
    ppermute x7, starting transfers between devices, update(): part = lax.ppermute(chunk, ('level', 'subj'), perm)  13.3 us
    ppermute x8, starting transfers between devices, spread(): other = lax.ppermute(arrived[step], 'subj', [(i, i ^ 1) for i in range(8)])  12.1 us
    pallas_call x1, Pallas kernels, relax(): pl.pallas_call(relax_kernel, grid=(), in_specs=[pl.BlockSpec(memory_space...  10.9 us
    pallas_call x1, Pallas kernels, warp(): pl.pallas_call(warp_kernel, grid=(), in_specs=[smem, smem, vmem, vmem, vm...  9.57 us
    pallas_call x1, Pallas kernels, blur(): pl.pallas_call(blur_kernel, grid=(), in_specs=[pl.BlockSpec(memory_space=...  9.03 us
    ppermute x6, starting transfers between devices, spread(): arrived[step] = lax.ppermute(parts[step], 'subj', perm)  8.78 us
    ppermute x6, waiting for transfers between devices, spread(): arrived[step] = lax.ppermute(parts[step], 'subj', perm)  8.55 us
    ppermute x8, starting transfers between devices, update(): lax.ppermute(part, 'subj', [(i, i ^ 1) for i in range(8)])  6.04 us
  transfers between devices with their start and end apart: 34, of which 10 were waited for; matrix products, arithmetic and copies ran while one was open for 2% of the time, Pallas kernels for 11%

profile of v4, /device:TPU:7, one launch (start us, length us, event | category | flops | bytes accessed | tf_op | source)
XLA Modules:
  0.0 133.5 jit_solution(3688811356655762265)
XLA Ops:
  0.0 1.2 constant_dynamic-slice_fusion
  1.2 3.8 %collective-permute-start.8 = (f32[1,3,3,96,96]{4,3,2,1,0:T(8,128)S(1)}, f32[1,3,3,96,96]{4,3,2,1,0:T(8,128)S(1)}, u32[]{:S(2)}, u32[]{:S(2)}) collective-permute-start(f32[1,3,3,96,96]{4,3,2,1,0:T(8,128)S(1)} %get-tuple-element.29), channel_id=1, source_target_pairs={{64,1},{65,2},{66,3},{67,4},{68,5},{69,6},{70,7},{1,64},{2,65},{3,... | collective-permute-start | bytes 995336 | tf_op jit(solution)/shard_map/ppermute | solution.py:585
  5.0 0.7 pad_add_fusion.info
  5.7 3.9 %pack_images.1 = (bf16[2,12,80,128]{3,2,1,0:T(8,128)(2,1)}, bf16[2,12,80,128]{3,2,1,0:T(8,128)(2,1)}, bf16[2,12,80,128]{3,2,1,0:T(8,128)(2,1)}, bf16[2,12,80,128]{3,2,1,0:T(8,128)(2,1)}) custom-call(s32[3]{0:T(128)} %pad_add_fusion.info, bf16[2,24,192,192]{3,2,1,0:T(8,128)(2,1)} %images.1), custom_call_target="tpu_custom_call" | custom-call | tf_op jit(solution)/shard_map/pack_images/pallas_call | solution.py:106
  9.6 1.4 %collective-permute-start.1 = (bf16[2,12,80,128]{3,2,1,0:T(8,128)(2,1)}, bf16[2,12,80,128]{3,2,1,0:T(8,128)(2,1)S(1)}, u32[]{:S(2)}, u32[]{:S(2)}) collective-permute-start(bf16[2,12,80,128]{3,2,1,0:T(8,128)(2,1)} %get-tuple-element.18), channel_id=1, source_target_pairs={{0,16},{8,24},{16,0},{24,8},{32,48},{40,56},{48,32},{56,40},{1,17}... | collective-permute-start | bytes 1474568 | tf_op jit(solution)/shard_map/ppermute | solution.py:591
  10.9 2.6 %collective-permute-start.3 = (bf16[2,12,80,128]{3,2,1,0:T(8,128)(2,1)}, bf16[2,12,80,128]{3,2,1,0:T(8,128)(2,1)S(1)}, u32[]{:S(2)}, u32[]{:S(2)}) collective-permute-start(bf16[2,12,80,128]{3,2,1,0:T(8,128)(2,1)} %get-tuple-element.19), channel_id=1, source_target_pairs={{0,32},{8,40},{16,48},{24,56},{32,0},{40,8},{48,16},{56,24},{1,33}... | collective-permute-start | bytes 1474568 | tf_op jit(solution)/shard_map/ppermute | solution.py:591
  13.6 5.5 %collective-permute-start.7 = (f32[1,3,3,96,96]{4,3,2,1,0:T(8,128)S(1)}, f32[1,3,3,96,96]{4,3,2,1,0:T(8,128)S(1)}, u32[]{:S(2)}, u32[]{:S(2)}) collective-permute-start(f32[1,3,3,96,96]{4,3,2,1,0:T(8,128)S(1)} %get-tuple-element.30), channel_id=1, source_target_pairs={{0,1},{1,2},{2,3},{3,4},{4,5},{5,6},{6,7},{65,64},{66,65},{67,66},... | collective-permute-start | bytes 995336 | tf_op jit(solution)/shard_map/ppermute | solution.py:584
  19.1 2.1 %collective-permute-start = (bf16[2,12,80,128]{3,2,1,0:T(8,128)(2,1)}, bf16[2,12,80,128]{3,2,1,0:T(8,128)(2,1)S(1)}, u32[]{:S(2)}, u32[]{:S(2)}) collective-permute-start(bf16[2,12,80,128]{3,2,1,0:T(8,128)(2,1)} %get-tuple-element.17.refs_0_.rest_0_), channel_id=1, source_target_pairs={{0,8},{8,0},{16,24},{24,16},{32,40},{40,32},{48,56},{56,48},{1,9},... | collective-permute-start | bytes 1474568 | tf_op jit(solution)/shard_map/ppermute | solution.py:594
  21.2 5.7 %collective-permute-done.7.halo = f32[1,3,3,96,96]{4,3,2,1,0:T(8,128)S(1)} collective-permute-done((f32[1,3,3,96,96]{4,3,2,1,0:T(8,128)S(1)}, f32[1,3,3,96,96]{4,3,2,1,0:T(8,128)S(1)}, u32[]{:S(2)}, u32[]{:S(2)}) %collective-permute-start.7) | collective-permute-done | bytes 331808 | tf_op jit(solution)/shard_map/ppermute | solution.py:584
  26.9 0.8 copy-done.8
  27.6 9.0 %blur_momenta.1 = (bf16[2,560,128]{2,1,0:T(8,128)(2,1)}, bf16[2,560,128]{2,1,0:T(8,128)(2,1)}, bf16[2,560,128]{2,1,0:T(8,128)(2,1)}, bf16[2,560,128]{2,1,0:T(8,128)(2,1)}) custom-call(s32[3]{0:T(128)} %pad_add_fusion.info, f32[2,12,3,96,96]{4,3,2,1,0:T(8,128)} %momenta.1, f32[1,3,3,96,96]{4,3,2,1,0:T(8,128)} %copy-done.8, f32[1,3,3,96,96]{4,3,2,1,0:T(8,128)} %copy-done.7), custom_call_target="tpu_custom_call" | custom-call | tf_op jit(solution)/shard_map/blur_momenta/pallas_call | solution.py:193
  36.7 0.1 collective-permute-start.10
  36.8 0.0 collective-permute-done.1.refs_2_.rest_2_
  36.8 2.9 %collective-permute-start.2 = (bf16[2,12,80,128]{3,2,1,0:T(8,128)(2,1)S(1)}, bf16[2,12,80,128]{3,2,1,0:T(8,128)(2,1)S(1)}, u32[]{:S(2)}, u32[]{:S(2)}) collective-permute-start(bf16[2,12,80,128]{3,2,1,0:T(8,128)(2,1)S(1)} %collective-permute-done.1.refs_2_.rest_2_), channel_id=1, source_target_pairs={{0,8},{8,0},{16,24},{24,16},{32,40},{40,32},{48,56},{56,48},{1,9},... | collective-permute-start | bytes 1474568 | tf_op jit(solution)/shard_map/ppermute | solution.py:594
  39.7 0.1 collective-permute-start.4
  39.8 0.0 collective-permute-done.5.refs_6_.rest_6_
  39.8 3.8 %collective-permute-start.12 = (bf16[2,560,128]{2,1,0:T(8,128)(2,1)}, bf16[2,560,128]{2,1,0:T(8,128)(2,1)}, u32[]{:S(2)}, u32[]{:S(2)}) collective-permute-start(bf16[2,560,128]{2,1,0:T(8,128)(2,1)} %get-tuple-element.23), channel_id=1, source_target_pairs={{0,32},{8,40},{16,48},{24,56},{32,0},{40,8},{48,16},{56,24},{1,33}... | collective-permute-start | bytes 860168 | tf_op jit(solution)/shard_map/ppermute | solution.py:591
  43.6 0.0 collective-permute-done.refs_1_.rest_1_
  43.6 0.7 collective-permute-start.6
  44.3 0.9 collective-permute-start.14
  45.2 5.8 %collective-permute-done.12.rest_12_ = bf16[2,560,128]{2,1,0:T(8,128)(2,1)} collective-permute-done((bf16[2,560,128]{2,1,0:T(8,128)(2,1)}, bf16[2,560,128]{2,1,0:T(8,128)(2,1)}, u32[]{:S(2)}, u32[]{:S(2)}) %collective-permute-start.12) | collective-permute-done | bytes 286752 | tf_op jit(solution)/shard_map/ppermute | solution.py:591
  51.0 3.9 %collective-permute-start.9 = (bf16[2,560,128]{2,1,0:T(8,128)(2,1)}, bf16[2,560,128]{2,1,0:T(8,128)(2,1)}, u32[]{:S(2)}, u32[]{:S(2)}) collective-permute-start(bf16[2,560,128]{2,1,0:T(8,128)(2,1)} %get-tuple-element.21.rest_8_), channel_id=1, source_target_pairs={{0,8},{8,0},{16,24},{24,16},{32,40},{40,32},{48,56},{56,48},{1,9},... | collective-permute-start | bytes 860168 | tf_op jit(solution)/shard_map/ppermute | solution.py:594
  54.9 2.7 %collective-permute-done.14.rest_14_ = bf16[2,560,128]{2,1,0:T(8,128)(2,1)} collective-permute-done((bf16[2,560,128]{2,1,0:T(8,128)(2,1)}, bf16[2,560,128]{2,1,0:T(8,128)(2,1)}, u32[]{:S(2)}, u32[]{:S(2)}) %collective-permute-start.14) | collective-permute-done | bytes 286752 | tf_op jit(solution)/shard_map/ppermute | solution.py:591
  57.6 1.9 %collective-permute-start.11 = (bf16[2,560,128]{2,1,0:T(8,128)(2,1)}, bf16[2,560,128]{2,1,0:T(8,128)(2,1)}, u32[]{:S(2)}, u32[]{:S(2)}) collective-permute-start(bf16[2,560,128]{2,1,0:T(8,128)(2,1)} %collective-permute-done.10.rest_10_), channel_id=1, source_target_pairs={{0,8},{8,0},{16,24},{24,16},{32,40},{40,32},{48,56},{56,48},{1,9},... | collective-permute-start | bytes 860168 | tf_op jit(solution)/shard_map/ppermute | solution.py:594
  59.5 0.0 collective-permute-done.2.refs_3_.rest_3_
  59.5 0.1 collective-permute-start.13
  59.6 0.4 collective-permute-start.15
  60.0 0.0 collective-permute-done.6.refs_7_.rest_7_
  60.1 0.2 copy-done.4
  60.3 0.2 copy-done.5
  60.5 0.8 copy-done.6
  61.3 1.8 %cut_edges.1 = (bf16[8,80,128]{2,1,0:T(8,128)(2,1)}, bf16[8,80,128]{2,1,0:T(8,128)(2,1)}) custom-call(bf16[2,12,80,128]{3,2,1,0:T(8,128)(2,1)} %get-tuple-element.17.refs_0_.rest_0_, bf16[2,12,80,128]{3,2,1,0:T(8,128)(2,1)} %copy-done.3, bf16[2,12,80,128]{3,2,1,0:T(8,128)(2,1)} %copy-done, bf16[2,12,80,128]{3,2,1,0:T(8,128)(2,1)} %copy-done.4, ...), custom_call_target="tpu_custom_call" | custom-call | tf_op jit(solution)/shard_map/cut_edges/pallas_call | solution.py:242
  63.1 5.4 %collective-permute-start.16 = (bf16[8,80,128]{2,1,0:T(8,128)(2,1)}, bf16[8,80,128]{2,1,0:T(8,128)(2,1)S(1)}, u32[]{:S(2)}, u32[]{:S(2)}) collective-permute-start(bf16[8,80,128]{2,1,0:T(8,128)(2,1)} %get-tuple-element.25), channel_id=1, source_target_pairs={{0,64},{1,65},{2,66},{3,67},{4,68},{5,69},{6,70},{7,71},{64,1},{65... | collective-permute-start | bytes 491528 | tf_op jit(solution)/shard_map/ppermute | solution.py:603
  68.5 1.9 %collective-permute-start.17 = (bf16[8,80,128]{2,1,0:T(8,128)(2,1)}, bf16[8,80,128]{2,1,0:T(8,128)(2,1)S(1)}, u32[]{:S(2)}, u32[]{:S(2)}) collective-permute-start(bf16[8,80,128]{2,1,0:T(8,128)(2,1)} %get-tuple-element.26), channel_id=1, source_target_pairs={{64,0},{65,1},{66,2},{67,3},{68,4},{69,5},{70,6},{71,7},{1,64},{2,... | collective-permute-start | bytes 491528 | tf_op jit(solution)/shard_map/ppermute | solution.py:604
  70.4 0.0 collective-permute-done.13.rest_13_
  70.4 0.0 collective-permute-done.15.rest_15_
  70.4 1.5 %collective-permute-done.16.rest_16_ = bf16[8,80,128]{2,1,0:T(8,128)(2,1)S(1)} collective-permute-done((bf16[8,80,128]{2,1,0:T(8,128)(2,1)}, bf16[8,80,128]{2,1,0:T(8,128)(2,1)S(1)}, u32[]{:S(2)}, u32[]{:S(2)}) %collective-permute-start.16) | collective-permute-done | bytes 163872 | tf_op jit(solution)/shard_map/ppermute | solution.py:603
  72.0 4.6 %collective-permute-done.17.rest_17_ = bf16[8,80,128]{2,1,0:T(8,128)(2,1)S(1)} collective-permute-done((bf16[8,80,128]{2,1,0:T(8,128)(2,1)}, bf16[8,80,128]{2,1,0:T(8,128)(2,1)S(1)}, u32[]{:S(2)}, u32[]{:S(2)}) %collective-permute-start.17) | collective-permute-done | bytes 163872 | tf_op jit(solution)/shard_map/ppermute | solution.py:604
  76.6 0.7 copy-done.10
  77.2 9.6 %warp_sum.1 = (f32[432,128]{1,0:T(8,128)}, f32[72,128]{1,0:T(8,128)}) custom-call(s32[3]{0:T(128)} %pad_add_fusion.info, s32[16]{0:T(128)} %assign.1, bf16[288,112]{1,0:T(8,128)(2,1)} %constant.27.clone.zy, bf16[256,256]{1,0:T(8,128)(2,1)} %constant.28.clone.x0, bf16[256,256]{1,0:T(8,128)(2,1)} %constant.29.clone.x1, ...), custom_call_target="tpu_custom_call" | custom-call | tf_op jit(solution)/shard_map/warp_sum/pallas_call | solution.py:389
  86.8 0.8 convert_element_type.14
  87.6 2.2 %collective-permute-start.18 = (f16[72,128]{1,0:T(8,128)(2,1)S(1)}, f16[72,128]{1,0:T(8,128)(2,1)S(1)}, u32[]{:S(2)}, u32[]{:S(2)}) collective-permute-start(f16[72,128]{1,0:T(8,128)(2,1)S(1)} %convert_element_type.14), channel_id=1, source_target_pairs={{64,1},{65,2},{66,3},{67,4},{68,5},{69,6},{70,7},{1,64},{2,65},{3,... | collective-permute-start | bytes 55304 | tf_op jit(solution)/shard_map/ppermute | solution.py:606
  89.8 1.0 convert_element_type.13
  90.8 2.2 %collective-permute-done.18 = f16[72,128]{1,0:T(8,128)(2,1)S(1)} collective-permute-done((f16[72,128]{1,0:T(8,128)(2,1)S(1)}, f16[72,128]{1,0:T(8,128)(2,1)S(1)}, u32[]{:S(2)}, u32[]{:S(2)}) %collective-permute-start.18) | collective-permute-done | bytes 18464 | tf_op jit(solution)/shard_map/ppermute | solution.py:606
  93.0 0.1 collective-permute-start.20
  93.1 2.4 %collective-permute-start.19 = (f16[504,128]{1,0:T(8,128)(2,1)S(1)}, f16[504,128]{1,0:T(8,128)(2,1)S(1)}, u32[]{:S(2)}, u32[]{:S(2)}) collective-permute-start(f16[504,128]{1,0:T(8,128)(2,1)S(1)} %pad_maximum_fusion), channel_id=1, source_target_pairs={{0,8},{8,0},{16,24},{24,16},{32,40},{40,32},{48,56},{56,48},{1,9},... | collective-permute-start | bytes 387080 | tf_op jit(solution)/shard_map/ppermute | solution.py:617
  95.5 7.1 %collective-permute-start.30 = (f16[504,128]{1,0:T(8,128)(2,1)S(1)}, f16[504,128]{1,0:T(8,128)(2,1)S(1)}, u32[]{:S(2)}, u32[]{:S(2)}) collective-permute-start(f16[504,128]{1,0:T(8,128)(2,1)S(1)} %pad_maximum_fusion), channel_id=1, source_target_pairs={{0,96},{8,104},{16,112},{24,120},{32,64},{40,72},{48,80},{56,88},{... | collective-permute-start | bytes 387080 | tf_op jit(solution)/shard_map/ppermute | solution.py:616
  102.7 0.9 collective-permute-start.26
  103.6 1.0 collective-permute-start.24
  104.6 1.2 collective-permute-start.21
  105.9 0.9 collective-permute-done.21
  106.8 2.5 %collective-permute-start.22 = (f16[504,128]{1,0:T(8,128)(2,1)S(1)}, f16[504,128]{1,0:T(8,128)(2,1)S(1)}, u32[]{:S(2)}, u32[]{:S(2)}) collective-permute-start(f16[504,128]{1,0:T(8,128)(2,1)S(1)} %pad_maximum_fusion), channel_id=1, source_target_pairs={{0,32},{8,40},{16,48},{24,56},{32,0},{40,8},{48,16},{56,24},{64,96... | collective-permute-start | bytes 387080 | tf_op jit(solution)/shard_map/ppermute | solution.py:616
  109.4 1.6 %collective-permute-start.32 = (f16[504,128]{1,0:T(8,128)(2,1)S(1)}, f16[504,128]{1,0:T(8,128)(2,1)S(1)}, u32[]{:S(2)}, u32[]{:S(2)}) collective-permute-start(f16[504,128]{1,0:T(8,128)(2,1)S(1)} %pad_maximum_fusion), channel_id=1, source_target_pairs={{0,112},{8,120},{16,96},{24,104},{32,80},{40,88},{48,64},{56,72},{... | collective-permute-start | bytes 387080 | tf_op jit(solution)/shard_map/ppermute | solution.py:616
  111.0 2.5 %collective-permute-done.22 = f16[504,128]{1,0:T(8,128)(2,1)S(1)} collective-permute-done((f16[504,128]{1,0:T(8,128)(2,1)S(1)}, f16[504,128]{1,0:T(8,128)(2,1)S(1)}, u32[]{:S(2)}, u32[]{:S(2)}) %collective-permute-start.22) | collective-permute-done | bytes 129056 | tf_op jit(solution)/shard_map/ppermute | solution.py:616
  113.5 1.0 collective-permute-start.23
  114.6 0.1 collective-permute-start.31
  114.7 0.5 collective-permute-start.29
  115.2 0.3 collective-permute-start.27
  115.5 2.8 %collective-permute-done.32 = f16[504,128]{1,0:T(8,128)(2,1)S(1)} collective-permute-done((f16[504,128]{1,0:T(8,128)(2,1)S(1)}, f16[504,128]{1,0:T(8,128)(2,1)S(1)}, u32[]{:S(2)}, u32[]{:S(2)}) %collective-permute-start.32) | collective-permute-done | bytes 129056 | tf_op jit(solution)/shard_map/ppermute | solution.py:616
  118.3 0.5 collective-permute-start.25
  118.7 0.0 collective-permute-start.33
  118.9 0.9 collective-permute-done.25
  120.2 2.2 %convert.1.chunks = f32[2,8,504,128]{3,2,1,0:T(8,128)} convert(f16[2,8,504,128]{3,2,1,0:T(8,128)(2,1)S(1)} %bitcast.37) | non-fusion elementwise | flops 1032192 | bytes 6193152 | tf_op jit(solution)/shard_map/convert_element_type | solution.py:618
  122.4 10.9 %relax.1 = f32[24,192,192]{2,1,0:T(8,128)} custom-call(s32[3]{0:T(128)} %pad_add_fusion.info, f32[2,8,504,128]{3,2,1,0:T(8,128)} %convert.1.chunks), custom_call_target="tpu_custom_call" | custom-call | tf_op jit(solution)/shard_map/relax/pallas_call | solution.py:548
  (53 shorter events, 0.8 us)
Async XLA Ops:
  1.2 17.9 %collective-permute-start.8 = (f32[1,3,3,96,96]{4,3,2,1,0:T(8,128)S(1)}, f32[1,3,3,96,96]{4,3,2,1,0:T(8,128)S(1)}, u32[]{:S(2)}, u32[]{:S(2)}) collective-permute-start(f32[1,3,3,96,96]{4,3,2,1,0:T(8,128)S(1)} %get-tuple-element.29), channel_id=1, source_target_pairs={{64,1},{65,2},{66,3},{67,4},{68,5},{69,6},{70,7},{1,64},{2,65},{3,... | collective-permute-start | bytes 995336 | tf_op jit(solution)/shard_map/ppermute | solution.py:585
  9.6 27.2 %collective-permute-start.1 = (bf16[2,12,80,128]{3,2,1,0:T(8,128)(2,1)}, bf16[2,12,80,128]{3,2,1,0:T(8,128)(2,1)S(1)}, u32[]{:S(2)}, u32[]{:S(2)}) collective-permute-start(bf16[2,12,80,128]{3,2,1,0:T(8,128)(2,1)} %get-tuple-element.18), channel_id=1, source_target_pairs={{0,16},{8,24},{16,0},{24,8},{32,48},{40,56},{48,32},{56,40},{1,17}... | collective-permute-start | bytes 1474568 | tf_op jit(solution)/shard_map/ppermute | solution.py:591
  10.9 28.7 %collective-permute-start.3 = (bf16[2,12,80,128]{3,2,1,0:T(8,128)(2,1)}, bf16[2,12,80,128]{3,2,1,0:T(8,128)(2,1)S(1)}, u32[]{:S(2)}, u32[]{:S(2)}) collective-permute-start(bf16[2,12,80,128]{3,2,1,0:T(8,128)(2,1)} %get-tuple-element.19), channel_id=1, source_target_pairs={{0,32},{8,40},{16,48},{24,56},{32,0},{40,8},{48,16},{56,24},{1,33}... | collective-permute-start | bytes 1474568 | tf_op jit(solution)/shard_map/ppermute | solution.py:591
  13.6 26.2 %collective-permute-start.5 = (bf16[2,12,80,128]{3,2,1,0:T(8,128)(2,1)}, bf16[2,12,80,128]{3,2,1,0:T(8,128)(2,1)S(1)}, u32[]{:S(2)}, u32[]{:S(2)}) collective-permute-start(bf16[2,12,80,128]{3,2,1,0:T(8,128)(2,1)} %get-tuple-element.20), channel_id=1, source_target_pairs={{0,48},{8,56},{16,32},{24,40},{32,16},{40,24},{48,0},{56,8},{1,49}... | collective-permute-start | bytes 1474568 | tf_op jit(solution)/shard_map/ppermute | solution.py:591
  13.6 13.3 %collective-permute-start.7 = (f32[1,3,3,96,96]{4,3,2,1,0:T(8,128)S(1)}, f32[1,3,3,96,96]{4,3,2,1,0:T(8,128)S(1)}, u32[]{:S(2)}, u32[]{:S(2)}) collective-permute-start(f32[1,3,3,96,96]{4,3,2,1,0:T(8,128)S(1)} %get-tuple-element.30), channel_id=1, source_target_pairs={{0,1},{1,2},{2,3},{3,4},{4,5},{5,6},{6,7},{65,64},{66,65},{67,66},... | collective-permute-start | bytes 995336 | tf_op jit(solution)/shard_map/ppermute | solution.py:584
  19.1 7.8 %copy-start.7 = (f32[1,3,3,96,96]{4,3,2,1,0:T(8,128)}, f32[1,3,3,96,96]{4,3,2,1,0:T(8,128)S(1)}, u32[]{:S(2)}) copy-start(f32[1,3,3,96,96]{4,3,2,1,0:T(8,128)S(1)} %collective-permute-done.8.other) | copy-start | bytes 995332
  19.1 24.5 %collective-permute-start = (bf16[2,12,80,128]{3,2,1,0:T(8,128)(2,1)}, bf16[2,12,80,128]{3,2,1,0:T(8,128)(2,1)S(1)}, u32[]{:S(2)}, u32[]{:S(2)}) collective-permute-start(bf16[2,12,80,128]{3,2,1,0:T(8,128)(2,1)} %get-tuple-element.17.refs_0_.rest_0_), channel_id=1, source_target_pairs={{0,8},{8,0},{16,24},{24,16},{32,40},{40,32},{48,56},{56,48},{1,9},... | collective-permute-start | bytes 1474568 | tf_op jit(solution)/shard_map/ppermute | solution.py:594
  26.9 0.8 copy-start.8
  36.7 7.6 %collective-permute-start.10 = (bf16[2,560,128]{2,1,0:T(8,128)(2,1)}, bf16[2,560,128]{2,1,0:T(8,128)(2,1)}, u32[]{:S(2)}, u32[]{:S(2)}) collective-permute-start(bf16[2,560,128]{2,1,0:T(8,128)(2,1)} %get-tuple-element.22), channel_id=1, source_target_pairs={{0,16},{8,24},{16,0},{24,8},{32,48},{40,56},{48,32},{56,40},{1,17}... | collective-permute-start | bytes 860168 | tf_op jit(solution)/shard_map/ppermute | solution.py:591
  36.8 23.3 %copy-start = (bf16[2,12,80,128]{3,2,1,0:T(8,128)(2,1)}, bf16[2,12,80,128]{3,2,1,0:T(8,128)(2,1)S(1)}, u32[]{:S(2)}) copy-start(bf16[2,12,80,128]{3,2,1,0:T(8,128)(2,1)S(1)} %collective-permute-done.1.refs_2_.rest_2_) | copy-start | bytes 1474564
  36.8 22.7 %collective-permute-start.2 = (bf16[2,12,80,128]{3,2,1,0:T(8,128)(2,1)S(1)}, bf16[2,12,80,128]{3,2,1,0:T(8,128)(2,1)S(1)}, u32[]{:S(2)}, u32[]{:S(2)}) collective-permute-start(bf16[2,12,80,128]{3,2,1,0:T(8,128)(2,1)S(1)} %collective-permute-done.1.refs_2_.rest_2_), channel_id=1, source_target_pairs={{0,8},{8,0},{16,24},{24,16},{32,40},{40,32},{48,56},{56,48},{1,9},... | collective-permute-start | bytes 1474568 | tf_op jit(solution)/shard_map/ppermute | solution.py:594
  39.7 20.4 %copy-start.1 = (bf16[2,12,80,128]{3,2,1,0:T(8,128)(2,1)}, bf16[2,12,80,128]{3,2,1,0:T(8,128)(2,1)S(1)}, u32[]{:S(2)}) copy-start(bf16[2,12,80,128]{3,2,1,0:T(8,128)(2,1)S(1)} %collective-permute-done.3.refs_4_.rest_4_) | copy-start | bytes 1474564
  39.7 20.0 %collective-permute-start.4 = (bf16[2,12,80,128]{3,2,1,0:T(8,128)(2,1)S(1)}, bf16[2,12,80,128]{3,2,1,0:T(8,128)(2,1)S(1)}, u32[]{:S(2)}, u32[]{:S(2)}) collective-permute-start(bf16[2,12,80,128]{3,2,1,0:T(8,128)(2,1)S(1)} %collective-permute-done.3.refs_4_.rest_4_), channel_id=1, source_target_pairs={{0,8},{8,0},{16,24},{24,16},{32,40},{40,32},{48,56},{56,48},{1,9},... | collective-permute-start | bytes 1474568 | tf_op jit(solution)/shard_map/ppermute | solution.py:594
  39.8 20.3 %copy-start.2 = (bf16[2,12,80,128]{3,2,1,0:T(8,128)(2,1)}, bf16[2,12,80,128]{3,2,1,0:T(8,128)(2,1)S(1)}, u32[]{:S(2)}) copy-start(bf16[2,12,80,128]{3,2,1,0:T(8,128)(2,1)S(1)} %collective-permute-done.5.refs_6_.rest_6_) | copy-start | bytes 1474564
  39.8 11.2 %collective-permute-start.12 = (bf16[2,560,128]{2,1,0:T(8,128)(2,1)}, bf16[2,560,128]{2,1,0:T(8,128)(2,1)}, u32[]{:S(2)}, u32[]{:S(2)}) collective-permute-start(bf16[2,560,128]{2,1,0:T(8,128)(2,1)} %get-tuple-element.23), channel_id=1, source_target_pairs={{0,32},{8,40},{16,48},{24,56},{32,0},{40,8},{48,16},{56,24},{1,33}... | collective-permute-start | bytes 860168 | tf_op jit(solution)/shard_map/ppermute | solution.py:591
  43.6 16.5 %copy-start.3 = (bf16[2,12,80,128]{3,2,1,0:T(8,128)(2,1)}, bf16[2,12,80,128]{3,2,1,0:T(8,128)(2,1)S(1)}, u32[]{:S(2)}) copy-start(bf16[2,12,80,128]{3,2,1,0:T(8,128)(2,1)S(1)} %collective-permute-done.refs_1_.rest_1_) | copy-start | bytes 1474564
  43.6 16.4 %collective-permute-start.6 = (bf16[2,12,80,128]{3,2,1,0:T(8,128)(2,1)S(1)}, bf16[2,12,80,128]{3,2,1,0:T(8,128)(2,1)S(1)}, u32[]{:S(2)}, u32[]{:S(2)}) collective-permute-start(bf16[2,12,80,128]{3,2,1,0:T(8,128)(2,1)S(1)} %collective-permute-done.5.refs_6_.rest_6_), channel_id=1, source_target_pairs={{0,8},{8,0},{16,24},{24,16},{32,40},{40,32},{48,56},{56,48},{1,9},... | collective-permute-start | bytes 1474568 | tf_op jit(solution)/shard_map/ppermute | solution.py:594
  44.3 13.3 %collective-permute-start.14 = (bf16[2,560,128]{2,1,0:T(8,128)(2,1)}, bf16[2,560,128]{2,1,0:T(8,128)(2,1)}, u32[]{:S(2)}, u32[]{:S(2)}) collective-permute-start(bf16[2,560,128]{2,1,0:T(8,128)(2,1)} %get-tuple-element.24), channel_id=1, source_target_pairs={{0,48},{8,56},{16,32},{24,40},{32,16},{40,24},{48,0},{56,8},{1,49}... | collective-permute-start | bytes 860168 | tf_op jit(solution)/shard_map/ppermute | solution.py:591
  51.0 17.5 %collective-permute-start.9 = (bf16[2,560,128]{2,1,0:T(8,128)(2,1)}, bf16[2,560,128]{2,1,0:T(8,128)(2,1)}, u32[]{:S(2)}, u32[]{:S(2)}) collective-permute-start(bf16[2,560,128]{2,1,0:T(8,128)(2,1)} %get-tuple-element.21.rest_8_), channel_id=1, source_target_pairs={{0,8},{8,0},{16,24},{24,16},{32,40},{40,32},{48,56},{56,48},{1,9},... | collective-permute-start | bytes 860168 | tf_op jit(solution)/shard_map/ppermute | solution.py:594
  57.6 12.8 %collective-permute-start.11 = (bf16[2,560,128]{2,1,0:T(8,128)(2,1)}, bf16[2,560,128]{2,1,0:T(8,128)(2,1)}, u32[]{:S(2)}, u32[]{:S(2)}) collective-permute-start(bf16[2,560,128]{2,1,0:T(8,128)(2,1)} %collective-permute-done.10.rest_10_), channel_id=1, source_target_pairs={{0,8},{8,0},{16,24},{24,16},{32,40},{40,32},{48,56},{56,48},{1,9},... | collective-permute-start | bytes 860168 | tf_op jit(solution)/shard_map/ppermute | solution.py:594
  59.5 0.8 copy-start.4
  59.5 10.9 %collective-permute-start.13 = (bf16[2,560,128]{2,1,0:T(8,128)(2,1)}, bf16[2,560,128]{2,1,0:T(8,128)(2,1)}, u32[]{:S(2)}, u32[]{:S(2)}) collective-permute-start(bf16[2,560,128]{2,1,0:T(8,128)(2,1)} %collective-permute-done.12.rest_12_), channel_id=1, source_target_pairs={{0,8},{8,0},{16,24},{24,16},{32,40},{40,32},{48,56},{56,48},{1,9},... | collective-permute-start | bytes 860168 | tf_op jit(solution)/shard_map/ppermute | solution.py:594
  59.6 0.9 copy-start.5
  59.6 10.8 %collective-permute-start.15 = (bf16[2,560,128]{2,1,0:T(8,128)(2,1)}, bf16[2,560,128]{2,1,0:T(8,128)(2,1)}, u32[]{:S(2)}, u32[]{:S(2)}) collective-permute-start(bf16[2,560,128]{2,1,0:T(8,128)(2,1)} %collective-permute-done.14.rest_14_), channel_id=1, source_target_pairs={{0,8},{8,0},{16,24},{24,16},{32,40},{40,32},{48,56},{56,48},{1,9},... | collective-permute-start | bytes 860168 | tf_op jit(solution)/shard_map/ppermute | solution.py:594
  60.5 0.8 copy-start.6
  63.1 8.9 %collective-permute-start.16 = (bf16[8,80,128]{2,1,0:T(8,128)(2,1)}, bf16[8,80,128]{2,1,0:T(8,128)(2,1)S(1)}, u32[]{:S(2)}, u32[]{:S(2)}) collective-permute-start(bf16[8,80,128]{2,1,0:T(8,128)(2,1)} %get-tuple-element.25), channel_id=1, source_target_pairs={{0,64},{1,65},{2,66},{3,67},{4,68},{5,69},{6,70},{7,71},{64,1},{65... | collective-permute-start | bytes 491528 | tf_op jit(solution)/shard_map/ppermute | solution.py:603
  68.5 8.1 %collective-permute-start.17 = (bf16[8,80,128]{2,1,0:T(8,128)(2,1)}, bf16[8,80,128]{2,1,0:T(8,128)(2,1)S(1)}, u32[]{:S(2)}, u32[]{:S(2)}) collective-permute-start(bf16[8,80,128]{2,1,0:T(8,128)(2,1)} %get-tuple-element.26), channel_id=1, source_target_pairs={{64,0},{65,1},{66,2},{67,3},{68,4},{69,5},{70,6},{71,7},{1,64},{2,... | collective-permute-start | bytes 491528 | tf_op jit(solution)/shard_map/ppermute | solution.py:604
  72.0 4.6 %copy-start.9 = (bf16[8,80,128]{2,1,0:T(8,128)(2,1)}, bf16[8,80,128]{2,1,0:T(8,128)(2,1)S(1)}, u32[]{:S(2)}) copy-start(bf16[8,80,128]{2,1,0:T(8,128)(2,1)S(1)} %collective-permute-done.16.rest_16_) | copy-start | bytes 491524
  76.6 0.7 copy-start.10
  87.6 5.4 %collective-permute-start.18 = (f16[72,128]{1,0:T(8,128)(2,1)S(1)}, f16[72,128]{1,0:T(8,128)(2,1)S(1)}, u32[]{:S(2)}, u32[]{:S(2)}) collective-permute-start(f16[72,128]{1,0:T(8,128)(2,1)S(1)} %convert_element_type.14), channel_id=1, source_target_pairs={{64,1},{65,2},{66,3},{67,4},{68,5},{69,6},{70,7},{1,64},{2,65},{3,... | collective-permute-start | bytes 55304 | tf_op jit(solution)/shard_map/ppermute | solution.py:606
  93.0 10.6 %collective-permute-start.20 = (f16[504,128]{1,0:T(8,128)(2,1)S(1)}, f16[504,128]{1,0:T(8,128)(2,1)S(1)}, u32[]{:S(2)}, u32[]{:S(2)}) collective-permute-start(f16[504,128]{1,0:T(8,128)(2,1)S(1)} %pad_maximum_fusion), channel_id=1, source_target_pairs={{0,16},{8,24},{16,0},{24,8},{32,48},{40,56},{48,32},{56,40},{64,80... | collective-permute-start | bytes 387080 | tf_op jit(solution)/shard_map/ppermute | solution.py:616
  93.1 11.5 %collective-permute-start.19 = (f16[504,128]{1,0:T(8,128)(2,1)S(1)}, f16[504,128]{1,0:T(8,128)(2,1)S(1)}, u32[]{:S(2)}, u32[]{:S(2)}) collective-permute-start(f16[504,128]{1,0:T(8,128)(2,1)S(1)} %pad_maximum_fusion), channel_id=1, source_target_pairs={{0,8},{8,0},{16,24},{24,16},{32,40},{40,32},{48,56},{56,48},{1,9},... | collective-permute-start | bytes 387080 | tf_op jit(solution)/shard_map/ppermute | solution.py:617
  95.5 13.8 %collective-permute-start.30 = (f16[504,128]{1,0:T(8,128)(2,1)S(1)}, f16[504,128]{1,0:T(8,128)(2,1)S(1)}, u32[]{:S(2)}, u32[]{:S(2)}) collective-permute-start(f16[504,128]{1,0:T(8,128)(2,1)S(1)} %pad_maximum_fusion), channel_id=1, source_target_pairs={{0,96},{8,104},{16,112},{24,120},{32,64},{40,72},{48,80},{56,88},{... | collective-permute-start | bytes 387080 | tf_op jit(solution)/shard_map/ppermute | solution.py:616
  102.7 12.0 %collective-permute-start.28 = (f16[504,128]{1,0:T(8,128)(2,1)S(1)}, f16[504,128]{1,0:T(8,128)(2,1)S(1)}, u32[]{:S(2)}, u32[]{:S(2)}) collective-permute-start(f16[504,128]{1,0:T(8,128)(2,1)S(1)} %pad_maximum_fusion), channel_id=1, source_target_pairs={{0,80},{8,88},{16,64},{24,72},{32,112},{40,120},{48,96},{56,104},{... | collective-permute-start | bytes 387080 | tf_op jit(solution)/shard_map/ppermute | solution.py:616
  102.7 12.1 %collective-permute-start.26 = (f16[504,128]{1,0:T(8,128)(2,1)S(1)}, f16[504,128]{1,0:T(8,128)(2,1)S(1)}, u32[]{:S(2)}, u32[]{:S(2)}) collective-permute-start(f16[504,128]{1,0:T(8,128)(2,1)S(1)} %pad_maximum_fusion), channel_id=1, source_target_pairs={{0,64},{8,72},{16,80},{24,88},{32,96},{40,104},{48,112},{56,120},{... | collective-permute-start | bytes 387080 | tf_op jit(solution)/shard_map/ppermute | solution.py:616
  103.6 11.6 %collective-permute-start.24 = (f16[504,128]{1,0:T(8,128)(2,1)S(1)}, f16[504,128]{1,0:T(8,128)(2,1)S(1)}, u32[]{:S(2)}, u32[]{:S(2)}) collective-permute-start(f16[504,128]{1,0:T(8,128)(2,1)S(1)} %pad_maximum_fusion), channel_id=1, source_target_pairs={{0,48},{8,56},{16,32},{24,40},{32,16},{40,24},{48,0},{56,8},{64,11... | collective-permute-start | bytes 387080 | tf_op jit(solution)/shard_map/ppermute | solution.py:616
  104.6 2.2 %collective-permute-start.21 = (f16[504,128]{1,0:T(8,128)(2,1)S(1)}, f16[504,128]{1,0:T(8,128)(2,1)S(1)}, u32[]{:S(2)}, u32[]{:S(2)}) collective-permute-start(f16[504,128]{1,0:T(8,128)(2,1)S(1)} %collective-permute-done.20), channel_id=1, source_target_pairs={{0,8},{8,0},{16,24},{24,16},{32,40},{40,32},{48,56},{56,48},{1,9},... | collective-permute-start | bytes 387080 | tf_op jit(solution)/shard_map/ppermute | solution.py:617
  106.8 6.7 %collective-permute-start.22 = (f16[504,128]{1,0:T(8,128)(2,1)S(1)}, f16[504,128]{1,0:T(8,128)(2,1)S(1)}, u32[]{:S(2)}, u32[]{:S(2)}) collective-permute-start(f16[504,128]{1,0:T(8,128)(2,1)S(1)} %pad_maximum_fusion), channel_id=1, source_target_pairs={{0,32},{8,40},{16,48},{24,56},{32,0},{40,8},{48,16},{56,24},{64,96... | collective-permute-start | bytes 387080 | tf_op jit(solution)/shard_map/ppermute | solution.py:616
  109.4 8.9 %collective-permute-start.32 = (f16[504,128]{1,0:T(8,128)(2,1)S(1)}, f16[504,128]{1,0:T(8,128)(2,1)S(1)}, u32[]{:S(2)}, u32[]{:S(2)}) collective-permute-start(f16[504,128]{1,0:T(8,128)(2,1)S(1)} %pad_maximum_fusion), channel_id=1, source_target_pairs={{0,112},{8,120},{16,96},{24,104},{32,80},{40,88},{48,64},{56,72},{... | collective-permute-start | bytes 387080 | tf_op jit(solution)/shard_map/ppermute | solution.py:616
  113.5 5.2 %collective-permute-start.23 = (f16[504,128]{1,0:T(8,128)(2,1)S(1)}, f16[504,128]{1,0:T(8,128)(2,1)S(1)}, u32[]{:S(2)}, u32[]{:S(2)}) collective-permute-start(f16[504,128]{1,0:T(8,128)(2,1)S(1)} %collective-permute-done.22), channel_id=1, source_target_pairs={{0,8},{8,0},{16,24},{24,16},{32,40},{40,32},{48,56},{56,48},{1,9},... | collective-permute-start | bytes 387080 | tf_op jit(solution)/shard_map/ppermute | solution.py:617
  114.6 5.4 %collective-permute-start.31 = (f16[504,128]{1,0:T(8,128)(2,1)S(1)}, f16[504,128]{1,0:T(8,128)(2,1)S(1)}, u32[]{:S(2)}, u32[]{:S(2)}) collective-permute-start(f16[504,128]{1,0:T(8,128)(2,1)S(1)} %collective-permute-done.30), channel_id=1, source_target_pairs={{0,8},{8,0},{16,24},{24,16},{32,40},{40,32},{48,56},{56,48},{1,9},... | collective-permute-start | bytes 387080 | tf_op jit(solution)/shard_map/ppermute | solution.py:617
  114.7 5.2 %collective-permute-start.29 = (f16[504,128]{1,0:T(8,128)(2,1)S(1)}, f16[504,128]{1,0:T(8,128)(2,1)S(1)}, u32[]{:S(2)}, u32[]{:S(2)}) collective-permute-start(f16[504,128]{1,0:T(8,128)(2,1)S(1)} %collective-permute-done.28), channel_id=1, source_target_pairs={{0,8},{8,0},{16,24},{24,16},{32,40},{40,32},{48,56},{56,48},{1,9},... | collective-permute-start | bytes 387080 | tf_op jit(solution)/shard_map/ppermute | solution.py:617
  115.2 4.6 %collective-permute-start.27 = (f16[504,128]{1,0:T(8,128)(2,1)S(1)}, f16[504,128]{1,0:T(8,128)(2,1)S(1)}, u32[]{:S(2)}, u32[]{:S(2)}) collective-permute-start(f16[504,128]{1,0:T(8,128)(2,1)S(1)} %collective-permute-done.26), channel_id=1, source_target_pairs={{0,8},{8,0},{16,24},{24,16},{32,40},{40,32},{48,56},{56,48},{1,9},... | collective-permute-start | bytes 387080 | tf_op jit(solution)/shard_map/ppermute | solution.py:617
  118.3 1.5 %collective-permute-start.25 = (f16[504,128]{1,0:T(8,128)(2,1)S(1)}, f16[504,128]{1,0:T(8,128)(2,1)S(1)}, u32[]{:S(2)}, u32[]{:S(2)}) collective-permute-start(f16[504,128]{1,0:T(8,128)(2,1)S(1)} %collective-permute-done.24), channel_id=1, source_target_pairs={{0,8},{8,0},{16,24},{24,16},{32,40},{40,32},{48,56},{56,48},{1,9},... | collective-permute-start | bytes 387080 | tf_op jit(solution)/shard_map/ppermute | solution.py:617
  118.7 1.4 %collective-permute-start.33 = (f16[504,128]{1,0:T(8,128)(2,1)S(1)}, f16[504,128]{1,0:T(8,128)(2,1)S(1)}, u32[]{:S(2)}, u32[]{:S(2)}) collective-permute-start(f16[504,128]{1,0:T(8,128)(2,1)S(1)} %collective-permute-done.32), channel_id=1, source_target_pairs={{0,8},{8,0},{16,24},{24,16},{32,40},{40,32},{48,56},{56,48},{1,9},... | collective-permute-start | bytes 387080 | tf_op jit(solution)/shard_map/ppermute | solution.py:617

commit v5 on v1

--- a/solution.py
+++ b/solution.py
@@ -16,6 +16,7 @@
 VR = CZ * CW
 VROWS = 5 * VR
 PROWS = 80
+SPREAD = (1, 3, 7, 5, 2, 6, 4)
 SCALE = 128.0
 
 
@@ -118,7 +119,7 @@
     )(info, images)
 
 
-def blur_kernel(info, momenta, halo, other, *rest):
+def blur_kernel(info, momenta, halo, *rest):
     outs = rest[:8]
     held, stage, tall, wide, third, piece, sems, gone = rest[8:]
     level, me = info[0], info[1]
@@ -126,17 +127,14 @@
     own = pltpu.make_async_copy(
         momenta.at[:, pl.ds(3 * level, 9)], held.at[:, pl.ds(3 - 3 * level, 9)], sems.at[0]
     )
-    sides = [
-        pltpu.make_async_copy(rows.at[0], held.at[j, pl.ds(9 * level, 3)], sems.at[1 + j])
-        for j, rows in enumerate((halo, other))
-    ]
-    for copy in [own] + sides:
-        copy.start()
+    side = pltpu.make_async_copy(halo, held.at[:, pl.ds(9 * level, 3)], sems.at[1])
+    own.start()
+    side.start()
     for held_rows in (tall, wide):
         held_rows[:, :8] = jnp.zeros((CZ, 8, 128), F32)
         held_rows[:, 104:] = jnp.zeros((CZ, 8, 128), F32)
-    for copy in [own] + sides:
-        copy.wait()
+    own.wait()
+    side.wait()
     first = (half > 0).astype(F32)
     last = (half < 15).astype(F32)
     spare = jnp.zeros((96, 32), F32)
@@ -186,14 +184,13 @@
         copy.wait()
 
 
-def blur(info, momenta, halo, other):
+def blur(info, momenta, halo):
     rows = VROWS
     return pl.pallas_call(
         blur_kernel,
         grid=(),
         in_specs=[
             pl.BlockSpec(memory_space=pltpu.SMEM),
-            pl.BlockSpec(memory_space=pl.ANY),
             pl.BlockSpec(memory_space=pl.ANY),
             pl.BlockSpec(memory_space=pl.ANY),
         ],
@@ -206,11 +203,11 @@
             pltpu.VMEM((CZ, 112, 128), F32),
             pltpu.VMEM((CZ, 96, 128), F32),
             pltpu.VMEM((VR, 128), F32),
-            pltpu.SemaphoreType.DMA((3,)),
+            pltpu.SemaphoreType.DMA((2,)),
             pltpu.SemaphoreType.DMA((8,)),
         ],
         name="blur_momenta",
-    )(info, momenta, halo, other)
+    )(info, momenta, halo)
 
 
 def edge_kernel(*refs):
@@ -266,11 +263,11 @@
         copies.append(
             pltpu.make_async_copy(planes[k], image.at[k, 1 : HZ + 1], sems.at[k])
         )
-        copies.append(pltpu.make_async_copy(fields[k], field.at[k], sems.at[8 + k]))
-    for copy in copies:
+    first = [pltpu.make_async_copy(fields[k], field.at[k], sems.at[8 + k]) for k in range(8)]
+    for copy in first + copies:
         copy.start()
     acc[...] = jnp.zeros_like(acc)
-    for copy in copies:
+    for copy in first:
         copy.wait()
     lane = lax.broadcasted_iota(jnp.int32, (CY, 128), 1)
     sub = lax.broadcasted_iota(jnp.int32, (CY, 128), 0)
@@ -350,6 +347,8 @@
             acc[1, rows] += warped[2]
 
     interpolate(0, even)
+    for copy in copies:
+        copy.wait()
 
     def turn(step, carry):
         interpolate(2 * step + 1, odd)
@@ -405,7 +404,14 @@
     )(info, assign, *tables, *planes, *fields, below, above)
 
 
-def relax_kernel(info, chunks, out, flat, pair, flat2, pair2, even, odd, ready, sems):
+def relax_kernel(info, *rest):
+    parts = rest[:16]
+    out, chunks, arriving, flat, pair, flat2, pair2, even, odd, ready, sems = rest[16:]
+    copies = [
+        pltpu.make_async_copy(part, chunks.at[k], arriving.at[k]) for k, part in enumerate(parts)
+    ]
+    for copy in copies:
+        copy.start()
     level, me, zone = info[0], info[1], info[2]
     size = flat.shape[1] - 16
     for held in (flat, pair, flat2, pair2):
@@ -414,14 +420,16 @@
     for held in (flat, flat2):
         for z in (0, held.shape[0] - 1):
             held[z, 8 : 8 + size] = jnp.zeros((size, 128), F32)
+    for copy in copies:
+        copy.wait()
     narrow = lax.broadcasted_iota(jnp.int32, (CY, 128), 1)
     tail = HZ * 3 // 2
     for peer in range(8):
         rows = slice(8 + CY * peer, 8 + CY * (peer + 1))
-        slots = [(half ^ level) * 8 + (peer ^ me) for half in range(2)]
 
         def block(half, index):
-            return chunks[slots[half], CY * index : CY * (index + 1)]
+            slot = (half ^ level) * 8 + (peer ^ me)
+            return chunks[slot, CY * index : CY * (index + 1)]
 
         for half in range(2):
             for z in range(HZ):
@@ -473,9 +481,8 @@
             around = held[z - 1, start : start + count] + held[z + 1, start : start + count]
             around += held[z, start - 1 : start - 1 + count] + held[z, start + 1 : start + 1 + count]
             around += sums[b, start - 8 : start - 8 + count]
-            done.append(
-                (0.1 * scale) * held[z, start : start + count] + (0.15 * scale) * around
-            )
+            value = around + (2.0 / 3.0) * held[z, start : start + count]
+            done.append(value if scale is None else scale * value)
         return done
 
     def sweep(planes, store, scale, after):
@@ -500,7 +507,7 @@
         flat2[index + 16, start : start + count] = done[1]
         pair2[index, start : start + count] = done[2]
 
-    sweep((flat, pair), first, 1.0, lambda index: None)
+    sweep((flat, pair), first, None, lambda index: None)
     whole = lax.broadcasted_iota(jnp.int32, (size, 128), 1)
 
     @pl.when(zone == 0)
@@ -534,7 +541,7 @@
         def _():
             emit(index + 11).start()
 
-    sweep((flat2, pair2), second, 1.0 / SCALE, depart)
+    sweep((flat2, pair2), second, 0.15 * 0.15 / SCALE, depart)
 
     def finish(z, carry):
         emit(z).wait()
@@ -543,15 +550,17 @@
     lax.fori_loop(0, 24, finish, 0)
 
 
-def relax(info, chunks):
-    vmem = pl.BlockSpec(memory_space=pltpu.VMEM)
+def relax(info, parts):
+    hbm = pl.BlockSpec(memory_space=pl.ANY)
     return pl.pallas_call(
         relax_kernel,
         grid=(),
-        in_specs=[pl.BlockSpec(memory_space=pltpu.SMEM), vmem],
-        out_specs=pl.BlockSpec(memory_space=pl.ANY),
+        in_specs=[pl.BlockSpec(memory_space=pltpu.SMEM)] + [hbm] * 16,
+        out_specs=hbm,
         out_shape=jax.ShapeDtypeStruct((24, 192, 192), F32),
         scratch_shapes=[
+            pltpu.VMEM((16,) + parts[0].shape, F32),
+            pltpu.SemaphoreType.DMA((16,)),
             pltpu.VMEM((32, 208, 128), F32),
             pltpu.VMEM((16, 208, 128), F32),
             pltpu.VMEM((32, 208, 128), F32),
@@ -562,7 +571,7 @@
             pltpu.SemaphoreType.DMA((24,)),
         ],
         name="relax",
-    )(info, chunks)
+    )(info, *parts)
 
 
 def update(images, momenta, assign):
@@ -578,21 +587,18 @@
     cross += [(g + 1, zones + g) for g in range(zones - 1)]
     climb = [(g, zones + g) for g in range(zones)]
     climb += [(zones + g, g + 1) for g in range(zones - 1)]
-    part = (1, 3) + momenta.shape[2:]
-    rim = lax.dynamic_slice(momenta, (0, 9 * (1 - level), 0, 0, 0), part)
-    other = lax.dynamic_slice(momenta, (1, 9 * level, 0, 0, 0), part)
+    rim = lax.dynamic_slice_in_dim(momenta, 9 * (1 - level), 3, axis=1)
     rim = lax.ppermute(rim, nearest, outward)
-    other = lax.ppermute(other, nearest, cross)
 
     def spread(parts):
         arrived = {0: parts[0]}
-        for k in (3, 7, 5, 2, 6, 4, 1):
+        for k in SPREAD:
             arrived[k] = lax.ppermute(parts[k], "subj", [(i, i ^ k) for i in range(8)])
         return [arrived[k] for k in range(8)]
 
     packed = pack_images(info, images)
     planes = spread(packed)
-    blurred = blur(info, momenta, rim, other)
+    blurred = blur(info, momenta, rim)
     fields = spread(blurred)
     low, high = edges(planes)
     below = lax.ppermute(high, nearest, climb)
@@ -600,17 +606,17 @@
     chunk, edge = warp(info, assign, planes, fields, below, above)
     edge = lax.ppermute(edge.astype(jnp.float16), nearest, cross)
     chunk = jnp.concatenate([chunk.astype(jnp.float16), edge], axis=0)
-    mine = {(0, 0): chunk}
-    for far, step in ((0, 1), (0, 3), (1, 0), (0, 2), (1, 1), (1, 3), (1, 2)):
-        perm = [(8 * a + i, 8 * (a ^ far) + (i ^ (2 * step))) for a in range(2) for i in range(8)]
-        mine[far, step] = lax.ppermute(chunk, ("level", "subj"), perm)
     gathered = []
     for far in range(2):
         for step in range(4):
-            part = mine[far, step]
+            part = chunk
+            if far or step:
+                perm = [
+                    (8 * a + i, 8 * (a ^ far) + (i ^ (2 * step))) for a in range(2) for i in range(8)
+                ]
+                part = lax.ppermute(chunk, ("level", "subj"), perm)
             gathered += [part, lax.ppermute(part, "subj", [(i, i ^ 1) for i in range(8)])]
-    chunks = jnp.stack(gathered).astype(F32)
-    return relax(info, chunks)
+    return relax(info, [part.astype(F32) for part in gathered])
 
 
 def solution(mesh):

time: 137 us -> 147 us (1.073); the launches traced: 136 us -> 144 us
  other arithmetic: 4.57 us -> 13.9 us
  starting transfers between devices: 47.4 us -> 49.1 us
  waiting for transfers between devices: 43.6 us -> 42 us
    convert_element_type x1 -> x15, other arithmetic: 2.21 us -> 10.8 us  [update(): return relax(info, [part.astype(F32) for part in gathered])]
    ppermute x14, starting transfers between devices: 14.3 us -> 19.9 us  [spread(): arrived[k] = lax.ppermute(parts[k], 'subj', [(i, i ^ k) for i in range(8)])]
    ppermute x8 -> x7, starting transfers between devices: 16.3 us -> 14.2 us  [update(): part = lax.ppermute(chunk, ('level', 'subj'), perm)]
    ppermute x8, waiting for transfers between devices: 2 us -> 0.02 us  [update(): lax.ppermute(part, 'subj', [(i, i ^ 1) for i in range(8)])]
    unnamed x50 -> x34, local copies, waits for them, and re-layouts: 3.49 us -> 2.2 us
    ppermute x8 -> x7, waiting for transfers between devices: 5.55 us -> 5.06 us  [update(): part = lax.ppermute(chunk, ('level', 'subj'), perm)]
  transfers between devices with their start and end apart: 34 -> 33, of which waited for: 15 -> 14; matrix products, arithmetic and copies ran while one was open for 2% -> 8% of each run, Pallas kernels for 8% -> 10%
where the time goes in v5:
time: 147 us; the launch traced here: 144 us
  starting transfers between devices  49.1 us (33%)
  waiting for transfers between devices  42 us (29%)
  Pallas kernels  35.5 us (24%)
  other arithmetic  13.9 us (9%)
  local copies, waits for them, and re-layouts  3.43 us (2%)
    ppermute x14, waiting for transfers between devices, spread(): arrived[k] = lax.ppermute(parts[k], 'subj', [(i, i ^ k) for i in range(8)])  34.1 us
    ppermute x14, starting transfers between devices, spread(): arrived[k] = lax.ppermute(parts[k], 'subj', [(i, i ^ k) for i in range(8)])  19.9 us
    ppermute x7, starting transfers between devices, update(): part = lax.ppermute(chunk, ('level', 'subj'), perm)  14.2 us
    pallas_call x1, Pallas kernels, relax(): pl.pallas_call(relax_kernel, grid=(), in_specs=[pl.BlockSpec(memory_space...  11.8 us
    convert_element_type x15, other arithmetic, update(): return relax(info, [part.astype(F32) for part in gathered])  10.8 us
    pallas_call x1, Pallas kernels, blur(): pl.pallas_call(blur_kernel, grid=(), in_specs=[pl.BlockSpec(memory_space=...  9.09 us
    pallas_call x1, Pallas kernels, warp(): pl.pallas_call(warp_kernel, grid=(), in_specs=[smem, smem, vmem, vmem, vm...  8.95 us
    ppermute x7, waiting for transfers between devices, update(): part = lax.ppermute(chunk, ('level', 'subj'), perm)  5.06 us
  transfers between devices with their start and end apart: 33, of which 14 were waited for; matrix products, arithmetic and copies ran while one was open for 8% of the time, Pallas kernels for 10%

profile of v5, /device:TPU:96, one launch (start us, length us, event | category | flops | bytes accessed | tf_op | source)
XLA Modules:
  0.0 144.2 jit_solution(6091145984086697408)
XLA Ops:
  0.0 1.2 constant_dynamic-slice_fusion
  1.2 4.7 %collective-permute-start.7 = (f32[2,3,3,96,96]{4,3,2,1,0:T(8,128)S(1)}, f32[2,3,3,96,96]{4,3,2,1,0:T(8,128)S(1)}, u32[]{:S(2)}, u32[]{:S(2)}) collective-permute-start(f32[2,3,3,96,96]{4,3,2,1,0:T(8,128)S(1)} %constant_dynamic-slice_fusion), channel_id=1, source_target_pairs={{0,1},{1,2},{2,3},{3,4},{4,5},{5,6},{6,7},{65,64},{66,65},{67,66},... | collective-permute-start | bytes 1990664 | tf_op jit(solution)/shard_map/ppermute | solution.py:591
  5.9 0.6 pad_add_fusion.info
  6.5 3.9 %pack_images.1 = (bf16[12,80,128]{2,1,0:T(8,128)(2,1)}, bf16[12,80,128]{2,1,0:T(8,128)(2,1)}, bf16[12,80,128]{2,1,0:T(8,128)(2,1)}, bf16[12,80,128]{2,1,0:T(8,12...) custom-call(s32[3]{0:T(128)} %pad_add_fusion.info, ...), custom_call_target="tpu_custom_call" | custom-call | tf_op jit(solution)/shard_map/pack_images/pallas_call | solution.py:106
  10.5 1.7 %collective-permute-start.1 = (bf16[12,80,128]{2,1,0:T(8,128)(2,1)}, bf16[12,80,128]{2,1,0:T(8,128)(2,1)S(1)}, u32[]{:S(2)}, u32[]{:S(2)}) collective-permute-start(bf16[12,80,128]{2,1,0:T(8,128)(2,1)} %get-tuple-element.27), channel_id=1, source_target_pairs={{0,16},{8,24},{16,0},{24,8},{32,48},{40,56},{48,32},{56,40},{1,17}... | collective-permute-start | bytes 737288 | tf_op jit(solution)/shard_map/ppermute | solution.py:596
  12.3 3.2 %collective-permute-start.3 = (bf16[12,80,128]{2,1,0:T(8,128)(2,1)}, bf16[12,80,128]{2,1,0:T(8,128)(2,1)S(1)}, u32[]{:S(2)}, u32[]{:S(2)}) collective-permute-start(bf16[12,80,128]{2,1,0:T(8,128)(2,1)} %get-tuple-element.29), channel_id=1, source_target_pairs={{0,32},{8,40},{16,48},{24,56},{32,0},{40,8},{48,16},{56,24},{1,33}... | collective-permute-start | bytes 737288 | tf_op jit(solution)/shard_map/ppermute | solution.py:596
  15.6 4.0 %collective-permute-done.1.refs_2_.rest_2_ = bf16[12,80,128]{2,1,0:T(8,128)(2,1)S(1)} collective-permute-done((bf16[12,80,128]{2,1,0:T(8,128)(2,1)}, bf16[12,80,128]{2,1,0:T(8,128)(2,1)S(1)}, u32[]{:S(2)}, u32[]{:S(2)}) %collective-permute-start.1) | collective-permute-done | bytes 245792 | tf_op jit(solution)/shard_map/ppermute | solution.py:596
  19.6 3.0 %collective-permute-start.5 = (bf16[12,80,128]{2,1,0:T(8,128)(2,1)}, bf16[12,80,128]{2,1,0:T(8,128)(2,1)S(1)}, u32[]{:S(2)}, u32[]{:S(2)}) collective-permute-start(bf16[12,80,128]{2,1,0:T(8,128)(2,1)} %get-tuple-element.31), channel_id=1, source_target_pairs={{0,48},{8,56},{16,32},{24,40},{32,16},{40,24},{48,0},{56,8},{1,49}... | collective-permute-start | bytes 737288 | tf_op jit(solution)/shard_map/ppermute | solution.py:596
  22.6 1.4 %collective-permute-done.2.refs_3_.rest_3_ = bf16[12,80,128]{2,1,0:T(8,128)(2,1)S(1)} collective-permute-done((bf16[12,80,128]{2,1,0:T(8,128)(2,1)}, bf16[12,80,128]{2,1,0:T(8,128)(2,1)S(1)}, u32[]{:S(2)}, u32[]{:S(2)}) %collective-permute-start.2) | collective-permute-done | bytes 245792 | tf_op jit(solution)/shard_map/ppermute | solution.py:596
  24.1 3.5 %collective-permute-start.6 = (bf16[12,80,128]{2,1,0:T(8,128)(2,1)}, bf16[12,80,128]{2,1,0:T(8,128)(2,1)S(1)}, u32[]{:S(2)}, u32[]{:S(2)}) collective-permute-start(bf16[12,80,128]{2,1,0:T(8,128)(2,1)} %get-tuple-element.32), channel_id=1, source_target_pairs={{0,56},{8,48},{16,40},{24,32},{32,24},{40,16},{48,8},{56,0},{1,57}... | collective-permute-start | bytes 737288 | tf_op jit(solution)/shard_map/ppermute | solution.py:596
  27.6 5.1 %collective-permute-done.3.refs_4_.rest_4_ = bf16[12,80,128]{2,1,0:T(8,128)(2,1)S(1)} collective-permute-done((bf16[12,80,128]{2,1,0:T(8,128)(2,1)}, bf16[12,80,128]{2,1,0:T(8,128)(2,1)S(1)}, u32[]{:S(2)}, u32[]{:S(2)}) %collective-permute-start.3) | collective-permute-done | bytes 245792 | tf_op jit(solution)/shard_map/ppermute | solution.py:596
  32.7 4.2 %collective-permute-done.4.refs_5_.rest_5_ = bf16[12,80,128]{2,1,0:T(8,128)(2,1)S(1)} collective-permute-done((bf16[12,80,128]{2,1,0:T(8,128)(2,1)}, bf16[12,80,128]{2,1,0:T(8,128)(2,1)S(1)}, u32[]{:S(2)}, u32[]{:S(2)}) %collective-permute-start.4) | collective-permute-done | bytes 245792 | tf_op jit(solution)/shard_map/ppermute | solution.py:596
  36.9 2.7 %collective-permute-done.5.refs_6_.rest_6_ = bf16[12,80,128]{2,1,0:T(8,128)(2,1)S(1)} collective-permute-done((bf16[12,80,128]{2,1,0:T(8,128)(2,1)}, bf16[12,80,128]{2,1,0:T(8,128)(2,1)S(1)}, u32[]{:S(2)}, u32[]{:S(2)}) %collective-permute-start.5) | collective-permute-done | bytes 245792 | tf_op jit(solution)/shard_map/ppermute | solution.py:596
  39.6 3.5 %collective-permute-done.6.refs_7_.rest_7_ = bf16[12,80,128]{2,1,0:T(8,128)(2,1)S(1)} collective-permute-done((bf16[12,80,128]{2,1,0:T(8,128)(2,1)}, bf16[12,80,128]{2,1,0:T(8,128)(2,1)S(1)}, u32[]{:S(2)}, u32[]{:S(2)}) %collective-permute-start.6) | collective-permute-done | bytes 245792 | tf_op jit(solution)/shard_map/ppermute | solution.py:596
  43.2 0.7 copy-done.6
  43.8 1.8 %cut_edges.1 = (bf16[8,80,128]{2,1,0:T(8,128)(2,1)}, bf16[8,80,128]{2,1,0:T(8,128)(2,1)}) custom-call(bf16[12,80,128]{2,1,0:T(8,128)(2,1)} %get-tuple-element.25.refs_0_.rest_0_, bf16[12,80,128]{2,1,0:T(8,128)(2,1)} %copy-done, bf16[12,80,128]{2,1,0:T(8,128)(2,1)} %copy-done.1, bf16[12,80,128]{2,1,0:T(8,128)(2,1)} %copy-done.2, ...), custom_call_target="tpu_custom_call" | custom-call | tf_op jit(solution)/shard_map/cut_edges/pallas_call | solution.py:237
  45.6 2.0 %collective-permute-start.15 = (bf16[8,80,128]{2,1,0:T(8,128)(2,1)}, bf16[8,80,128]{2,1,0:T(8,128)(2,1)S(1)}, u32[]{:S(2)}, u32[]{:S(2)}) collective-permute-start(bf16[8,80,128]{2,1,0:T(8,128)(2,1)} %get-tuple-element.41), channel_id=1, source_target_pairs={{0,64},{1,65},{2,66},{3,67},{4,68},{5,69},{6,70},{7,71},{64,1},{65... | collective-permute-start | bytes 491528 | tf_op jit(solution)/shard_map/ppermute | solution.py:604
  47.6 3.9 %collective-permute-start.16 = (bf16[8,80,128]{2,1,0:T(8,128)(2,1)}, bf16[8,80,128]{2,1,0:T(8,128)(2,1)S(1)}, u32[]{:S(2)}, u32[]{:S(2)}) collective-permute-start(bf16[8,80,128]{2,1,0:T(8,128)(2,1)} %get-tuple-element.42), channel_id=1, source_target_pairs={{64,0},{65,1},{66,2},{67,3},{68,4},{69,5},{70,6},{71,7},{1,64},{2,... | collective-permute-start | bytes 491528 | tf_op jit(solution)/shard_map/ppermute | solution.py:605
  51.5 0.9 copy-done.7
  52.4 9.1 %blur_momenta.1 = (bf16[560,128]{1,0:T(8,128)(2,1)}, bf16[560,128]{1,0:T(8,128)(2,1)}, bf16[560,128]{1,0:T(8,128)(2,1)}, bf16[560,128]{1,0:T(8,128)(2,1)}, bf16[...) custom-call(s32[3]{0:T(128)} %pad_add_fusion.info, ...), custom_call_target="tpu_custom_call" | custom-call | tf_op jit(solution)/shard_map/blur_momenta/pallas_call | solution.py:189
  61.8 1.6 %collective-permute-start.10 = (bf16[560,128]{1,0:T(8,128)(2,1)}, bf16[560,128]{1,0:T(8,128)(2,1)S(1)}, u32[]{:S(2)}, u32[]{:S(2)}) collective-permute-start(bf16[560,128]{1,0:T(8,128)(2,1)} %get-tuple-element.36), channel_id=1, source_target_pairs={{0,24},{8,16},{16,8},{24,0},{32,56},{40,48},{48,40},{56,32},{1,25}... | collective-permute-start | bytes 430088 | tf_op jit(solution)/shard_map/ppermute | solution.py:596
  63.5 2.5 %collective-permute-start.11 = (bf16[560,128]{1,0:T(8,128)(2,1)}, bf16[560,128]{1,0:T(8,128)(2,1)S(1)}, u32[]{:S(2)}, u32[]{:S(2)}) collective-permute-start(bf16[560,128]{1,0:T(8,128)(2,1)} %get-tuple-element.37), channel_id=1, source_target_pairs={{0,32},{8,40},{16,48},{24,56},{32,0},{40,8},{48,16},{56,24},{1,33}... | collective-permute-start | bytes 430088 | tf_op jit(solution)/shard_map/ppermute | solution.py:596
  66.0 0.7 collective-permute-start.12
  66.7 2.8 %collective-permute-start.13 = (bf16[560,128]{1,0:T(8,128)(2,1)}, bf16[560,128]{1,0:T(8,128)(2,1)S(1)}, u32[]{:S(2)}, u32[]{:S(2)}) collective-permute-start(bf16[560,128]{1,0:T(8,128)(2,1)} %get-tuple-element.39), channel_id=1, source_target_pairs={{0,48},{8,56},{16,32},{24,40},{32,16},{40,24},{48,0},{56,8},{1,49}... | collective-permute-start | bytes 430088 | tf_op jit(solution)/shard_map/ppermute | solution.py:596
  69.7 0.8 collective-permute-done.10.rest_11_
  70.5 6.5 %collective-permute-done.11.rest_12_ = bf16[560,128]{1,0:T(8,128)(2,1)S(1)} collective-permute-done((bf16[560,128]{1,0:T(8,128)(2,1)}, bf16[560,128]{1,0:T(8,128)(2,1)S(1)}, u32[]{:S(2)}, u32[]{:S(2)}) %collective-permute-start.11) | collective-permute-done | bytes 143392 | tf_op jit(solution)/shard_map/ppermute | solution.py:596
  77.0 1.3 collective-permute-done.12.rest_13_
  78.3 2.6 %collective-permute-done.13.rest_14_ = bf16[560,128]{1,0:T(8,128)(2,1)S(1)} collective-permute-done((bf16[560,128]{1,0:T(8,128)(2,1)}, bf16[560,128]{1,0:T(8,128)(2,1)S(1)}, u32[]{:S(2)}, u32[]{:S(2)}) %collective-permute-start.13) | collective-permute-done | bytes 143392 | tf_op jit(solution)/shard_map/ppermute | solution.py:596
  80.9 2.0 %collective-permute-done.14.rest_15_ = bf16[560,128]{1,0:T(8,128)(2,1)S(1)} collective-permute-done((bf16[560,128]{1,0:T(8,128)(2,1)}, bf16[560,128]{1,0:T(8,128)(2,1)S(1)}, u32[]{:S(2)}, u32[]{:S(2)}) %collective-permute-start.14) | collective-permute-done | bytes 143392 | tf_op jit(solution)/shard_map/ppermute | solution.py:596
  82.9 0.6 copy-done.16
  83.5 8.9 %warp_sum.1 = (f32[432,128]{1,0:T(8,128)}, f32[72,128]{1,0:T(8,128)}) custom-call(s32[3]{0:T(128)} %pad_add_fusion.info, s32[16]{0:T(128)} %assign.1, bf16[288,112]{1,0:T(8,128)(2,1)} %constant.27.clone.zy, bf16[256,256]{1,0:T(8,128)(2,1)} %constant.28.clone.x0, bf16[256,256]{1,0:T(8,128)(2,1)} %constant.29.clone.x1, ...), custom_call_target="tpu_custom_call" | custom-call | tf_op jit(solution)/shard_map/warp_sum/pallas_call | solution.py:386
  92.5 0.8 convert_element_type.55
  93.3 2.9 %collective-permute-start.17 = (f16[72,128]{1,0:T(8,128)(2,1)S(1)}, f16[72,128]{1,0:T(8,128)(2,1)S(1)}, u32[]{:S(2)}, u32[]{:S(2)}) collective-permute-start(f16[72,128]{1,0:T(8,128)(2,1)S(1)} %convert_element_type.55), channel_id=1, source_target_pairs={{64,1},{65,2},{66,3},{67,4},{68,5},{69,6},{70,7},{1,64},{2,65},{3,... | collective-permute-start | bytes 55304 | tf_op jit(solution)/shard_map/ppermute | solution.py:607
  96.1 1.0 convert_element_type.54
  97.1 2.7 %collective-permute-done.17 = f16[72,128]{1,0:T(8,128)(2,1)S(1)} collective-permute-done((f16[72,128]{1,0:T(8,128)(2,1)S(1)}, f16[72,128]{1,0:T(8,128)(2,1)S(1)}, u32[]{:S(2)}, u32[]{:S(2)}) %collective-permute-start.17) | collective-permute-done | bytes 18464 | tf_op jit(solution)/shard_map/ppermute | solution.py:607
  99.8 0.7 pad_maximum_fusion
  100.5 3.7 %collective-permute-start.29 = (f16[504,128]{1,0:T(8,128)(2,1)S(1)}, f16[504,128]{1,0:T(8,128)(2,1)S(1)}, u32[]{:S(2)}, u32[]{:S(2)}) collective-permute-start(f16[504,128]{1,0:T(8,128)(2,1)S(1)} %get-tuple-element.45), channel_id=1, source_target_pairs={{0,96},{8,104},{16,112},{24,120},{32,64},{40,72},{48,80},{56,88},{... | collective-permute-start | bytes 387080 | tf_op jit(solution)/shard_map/ppermute | solution.py:617
  104.2 0.4 collective-permute-start.27
  104.6 2.5 %collective-permute-start.25 = (f16[504,128]{1,0:T(8,128)(2,1)S(1)}, f16[504,128]{1,0:T(8,128)(2,1)S(1)}, u32[]{:S(2)}, u32[]{:S(2)}) collective-permute-start(f16[504,128]{1,0:T(8,128)(2,1)S(1)} %get-tuple-element.45), channel_id=1, source_target_pairs={{0,64},{8,72},{16,80},{24,88},{32,96},{40,104},{48,112},{56,120},{... | collective-permute-start | bytes 387080 | tf_op jit(solution)/shard_map/ppermute | solution.py:617
  107.1 0.9 collective-permute-start.23
  108.0 1.8 %collective-permute-start.21 = (f16[504,128]{1,0:T(8,128)(2,1)S(1)}, f16[504,128]{1,0:T(8,128)(2,1)S(1)}, u32[]{:S(2)}, u32[]{:S(2)}) collective-permute-start(f16[504,128]{1,0:T(8,128)(2,1)S(1)} %get-tuple-element.45), channel_id=1, source_target_pairs={{0,32},{8,40},{16,48},{24,56},{32,0},{40,8},{48,16},{56,24},{64,96... | collective-permute-start | bytes 387080 | tf_op jit(solution)/shard_map/ppermute | solution.py:617
  109.8 1.4 collective-permute-start.19
  111.2 2.2 %collective-permute-done.25 = f16[504,128]{1,0:T(8,128)(2,1)S(1)} collective-permute-done((f16[504,128]{1,0:T(8,128)(2,1)S(1)}, f16[504,128]{1,0:T(8,128)(2,1)S(1)}, u32[]{:S(2)}, u32[]{:S(2)}) %collective-permute-start.25) | collective-permute-done | bytes 129056 | tf_op jit(solution)/shard_map/ppermute | solution.py:617
  113.4 3.6 %collective-permute-start.31 = (f16[504,128]{1,0:T(8,128)(2,1)S(1)}, f16[504,128]{1,0:T(8,128)(2,1)S(1)}, u32[]{:S(2)}, u32[]{:S(2)}) collective-permute-start(f16[504,128]{1,0:T(8,128)(2,1)S(1)} %get-tuple-element.45), channel_id=1, source_target_pairs={{0,112},{8,120},{16,96},{24,104},{32,80},{40,88},{48,64},{56,72},{... | collective-permute-start | bytes 387080 | tf_op jit(solution)/shard_map/ppermute | solution.py:617
  116.9 0.5 collective-permute-start.28
  117.5 0.4 collective-permute-start.24
  118.0 2.9 %collective-permute-done.31 = f16[504,128]{1,0:T(8,128)(2,1)S(1)} collective-permute-done((f16[504,128]{1,0:T(8,128)(2,1)S(1)}, f16[504,128]{1,0:T(8,128)(2,1)S(1)}, u32[]{:S(2)}, u32[]{:S(2)}) %collective-permute-start.31) | collective-permute-done | bytes 129056 | tf_op jit(solution)/shard_map/ppermute | solution.py:617
  120.8 0.5 collective-permute-start.20
  121.4 0.7 convert_element_type.70.rest_14_
  122.2 0.7 convert_element_type.58.rest_2_
  122.9 0.7 convert_element_type.60.rest_4_
  123.6 0.7 convert_element_type.62.rest_6_
  124.3 0.7 convert_element_type.64.rest_8_
  125.1 0.7 convert_element_type.66.rest_10_
  125.8 0.7 convert_element_type.68.rest_12_
  126.5 0.7 convert_element_type.57.rest_1_
  127.2 0.7 convert_element_type.69.rest_13_
  128.0 0.7 convert_element_type.67.rest_11_
  128.7 0.7 convert_element_type.65.rest_9_
  129.4 0.7 convert_element_type.63.rest_7_
  130.1 0.7 convert_element_type.61.rest_5_
  130.8 0.7 convert_element_type.59.rest_3_
  131.6 0.7 convert_element_type.71.rest_15_
  132.3 11.8 %relax.1 = f32[24,192,192]{2,1,0:T(8,128)} custom-call(s32[3]{0:T(128)} %pad_add_fusion.info, f32[504,128]{1,0:T(8,128)} %get-tuple-element.46.rest_0_, f32[504,128]{1,0:T(8,128)} %convert_element_type.57.rest_1_, f32[504,128]{1,0:T(8,128)} %convert_element_type.58.rest_2_, f32[504,128]{1,0:T(8,128)} %convert_element_type.59.rest_3_, ...), custom_call_target="tpu_custom_call" | custom-call | tf_op jit(solution)/shard_map/relax/pallas_call | solution.py:555
  (61 shorter events, 1.2 us)
Async XLA Ops:
  1.2 50.3 %collective-permute-start.7 = (f32[2,3,3,96,96]{4,3,2,1,0:T(8,128)S(1)}, f32[2,3,3,96,96]{4,3,2,1,0:T(8,128)S(1)}, u32[]{:S(2)}, u32[]{:S(2)}) collective-permute-start(f32[2,3,3,96,96]{4,3,2,1,0:T(8,128)S(1)} %constant_dynamic-slice_fusion), channel_id=1, source_target_pairs={{0,1},{1,2},{2,3},{3,4},{4,5},{5,6},{6,7},{65,64},{66,65},{67,66},... | collective-permute-start | bytes 1990664 | tf_op jit(solution)/shard_map/ppermute | solution.py:591
  10.4 5.1 %collective-permute-start = (bf16[12,80,128]{2,1,0:T(8,128)(2,1)}, bf16[12,80,128]{2,1,0:T(8,128)(2,1)S(1)}, u32[]{:S(2)}, u32[]{:S(2)}) collective-permute-start(bf16[12,80,128]{2,1,0:T(8,128)(2,1)} %get-tuple-element.26), channel_id=1, source_target_pairs={{0,8},{8,0},{16,24},{24,16},{32,40},{40,32},{48,56},{56,48},{1,9},... | collective-permute-start | bytes 737288 | tf_op jit(solution)/shard_map/ppermute | solution.py:596
  10.5 9.1 %collective-permute-start.1 = (bf16[12,80,128]{2,1,0:T(8,128)(2,1)}, bf16[12,80,128]{2,1,0:T(8,128)(2,1)S(1)}, u32[]{:S(2)}, u32[]{:S(2)}) collective-permute-start(bf16[12,80,128]{2,1,0:T(8,128)(2,1)} %get-tuple-element.27), channel_id=1, source_target_pairs={{0,16},{8,24},{16,0},{24,8},{32,48},{40,56},{48,32},{56,40},{1,17}... | collective-permute-start | bytes 737288 | tf_op jit(solution)/shard_map/ppermute | solution.py:596
  12.1 11.9 %collective-permute-start.2 = (bf16[12,80,128]{2,1,0:T(8,128)(2,1)}, bf16[12,80,128]{2,1,0:T(8,128)(2,1)S(1)}, u32[]{:S(2)}, u32[]{:S(2)}) collective-permute-start(bf16[12,80,128]{2,1,0:T(8,128)(2,1)} %get-tuple-element.28), channel_id=1, source_target_pairs={{0,24},{8,16},{16,8},{24,0},{32,56},{40,48},{48,40},{56,32},{1,25}... | collective-permute-start | bytes 737288 | tf_op jit(solution)/shard_map/ppermute | solution.py:596
  12.3 20.4 %collective-permute-start.3 = (bf16[12,80,128]{2,1,0:T(8,128)(2,1)}, bf16[12,80,128]{2,1,0:T(8,128)(2,1)S(1)}, u32[]{:S(2)}, u32[]{:S(2)}) collective-permute-start(bf16[12,80,128]{2,1,0:T(8,128)(2,1)} %get-tuple-element.29), channel_id=1, source_target_pairs={{0,32},{8,40},{16,48},{24,56},{32,0},{40,8},{48,16},{56,24},{1,33}... | collective-permute-start | bytes 737288 | tf_op jit(solution)/shard_map/ppermute | solution.py:596
  15.5 27.6 %copy-start = (bf16[12,80,128]{2,1,0:T(8,128)(2,1)}, bf16[12,80,128]{2,1,0:T(8,128)(2,1)S(1)}, u32[]{:S(2)}) copy-start(bf16[12,80,128]{2,1,0:T(8,128)(2,1)S(1)} %collective-permute-done.refs_1_.rest_1_) | copy-start | bytes 737284
  15.5 21.3 %collective-permute-start.4 = (bf16[12,80,128]{2,1,0:T(8,128)(2,1)}, bf16[12,80,128]{2,1,0:T(8,128)(2,1)S(1)}, u32[]{:S(2)}, u32[]{:S(2)}) collective-permute-start(bf16[12,80,128]{2,1,0:T(8,128)(2,1)} %get-tuple-element.30), channel_id=1, source_target_pairs={{0,40},{8,32},{16,56},{24,48},{32,8},{40,0},{48,24},{56,16},{1,41}... | collective-permute-start | bytes 737288 | tf_op jit(solution)/shard_map/ppermute | solution.py:596
  19.6 23.5 %copy-start.1 = (bf16[12,80,128]{2,1,0:T(8,128)(2,1)}, bf16[12,80,128]{2,1,0:T(8,128)(2,1)S(1)}, u32[]{:S(2)}) copy-start(bf16[12,80,128]{2,1,0:T(8,128)(2,1)S(1)} %collective-permute-done.1.refs_2_.rest_2_) | copy-start | bytes 737284
  19.6 20.0 %collective-permute-start.5 = (bf16[12,80,128]{2,1,0:T(8,128)(2,1)}, bf16[12,80,128]{2,1,0:T(8,128)(2,1)S(1)}, u32[]{:S(2)}, u32[]{:S(2)}) collective-permute-start(bf16[12,80,128]{2,1,0:T(8,128)(2,1)} %get-tuple-element.31), channel_id=1, source_target_pairs={{0,48},{8,56},{16,32},{24,40},{32,16},{40,24},{48,0},{56,8},{1,49}... | collective-permute-start | bytes 737288 | tf_op jit(solution)/shard_map/ppermute | solution.py:596
  24.1 19.1 %copy-start.2 = (bf16[12,80,128]{2,1,0:T(8,128)(2,1)}, bf16[12,80,128]{2,1,0:T(8,128)(2,1)S(1)}, u32[]{:S(2)}) copy-start(bf16[12,80,128]{2,1,0:T(8,128)(2,1)S(1)} %collective-permute-done.2.refs_3_.rest_3_) | copy-start | bytes 737284
  24.1 19.1 %collective-permute-start.6 = (bf16[12,80,128]{2,1,0:T(8,128)(2,1)}, bf16[12,80,128]{2,1,0:T(8,128)(2,1)S(1)}, u32[]{:S(2)}, u32[]{:S(2)}) collective-permute-start(bf16[12,80,128]{2,1,0:T(8,128)(2,1)} %get-tuple-element.32), channel_id=1, source_target_pairs={{0,56},{8,48},{16,40},{24,32},{32,24},{40,16},{48,8},{56,0},{1,57}... | collective-permute-start | bytes 737288 | tf_op jit(solution)/shard_map/ppermute | solution.py:596
  32.7 10.5 %copy-start.3 = (bf16[12,80,128]{2,1,0:T(8,128)(2,1)}, bf16[12,80,128]{2,1,0:T(8,128)(2,1)S(1)}, u32[]{:S(2)}) copy-start(bf16[12,80,128]{2,1,0:T(8,128)(2,1)S(1)} %collective-permute-done.3.refs_4_.rest_4_) | copy-start | bytes 737284
  36.9 6.3 %copy-start.4 = (bf16[12,80,128]{2,1,0:T(8,128)(2,1)}, bf16[12,80,128]{2,1,0:T(8,128)(2,1)S(1)}, u32[]{:S(2)}) copy-start(bf16[12,80,128]{2,1,0:T(8,128)(2,1)S(1)} %collective-permute-done.4.refs_5_.rest_5_) | copy-start | bytes 737284
  39.6 3.6 %copy-start.5 = (bf16[12,80,128]{2,1,0:T(8,128)(2,1)}, bf16[12,80,128]{2,1,0:T(8,128)(2,1)S(1)}, u32[]{:S(2)}) copy-start(bf16[12,80,128]{2,1,0:T(8,128)(2,1)S(1)} %collective-permute-done.5.refs_6_.rest_6_) | copy-start | bytes 737284
  43.1 0.7 copy-start.6
  45.6 17.8 %collective-permute-start.15 = (bf16[8,80,128]{2,1,0:T(8,128)(2,1)}, bf16[8,80,128]{2,1,0:T(8,128)(2,1)S(1)}, u32[]{:S(2)}, u32[]{:S(2)}) collective-permute-start(bf16[8,80,128]{2,1,0:T(8,128)(2,1)} %get-tuple-element.41), channel_id=1, source_target_pairs={{0,64},{1,65},{2,66},{3,67},{4,68},{5,69},{6,70},{7,71},{64,1},{65... | collective-permute-start | bytes 491528 | tf_op jit(solution)/shard_map/ppermute | solution.py:604
  47.6 18.4 %collective-permute-start.16 = (bf16[8,80,128]{2,1,0:T(8,128)(2,1)}, bf16[8,80,128]{2,1,0:T(8,128)(2,1)S(1)}, u32[]{:S(2)}, u32[]{:S(2)}) collective-permute-start(bf16[8,80,128]{2,1,0:T(8,128)(2,1)} %get-tuple-element.42), channel_id=1, source_target_pairs={{64,0},{65,1},{66,2},{67,3},{68,4},{69,5},{70,6},{71,7},{1,64},{2,... | collective-permute-start | bytes 491528 | tf_op jit(solution)/shard_map/ppermute | solution.py:605
  51.5 0.9 copy-start.7
  61.5 5.2 %collective-permute-start.8 = (bf16[560,128]{1,0:T(8,128)(2,1)}, bf16[560,128]{1,0:T(8,128)(2,1)S(1)}, u32[]{:S(2)}, u32[]{:S(2)}) collective-permute-start(bf16[560,128]{1,0:T(8,128)(2,1)} %get-tuple-element.34), channel_id=1, source_target_pairs={{0,8},{8,0},{16,24},{24,16},{32,40},{40,32},{48,56},{56,48},{1,9},... | collective-permute-start | bytes 430088 | tf_op jit(solution)/shard_map/ppermute | solution.py:596
  61.6 7.9 %collective-permute-start.9 = (bf16[560,128]{1,0:T(8,128)(2,1)}, bf16[560,128]{1,0:T(8,128)(2,1)S(1)}, u32[]{:S(2)}, u32[]{:S(2)}) collective-permute-start(bf16[560,128]{1,0:T(8,128)(2,1)} %get-tuple-element.35), channel_id=1, source_target_pairs={{0,16},{8,24},{16,0},{24,8},{32,48},{40,56},{48,32},{56,40},{1,17}... | collective-permute-start | bytes 430088 | tf_op jit(solution)/shard_map/ppermute | solution.py:596
  61.8 8.7 %collective-permute-start.10 = (bf16[560,128]{1,0:T(8,128)(2,1)}, bf16[560,128]{1,0:T(8,128)(2,1)S(1)}, u32[]{:S(2)}, u32[]{:S(2)}) collective-permute-start(bf16[560,128]{1,0:T(8,128)(2,1)} %get-tuple-element.36), channel_id=1, source_target_pairs={{0,24},{8,16},{16,8},{24,0},{32,56},{40,48},{48,40},{56,32},{1,25}... | collective-permute-start | bytes 430088 | tf_op jit(solution)/shard_map/ppermute | solution.py:596
  63.5 19.4 %copy-start.8 = (bf16[8,80,128]{2,1,0:T(8,128)(2,1)}, bf16[8,80,128]{2,1,0:T(8,128)(2,1)S(1)}, u32[]{:S(2)}) copy-start(bf16[8,80,128]{2,1,0:T(8,128)(2,1)S(1)} %collective-permute-done.15.rest_16_) | copy-start | bytes 491524
  63.5 13.5 %collective-permute-start.11 = (bf16[560,128]{1,0:T(8,128)(2,1)}, bf16[560,128]{1,0:T(8,128)(2,1)S(1)}, u32[]{:S(2)}, u32[]{:S(2)}) collective-permute-start(bf16[560,128]{1,0:T(8,128)(2,1)} %get-tuple-element.37), channel_id=1, source_target_pairs={{0,32},{8,40},{16,48},{24,56},{32,0},{40,8},{48,16},{56,24},{1,33}... | collective-permute-start | bytes 430088 | tf_op jit(solution)/shard_map/ppermute | solution.py:596
  66.0 16.9 %copy-start.9 = (bf16[8,80,128]{2,1,0:T(8,128)(2,1)}, bf16[8,80,128]{2,1,0:T(8,128)(2,1)S(1)}, u32[]{:S(2)}) copy-start(bf16[8,80,128]{2,1,0:T(8,128)(2,1)S(1)} %collective-permute-done.16.rest_17_) | copy-start | bytes 491524
  66.0 12.3 %collective-permute-start.12 = (bf16[560,128]{1,0:T(8,128)(2,1)}, bf16[560,128]{1,0:T(8,128)(2,1)S(1)}, u32[]{:S(2)}, u32[]{:S(2)}) collective-permute-start(bf16[560,128]{1,0:T(8,128)(2,1)} %get-tuple-element.38), channel_id=1, source_target_pairs={{0,40},{8,32},{16,56},{24,48},{32,8},{40,0},{48,24},{56,16},{1,41}... | collective-permute-start | bytes 430088 | tf_op jit(solution)/shard_map/ppermute | solution.py:596
  66.7 16.2 %copy-start.10 = (bf16[560,128]{1,0:T(8,128)(2,1)}, bf16[560,128]{1,0:T(8,128)(2,1)S(1)}, u32[]{:S(2)}) copy-start(bf16[560,128]{1,0:T(8,128)(2,1)S(1)} %collective-permute-done.8.rest_9_) | copy-start | bytes 430084
  66.7 14.2 %collective-permute-start.13 = (bf16[560,128]{1,0:T(8,128)(2,1)}, bf16[560,128]{1,0:T(8,128)(2,1)S(1)}, u32[]{:S(2)}, u32[]{:S(2)}) collective-permute-start(bf16[560,128]{1,0:T(8,128)(2,1)} %get-tuple-element.39), channel_id=1, source_target_pairs={{0,48},{8,56},{16,32},{24,40},{32,16},{40,24},{48,0},{56,8},{1,49}... | collective-permute-start | bytes 430088 | tf_op jit(solution)/shard_map/ppermute | solution.py:596
  69.5 13.4 %copy-start.11 = (bf16[560,128]{1,0:T(8,128)(2,1)}, bf16[560,128]{1,0:T(8,128)(2,1)S(1)}, u32[]{:S(2)}) copy-start(bf16[560,128]{1,0:T(8,128)(2,1)S(1)} %collective-permute-done.9.rest_10_) | copy-start | bytes 430084
  69.5 13.4 %collective-permute-start.14 = (bf16[560,128]{1,0:T(8,128)(2,1)}, bf16[560,128]{1,0:T(8,128)(2,1)S(1)}, u32[]{:S(2)}, u32[]{:S(2)}) collective-permute-start(bf16[560,128]{1,0:T(8,128)(2,1)} %get-tuple-element.40), channel_id=1, source_target_pairs={{0,56},{8,48},{16,40},{24,32},{32,24},{40,16},{48,8},{56,0},{1,57}... | collective-permute-start | bytes 430088 | tf_op jit(solution)/shard_map/ppermute | solution.py:596
  70.5 12.4 %copy-start.12 = (bf16[560,128]{1,0:T(8,128)(2,1)}, bf16[560,128]{1,0:T(8,128)(2,1)S(1)}, u32[]{:S(2)}) copy-start(bf16[560,128]{1,0:T(8,128)(2,1)S(1)} %collective-permute-done.10.rest_11_) | copy-start | bytes 430084
  77.0 5.9 %copy-start.13 = (bf16[560,128]{1,0:T(8,128)(2,1)}, bf16[560,128]{1,0:T(8,128)(2,1)S(1)}, u32[]{:S(2)}) copy-start(bf16[560,128]{1,0:T(8,128)(2,1)S(1)} %collective-permute-done.11.rest_12_) | copy-start | bytes 430084
  78.3 4.6 %copy-start.14 = (bf16[560,128]{1,0:T(8,128)(2,1)}, bf16[560,128]{1,0:T(8,128)(2,1)S(1)}, u32[]{:S(2)}) copy-start(bf16[560,128]{1,0:T(8,128)(2,1)S(1)} %collective-permute-done.12.rest_13_) | copy-start | bytes 430084
  80.9 2.0 %copy-start.15 = (bf16[560,128]{1,0:T(8,128)(2,1)}, bf16[560,128]{1,0:T(8,128)(2,1)S(1)}, u32[]{:S(2)}) copy-start(bf16[560,128]{1,0:T(8,128)(2,1)S(1)} %collective-permute-done.13.rest_14_) | copy-start | bytes 430084
  82.9 0.6 copy-start.16
  93.3 6.5 %collective-permute-start.17 = (f16[72,128]{1,0:T(8,128)(2,1)S(1)}, f16[72,128]{1,0:T(8,128)(2,1)S(1)}, u32[]{:S(2)}, u32[]{:S(2)}) collective-permute-start(f16[72,128]{1,0:T(8,128)(2,1)S(1)} %convert_element_type.55), channel_id=1, source_target_pairs={{64,1},{65,2},{66,3},{67,4},{68,5},{69,6},{70,7},{1,64},{2,65},{3,... | collective-permute-start | bytes 55304 | tf_op jit(solution)/shard_map/ppermute | solution.py:607
  100.5 9.2 %collective-permute-start.29 = (f16[504,128]{1,0:T(8,128)(2,1)S(1)}, f16[504,128]{1,0:T(8,128)(2,1)S(1)}, u32[]{:S(2)}, u32[]{:S(2)}) collective-permute-start(f16[504,128]{1,0:T(8,128)(2,1)S(1)} %get-tuple-element.45), channel_id=1, source_target_pairs={{0,96},{8,104},{16,112},{24,120},{32,64},{40,72},{48,80},{56,88},{... | collective-permute-start | bytes 387080 | tf_op jit(solution)/shard_map/ppermute | solution.py:617
  104.2 7.0 %collective-permute-start.27 = (f16[504,128]{1,0:T(8,128)(2,1)S(1)}, f16[504,128]{1,0:T(8,128)(2,1)S(1)}, u32[]{:S(2)}, u32[]{:S(2)}) collective-permute-start(f16[504,128]{1,0:T(8,128)(2,1)S(1)} %get-tuple-element.45), channel_id=1, source_target_pairs={{0,80},{8,88},{16,64},{24,72},{32,112},{40,120},{48,96},{56,104},{... | collective-permute-start | bytes 387080 | tf_op jit(solution)/shard_map/ppermute | solution.py:617
  104.6 8.7 %collective-permute-start.25 = (f16[504,128]{1,0:T(8,128)(2,1)S(1)}, f16[504,128]{1,0:T(8,128)(2,1)S(1)}, u32[]{:S(2)}, u32[]{:S(2)}) collective-permute-start(f16[504,128]{1,0:T(8,128)(2,1)S(1)} %get-tuple-element.45), channel_id=1, source_target_pairs={{0,64},{8,72},{16,80},{24,88},{32,96},{40,104},{48,112},{56,120},{... | collective-permute-start | bytes 387080 | tf_op jit(solution)/shard_map/ppermute | solution.py:617
  107.1 9.8 %collective-permute-start.23 = (f16[504,128]{1,0:T(8,128)(2,1)S(1)}, f16[504,128]{1,0:T(8,128)(2,1)S(1)}, u32[]{:S(2)}, u32[]{:S(2)}) collective-permute-start(f16[504,128]{1,0:T(8,128)(2,1)S(1)} %get-tuple-element.45), channel_id=1, source_target_pairs={{0,48},{8,56},{16,32},{24,40},{32,16},{40,24},{48,0},{56,8},{64,11... | collective-permute-start | bytes 387080 | tf_op jit(solution)/shard_map/ppermute | solution.py:617
  108.0 8.9 %collective-permute-start.21 = (f16[504,128]{1,0:T(8,128)(2,1)S(1)}, f16[504,128]{1,0:T(8,128)(2,1)S(1)}, u32[]{:S(2)}, u32[]{:S(2)}) collective-permute-start(f16[504,128]{1,0:T(8,128)(2,1)S(1)} %get-tuple-element.45), channel_id=1, source_target_pairs={{0,32},{8,40},{16,48},{24,56},{32,0},{40,8},{48,16},{56,24},{64,96... | collective-permute-start | bytes 387080 | tf_op jit(solution)/shard_map/ppermute | solution.py:617
  109.8 7.7 %collective-permute-start.19 = (f16[504,128]{1,0:T(8,128)(2,1)S(1)}, f16[504,128]{1,0:T(8,128)(2,1)S(1)}, u32[]{:S(2)}, u32[]{:S(2)}) collective-permute-start(f16[504,128]{1,0:T(8,128)(2,1)S(1)} %get-tuple-element.45), channel_id=1, source_target_pairs={{0,16},{8,24},{16,0},{24,8},{32,48},{40,56},{48,32},{56,40},{64,80... | collective-permute-start | bytes 387080 | tf_op jit(solution)/shard_map/ppermute | solution.py:617
  111.2 6.3 %collective-permute-start.18 = (f16[504,128]{1,0:T(8,128)(2,1)S(1)}, f16[504,128]{1,0:T(8,128)(2,1)S(1)}, u32[]{:S(2)}, u32[]{:S(2)}) collective-permute-start(f16[504,128]{1,0:T(8,128)(2,1)S(1)} %get-tuple-element.45), channel_id=1, source_target_pairs={{0,8},{8,0},{16,24},{24,16},{32,40},{40,32},{48,56},{56,48},{1,9},... | collective-permute-start | bytes 387080 | tf_op jit(solution)/shard_map/ppermute | solution.py:618
  113.4 7.5 %collective-permute-start.31 = (f16[504,128]{1,0:T(8,128)(2,1)S(1)}, f16[504,128]{1,0:T(8,128)(2,1)S(1)}, u32[]{:S(2)}, u32[]{:S(2)}) collective-permute-start(f16[504,128]{1,0:T(8,128)(2,1)S(1)} %get-tuple-element.45), channel_id=1, source_target_pairs={{0,112},{8,120},{16,96},{24,104},{32,80},{40,88},{48,64},{56,72},{... | collective-permute-start | bytes 387080 | tf_op jit(solution)/shard_map/ppermute | solution.py:617
  116.9 3.9 %collective-permute-start.30 = (f16[504,128]{1,0:T(8,128)(2,1)S(1)}, f16[504,128]{1,0:T(8,128)(2,1)S(1)}, u32[]{:S(2)}, u32[]{:S(2)}) collective-permute-start(f16[504,128]{1,0:T(8,128)(2,1)S(1)} %collective-permute-done.29), channel_id=1, source_target_pairs={{0,8},{8,0},{16,24},{24,16},{32,40},{40,32},{48,56},{56,48},{1,9},... | collective-permute-start | bytes 387080 | tf_op jit(solution)/shard_map/ppermute | solution.py:618
  116.9 4.4 %collective-permute-start.28 = (f16[504,128]{1,0:T(8,128)(2,1)S(1)}, f16[504,128]{1,0:T(8,128)(2,1)S(1)}, u32[]{:S(2)}, u32[]{:S(2)}) collective-permute-start(f16[504,128]{1,0:T(8,128)(2,1)S(1)} %collective-permute-done.27), channel_id=1, source_target_pairs={{0,8},{8,0},{16,24},{24,16},{32,40},{40,32},{48,56},{56,48},{1,9},... | collective-permute-start | bytes 387080 | tf_op jit(solution)/shard_map/ppermute | solution.py:618
  117.4 11.2 %collective-permute-start.26 = (f16[504,128]{1,0:T(8,128)(2,1)S(1)}, f16[504,128]{1,0:T(8,128)(2,1)S(1)}, u32[]{:S(2)}, u32[]{:S(2)}) collective-permute-start(f16[504,128]{1,0:T(8,128)(2,1)S(1)} %collective-permute-done.25), channel_id=1, source_target_pairs={{0,8},{8,0},{16,24},{24,16},{32,40},{40,32},{48,56},{56,48},{1,9},... | collective-permute-start | bytes 387080 | tf_op jit(solution)/shard_map/ppermute | solution.py:618
  117.5 11.9 %collective-permute-start.24 = (f16[504,128]{1,0:T(8,128)(2,1)S(1)}, f16[504,128]{1,0:T(8,128)(2,1)S(1)}, u32[]{:S(2)}, u32[]{:S(2)}) collective-permute-start(f16[504,128]{1,0:T(8,128)(2,1)S(1)} %collective-permute-done.23), channel_id=1, source_target_pairs={{0,8},{8,0},{16,24},{24,16},{32,40},{40,32},{48,56},{56,48},{1,9},... | collective-permute-start | bytes 387080 | tf_op jit(solution)/shard_map/ppermute | solution.py:618
  120.8 9.3 %collective-permute-start.22 = (f16[504,128]{1,0:T(8,128)(2,1)S(1)}, f16[504,128]{1,0:T(8,128)(2,1)S(1)}, u32[]{:S(2)}, u32[]{:S(2)}) collective-permute-start(f16[504,128]{1,0:T(8,128)(2,1)S(1)} %collective-permute-done.21), channel_id=1, source_target_pairs={{0,8},{8,0},{16,24},{24,16},{32,40},{40,32},{48,56},{56,48},{1,9},... | collective-permute-start | bytes 387080 | tf_op jit(solution)/shard_map/ppermute | solution.py:618
  120.8 10.0 %collective-permute-start.20 = (f16[504,128]{1,0:T(8,128)(2,1)S(1)}, f16[504,128]{1,0:T(8,128)(2,1)S(1)}, u32[]{:S(2)}, u32[]{:S(2)}) collective-permute-start(f16[504,128]{1,0:T(8,128)(2,1)S(1)} %collective-permute-done.19), channel_id=1, source_target_pairs={{0,8},{8,0},{16,24},{24,16},{32,40},{40,32},{48,56},{56,48},{1,9},... | collective-permute-start | bytes 387080 | tf_op jit(solution)/shard_map/ppermute | solution.py:618
  121.4 10.2 %collective-permute-start.32 = (f16[504,128]{1,0:T(8,128)(2,1)S(1)}, f16[504,128]{1,0:T(8,128)(2,1)S(1)}, u32[]{:S(2)}, u32[]{:S(2)}) collective-permute-start(f16[504,128]{1,0:T(8,128)(2,1)S(1)} %collective-permute-done.31), channel_id=1, source_target_pairs={{0,8},{8,0},{16,24},{24,16},{32,40},{40,32},{48,56},{56,48},{1,9},... | collective-permute-start | bytes 387080 | tf_op jit(solution)/shard_map/ppermute | solution.py:618

commit v6 on v1

--- a/solution.py
+++ b/solution.py
@@ -16,6 +16,7 @@
 VR = CZ * CW
 VROWS = 5 * VR
 PROWS = 80
+SPREAD = (1, 3, 7, 5, 2, 6, 4)
 SCALE = 128.0
 
 
@@ -266,11 +267,11 @@
         copies.append(
             pltpu.make_async_copy(planes[k], image.at[k, 1 : HZ + 1], sems.at[k])
         )
-        copies.append(pltpu.make_async_copy(fields[k], field.at[k], sems.at[8 + k]))
-    for copy in copies:
+    first = [pltpu.make_async_copy(fields[k], field.at[k], sems.at[8 + k]) for k in range(8)]
+    for copy in first + copies:
         copy.start()
     acc[...] = jnp.zeros_like(acc)
-    for copy in copies:
+    for copy in first:
         copy.wait()
     lane = lax.broadcasted_iota(jnp.int32, (CY, 128), 1)
     sub = lax.broadcasted_iota(jnp.int32, (CY, 128), 0)
@@ -350,6 +351,8 @@
             acc[1, rows] += warped[2]
 
     interpolate(0, even)
+    for copy in copies:
+        copy.wait()
 
     def turn(step, carry):
         interpolate(2 * step + 1, odd)
@@ -418,10 +421,10 @@
     tail = HZ * 3 // 2
     for peer in range(8):
         rows = slice(8 + CY * peer, 8 + CY * (peer + 1))
-        slots = [(half ^ level) * 8 + (peer ^ me) for half in range(2)]
 
         def block(half, index):
-            return chunks[slots[half], CY * index : CY * (index + 1)]
+            slot = (half ^ level) * 8 + (peer ^ me)
+            return chunks[slot, CY * index : CY * (index + 1)]
 
         for half in range(2):
             for z in range(HZ):
@@ -473,9 +476,8 @@
             around = held[z - 1, start : start + count] + held[z + 1, start : start + count]
             around += held[z, start - 1 : start - 1 + count] + held[z, start + 1 : start + 1 + count]
             around += sums[b, start - 8 : start - 8 + count]
-            done.append(
-                (0.1 * scale) * held[z, start : start + count] + (0.15 * scale) * around
-            )
+            value = around + (2.0 / 3.0) * held[z, start : start + count]
+            done.append(value if scale is None else scale * value)
         return done
 
     def sweep(planes, store, scale, after):
@@ -500,7 +502,7 @@
         flat2[index + 16, start : start + count] = done[1]
         pair2[index, start : start + count] = done[2]
 
-    sweep((flat, pair), first, 1.0, lambda index: None)
+    sweep((flat, pair), first, None, lambda index: None)
     whole = lax.broadcasted_iota(jnp.int32, (size, 128), 1)
 
     @pl.when(zone == 0)
@@ -534,7 +536,7 @@
         def _():
             emit(index + 11).start()
 
-    sweep((flat2, pair2), second, 1.0 / SCALE, depart)
+    sweep((flat2, pair2), second, 0.15 * 0.15 / SCALE, depart)
 
     def finish(z, carry):
         emit(z).wait()
@@ -586,7 +588,7 @@
 
     def spread(parts):
         arrived = {0: parts[0]}
-        for k in (3, 7, 5, 2, 6, 4, 1):
+        for k in SPREAD:
             arrived[k] = lax.ppermute(parts[k], "subj", [(i, i ^ k) for i in range(8)])
         return [arrived[k] for k in range(8)]
 
@@ -600,14 +602,15 @@
     chunk, edge = warp(info, assign, planes, fields, below, above)
     edge = lax.ppermute(edge.astype(jnp.float16), nearest, cross)
     chunk = jnp.concatenate([chunk.astype(jnp.float16), edge], axis=0)
-    mine = {(0, 0): chunk}
-    for far, step in ((0, 1), (0, 3), (1, 0), (0, 2), (1, 1), (1, 3), (1, 2)):
-        perm = [(8 * a + i, 8 * (a ^ far) + (i ^ (2 * step))) for a in range(2) for i in range(8)]
-        mine[far, step] = lax.ppermute(chunk, ("level", "subj"), perm)
     gathered = []
     for far in range(2):
         for step in range(4):
-            part = mine[far, step]
+            part = chunk
+            if far or step:
+                perm = [
+                    (8 * a + i, 8 * (a ^ far) + (i ^ (2 * step))) for a in range(2) for i in range(8)
+                ]
+                part = lax.ppermute(chunk, ("level", "subj"), perm)
             gathered += [part, lax.ppermute(part, "subj", [(i, i ^ 1) for i in range(8)])]
     chunks = jnp.stack(gathered).astype(F32)
     return relax(info, chunks)

time: 137 us -> 137 us (level)
  no operation moved by 1% of the time
where the time goes in v6:
time: 137 us; the launch traced here: 135 us
  starting transfers between devices  47.4 us (35%)
  waiting for transfers between devices  43.6 us (32%)
  Pallas kernels  34.6 us (25%)
  local copies, waits for them, and re-layouts  4.74 us (3%)
  other arithmetic  4.57 us (3%)
    ppermute x14, waiting for transfers between devices, spread(): arrived[k] = lax.ppermute(parts[k], 'subj', [(i, i ^ k) for i in range(8)])  34.6 us
    ppermute x14, starting transfers between devices, spread(): arrived[k] = lax.ppermute(parts[k], 'subj', [(i, i ^ k) for i in range(8)])  14.3 us
    ppermute x7, starting transfers between devices, update(): part = lax.ppermute(chunk, ('level', 'subj'), perm)  13.1 us
    pallas_call x1, Pallas kernels, relax(): pl.pallas_call(relax_kernel, grid=(), in_specs=[pl.BlockSpec(memory_space...  10.9 us
    pallas_call x1, Pallas kernels, blur(): pl.pallas_call(blur_kernel, grid=(), in_specs=[pl.BlockSpec(memory_space=...  9.05 us
    pallas_call x1, Pallas kernels, warp(): pl.pallas_call(warp_kernel, grid=(), in_specs=[smem, smem, vmem, vmem, vm...  8.95 us
    ppermute x7, waiting for transfers between devices, update(): part = lax.ppermute(chunk, ('level', 'subj'), perm)  5.54 us
    ppermute x1, starting transfers between devices, update(): rim = lax.ppermute(rim, nearest, outward)  5.16 us
  transfers between devices with their start and end apart: 34, of which 15 were waited for; matrix products, arithmetic and copies ran while one was open for 2% of the time, Pallas kernels for 8%

profile of v6, /device:TPU:96, one launch (start us, length us, event | category | flops | bytes accessed | tf_op | source)
XLA Modules:
  0.0 135.4 jit_solution(18432607227314428459)
XLA Ops:
  0.0 0.6 pad_add_fusion.info
  0.6 3.9 %pack_images.1 = (bf16[12,80,128]{2,1,0:T(8,128)(2,1)}, bf16[12,80,128]{2,1,0:T(8,128)(2,1)}, bf16[12,80,128]{2,1,0:T(8,128)(2,1)}, bf16[12,80,128]{2,1,0:T(8,12...) custom-call(s32[3]{0:T(128)} %pad_add_fusion.info, ...), custom_call_target="tpu_custom_call" | custom-call | tf_op jit(solution)/shard_map/pack_images/pallas_call | solution.py:106
  4.4 0.1 collective-permute-start
  4.5 1.7 %collective-permute-start.1 = (bf16[12,80,128]{2,1,0:T(8,128)(2,1)}, bf16[12,80,128]{2,1,0:T(8,128)(2,1)S(1)}, u32[]{:S(2)}, u32[]{:S(2)}) collective-permute-start(bf16[12,80,128]{2,1,0:T(8,128)(2,1)} %get-tuple-element.27), channel_id=1, source_target_pairs={{0,16},{8,24},{16,0},{24,8},{32,48},{40,56},{48,32},{56,40},{1,17}... | collective-permute-start | bytes 737288 | tf_op jit(solution)/shard_map/ppermute | solution.py:592
  6.2 0.2 collective-permute-start.2
  6.4 3.2 %collective-permute-start.3 = (bf16[12,80,128]{2,1,0:T(8,128)(2,1)}, bf16[12,80,128]{2,1,0:T(8,128)(2,1)S(1)}, u32[]{:S(2)}, u32[]{:S(2)}) collective-permute-start(bf16[12,80,128]{2,1,0:T(8,128)(2,1)} %get-tuple-element.29), channel_id=1, source_target_pairs={{0,32},{8,40},{16,48},{24,56},{32,0},{40,8},{48,16},{56,24},{1,33}... | collective-permute-start | bytes 737288 | tf_op jit(solution)/shard_map/ppermute | solution.py:592
  9.6 1.2 constant_dynamic-slice_fusion
  10.8 3.2 %collective-permute-start.8 = (f32[1,3,3,96,96]{4,3,2,1,0:T(8,128)S(1)}, f32[1,3,3,96,96]{4,3,2,1,0:T(8,128)S(1)}, u32[]{:S(2)}, u32[]{:S(2)}) collective-permute-start(f32[1,3,3,96,96]{4,3,2,1,0:T(8,128)S(1)} %get-tuple-element.45), channel_id=1, source_target_pairs={{64,1},{65,2},{66,3},{67,4},{68,5},{69,6},{70,7},{1,64},{2,65},{3,... | collective-permute-start | bytes 995336 | tf_op jit(solution)/shard_map/ppermute | solution.py:587
  14.0 0.0 collective-permute-done.refs_1_.rest_1_
  14.0 5.2 %collective-permute-start.7 = (f32[1,3,3,96,96]{4,3,2,1,0:T(8,128)S(1)}, f32[1,3,3,96,96]{4,3,2,1,0:T(8,128)S(1)}, u32[]{:S(2)}, u32[]{:S(2)}) collective-permute-start(f32[1,3,3,96,96]{4,3,2,1,0:T(8,128)S(1)} %get-tuple-element.46), channel_id=1, source_target_pairs={{0,1},{1,2},{2,3},{3,4},{4,5},{5,6},{6,7},{65,64},{66,65},{67,66},... | collective-permute-start | bytes 995336 | tf_op jit(solution)/shard_map/ppermute | solution.py:586
  19.2 0.0 collective-permute-done.1.refs_2_.rest_2_
  19.2 0.1 collective-permute-start.4
  19.3 0.0 collective-permute-done.2.refs_3_.rest_3_
  19.3 2.5 %collective-permute-start.5 = (bf16[12,80,128]{2,1,0:T(8,128)(2,1)}, bf16[12,80,128]{2,1,0:T(8,128)(2,1)S(1)}, u32[]{:S(2)}, u32[]{:S(2)}) collective-permute-start(bf16[12,80,128]{2,1,0:T(8,128)(2,1)} %get-tuple-element.31), channel_id=1, source_target_pairs={{0,48},{8,56},{16,32},{24,40},{32,16},{40,24},{48,0},{56,8},{1,49}... | collective-permute-start | bytes 737288 | tf_op jit(solution)/shard_map/ppermute | solution.py:592
  21.8 4.9 %collective-permute-done.3.refs_4_.rest_4_ = bf16[12,80,128]{2,1,0:T(8,128)(2,1)S(1)} collective-permute-done((bf16[12,80,128]{2,1,0:T(8,128)(2,1)}, bf16[12,80,128]{2,1,0:T(8,128)(2,1)S(1)}, u32[]{:S(2)}, u32[]{:S(2)}) %collective-permute-start.3) | collective-permute-done | bytes 245792 | tf_op jit(solution)/shard_map/ppermute | solution.py:592
  26.7 0.0 collective-permute-start.6
  26.7 4.2 %collective-permute-done.4.refs_5_.rest_5_ = bf16[12,80,128]{2,1,0:T(8,128)(2,1)S(1)} collective-permute-done((bf16[12,80,128]{2,1,0:T(8,128)(2,1)}, bf16[12,80,128]{2,1,0:T(8,128)(2,1)S(1)}, u32[]{:S(2)}, u32[]{:S(2)}) %collective-permute-start.4) | collective-permute-done | bytes 245792 | tf_op jit(solution)/shard_map/ppermute | solution.py:592
  30.9 5.8 %collective-permute-done.5.refs_6_.rest_6_ = bf16[12,80,128]{2,1,0:T(8,128)(2,1)S(1)} collective-permute-done((bf16[12,80,128]{2,1,0:T(8,128)(2,1)}, bf16[12,80,128]{2,1,0:T(8,128)(2,1)S(1)}, u32[]{:S(2)}, u32[]{:S(2)}) %collective-permute-start.5) | collective-permute-done | bytes 245792 | tf_op jit(solution)/shard_map/ppermute | solution.py:592
  36.7 5.2 %collective-permute-done.6.refs_7_.rest_7_ = bf16[12,80,128]{2,1,0:T(8,128)(2,1)S(1)} collective-permute-done((bf16[12,80,128]{2,1,0:T(8,128)(2,1)}, bf16[12,80,128]{2,1,0:T(8,128)(2,1)S(1)}, u32[]{:S(2)}, u32[]{:S(2)}) %collective-permute-start.6) | collective-permute-done | bytes 245792 | tf_op jit(solution)/shard_map/ppermute | solution.py:592
  41.9 0.7 copy-done.6
  42.5 1.8 %cut_edges.1 = (bf16[8,80,128]{2,1,0:T(8,128)(2,1)}, bf16[8,80,128]{2,1,0:T(8,128)(2,1)}) custom-call(bf16[12,80,128]{2,1,0:T(8,128)(2,1)} %get-tuple-element.25.refs_0_.rest_0_, bf16[12,80,128]{2,1,0:T(8,128)(2,1)} %copy-done, bf16[12,80,128]{2,1,0:T(8,128)(2,1)} %copy-done.1, bf16[12,80,128]{2,1,0:T(8,128)(2,1)} %copy-done.2, ...), custom_call_target="tpu_custom_call" | custom-call | tf_op jit(solution)/shard_map/cut_edges/pallas_call | solution.py:241
  44.3 3.3 %collective-permute-start.16 = (bf16[8,80,128]{2,1,0:T(8,128)(2,1)}, bf16[8,80,128]{2,1,0:T(8,128)(2,1)S(1)}, u32[]{:S(2)}, u32[]{:S(2)}) collective-permute-start(bf16[8,80,128]{2,1,0:T(8,128)(2,1)} %get-tuple-element.41), channel_id=1, source_target_pairs={{0,64},{1,65},{2,66},{3,67},{4,68},{5,69},{6,70},{7,71},{64,1},{65... | collective-permute-start | bytes 491528 | tf_op jit(solution)/shard_map/ppermute | solution.py:600
  47.6 2.5 %collective-permute-start.17 = (bf16[8,80,128]{2,1,0:T(8,128)(2,1)}, bf16[8,80,128]{2,1,0:T(8,128)(2,1)S(1)}, u32[]{:S(2)}, u32[]{:S(2)}) collective-permute-start(bf16[8,80,128]{2,1,0:T(8,128)(2,1)} %get-tuple-element.42), channel_id=1, source_target_pairs={{64,0},{65,1},{66,2},{67,3},{68,4},{69,5},{70,6},{71,7},{1,64},{2,... | collective-permute-start | bytes 491528 | tf_op jit(solution)/shard_map/ppermute | solution.py:601
  50.2 0.0 collective-permute-done.8.other
  50.2 0.8 copy-done.7
  51.0 0.8 copy-done.8
  51.7 9.1 %blur_momenta.1 = (bf16[560,128]{1,0:T(8,128)(2,1)}, bf16[560,128]{1,0:T(8,128)(2,1)}, bf16[560,128]{1,0:T(8,128)(2,1)}, bf16[560,128]{1,0:T(8,128)(2,1)}, bf16[...) custom-call(s32[3]{0:T(128)} %pad_add_fusion.info, ...), custom_call_target="tpu_custom_call" | custom-call | tf_op jit(solution)/shard_map/blur_momenta/pallas_call | solution.py:192
  60.8 0.1 collective-permute-start.9
  60.9 0.3 collective-permute-start.10
  61.2 1.6 %collective-permute-start.11 = (bf16[560,128]{1,0:T(8,128)(2,1)}, bf16[560,128]{1,0:T(8,128)(2,1)S(1)}, u32[]{:S(2)}, u32[]{:S(2)}) collective-permute-start(bf16[560,128]{1,0:T(8,128)(2,1)} %get-tuple-element.36), channel_id=1, source_target_pairs={{0,24},{8,16},{16,8},{24,0},{32,56},{40,48},{48,40},{56,32},{1,25}... | collective-permute-start | bytes 430088 | tf_op jit(solution)/shard_map/ppermute | solution.py:592
  62.8 0.7 collective-permute-start.12
  63.4 2.5 %collective-permute-start.13 = (bf16[560,128]{1,0:T(8,128)(2,1)}, bf16[560,128]{1,0:T(8,128)(2,1)S(1)}, u32[]{:S(2)}, u32[]{:S(2)}) collective-permute-start(bf16[560,128]{1,0:T(8,128)(2,1)} %get-tuple-element.38), channel_id=1, source_target_pairs={{0,40},{8,32},{16,56},{24,48},{32,8},{40,0},{48,24},{56,16},{1,41}... | collective-permute-start | bytes 430088 | tf_op jit(solution)/shard_map/ppermute | solution.py:592
  66.0 0.3 collective-permute-start.14
  66.3 1.6 %collective-permute-done.10.rest_10_ = bf16[560,128]{1,0:T(8,128)(2,1)S(1)} collective-permute-done((bf16[560,128]{1,0:T(8,128)(2,1)}, bf16[560,128]{1,0:T(8,128)(2,1)S(1)}, u32[]{:S(2)}, u32[]{:S(2)}) %collective-permute-start.10) | collective-permute-done | bytes 143392 | tf_op jit(solution)/shard_map/ppermute | solution.py:592
  67.8 1.2 collective-permute-start.15
  69.0 0.8 collective-permute-done.11.rest_11_
  69.8 4.0 %collective-permute-done.12.rest_12_ = bf16[560,128]{1,0:T(8,128)(2,1)S(1)} collective-permute-done((bf16[560,128]{1,0:T(8,128)(2,1)}, bf16[560,128]{1,0:T(8,128)(2,1)S(1)}, u32[]{:S(2)}, u32[]{:S(2)}) %collective-permute-start.12) | collective-permute-done | bytes 143392 | tf_op jit(solution)/shard_map/ppermute | solution.py:592
  73.8 2.0 %collective-permute-done.13.rest_13_ = bf16[560,128]{1,0:T(8,128)(2,1)S(1)} collective-permute-done((bf16[560,128]{1,0:T(8,128)(2,1)}, bf16[560,128]{1,0:T(8,128)(2,1)S(1)}, u32[]{:S(2)}, u32[]{:S(2)}) %collective-permute-start.13) | collective-permute-done | bytes 143392 | tf_op jit(solution)/shard_map/ppermute | solution.py:592
  75.8 3.6 %collective-permute-done.14.rest_14_ = bf16[560,128]{1,0:T(8,128)(2,1)S(1)} collective-permute-done((bf16[560,128]{1,0:T(8,128)(2,1)}, bf16[560,128]{1,0:T(8,128)(2,1)S(1)}, u32[]{:S(2)}, u32[]{:S(2)}) %collective-permute-start.14) | collective-permute-done | bytes 143392 | tf_op jit(solution)/shard_map/ppermute | solution.py:592
  79.4 2.7 %collective-permute-done.15.rest_15_ = bf16[560,128]{1,0:T(8,128)(2,1)S(1)} collective-permute-done((bf16[560,128]{1,0:T(8,128)(2,1)}, bf16[560,128]{1,0:T(8,128)(2,1)S(1)}, u32[]{:S(2)}, u32[]{:S(2)}) %collective-permute-start.15) | collective-permute-done | bytes 143392 | tf_op jit(solution)/shard_map/ppermute | solution.py:592
  82.1 0.6 copy-done.17
  82.7 8.9 %warp_sum.1 = (f32[432,128]{1,0:T(8,128)}, f32[72,128]{1,0:T(8,128)}) custom-call(s32[3]{0:T(128)} %pad_add_fusion.info, s32[16]{0:T(128)} %assign.1, bf16[288,112]{1,0:T(8,128)(2,1)} %constant.27.clone.zy, bf16[256,256]{1,0:T(8,128)(2,1)} %constant.28.clone.x0, bf16[256,256]{1,0:T(8,128)(2,1)} %constant.29.clone.x1, ...), custom_call_target="tpu_custom_call" | custom-call | tf_op jit(solution)/shard_map/warp_sum/pallas_call | solution.py:390
  91.7 0.8 convert_element_type.10
  92.5 4.2 %collective-permute-start.18 = (f16[72,128]{1,0:T(8,128)(2,1)S(1)}, f16[72,128]{1,0:T(8,128)(2,1)S(1)}, u32[]{:S(2)}, u32[]{:S(2)}) collective-permute-start(f16[72,128]{1,0:T(8,128)(2,1)S(1)} %convert_element_type.10), channel_id=1, source_target_pairs={{64,1},{65,2},{66,3},{67,4},{68,5},{69,6},{70,7},{1,64},{2,65},{3,... | collective-permute-start | bytes 55304 | tf_op jit(solution)/shard_map/ppermute | solution.py:603
  96.6 1.0 convert_element_type.9
  97.6 1.4 %collective-permute-done.18 = f16[72,128]{1,0:T(8,128)(2,1)S(1)} collective-permute-done((f16[72,128]{1,0:T(8,128)(2,1)S(1)}, f16[72,128]{1,0:T(8,128)(2,1)S(1)}, u32[]{:S(2)}, u32[]{:S(2)}) %collective-permute-start.18) | collective-permute-done | bytes 18464 | tf_op jit(solution)/shard_map/ppermute | solution.py:603
  99.0 0.1 collective-permute-start.20
  99.1 0.1 collective-permute-start.19
  99.2 5.0 %collective-permute-start.30 = (f16[504,128]{1,0:T(8,128)(2,1)S(1)}, f16[504,128]{1,0:T(8,128)(2,1)S(1)}, u32[]{:S(2)}, u32[]{:S(2)}) collective-permute-start(f16[504,128]{1,0:T(8,128)(2,1)S(1)} %pad_maximum_fusion), channel_id=1, source_target_pairs={{0,96},{8,104},{16,112},{24,120},{32,64},{40,72},{48,80},{56,88},{... | collective-permute-start | bytes 387080 | tf_op jit(solution)/shard_map/ppermute | solution.py:613
  104.2 0.1 collective-permute-start.28
  104.4 0.9 collective-permute-start.26
  105.3 2.9 %collective-permute-start.24 = (f16[504,128]{1,0:T(8,128)(2,1)S(1)}, f16[504,128]{1,0:T(8,128)(2,1)S(1)}, u32[]{:S(2)}, u32[]{:S(2)}) collective-permute-start(f16[504,128]{1,0:T(8,128)(2,1)S(1)} %pad_maximum_fusion), channel_id=1, source_target_pairs={{0,48},{8,56},{16,32},{24,40},{32,16},{40,24},{48,0},{56,8},{64,11... | collective-permute-start | bytes 387080 | tf_op jit(solution)/shard_map/ppermute | solution.py:613
  108.3 1.2 collective-permute-done.21
  109.6 2.0 %collective-permute-start.22 = (f16[504,128]{1,0:T(8,128)(2,1)S(1)}, f16[504,128]{1,0:T(8,128)(2,1)S(1)}, u32[]{:S(2)}, u32[]{:S(2)}) collective-permute-start(f16[504,128]{1,0:T(8,128)(2,1)S(1)} %pad_maximum_fusion), channel_id=1, source_target_pairs={{0,32},{8,40},{16,48},{24,56},{32,0},{40,8},{48,16},{56,24},{64,96... | collective-permute-start | bytes 387080 | tf_op jit(solution)/shard_map/ppermute | solution.py:613
  111.6 2.1 %collective-permute-start.32 = (f16[504,128]{1,0:T(8,128)(2,1)S(1)}, f16[504,128]{1,0:T(8,128)(2,1)S(1)}, u32[]{:S(2)}, u32[]{:S(2)}) collective-permute-start(f16[504,128]{1,0:T(8,128)(2,1)S(1)} %pad_maximum_fusion), channel_id=1, source_target_pairs={{0,112},{8,120},{16,96},{24,104},{32,80},{40,88},{48,64},{56,72},{... | collective-permute-start | bytes 387080 | tf_op jit(solution)/shard_map/ppermute | solution.py:613
  113.6 3.0 %collective-permute-done.22 = f16[504,128]{1,0:T(8,128)(2,1)S(1)} collective-permute-done((f16[504,128]{1,0:T(8,128)(2,1)S(1)}, f16[504,128]{1,0:T(8,128)(2,1)S(1)}, u32[]{:S(2)}, u32[]{:S(2)}) %collective-permute-start.22) | collective-permute-done | bytes 129056 | tf_op jit(solution)/shard_map/ppermute | solution.py:613
  116.7 0.6 collective-permute-start.31
  117.3 0.3 collective-permute-start.29
  117.6 0.2 collective-permute-start.27
  117.8 2.5 %collective-permute-done.32 = f16[504,128]{1,0:T(8,128)(2,1)S(1)} collective-permute-done((f16[504,128]{1,0:T(8,128)(2,1)S(1)}, f16[504,128]{1,0:T(8,128)(2,1)S(1)}, u32[]{:S(2)}, u32[]{:S(2)}) %collective-permute-start.32) | collective-permute-done | bytes 129056 | tf_op jit(solution)/shard_map/ppermute | solution.py:613
  120.3 0.5 collective-permute-start.33
  121.0 0.7 collective-permute-done.25
  122.2 2.2 %convert_element_type.11.chunks = f32[16,504,128]{2,1,0:T(8,128)} convert(f16[16,504,128]{2,1,0:T(8,128)(2,1)S(1)} %bitcast_dynamic-update-slice_fusion) | non-fusion elementwise | flops 1032192 | bytes 6193152 | tf_op jit(solution)/shard_map/convert_element_type | solution.py:615
  124.4 10.9 %relax.1 = f32[24,192,192]{2,1,0:T(8,128)} custom-call(s32[3]{0:T(128)} %pad_add_fusion.info, f32[16,504,128]{2,1,0:T(8,128)} %convert_element_type.11.chunks), custom_call_target="tpu_custom_call" | custom-call | tf_op jit(solution)/shard_map/relax/pallas_call | solution.py:550
  (67 shorter events, 0.9 us)
Async XLA Ops:
  4.4 9.6 %collective-permute-start = (bf16[12,80,128]{2,1,0:T(8,128)(2,1)}, bf16[12,80,128]{2,1,0:T(8,128)(2,1)S(1)}, u32[]{:S(2)}, u32[]{:S(2)}) collective-permute-start(bf16[12,80,128]{2,1,0:T(8,128)(2,1)} %get-tuple-element.26), channel_id=1, source_target_pairs={{0,8},{8,0},{16,24},{24,16},{32,40},{40,32},{48,56},{56,48},{1,9},... | collective-permute-start | bytes 737288 | tf_op jit(solution)/shard_map/ppermute | solution.py:592
  4.5 14.7 %collective-permute-start.1 = (bf16[12,80,128]{2,1,0:T(8,128)(2,1)}, bf16[12,80,128]{2,1,0:T(8,128)(2,1)S(1)}, u32[]{:S(2)}, u32[]{:S(2)}) collective-permute-start(bf16[12,80,128]{2,1,0:T(8,128)(2,1)} %get-tuple-element.27), channel_id=1, source_target_pairs={{0,16},{8,24},{16,0},{24,8},{32,48},{40,56},{48,32},{56,40},{1,17}... | collective-permute-start | bytes 737288 | tf_op jit(solution)/shard_map/ppermute | solution.py:592
  6.2 13.1 %collective-permute-start.2 = (bf16[12,80,128]{2,1,0:T(8,128)(2,1)}, bf16[12,80,128]{2,1,0:T(8,128)(2,1)S(1)}, u32[]{:S(2)}, u32[]{:S(2)}) collective-permute-start(bf16[12,80,128]{2,1,0:T(8,128)(2,1)} %get-tuple-element.28), channel_id=1, source_target_pairs={{0,24},{8,16},{16,8},{24,0},{32,56},{40,48},{48,40},{56,32},{1,25}... | collective-permute-start | bytes 737288 | tf_op jit(solution)/shard_map/ppermute | solution.py:592
  6.4 20.4 %collective-permute-start.3 = (bf16[12,80,128]{2,1,0:T(8,128)(2,1)}, bf16[12,80,128]{2,1,0:T(8,128)(2,1)S(1)}, u32[]{:S(2)}, u32[]{:S(2)}) collective-permute-start(bf16[12,80,128]{2,1,0:T(8,128)(2,1)} %get-tuple-element.29), channel_id=1, source_target_pairs={{0,32},{8,40},{16,48},{24,56},{32,0},{40,8},{48,16},{56,24},{1,33}... | collective-permute-start | bytes 737288 | tf_op jit(solution)/shard_map/ppermute | solution.py:592
  10.8 39.4 %collective-permute-start.8 = (f32[1,3,3,96,96]{4,3,2,1,0:T(8,128)S(1)}, f32[1,3,3,96,96]{4,3,2,1,0:T(8,128)S(1)}, u32[]{:S(2)}, u32[]{:S(2)}) collective-permute-start(f32[1,3,3,96,96]{4,3,2,1,0:T(8,128)S(1)} %get-tuple-element.45), channel_id=1, source_target_pairs={{64,1},{65,2},{66,3},{67,4},{68,5},{69,6},{70,7},{1,64},{2,65},{3,... | collective-permute-start | bytes 995336 | tf_op jit(solution)/shard_map/ppermute | solution.py:587
  14.0 27.8 %copy-start = (bf16[12,80,128]{2,1,0:T(8,128)(2,1)}, bf16[12,80,128]{2,1,0:T(8,128)(2,1)S(1)}, u32[]{:S(2)}) copy-start(bf16[12,80,128]{2,1,0:T(8,128)(2,1)S(1)} %collective-permute-done.refs_1_.rest_1_) | copy-start | bytes 737284
  14.0 36.2 %collective-permute-start.7 = (f32[1,3,3,96,96]{4,3,2,1,0:T(8,128)S(1)}, f32[1,3,3,96,96]{4,3,2,1,0:T(8,128)S(1)}, u32[]{:S(2)}, u32[]{:S(2)}) collective-permute-start(f32[1,3,3,96,96]{4,3,2,1,0:T(8,128)S(1)} %get-tuple-element.46), channel_id=1, source_target_pairs={{0,1},{1,2},{2,3},{3,4},{4,5},{5,6},{6,7},{65,64},{66,65},{67,66},... | collective-permute-start | bytes 995336 | tf_op jit(solution)/shard_map/ppermute | solution.py:586
  19.2 22.6 %copy-start.1 = (bf16[12,80,128]{2,1,0:T(8,128)(2,1)}, bf16[12,80,128]{2,1,0:T(8,128)(2,1)S(1)}, u32[]{:S(2)}) copy-start(bf16[12,80,128]{2,1,0:T(8,128)(2,1)S(1)} %collective-permute-done.1.refs_2_.rest_2_) | copy-start | bytes 737284
  19.2 11.7 %collective-permute-start.4 = (bf16[12,80,128]{2,1,0:T(8,128)(2,1)}, bf16[12,80,128]{2,1,0:T(8,128)(2,1)S(1)}, u32[]{:S(2)}, u32[]{:S(2)}) collective-permute-start(bf16[12,80,128]{2,1,0:T(8,128)(2,1)} %get-tuple-element.30), channel_id=1, source_target_pairs={{0,40},{8,32},{16,56},{24,48},{32,8},{40,0},{48,24},{56,16},{1,41}... | collective-permute-start | bytes 737288 | tf_op jit(solution)/shard_map/ppermute | solution.py:592
  19.3 22.5 %copy-start.2 = (bf16[12,80,128]{2,1,0:T(8,128)(2,1)}, bf16[12,80,128]{2,1,0:T(8,128)(2,1)S(1)}, u32[]{:S(2)}) copy-start(bf16[12,80,128]{2,1,0:T(8,128)(2,1)S(1)} %collective-permute-done.2.refs_3_.rest_3_) | copy-start | bytes 737284
  19.3 17.3 %collective-permute-start.5 = (bf16[12,80,128]{2,1,0:T(8,128)(2,1)}, bf16[12,80,128]{2,1,0:T(8,128)(2,1)S(1)}, u32[]{:S(2)}, u32[]{:S(2)}) collective-permute-start(bf16[12,80,128]{2,1,0:T(8,128)(2,1)} %get-tuple-element.31), channel_id=1, source_target_pairs={{0,48},{8,56},{16,32},{24,40},{32,16},{40,24},{48,0},{56,8},{1,49}... | collective-permute-start | bytes 737288 | tf_op jit(solution)/shard_map/ppermute | solution.py:592
  26.7 15.1 %copy-start.3 = (bf16[12,80,128]{2,1,0:T(8,128)(2,1)}, bf16[12,80,128]{2,1,0:T(8,128)(2,1)S(1)}, u32[]{:S(2)}) copy-start(bf16[12,80,128]{2,1,0:T(8,128)(2,1)S(1)} %collective-permute-done.3.refs_4_.rest_4_) | copy-start | bytes 737284
  26.7 15.1 %collective-permute-start.6 = (bf16[12,80,128]{2,1,0:T(8,128)(2,1)}, bf16[12,80,128]{2,1,0:T(8,128)(2,1)S(1)}, u32[]{:S(2)}, u32[]{:S(2)}) collective-permute-start(bf16[12,80,128]{2,1,0:T(8,128)(2,1)} %get-tuple-element.32), channel_id=1, source_target_pairs={{0,56},{8,48},{16,40},{24,32},{32,24},{40,16},{48,8},{56,0},{1,57}... | collective-permute-start | bytes 737288 | tf_op jit(solution)/shard_map/ppermute | solution.py:592
  30.9 11.0 %copy-start.4 = (bf16[12,80,128]{2,1,0:T(8,128)(2,1)}, bf16[12,80,128]{2,1,0:T(8,128)(2,1)S(1)}, u32[]{:S(2)}) copy-start(bf16[12,80,128]{2,1,0:T(8,128)(2,1)S(1)} %collective-permute-done.4.refs_5_.rest_5_) | copy-start | bytes 737284
  36.7 5.2 %copy-start.5 = (bf16[12,80,128]{2,1,0:T(8,128)(2,1)}, bf16[12,80,128]{2,1,0:T(8,128)(2,1)S(1)}, u32[]{:S(2)}) copy-start(bf16[12,80,128]{2,1,0:T(8,128)(2,1)S(1)} %collective-permute-done.5.refs_6_.rest_6_) | copy-start | bytes 737284
  41.8 0.7 copy-start.6
  44.3 18.4 %collective-permute-start.16 = (bf16[8,80,128]{2,1,0:T(8,128)(2,1)}, bf16[8,80,128]{2,1,0:T(8,128)(2,1)S(1)}, u32[]{:S(2)}, u32[]{:S(2)}) collective-permute-start(bf16[8,80,128]{2,1,0:T(8,128)(2,1)} %get-tuple-element.41), channel_id=1, source_target_pairs={{0,64},{1,65},{2,66},{3,67},{4,68},{5,69},{6,70},{7,71},{64,1},{65... | collective-permute-start | bytes 491528 | tf_op jit(solution)/shard_map/ppermute | solution.py:600
  47.6 15.8 %collective-permute-start.17 = (bf16[8,80,128]{2,1,0:T(8,128)(2,1)}, bf16[8,80,128]{2,1,0:T(8,128)(2,1)S(1)}, u32[]{:S(2)}, u32[]{:S(2)}) collective-permute-start(bf16[8,80,128]{2,1,0:T(8,128)(2,1)} %get-tuple-element.42), channel_id=1, source_target_pairs={{64,0},{65,1},{66,2},{67,3},{68,4},{69,5},{70,6},{71,7},{1,64},{2,... | collective-permute-start | bytes 491528 | tf_op jit(solution)/shard_map/ppermute | solution.py:601
  50.2 0.8 copy-start.7
  51.0 0.8 copy-start.8
  60.8 5.2 %collective-permute-start.9 = (bf16[560,128]{1,0:T(8,128)(2,1)}, bf16[560,128]{1,0:T(8,128)(2,1)S(1)}, u32[]{:S(2)}, u32[]{:S(2)}) collective-permute-start(bf16[560,128]{1,0:T(8,128)(2,1)} %get-tuple-element.34), channel_id=1, source_target_pairs={{0,8},{8,0},{16,24},{24,16},{32,40},{40,32},{48,56},{56,48},{1,9},... | collective-permute-start | bytes 430088 | tf_op jit(solution)/shard_map/ppermute | solution.py:592
  60.9 6.9 %collective-permute-start.10 = (bf16[560,128]{1,0:T(8,128)(2,1)}, bf16[560,128]{1,0:T(8,128)(2,1)S(1)}, u32[]{:S(2)}, u32[]{:S(2)}) collective-permute-start(bf16[560,128]{1,0:T(8,128)(2,1)} %get-tuple-element.35), channel_id=1, source_target_pairs={{0,16},{8,24},{16,0},{24,8},{32,48},{40,56},{48,32},{56,40},{1,17}... | collective-permute-start | bytes 430088 | tf_op jit(solution)/shard_map/ppermute | solution.py:592
  61.2 8.6 %collective-permute-start.11 = (bf16[560,128]{1,0:T(8,128)(2,1)}, bf16[560,128]{1,0:T(8,128)(2,1)S(1)}, u32[]{:S(2)}, u32[]{:S(2)}) collective-permute-start(bf16[560,128]{1,0:T(8,128)(2,1)} %get-tuple-element.36), channel_id=1, source_target_pairs={{0,24},{8,16},{16,8},{24,0},{32,56},{40,48},{48,40},{56,32},{1,25}... | collective-permute-start | bytes 430088 | tf_op jit(solution)/shard_map/ppermute | solution.py:592
  62.8 19.3 %copy-start.9 = (bf16[8,80,128]{2,1,0:T(8,128)(2,1)}, bf16[8,80,128]{2,1,0:T(8,128)(2,1)S(1)}, u32[]{:S(2)}) copy-start(bf16[8,80,128]{2,1,0:T(8,128)(2,1)S(1)} %collective-permute-done.16.rest_16_) | copy-start | bytes 491524
  62.8 11.0 %collective-permute-start.12 = (bf16[560,128]{1,0:T(8,128)(2,1)}, bf16[560,128]{1,0:T(8,128)(2,1)S(1)}, u32[]{:S(2)}, u32[]{:S(2)}) collective-permute-start(bf16[560,128]{1,0:T(8,128)(2,1)} %get-tuple-element.37), channel_id=1, source_target_pairs={{0,32},{8,40},{16,48},{24,56},{32,0},{40,8},{48,16},{56,24},{1,33}... | collective-permute-start | bytes 430088 | tf_op jit(solution)/shard_map/ppermute | solution.py:592
  63.4 18.6 %copy-start.10 = (bf16[8,80,128]{2,1,0:T(8,128)(2,1)}, bf16[8,80,128]{2,1,0:T(8,128)(2,1)S(1)}, u32[]{:S(2)}) copy-start(bf16[8,80,128]{2,1,0:T(8,128)(2,1)S(1)} %collective-permute-done.17.rest_17_) | copy-start | bytes 491524
  63.4 12.3 %collective-permute-start.13 = (bf16[560,128]{1,0:T(8,128)(2,1)}, bf16[560,128]{1,0:T(8,128)(2,1)S(1)}, u32[]{:S(2)}, u32[]{:S(2)}) collective-permute-start(bf16[560,128]{1,0:T(8,128)(2,1)} %get-tuple-element.38), channel_id=1, source_target_pairs={{0,40},{8,32},{16,56},{24,48},{32,8},{40,0},{48,24},{56,16},{1,41}... | collective-permute-start | bytes 430088 | tf_op jit(solution)/shard_map/ppermute | solution.py:592
  66.0 16.1 %copy-start.11 = (bf16[560,128]{1,0:T(8,128)(2,1)}, bf16[560,128]{1,0:T(8,128)(2,1)S(1)}, u32[]{:S(2)}) copy-start(bf16[560,128]{1,0:T(8,128)(2,1)S(1)} %collective-permute-done.9.rest_9_) | copy-start | bytes 430084
  66.0 13.4 %collective-permute-start.14 = (bf16[560,128]{1,0:T(8,128)(2,1)}, bf16[560,128]{1,0:T(8,128)(2,1)S(1)}, u32[]{:S(2)}, u32[]{:S(2)}) collective-permute-start(bf16[560,128]{1,0:T(8,128)(2,1)} %get-tuple-element.39), channel_id=1, source_target_pairs={{0,48},{8,56},{16,32},{24,40},{32,16},{40,24},{48,0},{56,8},{1,49}... | collective-permute-start | bytes 430088 | tf_op jit(solution)/shard_map/ppermute | solution.py:592
  67.8 14.3 %copy-start.12 = (bf16[560,128]{1,0:T(8,128)(2,1)}, bf16[560,128]{1,0:T(8,128)(2,1)S(1)}, u32[]{:S(2)}) copy-start(bf16[560,128]{1,0:T(8,128)(2,1)S(1)} %collective-permute-done.10.rest_10_) | copy-start | bytes 430084
  67.8 14.2 %collective-permute-start.15 = (bf16[560,128]{1,0:T(8,128)(2,1)}, bf16[560,128]{1,0:T(8,128)(2,1)S(1)}, u32[]{:S(2)}, u32[]{:S(2)}) collective-permute-start(bf16[560,128]{1,0:T(8,128)(2,1)} %get-tuple-element.40), channel_id=1, source_target_pairs={{0,56},{8,48},{16,40},{24,32},{32,24},{40,16},{48,8},{56,0},{1,57}... | collective-permute-start | bytes 430088 | tf_op jit(solution)/shard_map/ppermute | solution.py:592
  69.8 12.3 %copy-start.13 = (bf16[560,128]{1,0:T(8,128)(2,1)}, bf16[560,128]{1,0:T(8,128)(2,1)S(1)}, u32[]{:S(2)}) copy-start(bf16[560,128]{1,0:T(8,128)(2,1)S(1)} %collective-permute-done.11.rest_11_) | copy-start | bytes 430084
  73.8 8.3 %copy-start.14 = (bf16[560,128]{1,0:T(8,128)(2,1)}, bf16[560,128]{1,0:T(8,128)(2,1)S(1)}, u32[]{:S(2)}) copy-start(bf16[560,128]{1,0:T(8,128)(2,1)S(1)} %collective-permute-done.12.rest_12_) | copy-start | bytes 430084
  75.8 6.4 %copy-start.15 = (bf16[560,128]{1,0:T(8,128)(2,1)}, bf16[560,128]{1,0:T(8,128)(2,1)S(1)}, u32[]{:S(2)}) copy-start(bf16[560,128]{1,0:T(8,128)(2,1)S(1)} %collective-permute-done.13.rest_13_) | copy-start | bytes 430084
  79.4 2.7 %copy-start.16 = (bf16[560,128]{1,0:T(8,128)(2,1)}, bf16[560,128]{1,0:T(8,128)(2,1)S(1)}, u32[]{:S(2)}) copy-start(bf16[560,128]{1,0:T(8,128)(2,1)S(1)} %collective-permute-done.14.rest_14_) | copy-start | bytes 430084
  82.1 0.7 copy-start.17
  92.5 6.5 %collective-permute-start.18 = (f16[72,128]{1,0:T(8,128)(2,1)S(1)}, f16[72,128]{1,0:T(8,128)(2,1)S(1)}, u32[]{:S(2)}, u32[]{:S(2)}) collective-permute-start(f16[72,128]{1,0:T(8,128)(2,1)S(1)} %convert_element_type.10), channel_id=1, source_target_pairs={{64,1},{65,2},{66,3},{67,4},{68,5},{69,6},{70,7},{1,64},{2,65},{3,... | collective-permute-start | bytes 55304 | tf_op jit(solution)/shard_map/ppermute | solution.py:603
  99.0 6.3 %collective-permute-start.20 = (f16[504,128]{1,0:T(8,128)(2,1)S(1)}, f16[504,128]{1,0:T(8,128)(2,1)S(1)}, u32[]{:S(2)}, u32[]{:S(2)}) collective-permute-start(f16[504,128]{1,0:T(8,128)(2,1)S(1)} %pad_maximum_fusion), channel_id=1, source_target_pairs={{0,16},{8,24},{16,0},{24,8},{32,48},{40,56},{48,32},{56,40},{64,80... | collective-permute-start | bytes 387080 | tf_op jit(solution)/shard_map/ppermute | solution.py:613
  99.1 9.1 %collective-permute-start.19 = (f16[504,128]{1,0:T(8,128)(2,1)S(1)}, f16[504,128]{1,0:T(8,128)(2,1)S(1)}, u32[]{:S(2)}, u32[]{:S(2)}) collective-permute-start(f16[504,128]{1,0:T(8,128)(2,1)S(1)} %pad_maximum_fusion), channel_id=1, source_target_pairs={{0,8},{8,0},{16,24},{24,16},{32,40},{40,32},{48,56},{56,48},{1,9},... | collective-permute-start | bytes 387080 | tf_op jit(solution)/shard_map/ppermute | solution.py:614
  99.2 12.4 %collective-permute-start.30 = (f16[504,128]{1,0:T(8,128)(2,1)S(1)}, f16[504,128]{1,0:T(8,128)(2,1)S(1)}, u32[]{:S(2)}, u32[]{:S(2)}) collective-permute-start(f16[504,128]{1,0:T(8,128)(2,1)S(1)} %pad_maximum_fusion), channel_id=1, source_target_pairs={{0,96},{8,104},{16,112},{24,120},{32,64},{40,72},{48,80},{56,88},{... | collective-permute-start | bytes 387080 | tf_op jit(solution)/shard_map/ppermute | solution.py:613
  104.2 12.4 %collective-permute-start.28 = (f16[504,128]{1,0:T(8,128)(2,1)S(1)}, f16[504,128]{1,0:T(8,128)(2,1)S(1)}, u32[]{:S(2)}, u32[]{:S(2)}) collective-permute-start(f16[504,128]{1,0:T(8,128)(2,1)S(1)} %pad_maximum_fusion), channel_id=1, source_target_pairs={{0,80},{8,88},{16,64},{24,72},{32,112},{40,120},{48,96},{56,104},{... | collective-permute-start | bytes 387080 | tf_op jit(solution)/shard_map/ppermute | solution.py:613
  104.4 12.9 %collective-permute-start.26 = (f16[504,128]{1,0:T(8,128)(2,1)S(1)}, f16[504,128]{1,0:T(8,128)(2,1)S(1)}, u32[]{:S(2)}, u32[]{:S(2)}) collective-permute-start(f16[504,128]{1,0:T(8,128)(2,1)S(1)} %pad_maximum_fusion), channel_id=1, source_target_pairs={{0,64},{8,72},{16,80},{24,88},{32,96},{40,104},{48,112},{56,120},{... | collective-permute-start | bytes 387080 | tf_op jit(solution)/shard_map/ppermute | solution.py:613
  105.3 12.2 %collective-permute-start.24 = (f16[504,128]{1,0:T(8,128)(2,1)S(1)}, f16[504,128]{1,0:T(8,128)(2,1)S(1)}, u32[]{:S(2)}, u32[]{:S(2)}) collective-permute-start(f16[504,128]{1,0:T(8,128)(2,1)S(1)} %pad_maximum_fusion), channel_id=1, source_target_pairs={{0,48},{8,56},{16,32},{24,40},{32,16},{40,24},{48,0},{56,8},{64,11... | collective-permute-start | bytes 387080 | tf_op jit(solution)/shard_map/ppermute | solution.py:613
  108.2 1.3 collective-permute-start.21
  109.6 7.1 %collective-permute-start.22 = (f16[504,128]{1,0:T(8,128)(2,1)S(1)}, f16[504,128]{1,0:T(8,128)(2,1)S(1)}, u32[]{:S(2)}, u32[]{:S(2)}) collective-permute-start(f16[504,128]{1,0:T(8,128)(2,1)S(1)} %pad_maximum_fusion), channel_id=1, source_target_pairs={{0,32},{8,40},{16,48},{24,56},{32,0},{40,8},{48,16},{56,24},{64,96... | collective-permute-start | bytes 387080 | tf_op jit(solution)/shard_map/ppermute | solution.py:613
  111.6 8.7 %collective-permute-start.32 = (f16[504,128]{1,0:T(8,128)(2,1)S(1)}, f16[504,128]{1,0:T(8,128)(2,1)S(1)}, u32[]{:S(2)}, u32[]{:S(2)}) collective-permute-start(f16[504,128]{1,0:T(8,128)(2,1)S(1)} %pad_maximum_fusion), channel_id=1, source_target_pairs={{0,112},{8,120},{16,96},{24,104},{32,80},{40,88},{48,64},{56,72},{... | collective-permute-start | bytes 387080 | tf_op jit(solution)/shard_map/ppermute | solution.py:613
  116.6 3.7 %collective-permute-start.23 = (f16[504,128]{1,0:T(8,128)(2,1)S(1)}, f16[504,128]{1,0:T(8,128)(2,1)S(1)}, u32[]{:S(2)}, u32[]{:S(2)}) collective-permute-start(f16[504,128]{1,0:T(8,128)(2,1)S(1)} %collective-permute-done.22), channel_id=1, source_target_pairs={{0,8},{8,0},{16,24},{24,16},{32,40},{40,32},{48,56},{56,48},{1,9},... | collective-permute-start | bytes 387080 | tf_op jit(solution)/shard_map/ppermute | solution.py:614
  116.7 5.3 %collective-permute-start.31 = (f16[504,128]{1,0:T(8,128)(2,1)S(1)}, f16[504,128]{1,0:T(8,128)(2,1)S(1)}, u32[]{:S(2)}, u32[]{:S(2)}) collective-permute-start(f16[504,128]{1,0:T(8,128)(2,1)S(1)} %collective-permute-done.30), channel_id=1, source_target_pairs={{0,8},{8,0},{16,24},{24,16},{32,40},{40,32},{48,56},{56,48},{1,9},... | collective-permute-start | bytes 387080 | tf_op jit(solution)/shard_map/ppermute | solution.py:614
  117.3 4.6 %collective-permute-start.29 = (f16[504,128]{1,0:T(8,128)(2,1)S(1)}, f16[504,128]{1,0:T(8,128)(2,1)S(1)}, u32[]{:S(2)}, u32[]{:S(2)}) collective-permute-start(f16[504,128]{1,0:T(8,128)(2,1)S(1)} %collective-permute-done.28), channel_id=1, source_target_pairs={{0,8},{8,0},{16,24},{24,16},{32,40},{40,32},{48,56},{56,48},{1,9},... | collective-permute-start | bytes 387080 | tf_op jit(solution)/shard_map/ppermute | solution.py:614
  117.6 4.2 %collective-permute-start.27 = (f16[504,128]{1,0:T(8,128)(2,1)S(1)}, f16[504,128]{1,0:T(8,128)(2,1)S(1)}, u32[]{:S(2)}, u32[]{:S(2)}) collective-permute-start(f16[504,128]{1,0:T(8,128)(2,1)S(1)} %collective-permute-done.26), channel_id=1, source_target_pairs={{0,8},{8,0},{16,24},{24,16},{32,40},{40,32},{48,56},{56,48},{1,9},... | collective-permute-start | bytes 387080 | tf_op jit(solution)/shard_map/ppermute | solution.py:614
  120.3 1.3 collective-permute-start.25
  120.3 1.7 %collective-permute-start.33 = (f16[504,128]{1,0:T(8,128)(2,1)S(1)}, f16[504,128]{1,0:T(8,128)(2,1)S(1)}, u32[]{:S(2)}, u32[]{:S(2)}) collective-permute-start(f16[504,128]{1,0:T(8,128)(2,1)S(1)} %collective-permute-done.32), channel_id=1, source_target_pairs={{0,8},{8,0},{16,24},{24,16},{32,40},{40,32},{48,56},{56,48},{1,9},... | collective-permute-start | bytes 387080 | tf_op jit(solution)/shard_map/ppermute | solution.py:614

commit v7 on v6

--- a/solution.py
+++ b/solution.py
@@ -408,9 +408,20 @@
     )(info, assign, *tables, *planes, *fields, below, above)
 
 
-def relax_kernel(info, chunks, out, flat, pair, flat2, pair2, even, odd, ready, sems):
+def relax_kernel(
+    info, source, out, chunks, flat, pair, flat2, pair2, even, odd, ready, sems, arriving
+):
     level, me, zone = info[0], info[1], info[2]
     size = flat.shape[1] - 16
+    copies = []
+    for peer in range(8):
+        for half in range(2):
+            slot = (half ^ level) * 8 + (peer ^ me)
+            copies.append(
+                pltpu.make_async_copy(source.at[slot], chunks.at[slot], arriving.at[slot])
+            )
+    for copy in copies:
+        copy.start()
     for held in (flat, pair, flat2, pair2):
         held[:, :8] = jnp.zeros((held.shape[0], 8, 128), F32)
         held[:, size + 8 :] = jnp.zeros((held.shape[0], 8, 128), F32)
@@ -421,6 +432,8 @@
     tail = HZ * 3 // 2
     for peer in range(8):
         rows = slice(8 + CY * peer, 8 + CY * (peer + 1))
+        for copy in copies[2 * peer : 2 * peer + 2]:
+            copy.wait()
 
         def block(half, index):
             slot = (half ^ level) * 8 + (peer ^ me)
@@ -546,14 +559,15 @@
 
 
 def relax(info, chunks):
-    vmem = pl.BlockSpec(memory_space=pltpu.VMEM)
+    hbm = pl.BlockSpec(memory_space=pl.ANY)
     return pl.pallas_call(
         relax_kernel,
         grid=(),
-        in_specs=[pl.BlockSpec(memory_space=pltpu.SMEM), vmem],
+        in_specs=[pl.BlockSpec(memory_space=pltpu.SMEM), hbm],
         out_specs=pl.BlockSpec(memory_space=pl.ANY),
         out_shape=jax.ShapeDtypeStruct((24, 192, 192), F32),
         scratch_shapes=[
+            pltpu.VMEM(chunks.shape, F32),
             pltpu.VMEM((32, 208, 128), F32),
             pltpu.VMEM((16, 208, 128), F32),
             pltpu.VMEM((32, 208, 128), F32),
@@ -562,6 +576,7 @@
             pltpu.VMEM((3, 192, 128), F32),
             pltpu.VMEM((28, 192, 192), F32),
             pltpu.SemaphoreType.DMA((24,)),
+            pltpu.SemaphoreType.DMA((16,)),
         ],
         name="relax",
     )(info, chunks)

time: 137 us -> 137 us (level)
  no operation moved by 1% of the time
where the time goes in v7:
time: 137 us; the launch traced here: 136 us
  starting transfers between devices  47.4 us (35%)
  waiting for transfers between devices  43.6 us (32%)
  Pallas kernels  35 us (26%)
  local copies, waits for them, and re-layouts  4.74 us (3%)
  other arithmetic  4.57 us (3%)
    ppermute x14, waiting for transfers between devices, spread(): arrived[k] = lax.ppermute(parts[k], 'subj', [(i, i ^ k) for i in range(8)])  34.6 us
    ppermute x14, starting transfers between devices, spread(): arrived[k] = lax.ppermute(parts[k], 'subj', [(i, i ^ k) for i in range(8)])  14.3 us
    ppermute x7, starting transfers between devices, update(): part = lax.ppermute(chunk, ('level', 'subj'), perm)  13.1 us
    pallas_call x1, Pallas kernels, relax(): pl.pallas_call(relax_kernel, grid=(), in_specs=[pl.BlockSpec(memory_space...  11.3 us
    pallas_call x1, Pallas kernels, blur(): pl.pallas_call(blur_kernel, grid=(), in_specs=[pl.BlockSpec(memory_space=...  9.05 us
    pallas_call x1, Pallas kernels, warp(): pl.pallas_call(warp_kernel, grid=(), in_specs=[smem, smem, vmem, vmem, vm...  8.95 us
    ppermute x7, waiting for transfers between devices, update(): part = lax.ppermute(chunk, ('level', 'subj'), perm)  5.54 us
    ppermute x1, starting transfers between devices, update(): rim = lax.ppermute(rim, nearest, outward)  5.16 us
  transfers between devices with their start and end apart: 34, of which 15 were waited for; matrix products, arithmetic and copies ran while one was open for 2% of the time, Pallas kernels for 8%

profile of v7, /device:TPU:96, one launch (start us, length us, event | category | flops | bytes accessed | tf_op | source)
XLA Modules:
  0.0 135.8 jit_solution(12213439777638213025)
XLA Ops:
  0.0 0.6 pad_add_fusion.info
  0.6 3.9 %pack_images.1 = (bf16[12,80,128]{2,1,0:T(8,128)(2,1)}, bf16[12,80,128]{2,1,0:T(8,128)(2,1)}, bf16[12,80,128]{2,1,0:T(8,128)(2,1)}, bf16[12,80,128]{2,1,0:T(8,12...) custom-call(s32[3]{0:T(128)} %pad_add_fusion.info, ...), custom_call_target="tpu_custom_call" | custom-call | tf_op jit(solution)/shard_map/pack_images/pallas_call | solution.py:106
  4.4 0.1 collective-permute-start
  4.5 1.7 %collective-permute-start.1 = (bf16[12,80,128]{2,1,0:T(8,128)(2,1)}, bf16[12,80,128]{2,1,0:T(8,128)(2,1)S(1)}, u32[]{:S(2)}, u32[]{:S(2)}) collective-permute-start(bf16[12,80,128]{2,1,0:T(8,128)(2,1)} %get-tuple-element.27), channel_id=1, source_target_pairs={{0,16},{8,24},{16,0},{24,8},{32,48},{40,56},{48,32},{56,40},{1,17}... | collective-permute-start | bytes 737288 | tf_op jit(solution)/shard_map/ppermute | solution.py:607
  6.2 0.2 collective-permute-start.2
  6.4 3.2 %collective-permute-start.3 = (bf16[12,80,128]{2,1,0:T(8,128)(2,1)}, bf16[12,80,128]{2,1,0:T(8,128)(2,1)S(1)}, u32[]{:S(2)}, u32[]{:S(2)}) collective-permute-start(bf16[12,80,128]{2,1,0:T(8,128)(2,1)} %get-tuple-element.29), channel_id=1, source_target_pairs={{0,32},{8,40},{16,48},{24,56},{32,0},{40,8},{48,16},{56,24},{1,33}... | collective-permute-start | bytes 737288 | tf_op jit(solution)/shard_map/ppermute | solution.py:607
  9.6 1.2 constant_dynamic-slice_fusion
  10.8 3.2 %collective-permute-start.8 = (f32[1,3,3,96,96]{4,3,2,1,0:T(8,128)S(1)}, f32[1,3,3,96,96]{4,3,2,1,0:T(8,128)S(1)}, u32[]{:S(2)}, u32[]{:S(2)}) collective-permute-start(f32[1,3,3,96,96]{4,3,2,1,0:T(8,128)S(1)} %get-tuple-element.45), channel_id=1, source_target_pairs={{64,1},{65,2},{66,3},{67,4},{68,5},{69,6},{70,7},{1,64},{2,65},{3,... | collective-permute-start | bytes 995336 | tf_op jit(solution)/shard_map/ppermute | solution.py:602
  14.0 0.0 collective-permute-done.refs_1_.rest_1_
  14.0 5.2 %collective-permute-start.7 = (f32[1,3,3,96,96]{4,3,2,1,0:T(8,128)S(1)}, f32[1,3,3,96,96]{4,3,2,1,0:T(8,128)S(1)}, u32[]{:S(2)}, u32[]{:S(2)}) collective-permute-start(f32[1,3,3,96,96]{4,3,2,1,0:T(8,128)S(1)} %get-tuple-element.46), channel_id=1, source_target_pairs={{0,1},{1,2},{2,3},{3,4},{4,5},{5,6},{6,7},{65,64},{66,65},{67,66},... | collective-permute-start | bytes 995336 | tf_op jit(solution)/shard_map/ppermute | solution.py:601
  19.2 0.0 collective-permute-done.1.refs_2_.rest_2_
  19.2 0.1 collective-permute-start.4
  19.3 0.0 collective-permute-done.2.refs_3_.rest_3_
  19.3 2.5 %collective-permute-start.5 = (bf16[12,80,128]{2,1,0:T(8,128)(2,1)}, bf16[12,80,128]{2,1,0:T(8,128)(2,1)S(1)}, u32[]{:S(2)}, u32[]{:S(2)}) collective-permute-start(bf16[12,80,128]{2,1,0:T(8,128)(2,1)} %get-tuple-element.31), channel_id=1, source_target_pairs={{0,48},{8,56},{16,32},{24,40},{32,16},{40,24},{48,0},{56,8},{1,49}... | collective-permute-start | bytes 737288 | tf_op jit(solution)/shard_map/ppermute | solution.py:607
  21.8 4.9 %collective-permute-done.3.refs_4_.rest_4_ = bf16[12,80,128]{2,1,0:T(8,128)(2,1)S(1)} collective-permute-done((bf16[12,80,128]{2,1,0:T(8,128)(2,1)}, bf16[12,80,128]{2,1,0:T(8,128)(2,1)S(1)}, u32[]{:S(2)}, u32[]{:S(2)}) %collective-permute-start.3) | collective-permute-done | bytes 245792 | tf_op jit(solution)/shard_map/ppermute | solution.py:607
  26.7 0.0 collective-permute-start.6
  26.7 4.2 %collective-permute-done.4.refs_5_.rest_5_ = bf16[12,80,128]{2,1,0:T(8,128)(2,1)S(1)} collective-permute-done((bf16[12,80,128]{2,1,0:T(8,128)(2,1)}, bf16[12,80,128]{2,1,0:T(8,128)(2,1)S(1)}, u32[]{:S(2)}, u32[]{:S(2)}) %collective-permute-start.4) | collective-permute-done | bytes 245792 | tf_op jit(solution)/shard_map/ppermute | solution.py:607
  30.9 5.8 %collective-permute-done.5.refs_6_.rest_6_ = bf16[12,80,128]{2,1,0:T(8,128)(2,1)S(1)} collective-permute-done((bf16[12,80,128]{2,1,0:T(8,128)(2,1)}, bf16[12,80,128]{2,1,0:T(8,128)(2,1)S(1)}, u32[]{:S(2)}, u32[]{:S(2)}) %collective-permute-start.5) | collective-permute-done | bytes 245792 | tf_op jit(solution)/shard_map/ppermute | solution.py:607
  36.7 5.2 %collective-permute-done.6.refs_7_.rest_7_ = bf16[12,80,128]{2,1,0:T(8,128)(2,1)S(1)} collective-permute-done((bf16[12,80,128]{2,1,0:T(8,128)(2,1)}, bf16[12,80,128]{2,1,0:T(8,128)(2,1)S(1)}, u32[]{:S(2)}, u32[]{:S(2)}) %collective-permute-start.6) | collective-permute-done | bytes 245792 | tf_op jit(solution)/shard_map/ppermute | solution.py:607
  41.9 0.7 copy-done.6
  42.5 1.8 %cut_edges.1 = (bf16[8,80,128]{2,1,0:T(8,128)(2,1)}, bf16[8,80,128]{2,1,0:T(8,128)(2,1)}) custom-call(bf16[12,80,128]{2,1,0:T(8,128)(2,1)} %get-tuple-element.25.refs_0_.rest_0_, bf16[12,80,128]{2,1,0:T(8,128)(2,1)} %copy-done, bf16[12,80,128]{2,1,0:T(8,128)(2,1)} %copy-done.1, bf16[12,80,128]{2,1,0:T(8,128)(2,1)} %copy-done.2, ...), custom_call_target="tpu_custom_call" | custom-call | tf_op jit(solution)/shard_map/cut_edges/pallas_call | solution.py:241
  44.3 3.3 %collective-permute-start.16 = (bf16[8,80,128]{2,1,0:T(8,128)(2,1)}, bf16[8,80,128]{2,1,0:T(8,128)(2,1)S(1)}, u32[]{:S(2)}, u32[]{:S(2)}) collective-permute-start(bf16[8,80,128]{2,1,0:T(8,128)(2,1)} %get-tuple-element.41), channel_id=1, source_target_pairs={{0,64},{1,65},{2,66},{3,67},{4,68},{5,69},{6,70},{7,71},{64,1},{65... | collective-permute-start | bytes 491528 | tf_op jit(solution)/shard_map/ppermute | solution.py:615
  47.6 2.5 %collective-permute-start.17 = (bf16[8,80,128]{2,1,0:T(8,128)(2,1)}, bf16[8,80,128]{2,1,0:T(8,128)(2,1)S(1)}, u32[]{:S(2)}, u32[]{:S(2)}) collective-permute-start(bf16[8,80,128]{2,1,0:T(8,128)(2,1)} %get-tuple-element.42), channel_id=1, source_target_pairs={{64,0},{65,1},{66,2},{67,3},{68,4},{69,5},{70,6},{71,7},{1,64},{2,... | collective-permute-start | bytes 491528 | tf_op jit(solution)/shard_map/ppermute | solution.py:616
  50.2 0.0 collective-permute-done.8.other
  50.2 0.8 copy-done.7
  51.0 0.8 copy-done.8
  51.7 9.1 %blur_momenta.1 = (bf16[560,128]{1,0:T(8,128)(2,1)}, bf16[560,128]{1,0:T(8,128)(2,1)}, bf16[560,128]{1,0:T(8,128)(2,1)}, bf16[560,128]{1,0:T(8,128)(2,1)}, bf16[...) custom-call(s32[3]{0:T(128)} %pad_add_fusion.info, ...), custom_call_target="tpu_custom_call" | custom-call | tf_op jit(solution)/shard_map/blur_momenta/pallas_call | solution.py:192
  60.8 0.1 collective-permute-start.9
  60.9 0.3 collective-permute-start.10
  61.2 1.6 %collective-permute-start.11 = (bf16[560,128]{1,0:T(8,128)(2,1)}, bf16[560,128]{1,0:T(8,128)(2,1)S(1)}, u32[]{:S(2)}, u32[]{:S(2)}) collective-permute-start(bf16[560,128]{1,0:T(8,128)(2,1)} %get-tuple-element.36), channel_id=1, source_target_pairs={{0,24},{8,16},{16,8},{24,0},{32,56},{40,48},{48,40},{56,32},{1,25}... | collective-permute-start | bytes 430088 | tf_op jit(solution)/shard_map/ppermute | solution.py:607
  62.8 0.7 collective-permute-start.12
  63.4 2.5 %collective-permute-start.13 = (bf16[560,128]{1,0:T(8,128)(2,1)}, bf16[560,128]{1,0:T(8,128)(2,1)S(1)}, u32[]{:S(2)}, u32[]{:S(2)}) collective-permute-start(bf16[560,128]{1,0:T(8,128)(2,1)} %get-tuple-element.38), channel_id=1, source_target_pairs={{0,40},{8,32},{16,56},{24,48},{32,8},{40,0},{48,24},{56,16},{1,41}... | collective-permute-start | bytes 430088 | tf_op jit(solution)/shard_map/ppermute | solution.py:607
  66.0 0.3 collective-permute-start.14
  66.3 1.6 %collective-permute-done.10.rest_10_ = bf16[560,128]{1,0:T(8,128)(2,1)S(1)} collective-permute-done((bf16[560,128]{1,0:T(8,128)(2,1)}, bf16[560,128]{1,0:T(8,128)(2,1)S(1)}, u32[]{:S(2)}, u32[]{:S(2)}) %collective-permute-start.10) | collective-permute-done | bytes 143392 | tf_op jit(solution)/shard_map/ppermute | solution.py:607
  67.8 1.2 collective-permute-start.15
  69.0 0.8 collective-permute-done.11.rest_11_
  69.8 4.0 %collective-permute-done.12.rest_12_ = bf16[560,128]{1,0:T(8,128)(2,1)S(1)} collective-permute-done((bf16[560,128]{1,0:T(8,128)(2,1)}, bf16[560,128]{1,0:T(8,128)(2,1)S(1)}, u32[]{:S(2)}, u32[]{:S(2)}) %collective-permute-start.12) | collective-permute-done | bytes 143392 | tf_op jit(solution)/shard_map/ppermute | solution.py:607
  73.8 2.0 %collective-permute-done.13.rest_13_ = bf16[560,128]{1,0:T(8,128)(2,1)S(1)} collective-permute-done((bf16[560,128]{1,0:T(8,128)(2,1)}, bf16[560,128]{1,0:T(8,128)(2,1)S(1)}, u32[]{:S(2)}, u32[]{:S(2)}) %collective-permute-start.13) | collective-permute-done | bytes 143392 | tf_op jit(solution)/shard_map/ppermute | solution.py:607
  75.8 3.6 %collective-permute-done.14.rest_14_ = bf16[560,128]{1,0:T(8,128)(2,1)S(1)} collective-permute-done((bf16[560,128]{1,0:T(8,128)(2,1)}, bf16[560,128]{1,0:T(8,128)(2,1)S(1)}, u32[]{:S(2)}, u32[]{:S(2)}) %collective-permute-start.14) | collective-permute-done | bytes 143392 | tf_op jit(solution)/shard_map/ppermute | solution.py:607
  79.4 2.7 %collective-permute-done.15.rest_15_ = bf16[560,128]{1,0:T(8,128)(2,1)S(1)} collective-permute-done((bf16[560,128]{1,0:T(8,128)(2,1)}, bf16[560,128]{1,0:T(8,128)(2,1)S(1)}, u32[]{:S(2)}, u32[]{:S(2)}) %collective-permute-start.15) | collective-permute-done | bytes 143392 | tf_op jit(solution)/shard_map/ppermute | solution.py:607
  82.1 0.6 copy-done.17
  82.7 8.9 %warp_sum.1 = (f32[432,128]{1,0:T(8,128)}, f32[72,128]{1,0:T(8,128)}) custom-call(s32[3]{0:T(128)} %pad_add_fusion.info, s32[16]{0:T(128)} %assign.1, bf16[288,112]{1,0:T(8,128)(2,1)} %constant.27.clone.zy, bf16[256,256]{1,0:T(8,128)(2,1)} %constant.28.clone.x0, bf16[256,256]{1,0:T(8,128)(2,1)} %constant.29.clone.x1, ...), custom_call_target="tpu_custom_call" | custom-call | tf_op jit(solution)/shard_map/warp_sum/pallas_call | solution.py:390
  91.7 0.8 convert_element_type.10
  92.5 4.2 %collective-permute-start.18 = (f16[72,128]{1,0:T(8,128)(2,1)S(1)}, f16[72,128]{1,0:T(8,128)(2,1)S(1)}, u32[]{:S(2)}, u32[]{:S(2)}) collective-permute-start(f16[72,128]{1,0:T(8,128)(2,1)S(1)} %convert_element_type.10), channel_id=1, source_target_pairs={{64,1},{65,2},{66,3},{67,4},{68,5},{69,6},{70,7},{1,64},{2,65},{3,... | collective-permute-start | bytes 55304 | tf_op jit(solution)/shard_map/ppermute | solution.py:618
  96.6 1.0 convert_element_type.9
  97.6 1.4 %collective-permute-done.18 = f16[72,128]{1,0:T(8,128)(2,1)S(1)} collective-permute-done((f16[72,128]{1,0:T(8,128)(2,1)S(1)}, f16[72,128]{1,0:T(8,128)(2,1)S(1)}, u32[]{:S(2)}, u32[]{:S(2)}) %collective-permute-start.18) | collective-permute-done | bytes 18464 | tf_op jit(solution)/shard_map/ppermute | solution.py:618
  99.0 0.1 collective-permute-start.20
  99.1 0.1 collective-permute-start.19
  99.2 5.0 %collective-permute-start.30 = (f16[504,128]{1,0:T(8,128)(2,1)S(1)}, f16[504,128]{1,0:T(8,128)(2,1)S(1)}, u32[]{:S(2)}, u32[]{:S(2)}) collective-permute-start(f16[504,128]{1,0:T(8,128)(2,1)S(1)} %pad_maximum_fusion), channel_id=1, source_target_pairs={{0,96},{8,104},{16,112},{24,120},{32,64},{40,72},{48,80},{56,88},{... | collective-permute-start | bytes 387080 | tf_op jit(solution)/shard_map/ppermute | solution.py:628
  104.2 0.1 collective-permute-start.28
  104.4 0.9 collective-permute-start.26
  105.3 2.9 %collective-permute-start.24 = (f16[504,128]{1,0:T(8,128)(2,1)S(1)}, f16[504,128]{1,0:T(8,128)(2,1)S(1)}, u32[]{:S(2)}, u32[]{:S(2)}) collective-permute-start(f16[504,128]{1,0:T(8,128)(2,1)S(1)} %pad_maximum_fusion), channel_id=1, source_target_pairs={{0,48},{8,56},{16,32},{24,40},{32,16},{40,24},{48,0},{56,8},{64,11... | collective-permute-start | bytes 387080 | tf_op jit(solution)/shard_map/ppermute | solution.py:628
  108.3 1.2 collective-permute-done.21
  109.6 2.0 %collective-permute-start.22 = (f16[504,128]{1,0:T(8,128)(2,1)S(1)}, f16[504,128]{1,0:T(8,128)(2,1)S(1)}, u32[]{:S(2)}, u32[]{:S(2)}) collective-permute-start(f16[504,128]{1,0:T(8,128)(2,1)S(1)} %pad_maximum_fusion), channel_id=1, source_target_pairs={{0,32},{8,40},{16,48},{24,56},{32,0},{40,8},{48,16},{56,24},{64,96... | collective-permute-start | bytes 387080 | tf_op jit(solution)/shard_map/ppermute | solution.py:628
  111.6 2.1 %collective-permute-start.32 = (f16[504,128]{1,0:T(8,128)(2,1)S(1)}, f16[504,128]{1,0:T(8,128)(2,1)S(1)}, u32[]{:S(2)}, u32[]{:S(2)}) collective-permute-start(f16[504,128]{1,0:T(8,128)(2,1)S(1)} %pad_maximum_fusion), channel_id=1, source_target_pairs={{0,112},{8,120},{16,96},{24,104},{32,80},{40,88},{48,64},{56,72},{... | collective-permute-start | bytes 387080 | tf_op jit(solution)/shard_map/ppermute | solution.py:628
  113.6 3.0 %collective-permute-done.22 = f16[504,128]{1,0:T(8,128)(2,1)S(1)} collective-permute-done((f16[504,128]{1,0:T(8,128)(2,1)S(1)}, f16[504,128]{1,0:T(8,128)(2,1)S(1)}, u32[]{:S(2)}, u32[]{:S(2)}) %collective-permute-start.22) | collective-permute-done | bytes 129056 | tf_op jit(solution)/shard_map/ppermute | solution.py:628
  116.7 0.6 collective-permute-start.31
  117.3 0.3 collective-permute-start.29
  117.6 0.2 collective-permute-start.27
  117.8 2.5 %collective-permute-done.32 = f16[504,128]{1,0:T(8,128)(2,1)S(1)} collective-permute-done((f16[504,128]{1,0:T(8,128)(2,1)S(1)}, f16[504,128]{1,0:T(8,128)(2,1)S(1)}, u32[]{:S(2)}, u32[]{:S(2)}) %collective-permute-start.32) | collective-permute-done | bytes 129056 | tf_op jit(solution)/shard_map/ppermute | solution.py:628
  120.3 0.5 collective-permute-start.33
  121.0 0.7 collective-permute-done.25
  122.2 2.2 %convert_element_type.11.source = f32[16,504,128]{2,1,0:T(8,128)} convert(f16[16,504,128]{2,1,0:T(8,128)(2,1)S(1)} %bitcast_dynamic-update-slice_fusion) | non-fusion elementwise | flops 1032192 | bytes 6193152 | tf_op jit(solution)/shard_map/convert_element_type | solution.py:630
  124.4 11.3 %relax.1 = f32[24,192,192]{2,1,0:T(8,128)} custom-call(s32[3]{0:T(128)} %pad_add_fusion.info, f32[16,504,128]{2,1,0:T(8,128)} %convert_element_type.11.source), custom_call_target="tpu_custom_call" | custom-call | tf_op jit(solution)/shard_map/relax/pallas_call | solution.py:563
  (67 shorter events, 0.9 us)
Async XLA Ops:
  4.4 9.6 %collective-permute-start = (bf16[12,80,128]{2,1,0:T(8,128)(2,1)}, bf16[12,80,128]{2,1,0:T(8,128)(2,1)S(1)}, u32[]{:S(2)}, u32[]{:S(2)}) collective-permute-start(bf16[12,80,128]{2,1,0:T(8,128)(2,1)} %get-tuple-element.26), channel_id=1, source_target_pairs={{0,8},{8,0},{16,24},{24,16},{32,40},{40,32},{48,56},{56,48},{1,9},... | collective-permute-start | bytes 737288 | tf_op jit(solution)/shard_map/ppermute | solution.py:607
  4.5 14.7 %collective-permute-start.1 = (bf16[12,80,128]{2,1,0:T(8,128)(2,1)}, bf16[12,80,128]{2,1,0:T(8,128)(2,1)S(1)}, u32[]{:S(2)}, u32[]{:S(2)}) collective-permute-start(bf16[12,80,128]{2,1,0:T(8,128)(2,1)} %get-tuple-element.27), channel_id=1, source_target_pairs={{0,16},{8,24},{16,0},{24,8},{32,48},{40,56},{48,32},{56,40},{1,17}... | collective-permute-start | bytes 737288 | tf_op jit(solution)/shard_map/ppermute | solution.py:607
  6.2 13.1 %collective-permute-start.2 = (bf16[12,80,128]{2,1,0:T(8,128)(2,1)}, bf16[12,80,128]{2,1,0:T(8,128)(2,1)S(1)}, u32[]{:S(2)}, u32[]{:S(2)}) collective-permute-start(bf16[12,80,128]{2,1,0:T(8,128)(2,1)} %get-tuple-element.28), channel_id=1, source_target_pairs={{0,24},{8,16},{16,8},{24,0},{32,56},{40,48},{48,40},{56,32},{1,25}... | collective-permute-start | bytes 737288 | tf_op jit(solution)/shard_map/ppermute | solution.py:607
  6.4 20.4 %collective-permute-start.3 = (bf16[12,80,128]{2,1,0:T(8,128)(2,1)}, bf16[12,80,128]{2,1,0:T(8,128)(2,1)S(1)}, u32[]{:S(2)}, u32[]{:S(2)}) collective-permute-start(bf16[12,80,128]{2,1,0:T(8,128)(2,1)} %get-tuple-element.29), channel_id=1, source_target_pairs={{0,32},{8,40},{16,48},{24,56},{32,0},{40,8},{48,16},{56,24},{1,33}... | collective-permute-start | bytes 737288 | tf_op jit(solution)/shard_map/ppermute | solution.py:607
  10.8 39.4 %collective-permute-start.8 = (f32[1,3,3,96,96]{4,3,2,1,0:T(8,128)S(1)}, f32[1,3,3,96,96]{4,3,2,1,0:T(8,128)S(1)}, u32[]{:S(2)}, u32[]{:S(2)}) collective-permute-start(f32[1,3,3,96,96]{4,3,2,1,0:T(8,128)S(1)} %get-tuple-element.45), channel_id=1, source_target_pairs={{64,1},{65,2},{66,3},{67,4},{68,5},{69,6},{70,7},{1,64},{2,65},{3,... | collective-permute-start | bytes 995336 | tf_op jit(solution)/shard_map/ppermute | solution.py:602
  14.0 27.8 %copy-start = (bf16[12,80,128]{2,1,0:T(8,128)(2,1)}, bf16[12,80,128]{2,1,0:T(8,128)(2,1)S(1)}, u32[]{:S(2)}) copy-start(bf16[12,80,128]{2,1,0:T(8,128)(2,1)S(1)} %collective-permute-done.refs_1_.rest_1_) | copy-start | bytes 737284
  14.0 36.2 %collective-permute-start.7 = (f32[1,3,3,96,96]{4,3,2,1,0:T(8,128)S(1)}, f32[1,3,3,96,96]{4,3,2,1,0:T(8,128)S(1)}, u32[]{:S(2)}, u32[]{:S(2)}) collective-permute-start(f32[1,3,3,96,96]{4,3,2,1,0:T(8,128)S(1)} %get-tuple-element.46), channel_id=1, source_target_pairs={{0,1},{1,2},{2,3},{3,4},{4,5},{5,6},{6,7},{65,64},{66,65},{67,66},... | collective-permute-start | bytes 995336 | tf_op jit(solution)/shard_map/ppermute | solution.py:601
  19.2 22.6 %copy-start.1 = (bf16[12,80,128]{2,1,0:T(8,128)(2,1)}, bf16[12,80,128]{2,1,0:T(8,128)(2,1)S(1)}, u32[]{:S(2)}) copy-start(bf16[12,80,128]{2,1,0:T(8,128)(2,1)S(1)} %collective-permute-done.1.refs_2_.rest_2_) | copy-start | bytes 737284
  19.2 11.7 %collective-permute-start.4 = (bf16[12,80,128]{2,1,0:T(8,128)(2,1)}, bf16[12,80,128]{2,1,0:T(8,128)(2,1)S(1)}, u32[]{:S(2)}, u32[]{:S(2)}) collective-permute-start(bf16[12,80,128]{2,1,0:T(8,128)(2,1)} %get-tuple-element.30), channel_id=1, source_target_pairs={{0,40},{8,32},{16,56},{24,48},{32,8},{40,0},{48,24},{56,16},{1,41}... | collective-permute-start | bytes 737288 | tf_op jit(solution)/shard_map/ppermute | solution.py:607
  19.3 22.5 %copy-start.2 = (bf16[12,80,128]{2,1,0:T(8,128)(2,1)}, bf16[12,80,128]{2,1,0:T(8,128)(2,1)S(1)}, u32[]{:S(2)}) copy-start(bf16[12,80,128]{2,1,0:T(8,128)(2,1)S(1)} %collective-permute-done.2.refs_3_.rest_3_) | copy-start | bytes 737284
  19.3 17.3 %collective-permute-start.5 = (bf16[12,80,128]{2,1,0:T(8,128)(2,1)}, bf16[12,80,128]{2,1,0:T(8,128)(2,1)S(1)}, u32[]{:S(2)}, u32[]{:S(2)}) collective-permute-start(bf16[12,80,128]{2,1,0:T(8,128)(2,1)} %get-tuple-element.31), channel_id=1, source_target_pairs={{0,48},{8,56},{16,32},{24,40},{32,16},{40,24},{48,0},{56,8},{1,49}... | collective-permute-start | bytes 737288 | tf_op jit(solution)/shard_map/ppermute | solution.py:607
  26.7 15.1 %copy-start.3 = (bf16[12,80,128]{2,1,0:T(8,128)(2,1)}, bf16[12,80,128]{2,1,0:T(8,128)(2,1)S(1)}, u32[]{:S(2)}) copy-start(bf16[12,80,128]{2,1,0:T(8,128)(2,1)S(1)} %collective-permute-done.3.refs_4_.rest_4_) | copy-start | bytes 737284
  26.7 15.1 %collective-permute-start.6 = (bf16[12,80,128]{2,1,0:T(8,128)(2,1)}, bf16[12,80,128]{2,1,0:T(8,128)(2,1)S(1)}, u32[]{:S(2)}, u32[]{:S(2)}) collective-permute-start(bf16[12,80,128]{2,1,0:T(8,128)(2,1)} %get-tuple-element.32), channel_id=1, source_target_pairs={{0,56},{8,48},{16,40},{24,32},{32,24},{40,16},{48,8},{56,0},{1,57}... | collective-permute-start | bytes 737288 | tf_op jit(solution)/shard_map/ppermute | solution.py:607
  30.9 11.0 %copy-start.4 = (bf16[12,80,128]{2,1,0:T(8,128)(2,1)}, bf16[12,80,128]{2,1,0:T(8,128)(2,1)S(1)}, u32[]{:S(2)}) copy-start(bf16[12,80,128]{2,1,0:T(8,128)(2,1)S(1)} %collective-permute-done.4.refs_5_.rest_5_) | copy-start | bytes 737284
  36.7 5.2 %copy-start.5 = (bf16[12,80,128]{2,1,0:T(8,128)(2,1)}, bf16[12,80,128]{2,1,0:T(8,128)(2,1)S(1)}, u32[]{:S(2)}) copy-start(bf16[12,80,128]{2,1,0:T(8,128)(2,1)S(1)} %collective-permute-done.5.refs_6_.rest_6_) | copy-start | bytes 737284
  41.8 0.7 copy-start.6
  44.3 18.4 %collective-permute-start.16 = (bf16[8,80,128]{2,1,0:T(8,128)(2,1)}, bf16[8,80,128]{2,1,0:T(8,128)(2,1)S(1)}, u32[]{:S(2)}, u32[]{:S(2)}) collective-permute-start(bf16[8,80,128]{2,1,0:T(8,128)(2,1)} %get-tuple-element.41), channel_id=1, source_target_pairs={{0,64},{1,65},{2,66},{3,67},{4,68},{5,69},{6,70},{7,71},{64,1},{65... | collective-permute-start | bytes 491528 | tf_op jit(solution)/shard_map/ppermute | solution.py:615
  47.6 15.8 %collective-permute-start.17 = (bf16[8,80,128]{2,1,0:T(8,128)(2,1)}, bf16[8,80,128]{2,1,0:T(8,128)(2,1)S(1)}, u32[]{:S(2)}, u32[]{:S(2)}) collective-permute-start(bf16[8,80,128]{2,1,0:T(8,128)(2,1)} %get-tuple-element.42), channel_id=1, source_target_pairs={{64,0},{65,1},{66,2},{67,3},{68,4},{69,5},{70,6},{71,7},{1,64},{2,... | collective-permute-start | bytes 491528 | tf_op jit(solution)/shard_map/ppermute | solution.py:616
  50.2 0.8 copy-start.7
  51.0 0.8 copy-start.8
  60.8 5.2 %collective-permute-start.9 = (bf16[560,128]{1,0:T(8,128)(2,1)}, bf16[560,128]{1,0:T(8,128)(2,1)S(1)}, u32[]{:S(2)}, u32[]{:S(2)}) collective-permute-start(bf16[560,128]{1,0:T(8,128)(2,1)} %get-tuple-element.34), channel_id=1, source_target_pairs={{0,8},{8,0},{16,24},{24,16},{32,40},{40,32},{48,56},{56,48},{1,9},... | collective-permute-start | bytes 430088 | tf_op jit(solution)/shard_map/ppermute | solution.py:607
  60.9 6.9 %collective-permute-start.10 = (bf16[560,128]{1,0:T(8,128)(2,1)}, bf16[560,128]{1,0:T(8,128)(2,1)S(1)}, u32[]{:S(2)}, u32[]{:S(2)}) collective-permute-start(bf16[560,128]{1,0:T(8,128)(2,1)} %get-tuple-element.35), channel_id=1, source_target_pairs={{0,16},{8,24},{16,0},{24,8},{32,48},{40,56},{48,32},{56,40},{1,17}... | collective-permute-start | bytes 430088 | tf_op jit(solution)/shard_map/ppermute | solution.py:607
  61.2 8.6 %collective-permute-start.11 = (bf16[560,128]{1,0:T(8,128)(2,1)}, bf16[560,128]{1,0:T(8,128)(2,1)S(1)}, u32[]{:S(2)}, u32[]{:S(2)}) collective-permute-start(bf16[560,128]{1,0:T(8,128)(2,1)} %get-tuple-element.36), channel_id=1, source_target_pairs={{0,24},{8,16},{16,8},{24,0},{32,56},{40,48},{48,40},{56,32},{1,25}... | collective-permute-start | bytes 430088 | tf_op jit(solution)/shard_map/ppermute | solution.py:607
  62.8 19.3 %copy-start.9 = (bf16[8,80,128]{2,1,0:T(8,128)(2,1)}, bf16[8,80,128]{2,1,0:T(8,128)(2,1)S(1)}, u32[]{:S(2)}) copy-start(bf16[8,80,128]{2,1,0:T(8,128)(2,1)S(1)} %collective-permute-done.16.rest_16_) | copy-start | bytes 491524
  62.8 11.0 %collective-permute-start.12 = (bf16[560,128]{1,0:T(8,128)(2,1)}, bf16[560,128]{1,0:T(8,128)(2,1)S(1)}, u32[]{:S(2)}, u32[]{:S(2)}) collective-permute-start(bf16[560,128]{1,0:T(8,128)(2,1)} %get-tuple-element.37), channel_id=1, source_target_pairs={{0,32},{8,40},{16,48},{24,56},{32,0},{40,8},{48,16},{56,24},{1,33}... | collective-permute-start | bytes 430088 | tf_op jit(solution)/shard_map/ppermute | solution.py:607
  63.4 18.6 %copy-start.10 = (bf16[8,80,128]{2,1,0:T(8,128)(2,1)}, bf16[8,80,128]{2,1,0:T(8,128)(2,1)S(1)}, u32[]{:S(2)}) copy-start(bf16[8,80,128]{2,1,0:T(8,128)(2,1)S(1)} %collective-permute-done.17.rest_17_) | copy-start | bytes 491524
  63.4 12.3 %collective-permute-start.13 = (bf16[560,128]{1,0:T(8,128)(2,1)}, bf16[560,128]{1,0:T(8,128)(2,1)S(1)}, u32[]{:S(2)}, u32[]{:S(2)}) collective-permute-start(bf16[560,128]{1,0:T(8,128)(2,1)} %get-tuple-element.38), channel_id=1, source_target_pairs={{0,40},{8,32},{16,56},{24,48},{32,8},{40,0},{48,24},{56,16},{1,41}... | collective-permute-start | bytes 430088 | tf_op jit(solution)/shard_map/ppermute | solution.py:607
  66.0 16.1 %copy-start.11 = (bf16[560,128]{1,0:T(8,128)(2,1)}, bf16[560,128]{1,0:T(8,128)(2,1)S(1)}, u32[]{:S(2)}) copy-start(bf16[560,128]{1,0:T(8,128)(2,1)S(1)} %collective-permute-done.9.rest_9_) | copy-start | bytes 430084
  66.0 13.4 %collective-permute-start.14 = (bf16[560,128]{1,0:T(8,128)(2,1)}, bf16[560,128]{1,0:T(8,128)(2,1)S(1)}, u32[]{:S(2)}, u32[]{:S(2)}) collective-permute-start(bf16[560,128]{1,0:T(8,128)(2,1)} %get-tuple-element.39), channel_id=1, source_target_pairs={{0,48},{8,56},{16,32},{24,40},{32,16},{40,24},{48,0},{56,8},{1,49}... | collective-permute-start | bytes 430088 | tf_op jit(solution)/shard_map/ppermute | solution.py:607
  67.8 14.3 %copy-start.12 = (bf16[560,128]{1,0:T(8,128)(2,1)}, bf16[560,128]{1,0:T(8,128)(2,1)S(1)}, u32[]{:S(2)}) copy-start(bf16[560,128]{1,0:T(8,128)(2,1)S(1)} %collective-permute-done.10.rest_10_) | copy-start | bytes 430084
  67.8 14.2 %collective-permute-start.15 = (bf16[560,128]{1,0:T(8,128)(2,1)}, bf16[560,128]{1,0:T(8,128)(2,1)S(1)}, u32[]{:S(2)}, u32[]{:S(2)}) collective-permute-start(bf16[560,128]{1,0:T(8,128)(2,1)} %get-tuple-element.40), channel_id=1, source_target_pairs={{0,56},{8,48},{16,40},{24,32},{32,24},{40,16},{48,8},{56,0},{1,57}... | collective-permute-start | bytes 430088 | tf_op jit(solution)/shard_map/ppermute | solution.py:607
  69.8 12.3 %copy-start.13 = (bf16[560,128]{1,0:T(8,128)(2,1)}, bf16[560,128]{1,0:T(8,128)(2,1)S(1)}, u32[]{:S(2)}) copy-start(bf16[560,128]{1,0:T(8,128)(2,1)S(1)} %collective-permute-done.11.rest_11_) | copy-start | bytes 430084
  73.8 8.3 %copy-start.14 = (bf16[560,128]{1,0:T(8,128)(2,1)}, bf16[560,128]{1,0:T(8,128)(2,1)S(1)}, u32[]{:S(2)}) copy-start(bf16[560,128]{1,0:T(8,128)(2,1)S(1)} %collective-permute-done.12.rest_12_) | copy-start | bytes 430084
  75.8 6.4 %copy-start.15 = (bf16[560,128]{1,0:T(8,128)(2,1)}, bf16[560,128]{1,0:T(8,128)(2,1)S(1)}, u32[]{:S(2)}) copy-start(bf16[560,128]{1,0:T(8,128)(2,1)S(1)} %collective-permute-done.13.rest_13_) | copy-start | bytes 430084
  79.4 2.7 %copy-start.16 = (bf16[560,128]{1,0:T(8,128)(2,1)}, bf16[560,128]{1,0:T(8,128)(2,1)S(1)}, u32[]{:S(2)}) copy-start(bf16[560,128]{1,0:T(8,128)(2,1)S(1)} %collective-permute-done.14.rest_14_) | copy-start | bytes 430084
  82.1 0.7 copy-start.17
  92.5 6.5 %collective-permute-start.18 = (f16[72,128]{1,0:T(8,128)(2,1)S(1)}, f16[72,128]{1,0:T(8,128)(2,1)S(1)}, u32[]{:S(2)}, u32[]{:S(2)}) collective-permute-start(f16[72,128]{1,0:T(8,128)(2,1)S(1)} %convert_element_type.10), channel_id=1, source_target_pairs={{64,1},{65,2},{66,3},{67,4},{68,5},{69,6},{70,7},{1,64},{2,65},{3,... | collective-permute-start | bytes 55304 | tf_op jit(solution)/shard_map/ppermute | solution.py:618
  99.0 6.3 %collective-permute-start.20 = (f16[504,128]{1,0:T(8,128)(2,1)S(1)}, f16[504,128]{1,0:T(8,128)(2,1)S(1)}, u32[]{:S(2)}, u32[]{:S(2)}) collective-permute-start(f16[504,128]{1,0:T(8,128)(2,1)S(1)} %pad_maximum_fusion), channel_id=1, source_target_pairs={{0,16},{8,24},{16,0},{24,8},{32,48},{40,56},{48,32},{56,40},{64,80... | collective-permute-start | bytes 387080 | tf_op jit(solution)/shard_map/ppermute | solution.py:628
  99.1 9.1 %collective-permute-start.19 = (f16[504,128]{1,0:T(8,128)(2,1)S(1)}, f16[504,128]{1,0:T(8,128)(2,1)S(1)}, u32[]{:S(2)}, u32[]{:S(2)}) collective-permute-start(f16[504,128]{1,0:T(8,128)(2,1)S(1)} %pad_maximum_fusion), channel_id=1, source_target_pairs={{0,8},{8,0},{16,24},{24,16},{32,40},{40,32},{48,56},{56,48},{1,9},... | collective-permute-start | bytes 387080 | tf_op jit(solution)/shard_map/ppermute | solution.py:629
  99.2 12.4 %collective-permute-start.30 = (f16[504,128]{1,0:T(8,128)(2,1)S(1)}, f16[504,128]{1,0:T(8,128)(2,1)S(1)}, u32[]{:S(2)}, u32[]{:S(2)}) collective-permute-start(f16[504,128]{1,0:T(8,128)(2,1)S(1)} %pad_maximum_fusion), channel_id=1, source_target_pairs={{0,96},{8,104},{16,112},{24,120},{32,64},{40,72},{48,80},{56,88},{... | collective-permute-start | bytes 387080 | tf_op jit(solution)/shard_map/ppermute | solution.py:628
  104.2 12.4 %collective-permute-start.28 = (f16[504,128]{1,0:T(8,128)(2,1)S(1)}, f16[504,128]{1,0:T(8,128)(2,1)S(1)}, u32[]{:S(2)}, u32[]{:S(2)}) collective-permute-start(f16[504,128]{1,0:T(8,128)(2,1)S(1)} %pad_maximum_fusion), channel_id=1, source_target_pairs={{0,80},{8,88},{16,64},{24,72},{32,112},{40,120},{48,96},{56,104},{... | collective-permute-start | bytes 387080 | tf_op jit(solution)/shard_map/ppermute | solution.py:628
  104.4 12.9 %collective-permute-start.26 = (f16[504,128]{1,0:T(8,128)(2,1)S(1)}, f16[504,128]{1,0:T(8,128)(2,1)S(1)}, u32[]{:S(2)}, u32[]{:S(2)}) collective-permute-start(f16[504,128]{1,0:T(8,128)(2,1)S(1)} %pad_maximum_fusion), channel_id=1, source_target_pairs={{0,64},{8,72},{16,80},{24,88},{32,96},{40,104},{48,112},{56,120},{... | collective-permute-start | bytes 387080 | tf_op jit(solution)/shard_map/ppermute | solution.py:628
  105.3 12.2 %collective-permute-start.24 = (f16[504,128]{1,0:T(8,128)(2,1)S(1)}, f16[504,128]{1,0:T(8,128)(2,1)S(1)}, u32[]{:S(2)}, u32[]{:S(2)}) collective-permute-start(f16[504,128]{1,0:T(8,128)(2,1)S(1)} %pad_maximum_fusion), channel_id=1, source_target_pairs={{0,48},{8,56},{16,32},{24,40},{32,16},{40,24},{48,0},{56,8},{64,11... | collective-permute-start | bytes 387080 | tf_op jit(solution)/shard_map/ppermute | solution.py:628
  108.2 1.3 collective-permute-start.21
  109.6 7.1 %collective-permute-start.22 = (f16[504,128]{1,0:T(8,128)(2,1)S(1)}, f16[504,128]{1,0:T(8,128)(2,1)S(1)}, u32[]{:S(2)}, u32[]{:S(2)}) collective-permute-start(f16[504,128]{1,0:T(8,128)(2,1)S(1)} %pad_maximum_fusion), channel_id=1, source_target_pairs={{0,32},{8,40},{16,48},{24,56},{32,0},{40,8},{48,16},{56,24},{64,96... | collective-permute-start | bytes 387080 | tf_op jit(solution)/shard_map/ppermute | solution.py:628
  111.6 8.7 %collective-permute-start.32 = (f16[504,128]{1,0:T(8,128)(2,1)S(1)}, f16[504,128]{1,0:T(8,128)(2,1)S(1)}, u32[]{:S(2)}, u32[]{:S(2)}) collective-permute-start(f16[504,128]{1,0:T(8,128)(2,1)S(1)} %pad_maximum_fusion), channel_id=1, source_target_pairs={{0,112},{8,120},{16,96},{24,104},{32,80},{40,88},{48,64},{56,72},{... | collective-permute-start | bytes 387080 | tf_op jit(solution)/shard_map/ppermute | solution.py:628
  116.6 3.7 %collective-permute-start.23 = (f16[504,128]{1,0:T(8,128)(2,1)S(1)}, f16[504,128]{1,0:T(8,128)(2,1)S(1)}, u32[]{:S(2)}, u32[]{:S(2)}) collective-permute-start(f16[504,128]{1,0:T(8,128)(2,1)S(1)} %collective-permute-done.22), channel_id=1, source_target_pairs={{0,8},{8,0},{16,24},{24,16},{32,40},{40,32},{48,56},{56,48},{1,9},... | collective-permute-start | bytes 387080 | tf_op jit(solution)/shard_map/ppermute | solution.py:629
  116.7 5.3 %collective-permute-start.31 = (f16[504,128]{1,0:T(8,128)(2,1)S(1)}, f16[504,128]{1,0:T(8,128)(2,1)S(1)}, u32[]{:S(2)}, u32[]{:S(2)}) collective-permute-start(f16[504,128]{1,0:T(8,128)(2,1)S(1)} %collective-permute-done.30), channel_id=1, source_target_pairs={{0,8},{8,0},{16,24},{24,16},{32,40},{40,32},{48,56},{56,48},{1,9},... | collective-permute-start | bytes 387080 | tf_op jit(solution)/shard_map/ppermute | solution.py:629
  117.3 4.6 %collective-permute-start.29 = (f16[504,128]{1,0:T(8,128)(2,1)S(1)}, f16[504,128]{1,0:T(8,128)(2,1)S(1)}, u32[]{:S(2)}, u32[]{:S(2)}) collective-permute-start(f16[504,128]{1,0:T(8,128)(2,1)S(1)} %collective-permute-done.28), channel_id=1, source_target_pairs={{0,8},{8,0},{16,24},{24,16},{32,40},{40,32},{48,56},{56,48},{1,9},... | collective-permute-start | bytes 387080 | tf_op jit(solution)/shard_map/ppermute | solution.py:629
  117.6 4.2 %collective-permute-start.27 = (f16[504,128]{1,0:T(8,128)(2,1)S(1)}, f16[504,128]{1,0:T(8,128)(2,1)S(1)}, u32[]{:S(2)}, u32[]{:S(2)}) collective-permute-start(f16[504,128]{1,0:T(8,128)(2,1)S(1)} %collective-permute-done.26), channel_id=1, source_target_pairs={{0,8},{8,0},{16,24},{24,16},{32,40},{40,32},{48,56},{56,48},{1,9},... | collective-permute-start | bytes 387080 | tf_op jit(solution)/shard_map/ppermute | solution.py:629
  120.3 1.3 collective-permute-start.25
  120.3 1.7 %collective-permute-start.33 = (f16[504,128]{1,0:T(8,128)(2,1)S(1)}, f16[504,128]{1,0:T(8,128)(2,1)S(1)}, u32[]{:S(2)}, u32[]{:S(2)}) collective-permute-start(f16[504,128]{1,0:T(8,128)(2,1)S(1)} %collective-permute-done.32), channel_id=1, source_target_pairs={{0,8},{8,0},{16,24},{24,16},{32,40},{40,32},{48,56},{56,48},{1,9},... | collective-permute-start | bytes 387080 | tf_op jit(solution)/shard_map/ppermute | solution.py:629
